TPU v7x, 128 devices: a whole 4x4x4 slice. The times are simulated.
128 devices in a mesh: slab: 16 (over y, x_lo, core), lat: 8 (over x_hi, z).
Axes of the slice: x: 4 (x_hi: 2, x_lo: 2; x = x_hi * 2 + x_lo), y: 4, z: 4, core: 2. Of those that a mesh axis runs over, the one named last changes fastest.
Arguments:
- nodes: bfloat16 [16384, 512], P('slab', 'lat')
- edges: bfloat16 [65536, 512], P(('slab', 'lat'))
- edge_tiles: int32 [2, 512], P(None, ('slab', 'lat')), may hold values from 0 to 11, as said below
- edge_offsets: int32 [2, 65536], P(None, ('slab', 'lat')), may hold values from 0 to 127
- tile_counts: int32 [16], P('slab'), may hold values from 10 to 32, as said below
- halo_blocks: int32 [16, 2, 2], P('slab'), may hold values from 0 to 7
- w_edge_in: bfloat16 [1536, 512], P(('slab', 'lat')), may hold values from -0.15625 to 0.15625
- w_edge_out: bfloat16 [512, 512], P(('slab', 'lat'))
- w_node_in: bfloat16 [1024, 512], P(('slab', 'lat')), may hold values from -0.1875 to 0.1875
- w_node_out: bfloat16 [512, 512], P(('slab', 'lat'))
- edge_gain: float32 [512], replicated, may hold values from 0.1 to 1.9
- node_gain: float32 [512], replicated, may hold values from 0.1 to 1.9
- node_cotangent: bfloat16 [16384, 512], P('slab', 'lat'), may hold values from -6 to 6
- edge_cotangent: bfloat16 [65536, 512], P(('slab', 'lat')), may hold values from -6 to 6
Outputs:
- new_nodes: bfloat16 [16384, 512], P('slab', 'lat')
- new_edges: bfloat16 [65536, 512], P(('slab', 'lat'))
- grad_nodes: bfloat16 [16384, 512], P('slab', 'lat')
- grad_edges: bfloat16 [65536, 512], P(('slab', 'lat'))
- grad_edge_in: float32 [1536, 512], P(('slab', 'lat'))
- grad_edge_out: float32 [512, 512], P(('slab', 'lat'))
- grad_node_in: float32 [1024, 512], P(('slab', 'lat'))
- grad_node_out: float32 [512, 512], P(('slab', 'lat'))
Inputs may be any that keep to these rules, and one draw needn't show every extreme that they name: `edge_tiles`: row 0 names each tile's receiver block among its slab's 8 blocks; row 1 its sender block among the 12 blocks of the extended slab (2 received from below, the slab's own, 2 received from above). Tiles of the first slab never name the blocks from below, tiles of the last slab never those from above. `tile_counts`: live tiles are the first ones of the slab's 32 slots; in every draw some slab has all slots live.
All inputs are finite; a program needn't handle non-finite values.
Results may differ from a plain program's by a relative error of at most 0.03.
The roundings to bfloat16 on the way count: a program that leaves them out, or rounds other values in their place, can miss the bound.
Values may be sent and summed in bfloat16 or wider, within the bound.
No kernel may reach another device: no remote copies, remote signals or barrier semaphores. Data moves between devices by JAX's collectives and lax.ppermute only.
A program may use at most 64 MiB of HBM per device.

v0:
```python
import jax
import jax.numpy as jnp
from jax import lax
from jax.sharding import PartitionSpec as P

L = 512
BLK = 128
HB = 2


EPSILON = 1e-05


def from_behind(value, axis, steps):
    count = lax.axis_size(axis)
    first, last = (max(0, -steps), min(count, count - steps))
    return lax.ppermute(value, axis, [(source, source + steps) for source in range(first, last)])


def layer_norm(values, gain_vector):
    average = jnp.mean(values, axis=-1, keepdims=True)
    centred = values - average
    variance = jnp.mean(centred * centred, axis=-1, keepdims=True)
    inverse = lax.rsqrt(variance + EPSILON)
    normed = centred * inverse
    return (normed * gain_vector, normed, inverse)


def norm_back(upstream, normed, inverse, gain_vector):
    scaled = upstream * gain_vector
    return inverse * (
        scaled
        - jnp.mean(scaled, axis=-1, keepdims=True)
        - normed * jnp.mean(scaled * normed, axis=-1, keepdims=True)
    )


def contract_rows(left, right):
    return lax.dot_general(
        left, right, (((0,), (0,)), ((), ())), preferred_element_type=jnp.float32
    )


def times_transpose(left, weight):
    return lax.dot_general(
        left, weight, (((1,), (1,)), ((), ())), preferred_element_type=jnp.float32
    )


def pick_blocks(source_table, blocks):
    width = source_table.shape[1]
    return jnp.take(source_table.reshape(-1, BLK, width), blocks, axis=0).reshape(-1, width)


def add_blocks(source_table, blocks, values):
    width = source_table.shape[1]
    shaped = source_table.reshape(-1, BLK, width).at[blocks].add(values.reshape(-1, BLK, width))
    return shaped.reshape(-1, width)


def per_device(
    nodes,
    edges,
    edge_tiles,
    edge_offsets,
    tile_counts,
    halo_blocks,
    w_edge_in,
    w_edge_out,
    w_node_in,
    w_node_out,
    edge_gain,
    node_gain,
    node_cotangent,
    edge_cotangent,
):
    lat_size = lax.axis_size("lat")
    lat_index = lax.axis_index("lat")
    slab_rows = nodes.shape[0]
    own_rows = slab_rows // lat_size
    halo_rows = HB * BLK
    edge_in, edge_out, node_in, node_out = (
        lax.all_gather(w_edge_in, ("slab", "lat"), axis=0, tiled=True),
        lax.all_gather(w_edge_out, ("slab", "lat"), axis=0, tiled=True),
        lax.all_gather(w_node_in, ("slab", "lat"), axis=0, tiled=True),
        lax.all_gather(w_node_out, ("slab", "lat"), axis=0, tiled=True),
    )
    up_list = halo_blocks[0, 0]
    down_list = halo_blocks[0, 1]
    slab_full = lax.all_gather(nodes, "lat", axis=1, tiled=True)
    from_lower = from_behind(pick_blocks(slab_full, up_list), "slab", 1)
    from_upper = from_behind(pick_blocks(slab_full, down_list), "slab", -1)
    extended = jnp.concatenate([from_lower, slab_full, from_upper], axis=0)
    tile_slots = edge_tiles.shape[1]
    tile_of = jnp.arange(edges.shape[0], dtype=jnp.int32) // BLK
    dst_row = edge_tiles[0][tile_of] * BLK + edge_offsets[0]
    src_row = edge_tiles[1][tile_of] * BLK + edge_offsets[1]
    live_mask = (lat_index * tile_slots + tile_of < tile_counts[0]).astype(jnp.float32)[:, None]
    joined = jnp.concatenate([edges, extended[src_row], slab_full[dst_row]], axis=1)
    edge_first = jax.nn.relu(jnp.dot(joined, edge_in, preferred_element_type=jnp.float32)).astype(
        jnp.bfloat16
    )
    edge_second = jnp.dot(edge_first, edge_out, preferred_element_type=jnp.float32)
    edge_update, edge_normed, edge_inverse = layer_norm(edge_second, edge_gain)
    message = edge_update * live_mask
    new_edges = (edges.astype(jnp.float32) + message).astype(jnp.bfloat16)
    partial_sums = jnp.zeros((slab_rows, L), jnp.float32).at[dst_row].add(message)
    aggregated = lax.psum_scatter(partial_sums, "lat", scatter_dimension=0, tiled=True).astype(
        jnp.bfloat16
    )
    row_start = lat_index * own_rows
    own_latents = lax.dynamic_slice_in_dim(slab_full, row_start, own_rows, 0)
    node_joined = jnp.concatenate([own_latents, aggregated], axis=1)
    node_first = jax.nn.relu(
        jnp.dot(node_joined, node_in, preferred_element_type=jnp.float32)
    ).astype(jnp.bfloat16)
    node_second = jnp.dot(node_first, node_out, preferred_element_type=jnp.float32)
    node_update, node_normed, node_inverse = layer_norm(node_second, node_gain)
    new_rows = (own_latents.astype(jnp.float32) + node_update).astype(jnp.bfloat16)
    new_nodes = lax.all_to_all(new_rows, "lat", split_axis=1, concat_axis=0, tiled=True)
    edge_in, edge_out, node_in, node_out = (
        lax.all_gather(w_edge_in, ("slab", "lat"), axis=0, tiled=True),
        lax.all_gather(w_edge_out, ("slab", "lat"), axis=0, tiled=True),
        lax.all_gather(w_node_in, ("slab", "lat"), axis=0, tiled=True),
        lax.all_gather(w_node_out, ("slab", "lat"), axis=0, tiled=True),
    )
    node_upstream = lax.all_to_all(
        node_cotangent, "lat", split_axis=0, concat_axis=1, tiled=True
    ).astype(jnp.float32)
    d_node_second = norm_back(node_upstream, node_normed, node_inverse, node_gain).astype(
        jnp.bfloat16
    )
    g_node_out = contract_rows(node_first, d_node_second)
    d_node_first = (times_transpose(d_node_second, node_out) * (node_first > 0)).astype(
        jnp.bfloat16
    )
    g_node_in = contract_rows(node_joined, d_node_first)
    d_node_joined = times_transpose(d_node_first, node_in)
    d_direct = d_node_joined[:, :L]
    d_aggregated = d_node_joined[:, L:].astype(jnp.bfloat16)
    d_agg_slab = lax.all_gather(d_aggregated, "lat", axis=0, tiled=True)
    edge_upstream = edge_cotangent.astype(jnp.float32)
    d_message = (edge_upstream + d_agg_slab[dst_row].astype(jnp.float32)) * live_mask
    d_edge_second = norm_back(d_message, edge_normed, edge_inverse, edge_gain).astype(jnp.bfloat16)
    g_edge_out = contract_rows(edge_first, d_edge_second)
    d_edge_first = (times_transpose(d_edge_second, edge_out) * (edge_first > 0)).astype(
        jnp.bfloat16
    )
    g_edge_in = contract_rows(joined, d_edge_first)
    d_joined = times_transpose(d_edge_first, edge_in)
    grad_edges = (edge_upstream + d_joined[:, :L]).astype(jnp.bfloat16)
    d_extended = jnp.zeros((extended.shape[0], L), jnp.float32)
    d_extended = d_extended.at[src_row].add(d_joined[:, L : 2 * L])
    d_extended = d_extended.at[halo_rows + dst_row].add(d_joined[:, 2 * L :])
    own_start = halo_rows + row_start
    own_grads = lax.dynamic_slice_in_dim(d_extended, own_start, own_rows, 0) + d_direct
    d_extended = lax.dynamic_update_slice_in_dim(d_extended, own_grads, own_start, 0)
    d_lower = d_extended[:halo_rows]
    d_middle = d_extended[halo_rows : halo_rows + slab_rows]
    d_upper = d_extended[halo_rows + slab_rows :]
    from_above = from_behind(d_lower.astype(jnp.bfloat16), "slab", -1).astype(d_lower.dtype)
    from_below = from_behind(d_upper.astype(jnp.bfloat16), "slab", 1).astype(d_upper.dtype)
    d_middle = add_blocks(add_blocks(d_middle, up_list, from_above), down_list, from_below)
    grad_slab = lax.psum_scatter(
        d_middle.astype(jnp.bfloat16), "lat", scatter_dimension=1, tiled=True
    )
    reduced_grads = (
        lax.psum_scatter(g_edge_in, ("slab", "lat"), scatter_dimension=0, tiled=True),
        lax.psum_scatter(g_edge_out, ("slab", "lat"), scatter_dimension=0, tiled=True),
        lax.psum_scatter(g_node_in, ("slab", "lat"), scatter_dimension=0, tiled=True),
        lax.psum_scatter(g_node_out, ("slab", "lat"), scatter_dimension=0, tiled=True),
    )
    return (
        new_nodes,
        new_edges,
        grad_slab,
        grad_edges,
        reduced_grads[0],
        reduced_grads[1],
        reduced_grads[2],
        reduced_grads[3],
    )


def solution(mesh):
    placed = (
        P("slab", "lat"),
        P(("slab", "lat"), None),
        P(None, ("slab", "lat")),
        P(None, ("slab", "lat")),
        P("slab"),
        P("slab", None, None),
        P(("slab", "lat"), None),
        P(("slab", "lat"), None),
        P(("slab", "lat"), None),
        P(("slab", "lat"), None),
        P(),
        P(),
        P("slab", "lat"),
        P(("slab", "lat"), None),
    )
    return jax.shard_map(
        per_device,
        mesh=mesh,
        in_specs=placed,
        out_specs=(
            P("slab", "lat"),
            P(("slab", "lat"), None),
            P("slab", "lat"),
            P(("slab", "lat"), None),
            P(("slab", "lat"), None),
            P(("slab", "lat"), None),
            P(("slab", "lat"), None),
            P(("slab", "lat"), None),
        ),
        check_vma=False,
    )
```

profile of v0, /device:TPU:0, one launch (start us, length us, event | category | flops | bytes accessed | tf_op | source)
XLA Modules:
  0.0 1704.4 jit_solution(14372097348663881991)
XLA Ops:
  11.7 6.5 compare_select_fusion
  18.8 321.8 %all-gather.1 = bf16[128,4,512]{2,1,0:T(4,128)(2,1)S(1)} all-gather(bf16[1,4,512]{2,1,0:T(4,128)(2,1)} %bitcast.96), channel_id=1, replica_groups=mesh['slab'=16,'lat'=8] {'slab','lat'}, dimensions={0}, use_global_device_ids=true | all-gather | bytes 528384 | tf_op jit(solution)/shard_map/all_gather | solution.py:84
  371.8 5.7 scatter_custom_fusion
  378.7 7.7 all-to-all-start.1
  386.4 319.3 %all-gather.2 = bf16[128,4,512]{2,1,0:T(4,128)(2,1)S(1)} all-gather(bf16[1,4,512]{2,1,0:T(4,128)(2,1)S(1)} %bitcast.97), channel_id=1, replica_groups=mesh['slab'=16,'lat'=8] {'slab','lat'}, dimensions={0}, use_global_device_ids=true | all-gather | bytes 528384 | tf_op jit(solution)/shard_map/all_gather | solution.py:86
  707.4 49.7 %all-gather.10.cloned.1.call-done = bf16[1024,512]{1,0:T(8,128)(2,1)} async-done(((bf16[8,512]{1,0:T(8,128)(2,1)}), bf16[1024,512]{1,0:T(8,128)(2,1)}) %all-gather.10.cloned.1.call-update) | async-done | bytes 1048592 | tf_op jit(solution)/shard_map/all_gather | solution.py:85
  765.3 45.2 %all-gather.12.cloned.1.call-done = bf16[1024,512]{1,0:T(8,128)(2,1)} async-done(((bf16[128,512]{1,0:T(8,128)(2,1)}), bf16[1024,512]{1,0:T(8,128)(2,1)}) %all-gather.12.cloned.1.call-update) | async-done | bytes 1048592 | tf_op jit(solution)/shard_map/all_gather | solution.py:141
  810.6 3.3 gather_fusion.2
  822.4 5.1 scatter_custom_fusion.1
  827.5 5.5 scatter_custom_fusion.2
  853.1 346.0 %fusion = f32[16,512]{1,0:T(8,128)S(1)} fusion(f32[1536,512]{1,0:T(8,128)S(1)} %fusion.39), kind=kCustom, calls=%all-reduce-scatter | all-reduce-scatter fusion | flops 1048577 | bytes 3178496
  1209.2 3.4 all-to-all-start
  1212.5 8.7 collective-permute-start.16
  1221.3 3.4 collective-permute-start.17
  1224.7 12.2 collective-permute-start.18
  1241.0 3.9 collective-permute-start.21
  1244.9 3.7 collective-permute-start.22
  1252.4 3.8 collective-permute-start.25
  1278.2 3.7 collective-permute-start.5
  1281.9 4.8 collective-permute-start.6
  1289.0 3.7 collective-permute-start.8
  1292.7 4.4 collective-permute-start.9
  1299.5 10.2 concatenate.12
  1313.0 384.5 %reduce-scatter.10.cloned.1.call-done = f32[8,512]{1,0:T(8,128)} async-done(((f32[1024,512]{1,0:T(8,128)}), f32[8,512]{1,0:T(8,128)}) %reduce-scatter.10.cloned.1.call-update) | async-done | bytes 16400 | tf_op jit(solution)/shard_map/reduce_scatter | solution.py:170
  (228 shorter events, 122.3 us)
Async XLA Ops:
  7.2 333.4 %all-gather.8.cloned.1.call-start = ((), (), s32[]{:S(2)}) async-start(), calls=%async_computation.5 | async-start | bytes 1179648 | tf_op jit(solution)/shard_map/all_gather | solution.py:90
  7.9 354.2 %all-gather.14.cloned.1.call-start = ((), (), s32[]{:S(2)}) async-start(), calls=%async_computation.11 | async-start | bytes 2113536 | tf_op jit(solution)/shard_map/all_gather | solution.py:83
  8.7 697.7 %reduce-scatter.6.cloned.1.call-start = ((), (), s32[]{:S(2)}) async-start(), calls=%async_computation.6 | async-start | bytes 2359296 | tf_op jit(solution)/shard_map/reduce_scatter | solution.py:108
  377.4 379.6 %all-gather.10.cloned.1.call-start = ((), (), s32[]{:S(2)}) async-start(), calls=%async_computation.7 | async-start | bytes 1056768 | tf_op jit(solution)/shard_map/all_gather | solution.py:85
  378.7 327.3 %all-to-all-start.1 = ((bf16[8,128,64]{1,2,0:T(8,128)(2,1)}), bf16[8,128,64]{1,2,0:T(8,128)(2,1)S(1)}, u32[]{:S(2)}, u32[]{:S(2)}) async-start(bf16[8,128,64]{1,2,0:T(8,128)(2,1)} %copy_bitcast_fusion.1), calls=%async_computation.2 | async-start | bytes 262144 | tf_op jit(solution)/shard_map/all_to_all | solution.py:127
  386.4 424.2 %all-gather.12.cloned.1.call-start = ((), (), s32[]{:S(2)}) async-start(), calls=%async_computation.8 | async-start | bytes 1179648 | tf_op jit(solution)/shard_map/all_gather | solution.py:141
  762.5 547.9 %all-reduce.7.cloned.1.call-start = ((), (), s32[]{:S(2)}) async-start(), calls=%async_computation.12 | async-start | bytes 4194304
  819.0 494.0 %reduce-scatter.8.cloned.1.call-start = ((), (), s32[]{:S(2)}) async-start(), calls=%async_computation.9 | async-start | bytes 1179648 | tf_op jit(solution)/shard_map/reduce_scatter | solution.py:164
  848.4 849.1 %reduce-scatter.10.cloned.1.call-start = ((), (), s32[]{:S(2)}) async-start(), calls=%async_computation.10 | async-start | bytes 2113536 | tf_op jit(solution)/shard_map/reduce_scatter | solution.py:170
  1203.2 18.1 %collective-permute-start.12 = (f32[16,512]{1,0:T(8,128)S(1)}, f32[16,512]{1,0:T(8,128)S(1)}, u32[]{:S(2)}, u32[]{:S(2)}) collective-permute-start(f32[16,512]{1,0:T(8,128)S(1)} %fusion), channel_id=1, source_target_pairs={{0,9},{1,10},{2,11},{3,12},{4,13},{5,14},{6,15},{7,16},{8,17},{9,1... | collective-permute-start | bytes 98312
  1204.5 20.2 %collective-permute-start.13 = (f32[16,512]{1,0:T(8,128)S(1)}, f32[16,512]{1,0:T(8,128)S(1)}, u32[]{:S(2)}, u32[]{:S(2)}) collective-permute-start(f32[16,512]{1,0:T(8,128)S(1)} %fusion), channel_id=1, source_target_pairs={{0,10},{1,11},{2,12},{3,13},{4,14},{5,15},{6,16},{7,17},{8,18},{9,... | collective-permute-start | bytes 98312
  1205.8 31.1 %collective-permute-start.14 = (f32[16,512]{1,0:T(8,128)S(1)}, f32[16,512]{1,0:T(8,128)S(1)}, u32[]{:S(2)}, u32[]{:S(2)}) collective-permute-start(f32[16,512]{1,0:T(8,128)S(1)} %fusion), channel_id=1, source_target_pairs={{0,11},{1,12},{2,13},{3,14},{4,15},{5,16},{6,17},{7,18},{8,19},{9,... | collective-permute-start | bytes 98312
  1207.1 31.1 %collective-permute-start.15 = (f32[16,512]{1,0:T(8,128)S(1)}, f32[16,512]{1,0:T(8,128)S(1)}, u32[]{:S(2)}, u32[]{:S(2)}) collective-permute-start(f32[16,512]{1,0:T(8,128)S(1)} %fusion), channel_id=1, source_target_pairs={{0,12},{1,13},{2,14},{3,15},{4,16},{5,17},{6,18},{7,19},{8,20},{9,... | collective-permute-start | bytes 98312
  1209.2 68.0 %all-to-all-start = ((bf16[128,8,64]{0,2,1:T(8,128)(2,1)}), bf16[128,8,64]{0,2,1:T(8,128)(2,1)S(1)}, u32[]{:S(2)}, u32[]{:S(2)}) async-start(bf16[128,8,64]{0,2,1:T(8,128)(2,1)} %bitcast.21), calls=%async_computation.1 | async-start | bytes 262144 | tf_op jit(solution)/shard_map/all_to_all | solution.py:120
  1212.5 28.5 %collective-permute-start.16 = (f32[16,512]{1,0:T(8,128)S(1)}, f32[16,512]{1,0:T(8,128)S(1)}, u32[]{:S(2)}, u32[]{:S(2)}) collective-permute-start(f32[16,512]{1,0:T(8,128)S(1)} %fusion), channel_id=1, source_target_pairs={{0,13},{1,14},{2,15},{3,16},{4,17},{5,18},{6,19},{7,20},{8,21},{9,... | collective-permute-start | bytes 98312
  1221.3 23.7 %collective-permute-start.17 = (f32[16,512]{1,0:T(8,128)S(1)}, f32[16,512]{1,0:T(8,128)S(1)}, u32[]{:S(2)}, u32[]{:S(2)}) collective-permute-start(f32[16,512]{1,0:T(8,128)S(1)} %fusion), channel_id=1, source_target_pairs={{0,14},{1,15},{2,16},{3,17},{4,18},{5,19},{6,20},{7,21},{8,22},{9,... | collective-permute-start | bytes 98312
  1224.7 24.0 %collective-permute-start.18 = (f32[16,512]{1,0:T(8,128)S(1)}, f32[16,512]{1,0:T(8,128)S(1)}, u32[]{:S(2)}, u32[]{:S(2)}) collective-permute-start(f32[16,512]{1,0:T(8,128)S(1)} %fusion), channel_id=1, source_target_pairs={{0,15},{1,16},{2,17},{3,18},{4,19},{5,20},{6,21},{7,22},{8,23},{9,... | collective-permute-start | bytes 98312
  1241.0 15.1 collective-permute-start.21
  1267.1 14.8 collective-permute-start.32
  1269.7 17.1 %collective-permute-start.33 = (f32[16,512]{1,0:T(8,128)S(1)}, f32[16,512]{1,0:T(8,128)}, u32[]{:S(2)}, u32[]{:S(2)}) collective-permute-start(f32[16,512]{1,0:T(8,128)S(1)} %fusion), channel_id=1, source_target_pairs={{0,30},{1,31},{2,32},{3,33},{4,34},{5,35},{6,36},{7,37},{8,38},{9,... | collective-permute-start | bytes 98312
  1272.7 16.2 collective-permute-start.34
  1274.6 18.0 %collective-permute-start.4 = (f32[16,512]{1,0:T(8,128)S(1)}, f32[16,512]{1,0:T(8,128)}, u32[]{:S(2)}, u32[]{:S(2)}) collective-permute-start(f32[16,512]{1,0:T(8,128)S(1)} %fusion), channel_id=1, source_target_pairs={{0,1},{1,2},{2,3},{3,4},{4,5},{5,6},{6,7},{7,8},{8,9},{9,10},{10,1... | collective-permute-start | bytes 98312
  1278.2 20.0 %collective-permute-start.5 = (f32[16,512]{1,0:T(8,128)S(1)}, f32[16,512]{1,0:T(8,128)S(1)}, u32[]{:S(2)}, u32[]{:S(2)}) collective-permute-start(f32[16,512]{1,0:T(8,128)S(1)} %fusion), channel_id=1, source_target_pairs={{0,2},{1,3},{2,4},{3,5},{4,6},{5,7},{6,8},{7,9},{8,10},{9,11},{10,... | collective-permute-start | bytes 98312
  1281.9 16.3 collective-permute-start.6
  (53 other events, 1968.6 us)
Sparse Core Ops, SparseCore 0:
  10.4 48.9 all-gather.7
  61.0 301.0 all-gather.13
  377.6 77.6 reduce-scatter.5
  456.8 300.2 all-gather.9
  762.6 47.9 all-gather.11
  819.1 152.0 all-reduce.6
  975.4 71.8 reduce-scatter.7
  1050.3 647.1 reduce-scatter.9
where the time goes:
time: 1710 us; the launch traced here: 1700 us
  blocking collectives  987 us (58%)
  waiting for transfers between devices  484 us (28%)
  starting transfers between devices  109 us (6%)
  local copies, waits for them, and re-layouts  52.1 us (3%)
  other arithmetic  39.4 us (2%)
  matrix products  17.1 us (1%)
    reduce_scatter x1, waiting for transfers between devices, per_device(): lax.psum_scatter(g_node_in, ('slab', 'lat'), scatter_dimension=0, tiled=T...  385 us
    unnamed x1, blocking collectives  346 us
    all_gather x1, blocking collectives, per_device(): lax.all_gather(w_edge_out, ('slab', 'lat'), axis=0, tiled=True)  322 us
    all_gather x1, blocking collectives, per_device(): lax.all_gather(w_node_out, ('slab', 'lat'), axis=0, tiled=True)  319 us
    unnamed x33, starting transfers between devices  90.4 us
    all_gather x1, waiting for transfers between devices, per_device(): lax.all_gather(w_node_in, ('slab', 'lat'), axis=0, tiled=True)  49.7 us
    all_gather x1, waiting for transfers between devices, per_device(): d_agg_slab = lax.all_gather(d_aggregated, 'lat', axis=0, tiled=True)  45.2 us
  transfers between devices with their start and end apart: 46, of which 4 were waited for; matrix products, arithmetic and copies ran while one was open for 25% of the time, Pallas kernels for 0%

commit v1 on v0

v1 whole, which is shorter than its diff:
```python
import jax
import jax.numpy as jnp
from jax import lax
from jax.sharding import Mesh, PartitionSpec as P

L = 512
BLK = 128
HB = 2
EPSILON = 1e-05

SLAB = ("y", "xl", "c")
LAT = ("xh", "z")
CHIP = ("y", "xl", "xh", "z")
BF = jnp.bfloat16
F32 = jnp.float32


def from_behind(value, steps):
    count = lax.axis_size(SLAB)
    first, last = (max(0, -steps), min(count, count - steps))
    return lax.ppermute(value, SLAB, [(source, source + steps) for source in range(first, last)])


def layer_norm(values, gain_vector):
    average = jnp.mean(values, axis=-1, keepdims=True)
    centred = values - average
    variance = jnp.mean(centred * centred, axis=-1, keepdims=True)
    inverse = lax.rsqrt(variance + EPSILON)
    normed = centred * inverse
    return (normed * gain_vector, normed, inverse)


def norm_back(upstream, normed, inverse, gain_vector):
    scaled = upstream * gain_vector
    return inverse * (
        scaled
        - jnp.mean(scaled, axis=-1, keepdims=True)
        - normed * jnp.mean(scaled * normed, axis=-1, keepdims=True)
    )


def contract_rows(left, right):
    return lax.dot_general(left, right, (((0,), (0,)), ((), ())), preferred_element_type=F32)


def times_transpose(left, weight):
    return lax.dot_general(left, weight, (((1,), (1,)), ((), ())), preferred_element_type=F32)


def pick_blocks(source_table, blocks):
    width = source_table.shape[1]
    return jnp.take(source_table.reshape(-1, BLK, width), blocks, axis=0).reshape(-1, width)


def pair(value):
    half = value.shape[-2] // 2
    return jnp.concatenate([value[..., :half, :], value[..., half:, :]], axis=-1)


def unpair(value):
    half = value.shape[-1] // 2
    return jnp.concatenate([value[..., :half], value[..., half:]], axis=-2)


def gather_weights(pieces):
    rows = sum(piece.shape[0] for piece in pieces)
    packed = jnp.concatenate(pieces + [jnp.zeros((-rows % 8, L), BF)], axis=0)
    chips = lax.axis_size(CHIP)
    core = lax.axis_index("c")
    mine = lax.all_to_all(jnp.broadcast_to(packed, (chips,) + packed.shape), CHIP, 0, 0)
    theirs = lax.ppermute(mine, "c", [(0, 1), (1, 0)])
    lat = lax.axis_size(LAT)
    shape = (chips // lat, 1, lat) + packed.shape
    mine, theirs = mine.reshape(shape), theirs.reshape(shape)
    first = jnp.where(core == 0, mine, theirs)
    second = jnp.where(core == 0, theirs, mine)
    full = jnp.concatenate([first, second], axis=1).reshape((2 * chips,) + packed.shape)
    out, at = [], 0
    for piece in pieces:
        count = piece.shape[0]
        out.append(full[:, at : at + count].reshape(-1, L))
        at += count
    return out


def scatter_grads(grads):
    chips = lax.axis_size(CHIP)
    lat = lax.axis_size(LAT)
    core = lax.axis_index("c")
    parts = [grad.reshape(2 * chips, -1, L) for grad in grads]
    counts = [part.shape[1] for part in parts]
    packed = jnp.concatenate(parts, axis=1)
    rows = packed.shape[1]
    shaped = packed.reshape(chips // lat, 2, lat, rows, L)
    kept = jnp.where(core == 0, shaped[:, 0], shaped[:, 1])
    sent = jnp.where(core == 0, shaped[:, 1], shaped[:, 0]).astype(BF)
    arrived = lax.ppermute(sent, "c", [(0, 1), (1, 0)])
    summed = (kept + arrived.astype(F32)).astype(BF).reshape(chips, rows, L)
    summed = jnp.pad(summed, ((0, 0), (0, -rows % 8), (0, 0)))
    spread = lax.all_to_all(summed, CHIP, 0, 0)
    total = jnp.sum(spread.astype(F32), axis=0)
    out, at = [], 0
    for count in counts:
        out.append(total[at : at + count])
        at += count
    return out


def per_device(
    nodes,
    edges,
    edge_tiles,
    edge_offsets,
    tile_counts,
    halo_blocks,
    w_edge_in,
    w_edge_out,
    w_node_in,
    w_node_out,
    edge_gain,
    node_gain,
    node_cotangent,
    edge_cotangent,
):
    lat_size = lax.axis_size(LAT)
    lat_index = lax.axis_index(LAT)
    slab_rows, width = nodes.shape
    own_rows = slab_rows // lat_size
    halo_rows = HB * BLK
    ext_rows = slab_rows + 2 * halo_rows
    up_list = halo_blocks[0, 0]
    down_list = halo_blocks[0, 1]

    from_lower = unpair(from_behind(pair(pick_blocks(nodes, up_list)), 1))
    from_upper = unpair(from_behind(pair(pick_blocks(nodes, down_list)), -1))
    table = pair(jnp.concatenate([from_lower, nodes, from_upper], axis=0))
    cot = pair(node_cotangent.reshape(lat_size, own_rows, width))
    message_out = jnp.concatenate(
        [jnp.broadcast_to(table, (lat_size,) + table.shape), cot], axis=1
    )
    arrived = lax.all_to_all(message_out, LAT, 0, 0)
    extended = unpair(arrived[:, : ext_rows // 2]).transpose(1, 0, 2).reshape(ext_rows, L)
    upstream_rows = unpair(arrived[:, ext_rows // 2 :]).transpose(1, 0, 2).reshape(own_rows, L)
    slab_full = extended[halo_rows : halo_rows + slab_rows]

    edge_in, edge_out, node_in, node_out = gather_weights(
        [w_edge_in, w_edge_out, w_node_in, w_node_out]
    )

    tile_slots = edge_tiles.shape[1]
    tile_of = jnp.arange(edges.shape[0], dtype=jnp.int32) // BLK
    dst_row = edge_tiles[0][tile_of] * BLK + edge_offsets[0]
    src_row = edge_tiles[1][tile_of] * BLK + edge_offsets[1]
    live_mask = (lat_index * tile_slots + tile_of < tile_counts[0]).astype(F32)[:, None]
    joined = jnp.concatenate([edges, extended[src_row], slab_full[dst_row]], axis=1)
    edge_first = jax.nn.relu(jnp.dot(joined, edge_in, preferred_element_type=F32)).astype(BF)
    edge_second = jnp.dot(edge_first, edge_out, preferred_element_type=F32)
    edge_update, edge_normed, edge_inverse = layer_norm(edge_second, edge_gain)
    message = edge_update * live_mask
    new_edges = (edges.astype(F32) + message).astype(BF)
    partial_sums = jnp.zeros((slab_rows, L), F32).at[dst_row].add(message)
    spread = lax.all_to_all(partial_sums.reshape(lat_size, own_rows, L), LAT, 0, 0)
    aggregated = jnp.sum(spread, axis=0).astype(BF)
    row_start = lat_index * own_rows
    own_latents = lax.dynamic_slice_in_dim(slab_full, row_start, own_rows, 0)
    node_joined = jnp.concatenate([own_latents, aggregated], axis=1)
    node_first = jax.nn.relu(jnp.dot(node_joined, node_in, preferred_element_type=F32)).astype(BF)
    node_second = jnp.dot(node_first, node_out, preferred_element_type=F32)
    node_update, node_normed, node_inverse = layer_norm(node_second, node_gain)
    new_rows = (own_latents.astype(F32) + node_update).astype(BF)

    d_node_second = norm_back(
        upstream_rows.astype(F32), node_normed, node_inverse, node_gain
    ).astype(BF)
    g_node_out = contract_rows(node_first, d_node_second)
    d_node_first = (times_transpose(d_node_second, node_out) * (node_first > 0)).astype(BF)
    g_node_in = contract_rows(node_joined, d_node_first)
    d_node_joined = times_transpose(d_node_first, node_in)
    d_direct = d_node_joined[:, :L]
    d_aggregated = d_node_joined[:, L:].astype(BF)

    groups = L // width
    group_rows = own_rows // groups
    rows_out = (
        new_rows.reshape(groups, group_rows, lat_size, width)
        .transpose(2, 1, 0, 3)
        .reshape(lat_size, group_rows, L)
    )
    second_out = jnp.concatenate(
        [jnp.broadcast_to(d_aggregated, (lat_size,) + d_aggregated.shape), rows_out], axis=1
    )
    second_in = lax.all_to_all(second_out, LAT, 0, 0)
    d_agg_slab = second_in[:, :own_rows].reshape(slab_rows, L)
    new_nodes = (
        second_in[:, own_rows:]
        .reshape(lat_size, group_rows, groups, width)
        .transpose(0, 2, 1, 3)
        .reshape(slab_rows, width)
    )

    edge_upstream = edge_cotangent.astype(F32)
    d_message = (edge_upstream + d_agg_slab[dst_row].astype(F32)) * live_mask
    d_edge_second = norm_back(d_message, edge_normed, edge_inverse, edge_gain).astype(BF)
    g_edge_out = contract_rows(edge_first, d_edge_second)
    d_edge_first = (times_transpose(d_edge_second, edge_out) * (edge_first > 0)).astype(BF)
    g_edge_in = contract_rows(joined, d_edge_first)
    d_joined = times_transpose(d_edge_first, edge_in)
    grad_edges = (edge_upstream + d_joined[:, :L]).astype(BF)
    d_extended = jnp.zeros((ext_rows, L), F32)
    d_extended = d_extended.at[src_row].add(d_joined[:, L : 2 * L])
    d_extended = d_extended.at[halo_rows + dst_row].add(d_joined[:, 2 * L :])
    own_start = halo_rows + row_start
    own_grads = lax.dynamic_slice_in_dim(d_extended, own_start, own_rows, 0) + d_direct
    d_extended = lax.dynamic_update_slice_in_dim(d_extended, own_grads, own_start, 0)

    columns = pair(d_extended.astype(BF).reshape(ext_rows, lat_size, width).transpose(1, 0, 2))
    summed = unpair(jnp.sum(lax.all_to_all(columns, LAT, 0, 0).astype(F32), axis=0))
    d_lower = pair(summed[:halo_rows].astype(BF))
    d_middle = summed[halo_rows : halo_rows + slab_rows]
    d_upper = pair(summed[halo_rows + slab_rows :].astype(BF))
    from_above = unpair(from_behind(d_lower, -1)).astype(F32).reshape(HB, BLK, width)
    from_below = unpair(from_behind(d_upper, 1)).astype(F32).reshape(HB, BLK, width)
    blocks = d_middle.reshape(-1, BLK, width)
    numbers = jnp.arange(blocks.shape[0])
    for j in range(HB):
        blocks = blocks + jnp.where((numbers == up_list[j])[:, None, None], from_above[j], 0.0)
        blocks = blocks + jnp.where((numbers == down_list[j])[:, None, None], from_below[j], 0.0)
    grad_slab = blocks.reshape(slab_rows, width).astype(BF)
    reduced = scatter_grads([g_edge_in, g_edge_out, g_node_in, g_node_out])
    return (new_nodes, new_edges, grad_slab, grad_edges) + tuple(reduced)


def solution(mesh):
    fine = Mesh(mesh.devices.reshape(4, 2, 2, 2, 4), ("y", "xl", "c", "xh", "z"))
    every = SLAB + LAT
    by_rows = P(every, None)
    split = P(SLAB, LAT)
    placed = (
        split,
        by_rows,
        P(None, every),
        P(None, every),
        P(SLAB),
        P(SLAB, None, None),
        by_rows,
        by_rows,
        by_rows,
        by_rows,
        P(),
        P(),
        split,
        by_rows,
    )
    return jax.shard_map(
        per_device,
        mesh=fine,
        in_specs=placed,
        out_specs=(split, by_rows, split, by_rows, by_rows, by_rows, by_rows, by_rows),
        check_vma=False,
    )
```

time: 1710 us -> 305 us (0.18)
  blocking collectives: 987 us -> 0 us
  waiting for transfers between devices: 484 us -> 106 us
  starting transfers between devices: 109 us -> 45.8 us
  other arithmetic: 39.4 us -> 61.4 us
  local copies, waits for them, and re-layouts: 52.1 us -> 69.7 us
    all_gather x2 -> x0, blocking collectives: 641 us -> none  [the longest x1 322 us: per_device(): lax.all_gather(w_edge_out, ('slab', 'lat'), axis=0, tiled=True)]
    reduce_scatter x3 -> x0, waiting for transfers between devices: 385 us -> none  [the longest x1 385 us: per_device(): lax.psum_scatter(g_node_in, ('slab', 'lat'), scatter_dimension=0, tiled=T...]
    unnamed x1 -> x0, blocking collectives: 346 us -> none
    all_to_all x2 -> x6, waiting for transfers between devices: 0.01 us -> 102 us  [the longest x1 22.8 us: per_device(): lax.all_to_all(partial_sums.reshape(lat_size, own_rows, L), LAT, 0, 0)]
    all_gather x4 -> x0, waiting for transfers between devices: 97.3 us -> none  [the longest x1 49.7 us: per_device(): lax.all_gather(w_node_in, ('slab', 'lat'), axis=0, tiled=True)]
    unnamed x33 -> x0, starting transfers between devices: 90.4 us -> none
    all_to_all x2 -> x6, starting transfers between devices: 11 us -> 38.3 us  [the longest x1 11.7 us: gather_weights(): lax.all_to_all(jnp.broadcast_to(packed, (chips,) + packed.shape), CHIP, 0...]
  transfers between devices with their start and end apart: 46 -> 12, of which waited for: 4 -> 8; matrix products, arithmetic and copies ran while one was open for 25% -> 19% of each run, Pallas kernels for 0% -> 0%
where the time goes in v1:
time: 305 us; the launch traced here: 300 us
  waiting for transfers between devices  106 us (35%)
  local copies, waits for them, and re-layouts  69.7 us (23%)
  other arithmetic  61.4 us (20%)
  starting transfers between devices  45.8 us (15%)
  matrix products  15.2 us (5%)
    all_to_all x1, waiting for transfers between devices, per_device(): lax.all_to_all(partial_sums.reshape(lat_size, own_rows, L), LAT, 0, 0)  22.8 us
    all_to_all x1, waiting for transfers between devices, scatter_grads(): spread = lax.all_to_all(summed, CHIP, 0, 0)  22.4 us
    all_to_all x1, waiting for transfers between devices, gather_weights(): lax.all_to_all(jnp.broadcast_to(packed, (chips,) + packed.shape), CHIP, 0...  21.3 us
    unnamed x79, local copies, waits for them, and re-layouts  19.1 us
    all_to_all x1, waiting for transfers between devices, per_device(): second_in = lax.all_to_all(second_out, LAT, 0, 0)  13.3 us
    all_to_all x1, waiting for transfers between devices, per_device(): arrived = lax.all_to_all(message_out, LAT, 0, 0)  13 us
    all_to_all x1, starting transfers between devices, gather_weights(): lax.all_to_all(jnp.broadcast_to(packed, (chips,) + packed.shape), CHIP, 0...  11.7 us
    all_to_all x1, waiting for transfers between devices, per_device(): lax.all_to_all(columns, LAT, 0, 0).astype(F32)  9.15 us
  transfers between devices with their start and end apart: 12, of which 8 were waited for; matrix products, arithmetic and copies ran while one was open for 19% of the time, Pallas kernels for 0%

profile of v1, /device:TPU:0, one launch (start us, length us, event | category | flops | bytes accessed | tf_op | source)
XLA Modules:
  0.0 300.3 jit_solution(8596056400029406633)
XLA Ops:
  0.6 2.8 concatenate.82
  5.1 11.7 %all-to-all-start.1 = ((bf16[64,32,512]{2,1,0:T(8,128)(2,1)}), bf16[64,32,512]{2,1,0:T(8,128)(2,1)S(1)}, u32[]{:S(2)}, u32[]{:S(2)}) async-start(bf16[64,32,512]{2,1,0:T(8,128)(2,1)} %broadcast_in_dim.122), calls=%async_computation.1 | async-start | bytes 4194304 | tf_op jit(solution)/shard_map/all_to_all | solution.py:70
  19.4 3.0 %collective-permute-start = (bf16[128,128]{0,1:T(8,128)(2,1)S(1)}, bf16[128,128]{0,1:T(8,128)(2,1)S(1)}, u32[]{:S(2)}, u32[]{:S(2)}) collective-permute-start(bf16[128,128]{0,1:T(8,128)(2,1)S(1)} %pad_maximum_fusion.15), channel_id=1, source_target_pairs={{0,8},{8,16},{16,24},{24,32},{32,40},{40,48},{48,56},{56,64},{64,7... | collective-permute-start | bytes 98312 | tf_op jit(solution)/shard_map/ppermute | solution.py:21
  25.0 21.3 %all-to-all-done.1 = bf16[64,32,512]{2,1,0:T(8,128)(2,1)S(1)} async-done(((bf16[64,32,512]{2,1,0:T(8,128)(2,1)}), bf16[64,32,512]{2,1,0:T(8,128)(2,1)S(1)}, u32[]{:S(2)}, u32[]{:S(2)}) %all-to-all-start.1) | async-done | bytes 2097184 | tf_op jit(solution)/shard_map/all_to_all | solution.py:70
  47.6 3.8 %all-to-all-start = ((bf16[8,832,128]{2,1,0:T(8,128)(2,1)}), bf16[8,832,128]{2,1,0:T(8,128)(2,1)S(1)}, u32[]{:S(2)}, u32[]{:S(2)}) async-start(bf16[8,832,128]{2,1,0:T(8,128)(2,1)} %pad_maximum_fusion.2), calls=%async_computation | async-start | bytes 3407872 | tf_op jit(solution)/shard_map/all_to_all | solution.py:141
  53.9 5.7 %compare_select_fusion = (s32[512,1]{0,1:T(1,128)}, s32[512,1]{0,1:T(1,128)S(1)}, s32[512,1]{0,1:T(1,128)S(1)}) fusion(s32[2,512]{1,0:T(2,128)S(1)} %copy-done.31, s32[]{:T(128)} %bitcast.11, s32[]{:T(128)} %bitcast.10, s32[]{:T(128)} %bitcast.9, s32[]{:T(128)} %bitcast.8, s32[]{:T(128)} %bitcast.18, s32[]{:T(128)} %bitcast.17, s32[]{:T(128)} %bitcast.16, ...), kind=kLoop, calls=%fused_computation.93 | loop fusion | flops 15872 | bytes 10272 | tf_op jit(solution)/shard_map/select_n | solution.py:211
  60.5 13.0 %all-to-all-done = bf16[8,832,128]{2,1,0:T(8,128)(2,1)S(1)} async-done(((bf16[8,832,128]{2,1,0:T(8,128)(2,1)}), bf16[8,832,128]{2,1,0:T(8,128)(2,1)S(1)}, u32[]{:S(2)}, u32[]{:S(2)}) %all-to-all-start) | async-done | bytes 1703968 | tf_op jit(solution)/shard_map/all_to_all | solution.py:141
  79.1 3.4 %pad_maximum_fusion.3 = (bf16[8,1536,64]{1,2,0:T(8,128)(2,1)}, bf16[1536,8,64]{0,2,1:T(8,128)(2,1)}) fusion(bf16[8,768,64]{1,2,0:T(8,128)(2,1)} %copy.102, bf16[8,768,64]{1,2,0:T(8,128)(2,1)} %copy.101), kind=kLoop, calls=%fused_computation.19 | loop fusion | flops 3145728 | bytes 4718592 | tf_op jit(solution)/shard_map/concatenate | solution.py:62
  105.5 3.0 %fusion.5 = bf16[512,512]{1,0:T(8,128)(2,1)S(1)} fusion(bf16[512,1536]{1,0:T(8,128)(2,1)} %constant_dynamic-update-slice_fusion, bf16[1536,512]{1,0:T(8,128)(2,1)} %reshape.362), kind=kOutput, calls=%fused_computation.28 | convolution fusion | flops 805830656 | bytes 3670016 | tf_op jit(solution)/shard_map/dot_general | solution.py:156
  112.2 5.7 %scatter_custom_fusion = f32[1024,512]{1,0:T(8,128)} fusion(s32[512]{0:T(512)S(1)} %bitcast.172, f32[512,512]{1,0:T(8,128)} %copy.85, f32[]{:T(128)} %constant.79.clone.1), kind=kCustom, calls=%fused_computation.46 | custom fusion | flops 262144 | bytes 2097664 | tf_op jit(solution)/shard_map/scatter-add | solution.py:161
  117.9 5.2 %all-to-all-start.2 = ((f32[8,128,512]{2,1,0:T(8,128)}), f32[8,128,512]{2,1,0:T(8,128)}, u32[]{:S(2)}, u32[]{:S(2)}) async-start(f32[8,128,512]{2,1,0:T(8,128)} %bitcast.151), calls=%async_computation.2 | async-start | bytes 4194304 | tf_op jit(solution)/shard_map/all_to_all | solution.py:162
  126.9 22.8 %all-to-all-done.2 = f32[8,128,512]{2,1,0:T(8,128)} async-done(((f32[8,128,512]{2,1,0:T(8,128)}), f32[8,128,512]{2,1,0:T(8,128)}, u32[]{:S(2)}, u32[]{:S(2)}) %all-to-all-start.2) | async-done | bytes 2097184 | tf_op jit(solution)/shard_map/all_to_all | solution.py:162
  158.6 4.8 %all-to-all-start.3 = ((bf16[8,144,512]{2,1,0:T(8,128)(2,1)}), bf16[8,144,512]{2,1,0:T(8,128)(2,1)}, u32[]{:S(2)}, u32[]{:S(2)}) async-start(bf16[8,144,512]{2,1,0:T(8,128)(2,1)} %pad_maximum_fusion.5), calls=%async_computation.3 | async-start | bytes 2359296 | tf_op jit(solution)/shard_map/all_to_all | solution.py:192
  167.0 13.3 %all-to-all-done.3 = bf16[8,144,512]{2,1,0:T(8,128)(2,1)} async-done(((bf16[8,144,512]{2,1,0:T(8,128)(2,1)}), bf16[8,144,512]{2,1,0:T(8,128)(2,1)}, u32[]{:S(2)}, u32[]{:S(2)}) %all-to-all-start.3) | async-done | bytes 1179680 | tf_op jit(solution)/shard_map/all_to_all | solution.py:192
  190.8 6.5 %scatter_custom_fusion.1 = f32[1536,512]{1,0:T(8,128)} fusion(s32[512]{0:T(512)} %bitcast.170, f32[]{:T(128)} %constant.79.clone.1, f32[512,1536]{1,0:T(8,128)} %fusion.58), kind=kCustom, calls=%fused_computation.21 | custom fusion | flops 262144 | bytes 4194816 | tf_op jit(solution)/shard_map/scatter-add | solution.py:210
  197.2 7.9 %scatter_custom_fusion.2 = f32[1536,512]{1,0:T(8,128)} fusion(f32[1536,512]{1,0:T(8,128)} %scatter_custom_fusion.1, s32[512]{0:T(512)} %bitcast.173, f32[512,1536]{1,0:T(8,128)} %fusion.58), kind=kCustom, calls=%fused_computation.37 | custom fusion | flops 262144 | bytes 4194304 | tf_op jit(solution)/shard_map/scatter-add | solution.py:211
  206.9 3.2 %convert_element_type.117 = bf16[1536,512]{1,0:T(8,128)(2,1)} convert(f32[1536,512]{1,0:T(8,128)} %fusion.23) | non-fusion elementwise | flops 786432 | bytes 4718592 | tf_op jit(solution)/shard_map/convert_element_type | solution.py:216
  217.4 4.1 %pad_maximum_fusion = f32[8,2,8,28,512]{4,3,2,1,0:T(8,128)S(1)} fusion(f32[8,2,8,4,512]{4,3,2,1,0:T(4,128)} %concatenate.96, f32[8,2,8,8,512]{4,3,2,1,0:T(8,128)} %bitcast.155, f32[8,2,8,4,512]{4,3,2,1,0:T(4,128)} %concatenate.94, f32[8,2,8,12,512]{4,3,2,1,0:T(8,128)} %concatenate.93), kind=kLoop, calls=%fused_computation.8 | loop fusion | flops 5505024 | bytes 14680064 | tf_op jit(solution)/shard_map/concatenate | solution.py:92
  226.7 4.7 %all-to-all-start.4 = ((bf16[8,768,128]{1,2,0:T(8,128)(2,1)}), bf16[8,768,128]{1,2,0:T(8,128)(2,1)S(1)}, u32[]{:S(2)}, u32[]{:S(2)}) async-start(bf16[8,768,128]{1,2,0:T(8,128)(2,1)} %pad_maximum_fusion.4), calls=%async_computation.4 | async-start | bytes 3145728 | tf_op jit(solution)/shard_map/all_to_all | solution.py:217
  243.3 9.2 %all-to-all-done.4 = bf16[8,768,128]{1,2,0:T(8,128)(2,1)S(1)} async-done(((bf16[8,768,128]{1,2,0:T(8,128)(2,1)}), bf16[8,768,128]{1,2,0:T(8,128)(2,1)S(1)}, u32[]{:S(2)}, u32[]{:S(2)}) %all-to-all-start.4) | async-done | bytes 1572896 | tf_op jit(solution)/shard_map/all_to_all | solution.py:217
  252.7 5.3 %fusion = bf16[8,8,28,512]{3,2,1,0:T(8,128)(2,1)S(1)} fusion(f32[8,2,8,28,512]{4,3,2,1,0:T(8,128)} %copy-done, bf16[8,8,28,512]{3,1,2,0:T(8,128)(2,1)} %collective-permute-done.5, pred[]{:T(512)S(6)} %eq.46), kind=kLoop, calls=%fused_computation.11 | loop fusion | flops 3670016 | bytes 11010049 | tf_op jit(solution)/shard_map/convert_element_type | solution.py:98
  259.8 8.3 %all-to-all-start.5 = ((bf16[64,32,512]{2,1,0:T(8,128)(2,1)}), bf16[64,32,512]{2,1,0:T(8,128)(2,1)S(1)}, u32[]{:S(2)}, u32[]{:S(2)}) async-start(bf16[64,32,512]{2,1,0:T(8,128)(2,1)} %pad.4), calls=%async_computation.5 | async-start | bytes 4194304 | tf_op jit(solution)/shard_map/all_to_all | solution.py:100
  271.1 3.2 %collective-permute-done.3 = bf16[128,128]{0,1:T(8,128)(2,1)S(1)} collective-permute-done((bf16[128,128]{0,1:T(8,128)(2,1)S(1)}, bf16[128,128]{0,1:T(8,128)(2,1)S(1)}, u32[]{:S(2)}, u32[]{:S(2)}) %collective-permute-start.3) | collective-permute-done | bytes 32800 | tf_op jit(solution)/shard_map/ppermute | solution.py:21
  275.4 22.4 %all-to-all-done.5 = bf16[64,32,512]{2,1,0:T(8,128)(2,1)S(1)} async-done(((bf16[64,32,512]{2,1,0:T(8,128)(2,1)}), bf16[64,32,512]{2,1,0:T(8,128)(2,1)S(1)}, u32[]{:S(2)}, u32[]{:S(2)}) %all-to-all-start.5) | async-done | bytes 2097184 | tf_op jit(solution)/shard_map/all_to_all | solution.py:100
  (216 shorter events, 103.5 us)
Async XLA Ops:
  5.1 11.7 %copy-start.19 = (bf16[1024,64]{0,1:T(8,128)(2,1)S(1)}, bf16[1024,64]{0,1:T(8,128)(2,1)}, u32[]{:S(2)}) copy-start(bf16[1024,64]{0,1:T(8,128)(2,1)} %param.16) | copy-start | bytes 393220
  5.1 11.7 %copy-start.28 = (s32[1,2,2]{2,1,0:T(2,128)S(1)}, s32[1,2,2]{2,1,0:T(2,128)}, u32[]{:S(2)}) copy-start(s32[1,2,2]{2,1,0:T(2,128)} %param.21) | copy-start | bytes 52
  5.1 17.4 %copy-start.21 = (bf16[1024,64]{0,1:T(8,128)(2,1)S(1)}, bf16[1024,64]{0,1:T(8,128)(2,1)}, u32[]{:S(2)}) copy-start(bf16[1024,64]{0,1:T(8,128)(2,1)} %param.28) | copy-start | bytes 393220
  5.1 41.2 %all-to-all-start.1 = ((bf16[64,32,512]{2,1,0:T(8,128)(2,1)}), bf16[64,32,512]{2,1,0:T(8,128)(2,1)S(1)}, u32[]{:S(2)}, u32[]{:S(2)}) async-start(bf16[64,32,512]{2,1,0:T(8,128)(2,1)} %broadcast_in_dim.122), calls=%async_computation.1 | async-start | bytes 4194304 | tf_op jit(solution)/shard_map/all_to_all | solution.py:70
  18.1 4.8 %collective-permute-start.1 = (bf16[128,128]{0,1:T(8,128)(2,1)S(1)}, bf16[128,128]{0,1:T(8,128)(2,1)S(1)}, u32[]{:S(2)}, u32[]{:S(2)}) collective-permute-start(bf16[128,128]{0,1:T(8,128)(2,1)S(1)} %pad_maximum_fusion.16), channel_id=1, source_target_pairs={{8,0},{16,8},{24,16},{32,24},{40,32},{48,40},{56,48},{64,56},{72,6... | collective-permute-start | bytes 98312 | tf_op jit(solution)/shard_map/ppermute | solution.py:21
  19.4 3.9 %collective-permute-start = (bf16[128,128]{0,1:T(8,128)(2,1)S(1)}, bf16[128,128]{0,1:T(8,128)(2,1)S(1)}, u32[]{:S(2)}, u32[]{:S(2)}) collective-permute-start(bf16[128,128]{0,1:T(8,128)(2,1)S(1)} %pad_maximum_fusion.15), channel_id=1, source_target_pairs={{0,8},{8,16},{16,24},{24,32},{32,40},{40,48},{48,56},{56,64},{64,7... | collective-permute-start | bytes 98312 | tf_op jit(solution)/shard_map/ppermute | solution.py:21
  25.0 26.6 %copy-start.12 = (bf16[512,512]{1,0:T(8,128)(2,1)S(1)}, bf16[512,512]{1,0:T(8,128)(2,1)}, u32[]{:S(2)}) copy-start(bf16[512,512]{1,0:T(8,128)(2,1)} %param.17) | copy-start | bytes 1572868
  25.0 28.3 %copy-start.27 = (s32[2,4]{1,0:T(2,128)S(1)}, s32[2,4]{1,0:T(2,128)}, u32[]{:S(2)}) copy-start(s32[2,4]{1,0:T(2,128)} %param.18) | copy-start | bytes 100
  25.0 28.9 %copy-start.31 = (s32[2,512]{1,0:T(2,128)S(1)}, s32[2,512]{1,0:T(2,128)}, u32[]{:S(2)}) copy-start(s32[2,512]{1,0:T(2,128)} %param.19) | copy-start | bytes 12292
  47.6 25.9 %all-to-all-start = ((bf16[8,832,128]{2,1,0:T(8,128)(2,1)}), bf16[8,832,128]{2,1,0:T(8,128)(2,1)S(1)}, u32[]{:S(2)}, u32[]{:S(2)}) async-start(bf16[8,832,128]{2,1,0:T(8,128)(2,1)} %pad_maximum_fusion.2), calls=%async_computation | async-start | bytes 3407872 | tf_op jit(solution)/shard_map/all_to_all | solution.py:141
  51.4 45.8 %collective-permute-start.2 = (bf16[64,32,512]{2,1,0:T(8,128)(2,1)}, bf16[64,32,512]{2,1,0:T(8,128)(2,1)}, u32[]{:S(2)}, u32[]{:S(2)}) collective-permute-start(bf16[64,32,512]{2,1,0:T(8,128)(2,1)} %copy-done.5), channel_id=1, source_target_pairs={{0,8},{8,0},{1,9},{9,1},{2,10},{10,2},{3,11},{11,3},{4,12},{12,4},... | collective-permute-start | bytes 6291464 | tf_op jit(solution)/shard_map/ppermute | solution.py:71
  59.5 15.7 %copy-start.30 = (s32[512,1]{0,1:T(1,128)}, s32[512,1]{0,1:T(1,128)S(1)}, u32[]{:S(2)}) copy-start(s32[512,1]{0,1:T(1,128)S(1)} %get-tuple-element.91) | copy-start | bytes 6148
  59.6 31.1 %copy-start.25 = (s32[1024]{0:T(1024)}, s32[1024]{0:T(1024)S(1)}, u32[]{:S(2)}) copy-start(s32[1024]{0:T(1024)S(1)} %get-tuple-element.112) | copy-start | bytes 12292
  73.5 9.0 %copy-start.2 = (bf16[8,832,128]{2,1,0:T(8,128)(2,1)}, bf16[8,832,128]{2,1,0:T(8,128)(2,1)S(1)}, u32[]{:S(2)}) copy-start(bf16[8,832,128]{2,1,0:T(8,128)(2,1)S(1)} %all-to-all-done) | copy-start | bytes 5111812
  117.9 31.8 %all-to-all-start.2 = ((f32[8,128,512]{2,1,0:T(8,128)}), f32[8,128,512]{2,1,0:T(8,128)}, u32[]{:S(2)}, u32[]{:S(2)}) async-start(f32[8,128,512]{2,1,0:T(8,128)} %bitcast.151), calls=%async_computation.2 | async-start | bytes 4194304 | tf_op jit(solution)/shard_map/all_to_all | solution.py:162
  158.6 21.8 %all-to-all-start.3 = ((bf16[8,144,512]{2,1,0:T(8,128)(2,1)}), bf16[8,144,512]{2,1,0:T(8,128)(2,1)}, u32[]{:S(2)}, u32[]{:S(2)}) async-start(bf16[8,144,512]{2,1,0:T(8,128)(2,1)} %pad_maximum_fusion.5), calls=%async_computation.3 | async-start | bytes 2359296 | tf_op jit(solution)/shard_map/all_to_all | solution.py:192
  163.6 20.8 %copy-start.3 = (bf16[512,512]{0,1:T(8,128)(2,1)}, bf16[512,512]{0,1:T(8,128)(2,1)S(1)}, u32[]{:S(2)}) copy-start(bf16[512,512]{0,1:T(8,128)(2,1)S(1)} %copy.92) | copy-start | bytes 1572868
  165.2 16.5 %copy-start.26 = (s32[1024]{0:T(1024)S(1)}, s32[1024]{0:T(1024)}, u32[]{:S(2)}) copy-start(s32[1024]{0:T(1024)} %copy-done.25) | copy-start | bytes 12292
  224.3 28.4 %collective-permute-start.5 = (bf16[8,8,28,512]{3,1,2,0:T(8,128)(2,1)}, bf16[8,8,28,512]{3,1,2,0:T(8,128)(2,1)}, u32[]{:S(2)}, u32[]{:S(2)}) collective-permute-start(bf16[8,8,28,512]{3,1,2,0:T(8,128)(2,1)} %copy.96), channel_id=1, source_target_pairs={{0,8},{8,0},{1,9},{9,1},{2,10},{10,2},{3,11},{11,3},{4,12},{12,4},... | collective-permute-start | bytes 5505032 | tf_op jit(solution)/shard_map/ppermute | solution.py:97
  226.7 8.1 %copy-start.15 = (bf16[512,512]{0,1:T(8,128)(2,1)S(1)}, bf16[512,512]{0,1:T(8,128)(2,1)}, u32[]{:S(2)}) copy-start(bf16[512,512]{0,1:T(8,128)(2,1)} %get-tuple-element.45) | copy-start | bytes 1572868
  226.7 25.7 %all-to-all-start.4 = ((bf16[8,768,128]{1,2,0:T(8,128)(2,1)}), bf16[8,768,128]{1,2,0:T(8,128)(2,1)S(1)}, u32[]{:S(2)}, u32[]{:S(2)}) async-start(bf16[8,768,128]{1,2,0:T(8,128)(2,1)} %pad_maximum_fusion.4), calls=%async_computation.4 | async-start | bytes 3145728 | tf_op jit(solution)/shard_map/all_to_all | solution.py:217
  259.8 38.0 %all-to-all-start.5 = ((bf16[64,32,512]{2,1,0:T(8,128)(2,1)}), bf16[64,32,512]{2,1,0:T(8,128)(2,1)S(1)}, u32[]{:S(2)}, u32[]{:S(2)}) async-start(bf16[64,32,512]{2,1,0:T(8,128)(2,1)} %pad.4), calls=%async_computation.5 | async-start | bytes 4194304 | tf_op jit(solution)/shard_map/all_to_all | solution.py:100
  268.1 3.0 collective-permute-start.4
  269.8 4.6 %collective-permute-start.3 = (bf16[128,128]{0,1:T(8,128)(2,1)S(1)}, bf16[128,128]{0,1:T(8,128)(2,1)S(1)}, u32[]{:S(2)}, u32[]{:S(2)}) collective-permute-start(bf16[128,128]{0,1:T(8,128)(2,1)S(1)} %pad_maximum_fusion.17), channel_id=1, source_target_pairs={{8,0},{16,8},{24,16},{32,24},{40,32},{48,40},{56,48},{64,56},{72,6... | collective-permute-start | bytes 98312 | tf_op jit(solution)/shard_map/ppermute | solution.py:21
  (22 other events, 63.2 us)

commit v2 on v1

v2 whole, which is shorter than its diff:
```python
import jax
import jax.numpy as jnp
from jax import lax
from jax.experimental import pallas as pl
from jax.experimental.pallas import tpu as pltpu
from jax.sharding import Mesh, PartitionSpec as P

L = 512
BLK = 128
HB = 2
EPSILON = 1e-05

SLAB = ("y", "xl", "c")
LAT = ("xh", "z")
NEAR = ("xl", "xh", "z")
BF = jnp.bfloat16
F32 = jnp.float32
HALF = 64


def shape_of(shape, dtype):
    return jax.ShapeDtypeStruct(shape, dtype)


def from_behind(value, steps):
    count = lax.axis_size(SLAB)
    first, last = (max(0, -steps), min(count, count - steps))
    return lax.ppermute(value, SLAB, [(source, source + steps) for source in range(first, last)])


def pick_blocks(source_table, blocks):
    width = source_table.shape[1]
    return jnp.take(source_table.reshape(-1, BLK, width), blocks, axis=0).reshape(-1, width)


def pair(value):
    half = value.shape[-2] // 2
    return jnp.concatenate([value[..., :half, :], value[..., half:, :]], axis=-1)


def unpair(value):
    half = value.shape[-1] // 2
    return jnp.concatenate([value[..., :half], value[..., half:]], axis=-2)


def dot(left, right):
    return jnp.dot(left, right, preferred_element_type=F32)


def dot_rows(left, right):
    return lax.dot_general(left, right, (((0,), (0,)), ((), ())), preferred_element_type=F32)


def dot_transpose(left, right):
    return lax.dot_general(left, right, (((1,), (1,)), ((), ())), preferred_element_type=F32)


def left_lanes(rows):
    return lax.broadcasted_iota(jnp.int32, (rows, 2 * HALF), 1) < HALF


def join_halves(first, second):
    low = left_lanes(first.shape[0])
    first, second = first.astype(F32), second.astype(F32)
    upper = jnp.where(low, first, pltpu.roll(second, HALF, 1))
    lower = jnp.where(low, pltpu.roll(first, HALF, 1), second)
    return upper, lower


def one_hot_columns(offsets):
    cells = lax.broadcasted_iota(jnp.int32, (BLK, BLK), 0)
    return (cells == offsets).astype(F32)


def norm_parts(values):
    average = jnp.mean(values, axis=-1, keepdims=True)
    centred = values - average
    variance = jnp.mean(centred * centred, axis=-1, keepdims=True)
    inverse = lax.rsqrt(variance + EPSILON)
    return centred * inverse, inverse


def norm_back(upstream, normed, inverse, gain_vector):
    scaled = upstream * gain_vector
    return inverse * (
        scaled
        - jnp.mean(scaled, axis=-1, keepdims=True)
        - normed * jnp.mean(scaled * normed, axis=-1, keepdims=True)
    )


def split_three(value):
    high = value.astype(BF)
    rest = value - high.astype(F32)
    middle = rest.astype(BF)
    return high, middle, (rest - middle.astype(F32)).astype(BF)


def unpack_weights(core, mine, theirs, outs, counts):
    total = sum(counts)

    def place(source, parity):
        for y in range(source.shape[0]):
            for x in range(source.shape[1] // total):
                slab = (y * (source.shape[1] // total) + x) * 2 + parity
                at = x * total
                for out, count in zip(outs, counts):
                    out[pl.ds(slab * count, count), :] = source[y, pl.ds(at, count), :]
                    at += count

    for parity in range(2):

        @pl.when(core == parity)
        def _():
            place(mine, parity)
            place(theirs, 1 - parity)


def pack_grads(core, grads, keep, send, counts):
    total = sum(counts)
    per = keep.shape[1] // total
    for target, parity in ((keep, core), (send, 1 - core)):
        for y in range(keep.shape[0]):
            for x in range(per):
                at = x * total
                for grad, count in zip(grads, counts):
                    start = pl.multiple_of(((y * per + x) * 2 + parity) * count, 32)
                    target[y, pl.ds(at, count), :] = grad[pl.ds(start, count), :].astype(BF)
                    at += count


def edge_forward(
    scal, arrived, edges, offsets, mine, theirs, gain,
    joined, first, normed, inverse, new_edges, partial, own, upstream, w_in, w_out,
    ext, second,
):
    tiles = edges.shape[0] // BLK
    slab_blocks = partial.shape[0]
    half_rows = ext.shape[0] // 2
    lat_index, core, count = scal[2 * tiles], scal[2 * tiles + 1], scal[2 * tiles + 2]
    slabs = w_in.shape[0] // 3 // 32
    unpack_weights(core, mine, theirs, (w_in, w_out), (3 * L // slabs, L // slabs))
    for block in range(half_rows // BLK):
        rows = pl.ds(block * BLK, BLK)
        for k in range(slab_blocks // 2):
            upper, lower = join_halves(arrived[2 * k, rows, :], arrived[2 * k + 1, rows, :])
            ext[rows, pl.ds(k * BLK, BLK)] = upper.astype(BF)
            ext[pl.ds(half_rows + block * BLK, BLK), pl.ds(k * BLK, BLK)] = lower.astype(BF)
    for k in range(slab_blocks // 2):
        rows = pl.ds(half_rows, BLK // 2)
        upper, lower = join_halves(arrived[2 * k, rows, :], arrived[2 * k + 1, rows, :])
        upstream[pl.ds(0, BLK // 2), pl.ds(k * BLK, BLK)] = upper.astype(BF)
        upstream[pl.ds(BLK // 2, BLK // 2), pl.ds(k * BLK, BLK)] = lower.astype(BF)
    own[...] = ext[pl.ds(pl.multiple_of((HB + lat_index) * BLK, BLK), BLK), :]
    for t in range(tiles):
        rows = pl.ds(t * BLK, BLK)
        joined[rows, pl.ds(0, L)] = edges[rows, :]
        to_src = one_hot_columns(offsets[1, pl.ds(t, 1), :]).T.astype(BF)
        to_dst = one_hot_columns(offsets[0, pl.ds(t, 1), :]).T.astype(BF)
        src = pl.ds(pl.multiple_of(scal[tiles + t] * BLK, BLK), BLK)
        dst = pl.ds(pl.multiple_of((scal[t] + HB) * BLK, BLK), BLK)
        joined[rows, pl.ds(L, L)] = dot(to_src, ext[src, :]).astype(BF)
        joined[rows, pl.ds(2 * L, L)] = dot(to_dst, ext[dst, :]).astype(BF)
    for n in range(2):
        columns = pl.ds(n * 256, 256)
        first[:, columns] = jnp.maximum(dot(joined[...], w_in[:, columns]), 0.0).astype(BF)
    for n in range(2):
        columns = pl.ds(n * 256, 256)
        second[:, columns] = dot(first[...], w_out[:, columns])
    partial[...] = jnp.zeros_like(partial)
    for t in range(tiles):
        rows = pl.ds(t * BLK, BLK)
        live = (lat_index * tiles + t < count).astype(F32)
        values, inv = norm_parts(second[rows, :])
        normed[rows, :] = values
        inverse[rows, :] = jnp.broadcast_to(inv, (BLK, BLK))
        message = values * gain[...] * live
        new_edges[rows, :] = (edges[rows, :].astype(F32) + message).astype(BF)
        second[rows, :] = message
    for t in range(tiles):
        rows = pl.ds(t * BLK, BLK)
        into = one_hot_columns(offsets[0, pl.ds(t, 1), :]).astype(BF)
        high, middle, low = split_three(second[rows, :])
        block = scal[t]
        partial[block] = partial[block] + (dot(into, low) + dot(into, middle) + dot(into, high))


def node_step(
    scal, spread, own, upstream, mine, theirs, gain,
    d_agg, d_direct, new_rows, keep, send,
    w_in, w_out, joined, first, g_in, g_out,
):
    core = scal[1]
    slabs = w_in.shape[0] // 2 // 32
    counts = (2 * L // slabs, L // slabs)
    unpack_weights(core, mine, theirs, (w_in, w_out), counts)
    total = spread[0]
    for l in range(1, spread.shape[0]):
        total = total + spread[l]
    joined[:, pl.ds(0, L)] = own[...]
    joined[:, pl.ds(L, L)] = total.astype(BF)
    first[...] = jnp.maximum(dot(joined[...], w_in[...]), 0.0).astype(BF)
    normed, inverse = norm_parts(dot(first[...], w_out[...]))
    new_rows[...] = (own[...].astype(F32) + normed * gain[...]).astype(BF)
    d_second = norm_back(upstream[...].astype(F32), normed, inverse, gain[...]).astype(BF)
    g_out[...] = dot_rows(first[...], d_second)
    d_first = dot_transpose(d_second, w_out[...])
    d_first = jnp.where(first[...].astype(F32) > 0, d_first, 0.0).astype(BF)
    g_in[...] = dot_rows(joined[...], d_first)
    d_direct[...] = dot_transpose(d_first, w_in[pl.ds(0, L), :])
    d_agg[...] = dot_transpose(d_first, w_in[pl.ds(L, L), :]).astype(BF)
    pack_grads(core, (g_in, g_out), keep, send, counts)


def edge_backward(
    scal, d_agg, cot, normed, inverse, first, joined, w_in, w_out, gain, offsets, d_direct,
    grad_edges, columns, keep, send,
    d_second, d_first, d_ext, d_joined, g_in, g_out,
):
    tiles = cot.shape[0] // BLK
    lat_index, core, count = scal[2 * tiles], scal[2 * tiles + 1], scal[2 * tiles + 2]
    slabs = w_in.shape[0] // 3 // 32
    for t in range(tiles):
        rows = pl.ds(t * BLK, BLK)
        live = (lat_index * tiles + t < count).astype(F32)
        to_dst = one_hot_columns(offsets[0, pl.ds(t, 1), :]).T.astype(BF)
        picked = dot(to_dst, d_agg[scal[t], pl.ds(0, BLK), :])
        d_message = (cot[rows, :].astype(F32) + picked) * live
        back = norm_back(d_message, normed[rows, :], inverse[rows, pl.ds(0, 1)], gain[...])
        d_second[rows, :] = back.astype(BF)
    for n in range(2):
        part = pl.ds(n * 256, 256)
        back = dot_transpose(d_second[...], w_out[part, :])
        d_first[:, part] = jnp.where(first[:, part].astype(F32) > 0, back, 0.0).astype(BF)
    for n in range(6):
        part = pl.ds(n * 256, 256)
        d_joined[:, part] = dot_transpose(d_first[...], w_in[part, :])
    for n in range(2):
        part = pl.ds(n * 256, 256)
        g_out[part, :] = dot_rows(first[:, part], d_second[...])
    for n in range(6):
        part = pl.ds(n * 256, 256)
        g_in[part, :] = dot_rows(joined[:, part], d_first[...])
    pack_grads(core, (g_in, g_out), keep, send, (3 * L // slabs, L // slabs))
    d_ext[...] = jnp.zeros_like(d_ext)
    for t in range(tiles):
        rows = pl.ds(t * BLK, BLK)
        grad_edges[rows, :] = (cot[rows, :].astype(F32) + d_joined[rows, pl.ds(0, L)]).astype(BF)
        for row, place, at in ((1, scal[tiles + t], L), (0, scal[t] + HB, 2 * L)):
            into = one_hot_columns(offsets[row, pl.ds(t, 1), :]).astype(BF)
            value = d_joined[rows, pl.ds(at, L)]
            high = value.astype(BF)
            low = (value - high.astype(F32)).astype(BF)
            d_ext[place] = d_ext[place] + (dot(into, low) + dot(into, high))
    d_ext[HB + lat_index] = d_ext[HB + lat_index] + d_direct[...]
    half_blocks = d_ext.shape[0] // 2
    for block in range(half_blocks):
        rows = pl.ds(block * BLK, BLK)
        for k in range(columns.shape[0] // 2):
            lanes = pl.ds(k * BLK, BLK)
            first_out, second_out = join_halves(
                d_ext[block, :, lanes], d_ext[half_blocks + block, :, lanes]
            )
            columns[2 * k, rows, :] = first_out.astype(BF)
            columns[2 * k + 1, rows, :] = second_out.astype(BF)


def call(kernel, out_shape, scratch, flops, operands):
    moved = sum(x.size * x.dtype.itemsize for x in operands)
    moved += sum(x.size * x.dtype.itemsize for x in out_shape)
    vmem = pl.BlockSpec(memory_space=pltpu.VMEM)
    return pl.pallas_call(
        kernel,
        out_shape=out_shape,
        in_specs=[pl.BlockSpec(memory_space=pltpu.SMEM)] + [vmem] * (len(operands) - 1),
        out_specs=[vmem] * len(out_shape),
        scratch_shapes=[pltpu.VMEM(shape, dtype) for shape, dtype in scratch],
        cost_estimate=pl.CostEstimate(flops=flops, bytes_accessed=moved, transcendentals=0),
        compiler_params=pltpu.CompilerParams(vmem_limit_bytes=48 << 20),
    )(*operands)


def run_edge_forward(scal, arrived, edges, offsets, mine, theirs, gain):
    rows = edges.shape[0]
    lat_size = arrived.shape[0]
    ext_rows = 2 * arrived.shape[1] - BLK
    return call(
        edge_forward,
        [
            shape_of((rows, 3 * L), BF),
            shape_of((rows, L), BF),
            shape_of((rows, L), F32),
            shape_of((rows, BLK), F32),
            shape_of((rows, L), BF),
            shape_of((lat_size, BLK, L), F32),
            shape_of((BLK, L), BF),
            shape_of((BLK, L), BF),
            shape_of((3 * L, L), BF),
            shape_of((L, L), BF),
        ],
        [((ext_rows, L), BF), ((rows, L), F32)],
        2 * rows * 4 * L * L,
        (scal, arrived, edges, offsets, mine, theirs, gain),
    )


def run_node_step(scal, spread, own, upstream, mine, theirs, gain):
    return call(
        node_step,
        [
            shape_of((BLK, L), BF),
            shape_of((BLK, L), F32),
            shape_of((BLK, L), BF),
            shape_of(mine.shape, BF),
            shape_of(mine.shape, BF),
        ],
        [
            ((2 * L, L), BF),
            ((L, L), BF),
            ((BLK, 2 * L), BF),
            ((BLK, L), BF),
            ((2 * L, L), F32),
            ((L, L), F32),
        ],
        2 * BLK * 9 * L * L,
        (scal, spread, own, upstream, mine, theirs, gain),
    )


def run_edge_backward(
    scal, d_agg, cot, normed, inverse, first, joined, w_in, w_out, gain, offsets, d_direct, width
):
    rows = cot.shape[0]
    lat_size = d_agg.shape[0]
    blocks = lat_size + 2 * HB
    return call(
        edge_backward,
        [
            shape_of((rows, L), BF),
            shape_of((lat_size, blocks * BLK // 2, BLK), BF),
            shape_of((4, L // 2, L), BF),
            shape_of((4, L // 2, L), BF),
        ],
        [
            ((rows, L), BF),
            ((rows, L), BF),
            ((blocks, BLK, L), F32),
            ((rows, 3 * L), F32),
            ((3 * L, L), F32),
            ((L, L), F32),
        ],
        2 * rows * 8 * L * L,
        (scal, d_agg, cot, normed, inverse, first, joined, w_in, w_out, gain, offsets, d_direct),
    )


def swap_cores(value):
    return lax.ppermute(value, "c", [(0, 1), (1, 0)])


def spread_rows(value, axes):
    return lax.all_to_all(value, axes, 0, 0)


def gather_over(value, axes):
    return spread_rows(jnp.broadcast_to(value, (lax.axis_size(axes),) + value.shape), axes)


def slab_rows_of(near, pieces):
    lat = lax.axis_size(LAT)
    shaped = near.reshape((-1, lat) + near.shape[1:])
    out, at = [], 0
    for count in pieces:
        out.append(shaped[:, :, at : at + count].reshape(shaped.shape[0], lat * count, L))
        at += count
    return jnp.concatenate(out, axis=1).reshape(-1, L)


def reduce_grads(keep, send, counts):
    lat = lax.axis_size(LAT)
    arrived = swap_cores(send)
    halves = (keep.astype(F32) + arrived.astype(F32)).astype(BF)
    over_y = jnp.sum(spread_rows(halves, "y").astype(F32), axis=0)
    shaped = over_y.reshape(lax.axis_size("xl"), lat * sum(counts), L)
    parts, at = [], 0
    for count in counts:
        parts.append(shaped[:, at : at + lat * count].reshape(-1, lat, count, L))
        at += lat * count
    return jnp.concatenate(parts, axis=2).reshape(-1, sum(counts), L).astype(BF)


def per_device(
    nodes,
    edges,
    edge_tiles,
    edge_offsets,
    tile_counts,
    halo_blocks,
    w_edge_in,
    w_edge_out,
    w_node_in,
    w_node_out,
    edge_gain,
    node_gain,
    node_cotangent,
    edge_cotangent,
):
    lat_size = lax.axis_size(LAT)
    lat_index = lax.axis_index(LAT)
    core = lax.axis_index("c")
    slab_rows, width = nodes.shape
    own_rows = slab_rows // lat_size
    halo_rows = HB * BLK
    ext_rows = slab_rows + 2 * halo_rows
    up_list = halo_blocks[0, 0]
    down_list = halo_blocks[0, 1]
    edge_counts = (w_edge_in.shape[0], w_edge_out.shape[0])
    node_counts = (w_node_in.shape[0], w_node_out.shape[0])

    scal = jnp.concatenate(
        [
            edge_tiles.reshape(-1),
            jnp.stack([lat_index, core]).astype(jnp.int32),
            tile_counts,
        ]
    )
    node_scal = jnp.stack([lat_index, core]).astype(jnp.int32)
    offsets = edge_offsets.reshape(2, -1, BLK)
    edge_gain_row = edge_gain.reshape(1, L)
    node_gain_row = node_gain.reshape(1, L)

    from_lower = unpair(from_behind(pair(pick_blocks(nodes, up_list)), 1))
    from_upper = unpair(from_behind(pair(pick_blocks(nodes, down_list)), -1))

    shards = [w_edge_in, w_edge_out, w_node_in, w_node_out]
    rows = sum(shard.shape[0] for shard in shards)
    near = gather_over(jnp.concatenate(shards + [jnp.zeros((-rows % 16, L), BF)], axis=0), NEAR)
    edge_part = slab_rows_of(near[:, : sum(edge_counts)], edge_counts)
    node_part = slab_rows_of(near[:, sum(edge_counts) : rows], node_counts)

    table = pair(jnp.concatenate([from_lower, nodes, from_upper], axis=0))
    cot = pair(node_cotangent.reshape(lat_size, own_rows, width))
    message_out = jnp.concatenate(
        [jnp.broadcast_to(table, (lat_size,) + table.shape), cot], axis=1
    )
    edge_mine = gather_over(edge_part, "y")
    arrived = spread_rows(message_out, LAT)
    edge_theirs = swap_cores(edge_mine)

    joined, first, normed, inverse, new_edges, partial, own, upstream, e_in, e_out = (
        run_edge_forward(scal, arrived, edges, offsets, edge_mine, edge_theirs, edge_gain_row)
    )
    spread = spread_rows(partial, LAT)
    node_mine = gather_over(node_part, "y")
    node_theirs = swap_cores(node_mine)
    d_agg, d_direct, new_rows, node_keep, node_send = run_node_step(
        node_scal, spread, own, upstream, node_mine, node_theirs, node_gain_row
    )

    groups = L // width
    group_rows = own_rows // groups
    rows_out = (
        new_rows.reshape(groups, group_rows, lat_size, width)
        .transpose(2, 1, 0, 3)
        .reshape(lat_size, group_rows, L)
    )
    second_out = jnp.concatenate(
        [jnp.broadcast_to(d_agg, (lat_size,) + d_agg.shape), rows_out], axis=1
    )
    second_in = spread_rows(second_out, LAT)
    new_nodes = (
        second_in[:, own_rows:]
        .reshape(lat_size, group_rows, groups, width)
        .transpose(0, 2, 1, 3)
        .reshape(slab_rows, width)
    )
    node_near = reduce_grads(node_keep, node_send, node_counts)

    grad_edges, columns, edge_keep, edge_send = run_edge_backward(
        scal, second_in, edge_cotangent, normed, inverse, first, joined, e_in, e_out,
        edge_gain_row, offsets, d_direct, width,
    )
    summed = unpair(jnp.sum(spread_rows(columns, LAT).astype(F32), axis=0))
    d_lower = pair(summed[:halo_rows].astype(BF))
    d_middle = summed[halo_rows : halo_rows + slab_rows]
    d_upper = pair(summed[halo_rows + slab_rows :].astype(BF))
    from_above = unpair(from_behind(d_lower, -1)).astype(F32).reshape(HB, BLK, width)
    from_below = unpair(from_behind(d_upper, 1)).astype(F32).reshape(HB, BLK, width)
    blocks = d_middle.reshape(-1, BLK, width)
    numbers = jnp.arange(blocks.shape[0])
    for j in range(HB):
        blocks = blocks + jnp.where((numbers == up_list[j])[:, None, None], from_above[j], 0.0)
        blocks = blocks + jnp.where((numbers == down_list[j])[:, None, None], from_below[j], 0.0)
    grad_slab = blocks.reshape(slab_rows, width).astype(BF)

    edge_near = reduce_grads(edge_keep, edge_send, edge_counts)
    both = jnp.concatenate([edge_near, node_near], axis=1)
    both = jnp.pad(both, ((0, 0), (0, -both.shape[1] % 16), (0, 0)))
    total = jnp.sum(spread_rows(both, NEAR).astype(F32), axis=0)
    out, at = [], 0
    for count in edge_counts + node_counts:
        out.append(total[at : at + count])
        at += count
    return (new_nodes, new_edges, grad_slab, grad_edges) + tuple(out)


def solution(mesh):
    fine = Mesh(mesh.devices.reshape(4, 2, 2, 2, 4), ("y", "xl", "c", "xh", "z"))
    every = SLAB + LAT
    by_rows = P(every, None)
    split = P(SLAB, LAT)
    placed = (
        split,
        by_rows,
        P(None, every),
        P(None, every),
        P(SLAB),
        P(SLAB, None, None),
        by_rows,
        by_rows,
        by_rows,
        by_rows,
        P(),
        P(),
        split,
        by_rows,
    )
    return jax.shard_map(
        per_device,
        mesh=fine,
        in_specs=placed,
        out_specs=(split, by_rows, split, by_rows, by_rows, by_rows, by_rows, by_rows),
        check_vma=False,
    )
```

time: 305 us -> 230 us (0.75); the launches traced: 300 us -> 229 us
  other arithmetic: 61.4 us -> 14.7 us
  local copies, waits for them, and re-layouts: 69.7 us -> 28.9 us
  Pallas kernels: 0 us -> 17.3 us
  matrix products: 15.2 us -> 0 us
  starting transfers between devices: 45.8 us -> 60.1 us
    scatter-add x3 -> x0, other arithmetic: 20 us -> none  [the longest x1 7.92 us: per_device(): d_extended = d_extended.at[halo_rows + dst_row].add(d_joined[:, 2 * L:])]
    pallas_call x0 -> x3, Pallas kernels: none -> 17.3 us  [call(): pl.pallas_call(kernel, out_shape=out_shape, in_specs=[pl.BlockSpec(memory...]
    dot_general x12 -> x0, matrix products: 15.2 us -> none  [the longest x4 5.17 us: times_transpose(): lax.dot_general(left, weight, (((1,), (1,)), ((), ())), preferred_element...]
    all_to_all x6 -> x10, starting transfers between devices: 38.3 us -> 52.9 us  [spread_rows(): return lax.all_to_all(value, axes, 0, 0)]
    convert_element_type x9 -> x2, other arithmetic: 12.1 us -> 2.45 us  [reduce_grads(): halves = (keep.astype(F32) + arrived.astype(F32)).astype(BF)]
    gather x5 -> x0, local copies, waits for them, and re-layouts: 8.06 us -> none  [the longest x1 2.64 us: per_device(): slab_full[dst_row]]
    concatenate x5, local copies, waits for them, and re-layouts: 10.7 us -> 3 us  [the longest x1 2.88 us: per_device(): jnp.concatenate(shards + [jnp.zeros((-rows % 16, L), BF)], axis=0)]
    select_n x3 -> x0, other arithmetic: 7.54 us -> none  [the longest x1 5.67 us: per_device(): d_extended = d_extended.at[halo_rows + dst_row].add(d_joined[:, 2 * L:])]
  transfers between devices with their start and end apart: 12 -> 18, of which waited for: 8 -> 10; matrix products, arithmetic and copies ran while one was open for 19% -> 10% of each run, Pallas kernels for 0% -> 6%
where the time goes in v2:
time: 230 us; the launch traced here: 229 us
  waiting for transfers between devices  106 us (46%)
  starting transfers between devices  60.1 us (26%)
  local copies, waits for them, and re-layouts  28.9 us (13%)
  Pallas kernels  17.3 us (8%)
  other arithmetic  14.7 us (6%)
    all_to_all x10, waiting for transfers between devices, spread_rows(): return lax.all_to_all(value, axes, 0, 0)  103 us
    all_to_all x10, starting transfers between devices, spread_rows(): return lax.all_to_all(value, axes, 0, 0)  52.9 us
    pallas_call x3, Pallas kernels, call(): pl.pallas_call(kernel, out_shape=out_shape, in_specs=[pl.BlockSpec(memory...  17.3 us
    unnamed x55, local copies, waits for them, and re-layouts  15.4 us
    ppermute x4, starting transfers between devices, from_behind(): lax.ppermute(value, SLAB, [(source, source + steps) for source in range(f...  7.08 us
  transfers between devices with their start and end apart: 18, of which 10 were waited for; matrix products, arithmetic and copies ran while one was open for 10% of the time, Pallas kernels for 6%

profile of v2, /device:TPU:0, one launch (start us, length us, event | category | flops | bytes accessed | tf_op | source)
XLA Modules:
  0.0 228.7 jit_solution(12367753551024828272)
XLA Ops:
  0.7 2.9 %concatenate.78 = bf16[32,512]{1,0:T(8,128)(2,1)S(1)} concatenate(bf16[12,512]{1,0:T(8,128)(2,1)} %param.22, bf16[4,512]{1,0:T(4,128)(2,1)} %param.23, bf16[8,512]{1,0:T(8,128)(2,1)} %param.24, bf16[4,512]{1,0:T(4,128)(2,1)} %param.25, bf16[4,512]{1,0:T(4,128)(2,1)S(1)} %broadcast_in_dim.99), dimensions={0} | concatenate | bytes 65536 | tf_op jit(solution)/shard_map/concatenate | solution.py:437
  4.4 8.0 %all-to-all-start.1 = ((bf16[16,32,512]{2,1,0:T(8,128)(2,1)}), bf16[16,32,512]{2,1,0:T(8,128)(2,1)S(1)}, u32[]{:S(2)}, u32[]{:S(2)}) async-start(bf16[16,32,512]{2,1,0:T(8,128)(2,1)} %broadcast_in_dim.100), calls=%async_computation.1 | async-start | bytes 1048576 | tf_op jit(solution)/shard_map/all_to_all | solution.py:362
  17.4 6.1 %all-to-all-done.1 = bf16[16,32,512]{2,1,0:T(8,128)(2,1)S(1)} async-done(((bf16[16,32,512]{2,1,0:T(8,128)(2,1)}), bf16[16,32,512]{2,1,0:T(8,128)(2,1)S(1)}, u32[]{:S(2)}, u32[]{:S(2)}) %all-to-all-start.1) | async-done | bytes 524320 | tf_op jit(solution)/shard_map/all_to_all | solution.py:362
  25.4 4.5 %all-to-all-start.2 = ((bf16[4,256,512]{2,1,0:T(8,128)(2,1)}), bf16[4,256,512]{2,1,0:T(8,128)(2,1)S(1)}, u32[]{:S(2)}, u32[]{:S(2)}) async-start(bf16[4,256,512]{2,1,0:T(8,128)(2,1)} %broadcast_in_dim.101), calls=%async_computation.2 | async-start | bytes 2097152 | tf_op jit(solution)/shard_map/all_to_all | solution.py:362
  31.7 11.8 %all-to-all-done.2.mine = bf16[4,256,512]{2,1,0:T(8,128)(2,1)S(1)} async-done(((bf16[4,256,512]{2,1,0:T(8,128)(2,1)}), bf16[4,256,512]{2,1,0:T(8,128)(2,1)S(1)}, u32[]{:S(2)}, u32[]{:S(2)}) %all-to-all-start.2) | async-done | bytes 1048608 | tf_op jit(solution)/shard_map/all_to_all | solution.py:362
  43.5 4.9 %all-to-all-start = ((bf16[8,832,128]{2,1,0:T(8,128)(2,1)}), bf16[8,832,128]{2,1,0:T(8,128)(2,1)}, u32[]{:S(2)}, u32[]{:S(2)}) async-start(bf16[8,832,128]{2,1,0:T(8,128)(2,1)} %maximum_maximum_fusion), calls=%async_computation | async-start | bytes 3407872 | tf_op jit(solution)/shard_map/all_to_all | solution.py:362
  48.6 19.7 %all-to-all-done.arrived = bf16[8,832,128]{2,1,0:T(8,128)(2,1)} async-done(((bf16[8,832,128]{2,1,0:T(8,128)(2,1)}), bf16[8,832,128]{2,1,0:T(8,128)(2,1)}, u32[]{:S(2)}, u32[]{:S(2)}) %all-to-all-start) | async-done | bytes 1703968 | tf_op jit(solution)/shard_map/all_to_all | solution.py:362
  69.4 3.5 %all-to-all-start.4 = ((bf16[4,192,512]{2,1,0:T(8,128)(2,1)}), bf16[4,192,512]{2,1,0:T(8,128)(2,1)S(1)}, u32[]{:S(2)}, u32[]{:S(2)}) async-start(bf16[4,192,512]{2,1,0:T(8,128)(2,1)} %broadcast_in_dim.102), calls=%async_computation.4 | async-start | bytes 1572864 | tf_op jit(solution)/shard_map/all_to_all | solution.py:362
  73.7 6.7 %shard_map.197 = (bf16[512,1536]{1,0:T(8,128)(2,1)}, bf16[512,512]{1,0:T(8,128)(2,1)S(1)}, f32[512,512]{1,0:T(8,128)S(1)}, f32[512,128]{1,0:T(8,128)S(1)}, bf16[...) custom-call(s32[11]{0:T(128)S(1)} %pad_add_fusion.1.scal, ...), custom_call_target="tpu_custom_call" | custom-call | flops 1073741824 | bytes 12720172 | tf_op jit(solution)/shard_map/pallas_call | solution.py:272
  84.4 6.0 %all-to-all-start.3 = ((f32[8,128,512]{2,1,0:T(8,128)}), f32[8,128,512]{2,1,0:T(8,128)S(1)}, u32[]{:S(2)}, u32[]{:S(2)}) async-start(f32[8,128,512]{2,1,0:T(8,128)} %get-tuple-element.28), calls=%async_computation.3 | async-start | bytes 4194304 | tf_op jit(solution)/shard_map/all_to_all | solution.py:362
  90.5 2.2 collective-permute-done.3.theirs
  93.6 22.3 %all-to-all-done.3.spread = f32[8,128,512]{2,1,0:T(8,128)S(1)} async-done(((f32[8,128,512]{2,1,0:T(8,128)}), f32[8,128,512]{2,1,0:T(8,128)S(1)}, u32[]{:S(2)}, u32[]{:S(2)}) %all-to-all-start.3) | async-done | bytes 2097184 | tf_op jit(solution)/shard_map/all_to_all | solution.py:362
  117.1 2.6 %shard_map.198 = (bf16[128,512]{1,0:T(8,128)(2,1)S(1)}, f32[128,512]{1,0:T(8,128)S(1)}, bf16[128,512]{1,0:T(8,128)(2,1)S(1)}, bf16[4,192,512]{2,1,0:T(8,128)(2,1)S(1)}, bf16[4,192,512]{2,1,0:T(8,128)(2,1)S(1)}) custom-call(s32[2]{0:T(128)S(1)} %pad_add_fusion.scal, f32[8,128,512]{2,1,0:T(8,128)S(1)} %all-to-all-done.3.spread, ...), custom_call_target="tpu_custom_call" | custom-call | flops 603979776 | bytes 6031368 | tf_op jit(solution)/shard_map/pallas_call | solution.py:272
  124.2 4.9 %all-to-all-start.5 = ((bf16[8,144,512]{2,1,0:T(8,128)(2,1)}), bf16[8,144,512]{2,1,0:T(8,128)(2,1)}, u32[]{:S(2)}, u32[]{:S(2)}) async-start(bf16[8,144,512]{2,1,0:T(8,128)(2,1)} %pad_maximum_fusion), calls=%async_computation.5 | async-start | bytes 2359296 | tf_op jit(solution)/shard_map/all_to_all | solution.py:362
  130.3 16.1 %all-to-all-done.5.d_agg = bf16[8,144,512]{2,1,0:T(8,128)(2,1)} async-done(((bf16[8,144,512]{2,1,0:T(8,128)(2,1)}), bf16[8,144,512]{2,1,0:T(8,128)(2,1)}, u32[]{:S(2)}, u32[]{:S(2)}) %all-to-all-start.5) | async-done | bytes 1179680 | tf_op jit(solution)/shard_map/all_to_all | solution.py:362
  146.4 4.4 %all-to-all-start.8 = ((bf16[4,192,512]{2,1,0:T(8,128)(2,1)}), bf16[4,192,512]{2,1,0:T(8,128)(2,1)}, u32[]{:S(2)}, u32[]{:S(2)}) async-start(bf16[4,192,512]{2,1,0:T(8,128)(2,1)} %add_convert_fusion.1), calls=%async_computation.8 | async-start | bytes 1572864 | tf_op jit(solution)/shard_map/all_to_all | solution.py:362
  154.9 8.0 %shard_map.199 = (bf16[512,512]{1,0:T(8,128)(2,1)}, bf16[8,768,128]{2,1,0:T(8,128)(2,1)}, bf16[4,256,512]{2,1,0:T(8,128)(2,1)S(1)}, bf16[4,256,512]{2,1,0:T(8,128)(2,1)S(1)}) custom-call(s32[11]{0:T(128)S(1)} %pad_add_fusion.1.scal, bf16[8,144,512]{2,1,0:T(8,128)(2,1)} %all-to-all-done.5.d_agg, bf16[512,512]{1,0:T(8,128)(2,1)S(1)} %copy-done.12, ...), custom_call_target="tpu_custom_call" | custom-call | flops 2147483648 | bytes 11671596 | tf_op jit(solution)/shard_map/pallas_call | solution.py:272
  162.9 5.4 %all-to-all-start.6 = ((bf16[8,768,128]{2,1,0:T(8,128)(2,1)}), bf16[8,768,128]{2,1,0:T(8,128)(2,1)}, u32[]{:S(2)}, u32[]{:S(2)}) async-start(bf16[8,768,128]{2,1,0:T(8,128)(2,1)} %get-tuple-element.41), calls=%async_computation.6 | async-start | bytes 3145728 | tf_op jit(solution)/shard_map/all_to_all | solution.py:362
  177.8 11.0 %all-to-all-done.6 = bf16[8,768,128]{2,1,0:T(8,128)(2,1)} async-done(((bf16[8,768,128]{2,1,0:T(8,128)(2,1)}), bf16[8,768,128]{2,1,0:T(8,128)(2,1)}, u32[]{:S(2)}, u32[]{:S(2)}) %all-to-all-start.6) | async-done | bytes 1572896 | tf_op jit(solution)/shard_map/all_to_all | solution.py:362
  188.9 4.3 %all-to-all-start.7 = ((bf16[4,256,512]{2,1,0:T(8,128)(2,1)}), bf16[4,256,512]{2,1,0:T(8,128)(2,1)S(1)}, u32[]{:S(2)}, u32[]{:S(2)}) async-start(bf16[4,256,512]{2,1,0:T(8,128)(2,1)} %add_convert_fusion), calls=%async_computation.7 | async-start | bytes 2097152 | tf_op jit(solution)/shard_map/all_to_all | solution.py:362
  196.6 3.0 %collective-permute-start.5 = (bf16[128,128]{1,0:T(8,128)(2,1)S(1)}, bf16[128,128]{1,0:T(8,128)(2,1)S(1)}, u32[]{:S(2)}, u32[]{:S(2)}) collective-permute-start(bf16[128,128]{1,0:T(8,128)(2,1)S(1)} %pad_maximum_fusion.11), channel_id=1, source_target_pairs={{0,8},{8,16},{16,24},{24,32},{32,40},{40,48},{48,56},{56,64},{64,7... | collective-permute-start | bytes 98312 | tf_op jit(solution)/shard_map/ppermute | solution.py:28
  200.5 7.3 %all-to-all-done.7 = bf16[4,256,512]{2,1,0:T(8,128)(2,1)S(1)} async-done(((bf16[4,256,512]{2,1,0:T(8,128)(2,1)}), bf16[4,256,512]{2,1,0:T(8,128)(2,1)S(1)}, u32[]{:S(2)}, u32[]{:S(2)}) %all-to-all-start.7) | async-done | bytes 1048608 | tf_op jit(solution)/shard_map/all_to_all | solution.py:362
  209.2 7.2 %all-to-all-start.9 = ((bf16[16,32,512]{2,1,0:T(8,128)(2,1)}), bf16[16,32,512]{2,1,0:T(8,128)(2,1)S(1)}, u32[]{:S(2)}, u32[]{:S(2)}) async-start(bf16[16,32,512]{2,1,0:T(8,128)(2,1)} %fusion.6), calls=%async_computation.9 | async-start | bytes 1048576 | tf_op jit(solution)/shard_map/all_to_all | solution.py:362
  218.5 8.3 %all-to-all-done.9 = bf16[16,32,512]{2,1,0:T(8,128)(2,1)S(1)} async-done(((bf16[16,32,512]{2,1,0:T(8,128)(2,1)}), bf16[16,32,512]{2,1,0:T(8,128)(2,1)S(1)}, u32[]{:S(2)}, u32[]{:S(2)}) %all-to-all-start.9) | async-done | bytes 524320 | tf_op jit(solution)/shard_map/all_to_all | solution.py:362
  (152 shorter events, 45.7 us)
Async XLA Ops:
  4.4 19.2 %all-to-all-start.1 = ((bf16[16,32,512]{2,1,0:T(8,128)(2,1)}), bf16[16,32,512]{2,1,0:T(8,128)(2,1)S(1)}, u32[]{:S(2)}, u32[]{:S(2)}) async-start(bf16[16,32,512]{2,1,0:T(8,128)(2,1)} %broadcast_in_dim.100), calls=%async_computation.1 | async-start | bytes 1048576 | tf_op jit(solution)/shard_map/all_to_all | solution.py:362
  14.4 15.4 %collective-permute-start = (bf16[128,128]{0,1:T(8,128)(2,1)S(1)}, bf16[128,128]{0,1:T(8,128)(2,1)S(1)}, u32[]{:S(2)}, u32[]{:S(2)}) collective-permute-start(bf16[128,128]{0,1:T(8,128)(2,1)S(1)} %pad_maximum_fusion.8), channel_id=1, source_target_pairs={{0,8},{8,16},{16,24},{24,32},{32,40},{40,48},{48,56},{56,64},{64,7... | collective-permute-start | bytes 98312 | tf_op jit(solution)/shard_map/ppermute | solution.py:28
  15.9 14.0 %collective-permute-start.1 = (bf16[128,128]{0,1:T(8,128)(2,1)S(1)}, bf16[128,128]{0,1:T(8,128)(2,1)S(1)}, u32[]{:S(2)}, u32[]{:S(2)}) collective-permute-start(bf16[128,128]{0,1:T(8,128)(2,1)S(1)} %pad_maximum_fusion.9), channel_id=1, source_target_pairs={{8,0},{16,8},{24,16},{32,24},{40,32},{48,40},{56,48},{64,56},{72,6... | collective-permute-start | bytes 98312 | tf_op jit(solution)/shard_map/ppermute | solution.py:28
  25.4 18.1 %all-to-all-start.2 = ((bf16[4,256,512]{2,1,0:T(8,128)(2,1)}), bf16[4,256,512]{2,1,0:T(8,128)(2,1)S(1)}, u32[]{:S(2)}, u32[]{:S(2)}) async-start(bf16[4,256,512]{2,1,0:T(8,128)(2,1)} %broadcast_in_dim.101), calls=%async_computation.2 | async-start | bytes 2097152 | tf_op jit(solution)/shard_map/all_to_all | solution.py:362
  43.5 24.8 %all-to-all-start = ((bf16[8,832,128]{2,1,0:T(8,128)(2,1)}), bf16[8,832,128]{2,1,0:T(8,128)(2,1)}, u32[]{:S(2)}, u32[]{:S(2)}) async-start(bf16[8,832,128]{2,1,0:T(8,128)(2,1)} %maximum_maximum_fusion), calls=%async_computation | async-start | bytes 3407872 | tf_op jit(solution)/shard_map/all_to_all | solution.py:362
  48.4 25.3 %collective-permute-start.2 = (bf16[4,256,512]{2,1,0:T(8,128)(2,1)S(1)}, bf16[4,256,512]{2,1,0:T(8,128)(2,1)S(1)}, u32[]{:S(2)}, u32[]{:S(2)}) collective-permute-start(bf16[4,256,512]{2,1,0:T(8,128)(2,1)S(1)} %all-to-all-done.2.mine), channel_id=1, source_target_pairs={{0,8},{8,0},{1,9},{9,1},{2,10},{10,2},{3,11},{11,3},{4,12},{12,4},... | collective-permute-start | bytes 3145736 | tf_op jit(solution)/shard_map/ppermute | solution.py:358
  48.5 25.0 %copy-start.25 = (s32[2,4]{1,0:T(2,128)S(1)}, s32[2,4]{1,0:T(2,128)}, u32[]{:S(2)}) copy-start(s32[2,4]{1,0:T(2,128)} %param.18) | copy-start | bytes 100
  48.5 25.1 %copy-start.24 = (s32[2,512]{1,0:T(2,128)S(1)}, s32[2,512]{1,0:T(2,128)}, u32[]{:S(2)}) copy-start(s32[2,512]{1,0:T(2,128)} %param.19) | copy-start | bytes 12292
  48.5 25.2 %copy-start.4 = (bf16[512,512]{1,0:T(8,128)(2,1)S(1)}, bf16[512,512]{1,0:T(8,128)(2,1)}, u32[]{:S(2)}) copy-start(bf16[512,512]{1,0:T(8,128)(2,1)} %edges.1) | copy-start | bytes 1572868
  48.5 25.2 %copy-start.7 = (f32[512]{0:T(512)S(1)}, f32[512]{0:T(512)}, u32[]{:S(2)}) copy-start(f32[512]{0:T(512)} %param.26) | copy-start | bytes 6148
  69.4 15.0 %all-to-all-start.4 = ((bf16[4,192,512]{2,1,0:T(8,128)(2,1)}), bf16[4,192,512]{2,1,0:T(8,128)(2,1)S(1)}, u32[]{:S(2)}, u32[]{:S(2)}) async-start(bf16[4,192,512]{2,1,0:T(8,128)(2,1)} %broadcast_in_dim.102), calls=%async_computation.4 | async-start | bytes 1572864 | tf_op jit(solution)/shard_map/all_to_all | solution.py:362
  84.4 31.6 %copy-start.6 = (bf16[128,512]{1,0:T(8,128)(2,1)S(1)}, bf16[128,512]{1,0:T(8,128)(2,1)}, u32[]{:S(2)}) copy-start(bf16[128,512]{1,0:T(8,128)(2,1)} %copy-done.5) | copy-start | bytes 393220
  84.4 31.6 %copy-start.8 = (f32[512]{0:T(512)S(1)}, f32[512]{0:T(512)}, u32[]{:S(2)}) copy-start(f32[512]{0:T(512)} %param.27) | copy-start | bytes 6148
  84.4 31.6 %all-to-all-start.3 = ((f32[8,128,512]{2,1,0:T(8,128)}), f32[8,128,512]{2,1,0:T(8,128)S(1)}, u32[]{:S(2)}, u32[]{:S(2)}) async-start(f32[8,128,512]{2,1,0:T(8,128)} %get-tuple-element.28), calls=%async_computation.3 | async-start | bytes 4194304 | tf_op jit(solution)/shard_map/all_to_all | solution.py:362
  90.4 2.3 collective-permute-start.3
  122.9 6.2 %collective-permute-start.7 = (bf16[4,192,512]{2,1,0:T(8,128)(2,1)}, bf16[4,192,512]{2,1,0:T(8,128)(2,1)S(1)}, u32[]{:S(2)}, u32[]{:S(2)}) collective-permute-start(bf16[4,192,512]{2,1,0:T(8,128)(2,1)} %copy-done.11), channel_id=1, source_target_pairs={{0,8},{8,0},{1,9},{9,1},{2,10},{10,2},{3,11},{11,3},{4,12},{12,4},... | collective-permute-start | bytes 2359304 | tf_op jit(solution)/shard_map/ppermute | solution.py:358
  124.2 22.2 %all-to-all-start.5 = ((bf16[8,144,512]{2,1,0:T(8,128)(2,1)}), bf16[8,144,512]{2,1,0:T(8,128)(2,1)}, u32[]{:S(2)}, u32[]{:S(2)}) async-start(bf16[8,144,512]{2,1,0:T(8,128)(2,1)} %pad_maximum_fusion), calls=%async_computation.5 | async-start | bytes 2359296 | tf_op jit(solution)/shard_map/all_to_all | solution.py:362
  146.4 16.4 %all-to-all-start.8 = ((bf16[4,192,512]{2,1,0:T(8,128)(2,1)}), bf16[4,192,512]{2,1,0:T(8,128)(2,1)}, u32[]{:S(2)}, u32[]{:S(2)}) async-start(bf16[4,192,512]{2,1,0:T(8,128)(2,1)} %add_convert_fusion.1), calls=%async_computation.8 | async-start | bytes 1572864 | tf_op jit(solution)/shard_map/all_to_all | solution.py:362
  162.9 26.0 %all-to-all-start.6 = ((bf16[8,768,128]{2,1,0:T(8,128)(2,1)}), bf16[8,768,128]{2,1,0:T(8,128)(2,1)}, u32[]{:S(2)}, u32[]{:S(2)}) async-start(bf16[8,768,128]{2,1,0:T(8,128)(2,1)} %get-tuple-element.41), calls=%async_computation.6 | async-start | bytes 3145728 | tf_op jit(solution)/shard_map/all_to_all | solution.py:362
  168.2 8.3 %collective-permute-start.6 = (bf16[4,256,512]{2,1,0:T(8,128)(2,1)S(1)}, bf16[4,256,512]{2,1,0:T(8,128)(2,1)S(1)}, u32[]{:S(2)}, u32[]{:S(2)}) collective-permute-start(bf16[4,256,512]{2,1,0:T(8,128)(2,1)S(1)} %get-tuple-element.44), channel_id=1, source_target_pairs={{0,8},{8,0},{1,9},{9,1},{2,10},{10,2},{3,11},{11,3},{4,12},{12,4},... | collective-permute-start | bytes 3145736 | tf_op jit(solution)/shard_map/ppermute | solution.py:358
  188.9 19.0 %all-to-all-start.7 = ((bf16[4,256,512]{2,1,0:T(8,128)(2,1)}), bf16[4,256,512]{2,1,0:T(8,128)(2,1)S(1)}, u32[]{:S(2)}, u32[]{:S(2)}) async-start(bf16[4,256,512]{2,1,0:T(8,128)(2,1)} %add_convert_fusion), calls=%async_computation.7 | async-start | bytes 2097152 | tf_op jit(solution)/shard_map/all_to_all | solution.py:362
  195.2 4.4 %collective-permute-start.4 = (bf16[128,128]{1,0:T(8,128)(2,1)S(1)}, bf16[128,128]{1,0:T(8,128)(2,1)S(1)}, u32[]{:S(2)}, u32[]{:S(2)}) collective-permute-start(bf16[128,128]{1,0:T(8,128)(2,1)S(1)} %pad_maximum_fusion.10), channel_id=1, source_target_pairs={{8,0},{16,8},{24,16},{32,24},{40,32},{48,40},{56,48},{64,56},{72,6... | collective-permute-start | bytes 98312 | tf_op jit(solution)/shard_map/ppermute | solution.py:28
  196.6 3.9 %collective-permute-start.5 = (bf16[128,128]{1,0:T(8,128)(2,1)S(1)}, bf16[128,128]{1,0:T(8,128)(2,1)S(1)}, u32[]{:S(2)}, u32[]{:S(2)}) collective-permute-start(bf16[128,128]{1,0:T(8,128)(2,1)S(1)} %pad_maximum_fusion.11), channel_id=1, source_target_pairs={{0,8},{8,16},{16,24},{24,32},{32,40},{40,48},{48,56},{56,64},{64,7... | collective-permute-start | bytes 98312 | tf_op jit(solution)/shard_map/ppermute | solution.py:28
  209.2 17.6 %all-to-all-start.9 = ((bf16[16,32,512]{2,1,0:T(8,128)(2,1)}), bf16[16,32,512]{2,1,0:T(8,128)(2,1)S(1)}, u32[]{:S(2)}, u32[]{:S(2)}) async-start(bf16[16,32,512]{2,1,0:T(8,128)(2,1)} %fusion.6), calls=%async_computation.9 | async-start | bytes 1048576 | tf_op jit(solution)/shard_map/all_to_all | solution.py:362
  (20 other events, 95.5 us)

commit v3 on v2

v3 whole, which is shorter than its diff:
```python
import jax
import jax.numpy as jnp
from jax import lax
from jax.experimental import pallas as pl
from jax.experimental.pallas import tpu as pltpu
from jax.sharding import Mesh, PartitionSpec as P

L = 512
BLK = 128
HB = 2
EPSILON = 1e-05

SLAB = ("y", "xl", "c")
LAT = ("xh", "z")
NEAR = ("xl", "xh", "z")
BF = jnp.bfloat16
F32 = jnp.float32
EDGE_MIB = 20
NODE_MIB = 14
BACK_MIB = 26


def shape_of(shape, dtype):
    return jax.ShapeDtypeStruct(shape, dtype)


def from_behind(value, steps):
    count = lax.axis_size(SLAB)
    first, last = (max(0, -steps), min(count, count - steps))
    return lax.ppermute(value, SLAB, [(source, source + steps) for source in range(first, last)])


def dot(left, right):
    return jnp.dot(left, right, preferred_element_type=F32)


def dot_rows(left, right):
    return lax.dot_general(left, right, (((0,), (0,)), ((), ())), preferred_element_type=F32)


def dot_transpose(left, right):
    return lax.dot_general(left, right, (((1,), (1,)), ((), ())), preferred_element_type=F32)


def one_hot_columns(offsets):
    cells = lax.broadcasted_iota(jnp.int32, (BLK, BLK), 0)
    return (cells == offsets).astype(F32)


def norm_parts(values):
    average = jnp.mean(values, axis=-1, keepdims=True)
    centred = values - average
    variance = jnp.mean(centred * centred, axis=-1, keepdims=True)
    inverse = lax.rsqrt(variance + EPSILON)
    return centred * inverse, inverse


def norm_back(upstream, normed, inverse, gain_vector):
    scaled = upstream * gain_vector
    return inverse * (
        scaled
        - jnp.mean(scaled, axis=-1, keepdims=True)
        - normed * jnp.mean(scaled * normed, axis=-1, keepdims=True)
    )


def split_three(value):
    high = value.astype(BF)
    rest = value - high.astype(F32)
    middle = rest.astype(BF)
    return high, middle, (rest - middle.astype(F32)).astype(BF)


def unpack_weights(core, y_index, shards, outs, counts):
    total = sum(counts)
    y_count = len(shards) // 2
    for number, source in enumerate(shards):
        step = number % y_count
        parity = core if number < y_count else 1 - core
        y = lax.rem(y_index - step + y_count, y_count)
        per = source.shape[0] // total
        for x in range(per):
            slab = (y * per + x) * 2 + parity
            at = x * total
            for out, count in zip(outs, counts):
                start = pl.multiple_of(slab * count, 32)
                out[pl.ds(start, count), :] = source[pl.ds(at, count), :]
                at += count


def pack_grads(core, y_index, grads, keep, send, counts):
    total = sum(counts)
    y_count = keep.shape[0]
    per = keep.shape[1] // total
    for target, parity in ((keep, core), (send, 1 - core)):
        for step in range(y_count):
            y = lax.rem(y_index + step, y_count)
            for x in range(per):
                at = x * total
                for grad, count in zip(grads, counts):
                    start = pl.multiple_of(((y * per + x) * 2 + parity) * count, 32)
                    target[step, pl.ds(at, count), :] = grad[pl.ds(start, count), :].astype(BF)
                    at += count


def block_at(number):
    return pl.ds(pl.multiple_of(number * BLK, BLK), BLK)


def edge_forward(scal, ext, edges, offsets, *refs):
    shards, refs = refs[:8], refs[8:]
    gain, joined, first, normed, inverse, new_edges, partial, w_in, w_out, second = refs
    tiles = edges.shape[0] // BLK
    lat_index, core, y_index, count = (scal[2 * tiles + i] for i in range(4))
    slabs = w_in.shape[0] // 3 // 32
    unpack_weights(core, y_index, shards, (w_in, w_out), (3 * L // slabs, L // slabs))
    for t in range(tiles):
        rows = pl.ds(t * BLK, BLK)
        joined[rows, pl.ds(0, L)] = edges[rows, :]
        to_src = one_hot_columns(offsets[1, pl.ds(t, 1), :]).T.astype(BF)
        to_dst = one_hot_columns(offsets[0, pl.ds(t, 1), :]).T.astype(BF)
        src, dst = block_at(scal[tiles + t]), block_at(scal[t] + HB)
        joined[rows, pl.ds(L, L)] = dot_transpose(to_src, ext[:, src]).astype(BF)
        joined[rows, pl.ds(2 * L, L)] = dot_transpose(to_dst, ext[:, dst]).astype(BF)
    for n in range(2):
        columns = pl.ds(n * 256, 256)
        first[:, columns] = jnp.maximum(dot(joined[...], w_in[:, columns]), 0.0).astype(BF)
    for n in range(2):
        columns = pl.ds(n * 256, 256)
        second[:, columns] = dot(first[...], w_out[:, columns])
    partial[...] = jnp.zeros_like(partial)
    for t in range(tiles):
        rows = pl.ds(t * BLK, BLK)
        live = (lat_index * tiles + t < count).astype(F32)
        values, inv = norm_parts(second[rows, :])
        normed[rows, :] = values
        inverse[rows, :] = jnp.broadcast_to(inv, (BLK, BLK))
        message = values * gain[...] * live
        new_edges[rows, :] = (edges[rows, :].astype(F32) + message).astype(BF)
        second[rows, :] = message
    for t in range(tiles):
        rows = pl.ds(t * BLK, BLK)
        into = one_hot_columns(offsets[0, pl.ds(t, 1), :]).astype(BF)
        high, middle, low = split_three(second[rows, :])
        block = scal[t]
        partial[block] = partial[block] + (dot(into, low) + dot(into, middle) + dot(into, high))


def node_step(scal, spread, ext, *refs):
    shards, refs = refs[:8], refs[8:]
    gain, out, d_direct, keep, send, w_in, w_out, joined, first, g_in, g_out = refs
    lat_index, core, y_index = scal[0], scal[1], scal[2]
    slabs = w_in.shape[0] // 2 // 32
    counts = (2 * L // slabs, L // slabs)
    unpack_weights(core, y_index, shards, (w_in, w_out), counts)
    total = spread[0]
    for l in range(1, spread.shape[0]):
        total = total + spread[l]
    own = ext[:, block_at(HB + lat_index)].astype(F32).T
    upstream = ext[:, pl.ds(ext.shape[1] - BLK, BLK)].astype(F32).T
    joined[:, pl.ds(0, L)] = own.astype(BF)
    joined[:, pl.ds(L, L)] = total.astype(BF)
    first[...] = jnp.maximum(dot(joined[...], w_in[...]), 0.0).astype(BF)
    normed, inverse = norm_parts(dot(first[...], w_out[...]))
    new_rows = (own + normed * gain[...]).T.astype(BF)
    d_second = norm_back(upstream, normed, inverse, gain[...]).astype(BF)
    g_out[...] = dot_rows(first[...], d_second)
    d_first = dot_transpose(d_second, w_out[...])
    d_first = jnp.where(first[...].astype(F32) > 0, d_first, 0.0).astype(BF)
    g_in[...] = dot_rows(joined[...], d_first)
    d_direct[...] = dot_transpose(w_in[pl.ds(0, L), :], d_first)
    d_agg = dot_transpose(w_in[pl.ds(L, L), :], d_first).astype(BF)
    width = L // out.shape[0]
    for l in range(out.shape[0]):
        out[l, pl.ds(0, L), :] = d_agg
        out[l, pl.ds(L, width), :] = new_rows[l * width : (l + 1) * width, :]
    pack_grads(core, y_index, (g_in, g_out), keep, send, counts)


def edge_backward(
    scal, d_agg, cot, normed, inverse, first, joined, w_in, w_out, gain, offsets, d_direct,
    grad_edges, columns, keep, send,
    d_second, d_first, d_ext, d_turned, g_in, g_out,
):
    tiles = cot.shape[0] // BLK
    lat_index, core, y_index, count = (scal[2 * tiles + i] for i in range(4))
    slabs = w_in.shape[0] // 3 // 32
    for t in range(tiles):
        rows = pl.ds(t * BLK, BLK)
        live = (lat_index * tiles + t < count).astype(F32)
        to_dst = one_hot_columns(offsets[0, pl.ds(t, 1), :]).T.astype(BF)
        picked = dot_transpose(to_dst, d_agg[scal[t], pl.ds(0, L), :])
        d_message = (cot[rows, :].astype(F32) + picked) * live
        back = norm_back(d_message, normed[rows, :], inverse[rows, pl.ds(0, 1)], gain[...])
        d_second[rows, :] = back.astype(BF)
    for n in range(2):
        part = pl.ds(n * 256, 256)
        back = dot_transpose(d_second[...], w_out[part, :])
        d_first[:, part] = jnp.where(first[:, part].astype(F32) > 0, back, 0.0).astype(BF)
    for n in range(2):
        part = pl.ds(n * 256, 256)
        back = dot_transpose(d_first[...], w_in[part, :])
        grad_edges[:, part] = (cot[:, part].astype(F32) + back).astype(BF)
    for n in range(4):
        d_turned[pl.ds(n * 256, 256), :] = dot_transpose(
            w_in[pl.ds(L + n * 256, 256), :], d_first[...]
        )
    for n in range(2):
        part = pl.ds(n * 256, 256)
        g_out[part, :] = dot_rows(first[:, part], d_second[...])
    for n in range(6):
        part = pl.ds(n * 256, 256)
        g_in[part, :] = dot_rows(joined[:, part], d_first[...])
    pack_grads(core, y_index, (g_in, g_out), keep, send, (3 * L // slabs, L // slabs))
    d_ext[...] = jnp.zeros_like(d_ext)
    for t in range(tiles):
        rows = pl.ds(t * BLK, BLK)
        for row, place, at in ((1, scal[tiles + t], 0), (0, scal[t] + HB, L)):
            into = one_hot_columns(offsets[row, pl.ds(t, 1), :]).T.astype(BF)
            value = d_turned[pl.ds(at, L), rows]
            high = value.astype(BF)
            low = (value - high.astype(F32)).astype(BF)
            d_ext[place] = d_ext[place] + (dot(low, into) + dot(high, into))
    d_ext[HB + lat_index] = d_ext[HB + lat_index] + d_direct[...]
    width = columns.shape[1]
    for block in range(d_ext.shape[0]):
        for l in range(columns.shape[0]):
            columns[l, :, pl.ds(block * BLK, BLK)] = d_ext[
                block, pl.ds(l * width, width), :
            ].astype(BF)


def call(kernel, out_shape, scratch, flops, mib, operands):
    moved = sum(x.size * x.dtype.itemsize for x in operands)
    moved += sum(x.size * x.dtype.itemsize for x in out_shape)
    vmem = pl.BlockSpec(memory_space=pltpu.VMEM)
    return pl.pallas_call(
        kernel,
        out_shape=out_shape,
        in_specs=[pl.BlockSpec(memory_space=pltpu.SMEM)] + [vmem] * (len(operands) - 1),
        out_specs=[vmem] * len(out_shape),
        scratch_shapes=[pltpu.VMEM(shape, dtype) for shape, dtype in scratch],
        cost_estimate=pl.CostEstimate(flops=flops, bytes_accessed=moved, transcendentals=0),
        compiler_params=pltpu.CompilerParams(vmem_limit_bytes=mib << 20),
    )(*operands)


def run_edge_forward(scal, ext, edges, offsets, shards, gain, lat_size):
    rows = edges.shape[0]
    return call(
        edge_forward,
        [
            shape_of((rows, 3 * L), BF),
            shape_of((rows, L), BF),
            shape_of((rows, L), F32),
            shape_of((rows, BLK), F32),
            shape_of((rows, L), BF),
            shape_of((lat_size, BLK, L), F32),
            shape_of((3 * L, L), BF),
            shape_of((L, L), BF),
        ],
        [((rows, L), F32)],
        2 * rows * 4 * L * L,
        EDGE_MIB,
        (scal, ext, edges, offsets, *shards, gain),
    )


def run_node_step(scal, spread, ext, shards, gain):
    lat_size = spread.shape[0]
    chunk = (len(shards) // 2,) + shards[0].shape
    return call(
        node_step,
        [
            shape_of((lat_size, L + L // lat_size, BLK), BF),
            shape_of((L, BLK), F32),
            shape_of(chunk, BF),
            shape_of(chunk, BF),
        ],
        [
            ((2 * L, L), BF),
            ((L, L), BF),
            ((BLK, 2 * L), BF),
            ((BLK, L), BF),
            ((2 * L, L), F32),
            ((L, L), F32),
        ],
        2 * BLK * 9 * L * L,
        NODE_MIB,
        (scal, spread, ext, *shards, gain),
    )


def run_edge_backward(
    scal, d_agg, cot, normed, inverse, first, joined, w_in, w_out, gain, offsets, d_direct, chunk
):
    rows = cot.shape[0]
    lat_size = d_agg.shape[0]
    blocks = lat_size + 2 * HB
    return call(
        edge_backward,
        [
            shape_of((rows, L), BF),
            shape_of((lat_size, L // lat_size, blocks * BLK), BF),
            shape_of(chunk, BF),
            shape_of(chunk, BF),
        ],
        [
            ((rows, L), BF),
            ((rows, L), BF),
            ((blocks, L, BLK), F32),
            ((2 * L, rows), F32),
            ((3 * L, L), F32),
            ((L, L), F32),
        ],
        2 * rows * 8 * L * L,
        BACK_MIB,
        (scal, d_agg, cot, normed, inverse, first, joined, w_in, w_out, gain, offsets, d_direct),
    )


def swap_cores(value):
    return lax.ppermute(value, "c", [(0, 1), (1, 0)])


def shift_y(value, step):
    count = lax.axis_size("y")
    return lax.ppermute(value, "y", [(i, (i + step) % count) for i in range(count)])


def spread_rows(value, axes):
    return lax.all_to_all(value, axes, 0, 0)


def gather_over(value, axes):
    return spread_rows(jnp.broadcast_to(value, (lax.axis_size(axes),) + value.shape), axes)


def gather_far(value):
    mine = [value] + [shift_y(value, k) for k in range(1, lax.axis_size("y"))]
    return mine + [swap_cores(one) for one in mine]


def slab_rows_of(near, pieces):
    lat = lax.axis_size(LAT)
    shaped = near.reshape((-1, lat) + near.shape[1:])
    out, at = [], 0
    for count in pieces:
        out.append(shaped[:, :, at : at + count].reshape(shaped.shape[0], lat * count, L))
        at += count
    return jnp.concatenate(out, axis=1).reshape(-1, L)


def reduce_grads(keep, send, counts):
    lat = lax.axis_size(LAT)
    arrived = swap_cores(send)
    over_y = keep[0].astype(F32) + arrived[0].astype(F32)
    for k in range(1, keep.shape[0]):
        both = (keep[k].astype(F32) + arrived[k].astype(F32)).astype(BF)
        over_y = over_y + shift_y(both, k).astype(F32)
    shaped = over_y.astype(BF).reshape(lax.axis_size("xl"), lat * sum(counts), L)
    parts, at = [], 0
    for count in counts:
        parts.append(shaped[:, at : at + lat * count].reshape(-1, lat, count, L))
        at += lat * count
    return jnp.concatenate(parts, axis=2).reshape(-1, sum(counts), L)


def per_device(
    nodes,
    edges,
    edge_tiles,
    edge_offsets,
    tile_counts,
    halo_blocks,
    w_edge_in,
    w_edge_out,
    w_node_in,
    w_node_out,
    edge_gain,
    node_gain,
    node_cotangent,
    edge_cotangent,
):
    lat_size = lax.axis_size(LAT)
    place = [lax.axis_index(LAT), lax.axis_index("c"), lax.axis_index("y")]
    slab_rows, width = nodes.shape
    own_rows = slab_rows // lat_size
    halo_rows = HB * BLK
    ext_rows = slab_rows + 2 * halo_rows
    up_list = halo_blocks[0, 0]
    down_list = halo_blocks[0, 1]
    edge_counts = (w_edge_in.shape[0], w_edge_out.shape[0])
    node_counts = (w_node_in.shape[0], w_node_out.shape[0])

    node_scal = jnp.stack(place).astype(jnp.int32)
    scal = jnp.concatenate([edge_tiles.reshape(-1), node_scal, tile_counts])
    offsets = edge_offsets.reshape(2, -1, BLK)
    edge_gain_row = edge_gain.reshape(1, L)
    node_gain_row = node_gain.reshape(1, L)

    turned = nodes.T

    def halo_of(blocks):
        picked = [
            lax.dynamic_slice(turned, (0, blocks[j] * BLK), (width, BLK)) for j in range(HB)
        ]
        return jnp.concatenate(picked, axis=1)

    from_lower = from_behind(halo_of(up_list), 1)
    from_upper = from_behind(halo_of(down_list), -1)

    shards = [w_edge_in, w_edge_out, w_node_in, w_node_out]
    rows = sum(shard.shape[0] for shard in shards)
    near = gather_over(jnp.concatenate(shards + [jnp.zeros((-rows % 16, L), BF)], axis=0), NEAR)
    edge_part = slab_rows_of(near[:, : sum(edge_counts)], edge_counts)
    node_part = slab_rows_of(near[:, sum(edge_counts) : rows], node_counts)

    table = jnp.concatenate([from_lower, turned, from_upper], axis=1)
    cot = node_cotangent.T.reshape(width, lat_size, own_rows).transpose(1, 0, 2)
    message_out = jnp.concatenate(
        [jnp.broadcast_to(table, (lat_size,) + table.shape), cot], axis=2
    )
    edge_shards = gather_far(edge_part)
    ext = spread_rows(message_out, LAT).reshape(L, ext_rows + own_rows)

    joined, first, normed, inverse, new_edges, partial, e_in, e_out = run_edge_forward(
        scal, ext, edges, offsets, edge_shards, edge_gain_row, lat_size
    )
    node_shards = gather_far(node_part)
    spread = spread_rows(partial, LAT)
    second_out, d_direct, node_keep, node_send = run_node_step(
        node_scal, spread, ext, node_shards, node_gain_row
    )
    second_in = spread_rows(second_out, LAT)
    new_nodes = second_in[:, L:].transpose(1, 0, 2).reshape(width, slab_rows).T
    node_near = reduce_grads(node_keep, node_send, node_counts)

    grad_edges, columns, edge_keep, edge_send = run_edge_backward(
        scal, second_in, edge_cotangent, normed, inverse, first, joined, e_in, e_out,
        edge_gain_row, offsets, d_direct, (lax.axis_size("y"),) + edge_part.shape,
    )
    edge_near = reduce_grads(edge_keep, edge_send, edge_counts)
    summed = jnp.sum(spread_rows(columns, LAT).astype(F32), axis=0)
    d_lower = summed[:, :halo_rows].astype(BF)
    d_middle = summed[:, halo_rows : halo_rows + slab_rows]
    d_upper = summed[:, halo_rows + slab_rows :].astype(BF)
    from_above = from_behind(d_lower, -1).astype(F32).reshape(width, HB, BLK)
    from_below = from_behind(d_upper, 1).astype(F32).reshape(width, HB, BLK)
    blocks = d_middle.reshape(width, -1, BLK)
    numbers = jnp.arange(blocks.shape[1])[None, :, None]
    for j in range(HB):
        blocks = blocks + jnp.where(numbers == up_list[j], from_above[:, j : j + 1], 0.0)
        blocks = blocks + jnp.where(numbers == down_list[j], from_below[:, j : j + 1], 0.0)
    grad_slab = blocks.reshape(width, slab_rows).astype(BF).T

    both = jnp.concatenate([edge_near, node_near], axis=1)
    both = jnp.pad(both, ((0, 0), (0, -both.shape[1] % 16), (0, 0)))
    total = jnp.sum(spread_rows(both, NEAR).astype(F32), axis=0)
    out, at = [], 0
    for count in edge_counts + node_counts:
        out.append(total[at : at + count])
        at += count
    return (new_nodes, new_edges, grad_slab, grad_edges) + tuple(out)


def solution(mesh):
    fine = Mesh(mesh.devices.reshape(4, 2, 2, 2, 4), ("y", "xl", "c", "xh", "z"))
    every = SLAB + LAT
    by_rows = P(every, None)
    split = P(SLAB, LAT)
    placed = (
        split,
        by_rows,
        P(None, every),
        P(None, every),
        P(SLAB),
        P(SLAB, None, None),
        by_rows,
        by_rows,
        by_rows,
        by_rows,
        P(),
        P(),
        split,
        by_rows,
    )
    return jax.shard_map(
        per_device,
        mesh=fine,
        in_specs=placed,
        out_specs=(split, by_rows, split, by_rows, by_rows, by_rows, by_rows, by_rows),
        check_vma=False,
    )
```

time: 230 us -> 210 us (0.913)
  waiting for transfers between devices: 106 us -> 81.1 us
  local copies, waits for them, and re-layouts: 28.9 us -> 32.7 us
  between operations: 1.94 us -> 4.41 us
    all_to_all x10 -> x6, waiting for transfers between devices: 103 us -> 49.7 us  [spread_rows(): return lax.all_to_all(value, axes, 0, 0)]
    ppermute x0 -> x12, waiting for transfers between devices: none -> 29.7 us  [shift_y(): lax.ppermute(value, 'y', [(i, (i + step) % count) for i in range(count)])]
    ppermute x0 -> x12, starting transfers between devices: none -> 16.7 us  [shift_y(): lax.ppermute(value, 'y', [(i, (i + step) % count) for i in range(count)])]
    all_to_all x10 -> x6, starting transfers between devices: 52.9 us -> 36.5 us  [spread_rows(): return lax.all_to_all(value, axes, 0, 0)]
    unnamed x55 -> x68, local copies, waits for them, and re-layouts: 15.4 us -> 23 us
    convert_element_type x5 -> x4, other arithmetic: 3.79 us -> 5.81 us  [the longest x2 3.4 us: reduce_grads(): both = (keep[k].astype(F32) + arrived[k].astype(F32)).astype(BF)]
  transfers between devices with their start and end apart: 18 -> 32, of which waited for: 10 -> 18; matrix products, arithmetic and copies ran while one was open for 10% -> 9% of each run, Pallas kernels for 6% -> 3%
where the time goes in v3:
time: 210 us; the launch traced here: 208 us
  waiting for transfers between devices  81.1 us (39%)
  starting transfers between devices  60.2 us (29%)
  local copies, waits for them, and re-layouts  32.7 us (16%)
  Pallas kernels  15.3 us (7%)
  other arithmetic  14.3 us (7%)
  between operations  4.41 us (2%)
    all_to_all x6, waiting for transfers between devices, spread_rows(): return lax.all_to_all(value, axes, 0, 0)  49.7 us
    all_to_all x6, starting transfers between devices, spread_rows(): return lax.all_to_all(value, axes, 0, 0)  36.5 us
    ppermute x12, waiting for transfers between devices, shift_y(): lax.ppermute(value, 'y', [(i, (i + step) % count) for i in range(count)])  29.7 us
    unnamed x68, local copies, waits for them, and re-layouts  23 us
    ppermute x12, starting transfers between devices, shift_y(): lax.ppermute(value, 'y', [(i, (i + step) % count) for i in range(count)])  16.7 us
    pallas_call x3, Pallas kernels, call(): pl.pallas_call(kernel, out_shape=out_shape, in_specs=[pl.BlockSpec(memory...  15.3 us
    ppermute x4, starting transfers between devices, from_behind(): lax.ppermute(value, SLAB, [(source, source + steps) for source in range(f...  6 us
  transfers between devices with their start and end apart: 32, of which 18 were waited for; matrix products, arithmetic and copies ran while one was open for 9% of the time, Pallas kernels for 3%

profile of v3, /device:TPU:0, one launch (start us, length us, event | category | flops | bytes accessed | tf_op | source)
XLA Modules:
  0.0 208.1 jit_solution(17368396478127195054)
XLA Ops:
  8.1 2.8 %concatenate.46 = bf16[32,512]{1,0:T(8,128)(2,1)S(1)} concatenate(bf16[12,512]{1,0:T(8,128)(2,1)} %param.20, bf16[4,512]{1,0:T(4,128)(2,1)} %param.21, bf16[8,512]{1,0:T(8,128)(2,1)} %param.22, bf16[4,512]{1,0:T(4,128)(2,1)} %param.23, bf16[4,512]{1,0:T(4,128)(2,1)S(1)} %broadcast_in_dim.96), dimensions={0} | concatenate | bytes 65536 | tf_op jit(solution)/shard_map/concatenate | solution.py:415
  11.8 10.7 %all-to-all-start.1 = ((bf16[16,32,512]{2,1,0:T(8,128)(2,1)}), bf16[16,32,512]{2,1,0:T(8,128)(2,1)S(1)}, u32[]{:S(2)}, u32[]{:S(2)}) async-start(bf16[16,32,512]{2,1,0:T(8,128)(2,1)} %broadcast_in_dim.97), calls=%async_computation.1 | async-start | bytes 1048576 | tf_op jit(solution)/shard_map/all_to_all | solution.py:332
  24.1 9.9 %all-to-all-done.1 = bf16[16,32,512]{2,1,0:T(8,128)(2,1)S(1)} async-done(((bf16[16,32,512]{2,1,0:T(8,128)(2,1)}), bf16[16,32,512]{2,1,0:T(8,128)(2,1)S(1)}, u32[]{:S(2)}, u32[]{:S(2)}) %all-to-all-start.1) | async-done | bytes 524320 | tf_op jit(solution)/shard_map/all_to_all | solution.py:332
  34.0 3.6 %all-to-all-start = ((bf16[8,64,1664]{2,1,0:T(8,128)(2,1)}), bf16[8,64,1664]{2,1,0:T(8,128)(2,1)S(1)}, u32[]{:S(2)}, u32[]{:S(2)}) async-start(bf16[8,64,1664]{2,1,0:T(8,128)(2,1)} %pad_maximum_fusion), calls=%async_computation | async-start | bytes 3407872 | tf_op jit(solution)/shard_map/all_to_all | solution.py:332
  40.2 2.8 %collective-permute-start.3 = (bf16[256,512]{1,0:T(8,128)(2,1)S(1)}, bf16[256,512]{1,0:T(8,128)(2,1)S(1)}, u32[]{:S(2)}, u32[]{:S(2)}) collective-permute-start(bf16[256,512]{1,0:T(8,128)(2,1)S(1)} %bitcast.128), channel_id=1, source_target_pairs={{0,64},{32,96},{64,0},{96,32},{1,65},{33,97},{65,1},{97,33},{2,66}... | collective-permute-start | bytes 786440 | tf_op jit(solution)/shard_map/ppermute | solution.py:328
  44.4 7.7 %collective-permute-done.2.refs_1_ = bf16[256,512]{1,0:T(8,128)(2,1)S(1)} collective-permute-done((bf16[256,512]{1,0:T(8,128)(2,1)S(1)}, bf16[256,512]{1,0:T(8,128)(2,1)S(1)}, u32[]{:S(2)}, u32[]{:S(2)}) %collective-permute-start.2) | collective-permute-done | bytes 262176 | tf_op jit(solution)/shard_map/ppermute | solution.py:328
  54.5 4.2 %all-to-all-done = bf16[8,64,1664]{2,1,0:T(8,128)(2,1)S(1)} async-done(((bf16[8,64,1664]{2,1,0:T(8,128)(2,1)}), bf16[8,64,1664]{2,1,0:T(8,128)(2,1)S(1)}, u32[]{:S(2)}, u32[]{:S(2)}) %all-to-all-start) | async-done | bytes 1703968 | tf_op jit(solution)/shard_map/all_to_all | solution.py:332
  58.7 4.4 %shard_map.197 = (bf16[512,1536]{1,0:T(8,128)(2,1)S(1)}, bf16[512,512]{1,0:T(8,128)(2,1)S(1)}, f32[512,512]{1,0:T(8,128)S(1)}, f32[512,128]{1,0:T(8,128)S(1)}, b...) custom-call(s32[12]{0:T(128)S(1)} %concatenate.41.scal, ...), custom_call_target="tpu_custom_call" | custom-call | flops 1073741824 | bytes 12458032 | tf_op jit(solution)/shard_map/pallas_call | solution.py:237
  70.1 4.9 %all-to-all-start.2 = ((f32[8,128,512]{2,1,0:T(8,128)}), f32[8,128,512]{2,1,0:T(8,128)}, u32[]{:S(2)}, u32[]{:S(2)}) async-start(f32[8,128,512]{2,1,0:T(8,128)} %copy-done.1), calls=%async_computation.2 | async-start | bytes 4194304 | tf_op jit(solution)/shard_map/all_to_all | solution.py:332
  75.8 2.5 %collective-permute-start.10 = (bf16[192,512]{1,0:T(8,128)(2,1)S(1)}, bf16[192,512]{1,0:T(8,128)(2,1)S(1)}, u32[]{:S(2)}, u32[]{:S(2)}) collective-permute-start(bf16[192,512]{1,0:T(8,128)(2,1)S(1)} %bitcast.133), channel_id=1, source_target_pairs={{0,64},{32,96},{64,0},{96,32},{1,65},{33,97},{65,1},{97,33},{2,66}... | collective-permute-start | bytes 589832 | tf_op jit(solution)/shard_map/ppermute | solution.py:328
  79.7 7.5 %collective-permute-done.9.refs_1_ = bf16[192,512]{1,0:T(8,128)(2,1)S(1)} collective-permute-done((bf16[192,512]{1,0:T(8,128)(2,1)S(1)}, bf16[192,512]{1,0:T(8,128)(2,1)S(1)}, u32[]{:S(2)}, u32[]{:S(2)}) %collective-permute-start.9) | collective-permute-done | bytes 196640 | tf_op jit(solution)/shard_map/ppermute | solution.py:328
  91.1 10.6 %all-to-all-done.2.spread = f32[8,128,512]{2,1,0:T(8,128)} async-done(((f32[8,128,512]{2,1,0:T(8,128)}), f32[8,128,512]{2,1,0:T(8,128)}, u32[]{:S(2)}, u32[]{:S(2)}) %all-to-all-start.2) | async-done | bytes 2097184 | tf_op jit(solution)/shard_map/all_to_all | solution.py:332
  106.1 4.8 %shard_map.198 = (bf16[8,576,128]{2,1,0:T(8,128)(2,1)}, f32[512,128]{1,0:T(8,128)S(1)}, bf16[4,192,512]{2,1,0:T(8,128)(2,1)S(1)}, bf16[4,192,512]{2,1,0:T(8,128)(2,1)}) custom-call(s32[3]{0:T(128)S(1)} %copy-done.13, f32[8,128,512]{2,1,0:T(8,128)} %all-to-all-done.2.spread, bf16[512,1664]{1,0:T(8,128)(2,1)S(1)} %bitcast.126, bf16[192,512]{1,0:T(8,128)(2,1)S(1)} %bitcast.136, ...), custom_call_target="tpu_custom_call" | custom-call | flops 603979776 | bytes 8390668 | tf_op jit(solution)/shard_map/pallas_call | solution.py:237
  111.5 4.9 %all-to-all-start.3 = ((bf16[8,576,128]{2,1,0:T(8,128)(2,1)}), bf16[8,576,128]{2,1,0:T(8,128)(2,1)S(1)}, u32[]{:S(2)}, u32[]{:S(2)}) async-start(bf16[8,576,128]{2,1,0:T(8,128)(2,1)} %get-tuple-element.25), calls=%async_computation.3 | async-start | bytes 2359296 | tf_op jit(solution)/shard_map/all_to_all | solution.py:332
  116.4 16.9 %all-to-all-done.3.d_agg = bf16[8,576,128]{2,1,0:T(8,128)(2,1)S(1)} async-done(((bf16[8,576,128]{2,1,0:T(8,128)(2,1)}), bf16[8,576,128]{2,1,0:T(8,128)(2,1)S(1)}, u32[]{:S(2)}, u32[]{:S(2)}) %all-to-all-start.3) | async-done | bytes 1179680 | tf_op jit(solution)/shard_map/all_to_all | solution.py:332
  141.5 6.1 %shard_map.199 = (bf16[512,512]{1,0:T(8,128)(2,1)}, bf16[8,64,1536]{2,1,0:T(8,128)(2,1)}, bf16[4,256,512]{2,1,0:T(8,128)(2,1)S(1)}, bf16[4,256,512]{2,1,0:T(8,128)(2,1)}) custom-call(s32[12]{0:T(128)S(1)} %concatenate.41.scal, bf16[8,576,128]{2,1,0:T(8,128)(2,1)S(1)} %all-to-all-done.3.d_agg, bf16[512,512]{1,0:T(8,128)(2,1)S(1)} %copy-done.20, ...), custom_call_target="tpu_custom_call" | custom-call | flops 2147483648 | bytes 11671600 | tf_op jit(solution)/shard_map/pallas_call | solution.py:237
  150.3 4.6 %all-to-all-start.4 = ((bf16[8,64,1536]{2,1,0:T(8,128)(2,1)}), bf16[8,64,1536]{2,1,0:T(8,128)(2,1)}, u32[]{:S(2)}, u32[]{:S(2)}) async-start(bf16[8,64,1536]{2,1,0:T(8,128)(2,1)} %get-tuple-element.34), calls=%async_computation.4 | async-start | bytes 3145728 | tf_op jit(solution)/shard_map/all_to_all | solution.py:332
  157.0 2.3 %collective-permute-start.24 = (bf16[192,512]{1,0:T(8,128)(2,1)S(1)}, bf16[192,512]{1,0:T(8,128)(2,1)S(1)}, u32[]{:S(2)}, u32[]{:S(2)}) collective-permute-start(bf16[192,512]{1,0:T(8,128)(2,1)S(1)} %get-tuple-element.45), channel_id=1, source_target_pairs={{0,64},{32,96},{64,0},{96,32},{1,65},{33,97},{65,1},{97,33},{2,66}... | collective-permute-start | bytes 589832 | tf_op jit(solution)/shard_map/ppermute | solution.py:328
  160.7 2.1 %fusion.13 = (bf16[256,512]{1,0:T(8,128)(2,1)}, bf16[256,512]{1,0:T(8,128)(2,1)S(1)}, bf16[256,512]{1,0:T(8,128)(2,1)}) fusion(bf16[4,256,512]{2,1,0:T(8,128)(2,1)} %collective-permute-done.18, bf16[4,256,512]{2,1,0:T(8,128)(2,1)S(1)} %get-tuple-element.36), kind=kLoop, calls=%fused_computation.25 | loop fusion | flops 1572864 | bytes 2359296 | tf_op jit(solution)/shard_map/convert_element_type | solution.py:359
  164.7 4.0 %collective-permute-done.23 = bf16[192,512]{1,0:T(8,128)(2,1)S(1)} collective-permute-done((bf16[192,512]{1,0:T(8,128)(2,1)S(1)}, bf16[192,512]{1,0:T(8,128)(2,1)S(1)}, u32[]{:S(2)}, u32[]{:S(2)}) %collective-permute-start.23) | collective-permute-done | bytes 196640 | tf_op jit(solution)/shard_map/ppermute | solution.py:328
  172.2 7.9 %collective-permute-done.19 = bf16[256,512]{1,0:T(8,128)(2,1)} collective-permute-done((bf16[256,512]{1,0:T(8,128)(2,1)}, bf16[256,512]{1,0:T(8,128)(2,1)}, u32[]{:S(2)}, u32[]{:S(2)}) %collective-permute-start.19) | collective-permute-done | bytes 262176 | tf_op jit(solution)/shard_map/ppermute | solution.py:328
  186.3 7.7 %all-to-all-start.5 = ((bf16[16,32,512]{2,1,0:T(8,128)(2,1)}), bf16[16,32,512]{2,1,0:T(8,128)(2,1)S(1)}, u32[]{:S(2)}, u32[]{:S(2)}) async-start(bf16[16,32,512]{2,1,0:T(8,128)(2,1)} %fusion.6), calls=%async_computation.5 | async-start | bytes 1048576 | tf_op jit(solution)/shard_map/all_to_all | solution.py:332
  194.0 2.1 %collective-permute-start.17 = (bf16[64,256]{1,0:T(8,128)(2,1)S(1)}, bf16[64,256]{1,0:T(8,128)(2,1)S(1)}, u32[]{:S(2)}, u32[]{:S(2)}) collective-permute-start(bf16[64,256]{1,0:T(8,128)(2,1)S(1)} %get-tuple-element.47), channel_id=1, source_target_pairs={{0,8},{8,16},{16,24},{24,32},{32,40},{40,48},{48,56},{56,64},{64,7... | collective-permute-start | bytes 98312 | tf_op jit(solution)/shard_map/ppermute | solution.py:30
  198.1 8.1 %all-to-all-done.5 = bf16[16,32,512]{2,1,0:T(8,128)(2,1)S(1)} async-done(((bf16[16,32,512]{2,1,0:T(8,128)(2,1)}), bf16[16,32,512]{2,1,0:T(8,128)(2,1)S(1)}, u32[]{:S(2)}, u32[]{:S(2)}) %all-to-all-start.5) | async-done | bytes 524320 | tf_op jit(solution)/shard_map/all_to_all | solution.py:332
  (172 shorter events, 60.4 us)
Async XLA Ops:
  5.5 17.1 %collective-permute-start = (bf16[64,256]{1,0:T(8,128)(2,1)S(1)}, bf16[64,256]{1,0:T(8,128)(2,1)S(1)}, u32[]{:S(2)}, u32[]{:S(2)}) collective-permute-start(bf16[64,256]{1,0:T(8,128)(2,1)S(1)} %pad_maximum_fusion.4), channel_id=1, source_target_pairs={{0,8},{8,16},{16,24},{24,32},{32,40},{40,48},{48,56},{56,64},{64,7... | collective-permute-start | bytes 98312 | tf_op jit(solution)/shard_map/ppermute | solution.py:30
  6.8 15.8 %collective-permute-start.1 = (bf16[64,256]{1,0:T(8,128)(2,1)S(1)}, bf16[64,256]{1,0:T(8,128)(2,1)S(1)}, u32[]{:S(2)}, u32[]{:S(2)}) collective-permute-start(bf16[64,256]{1,0:T(8,128)(2,1)S(1)} %pad_maximum_fusion.5), channel_id=1, source_target_pairs={{8,0},{16,8},{24,16},{32,24},{40,32},{48,40},{56,48},{64,56},{72,6... | collective-permute-start | bytes 98312 | tf_op jit(solution)/shard_map/ppermute | solution.py:30
  11.8 22.2 %all-to-all-start.1 = ((bf16[16,32,512]{2,1,0:T(8,128)(2,1)}), bf16[16,32,512]{2,1,0:T(8,128)(2,1)S(1)}, u32[]{:S(2)}, u32[]{:S(2)}) async-start(bf16[16,32,512]{2,1,0:T(8,128)(2,1)} %broadcast_in_dim.97), calls=%async_computation.1 | async-start | bytes 1048576 | tf_op jit(solution)/shard_map/all_to_all | solution.py:332
  34.0 24.6 %all-to-all-start = ((bf16[8,64,1664]{2,1,0:T(8,128)(2,1)}), bf16[8,64,1664]{2,1,0:T(8,128)(2,1)S(1)}, u32[]{:S(2)}, u32[]{:S(2)}) async-start(bf16[8,64,1664]{2,1,0:T(8,128)(2,1)} %pad_maximum_fusion), calls=%async_computation | async-start | bytes 3407872 | tf_op jit(solution)/shard_map/all_to_all | solution.py:332
  38.4 13.6 %collective-permute-start.2 = (bf16[256,512]{1,0:T(8,128)(2,1)S(1)}, bf16[256,512]{1,0:T(8,128)(2,1)S(1)}, u32[]{:S(2)}, u32[]{:S(2)}) collective-permute-start(bf16[256,512]{1,0:T(8,128)(2,1)S(1)} %bitcast.127), channel_id=1, source_target_pairs={{0,32},{32,64},{64,96},{96,0},{1,33},{33,65},{65,97},{97,1},{2,34}... | collective-permute-start | bytes 786440 | tf_op jit(solution)/shard_map/ppermute | solution.py:328
  40.2 11.9 %collective-permute-start.3 = (bf16[256,512]{1,0:T(8,128)(2,1)S(1)}, bf16[256,512]{1,0:T(8,128)(2,1)S(1)}, u32[]{:S(2)}, u32[]{:S(2)}) collective-permute-start(bf16[256,512]{1,0:T(8,128)(2,1)S(1)} %bitcast.128), channel_id=1, source_target_pairs={{0,64},{32,96},{64,0},{96,32},{1,65},{33,97},{65,1},{97,33},{2,66}... | collective-permute-start | bytes 786440 | tf_op jit(solution)/shard_map/ppermute | solution.py:328
  43.0 9.7 %collective-permute-start.4 = (bf16[256,512]{1,0:T(8,128)(2,1)S(1)}, bf16[256,512]{1,0:T(8,128)(2,1)S(1)}, u32[]{:S(2)}, u32[]{:S(2)}) collective-permute-start(bf16[256,512]{1,0:T(8,128)(2,1)S(1)} %bitcast.129), channel_id=1, source_target_pairs={{0,96},{32,0},{64,32},{96,64},{1,97},{33,1},{65,33},{97,65},{2,98}... | collective-permute-start | bytes 786440 | tf_op jit(solution)/shard_map/ppermute | solution.py:328
  44.4 9.2 %collective-permute-start.5 = (bf16[256,512]{1,0:T(8,128)(2,1)S(1)}, bf16[256,512]{1,0:T(8,128)(2,1)}, u32[]{:S(2)}, u32[]{:S(2)}) collective-permute-start(bf16[256,512]{1,0:T(8,128)(2,1)S(1)} %bitcast.130), channel_id=1, source_target_pairs={{0,8},{8,0},{1,9},{9,1},{2,10},{10,2},{3,11},{11,3},{4,12},{12,4},... | collective-permute-start | bytes 786440 | tf_op jit(solution)/shard_map/ppermute | solution.py:323
  70.1 31.6 %all-to-all-start.2 = ((f32[8,128,512]{2,1,0:T(8,128)}), f32[8,128,512]{2,1,0:T(8,128)}, u32[]{:S(2)}, u32[]{:S(2)}) async-start(f32[8,128,512]{2,1,0:T(8,128)} %copy-done.1), calls=%async_computation.2 | async-start | bytes 4194304 | tf_op jit(solution)/shard_map/all_to_all | solution.py:332
  75.2 12.0 %collective-permute-start.9 = (bf16[192,512]{1,0:T(8,128)(2,1)S(1)}, bf16[192,512]{1,0:T(8,128)(2,1)S(1)}, u32[]{:S(2)}, u32[]{:S(2)}) collective-permute-start(bf16[192,512]{1,0:T(8,128)(2,1)S(1)} %bitcast.132), channel_id=1, source_target_pairs={{0,32},{32,64},{64,96},{96,0},{1,33},{33,65},{65,97},{97,1},{2,34}... | collective-permute-start | bytes 589832 | tf_op jit(solution)/shard_map/ppermute | solution.py:328
  75.8 11.4 %collective-permute-start.10 = (bf16[192,512]{1,0:T(8,128)(2,1)S(1)}, bf16[192,512]{1,0:T(8,128)(2,1)S(1)}, u32[]{:S(2)}, u32[]{:S(2)}) collective-permute-start(bf16[192,512]{1,0:T(8,128)(2,1)S(1)} %bitcast.133), channel_id=1, source_target_pairs={{0,64},{32,96},{64,0},{96,32},{1,65},{33,97},{65,1},{97,33},{2,66}... | collective-permute-start | bytes 589832 | tf_op jit(solution)/shard_map/ppermute | solution.py:328
  78.3 9.5 %collective-permute-start.11 = (bf16[192,512]{1,0:T(8,128)(2,1)S(1)}, bf16[192,512]{1,0:T(8,128)(2,1)S(1)}, u32[]{:S(2)}, u32[]{:S(2)}) collective-permute-start(bf16[192,512]{1,0:T(8,128)(2,1)S(1)} %bitcast.134), channel_id=1, source_target_pairs={{0,96},{32,0},{64,32},{96,64},{1,97},{33,1},{65,33},{97,65},{2,98}... | collective-permute-start | bytes 589832 | tf_op jit(solution)/shard_map/ppermute | solution.py:328
  111.5 21.8 %all-to-all-start.3 = ((bf16[8,576,128]{2,1,0:T(8,128)(2,1)}), bf16[8,576,128]{2,1,0:T(8,128)(2,1)S(1)}, u32[]{:S(2)}, u32[]{:S(2)}) async-start(bf16[8,576,128]{2,1,0:T(8,128)(2,1)} %get-tuple-element.25), calls=%async_computation.3 | async-start | bytes 2359296 | tf_op jit(solution)/shard_map/all_to_all | solution.py:332
  116.4 38.6 %collective-permute-start.22 = (bf16[4,192,512]{2,1,0:T(8,128)(2,1)}, bf16[4,192,512]{2,1,0:T(8,128)(2,1)}, u32[]{:S(2)}, u32[]{:S(2)}) collective-permute-start(bf16[4,192,512]{2,1,0:T(8,128)(2,1)} %get-tuple-element.39), channel_id=1, source_target_pairs={{0,8},{8,0},{1,9},{9,1},{2,10},{10,2},{3,11},{11,3},{4,12},{12,4},... | collective-permute-start | bytes 2359304 | tf_op jit(solution)/shard_map/ppermute | solution.py:323
  147.6 13.1 %collective-permute-start.18 = (bf16[4,256,512]{2,1,0:T(8,128)(2,1)}, bf16[4,256,512]{2,1,0:T(8,128)(2,1)}, u32[]{:S(2)}, u32[]{:S(2)}) collective-permute-start(bf16[4,256,512]{2,1,0:T(8,128)(2,1)} %get-tuple-element.37), channel_id=1, source_target_pairs={{0,8},{8,0},{1,9},{9,1},{2,10},{10,2},{3,11},{11,3},{4,12},{12,4},... | collective-permute-start | bytes 3145736 | tf_op jit(solution)/shard_map/ppermute | solution.py:323
  150.3 32.0 %all-to-all-start.4 = ((bf16[8,64,1536]{2,1,0:T(8,128)(2,1)}), bf16[8,64,1536]{2,1,0:T(8,128)(2,1)}, u32[]{:S(2)}, u32[]{:S(2)}) async-start(bf16[8,64,1536]{2,1,0:T(8,128)(2,1)} %get-tuple-element.34), calls=%async_computation.4 | async-start | bytes 3145728 | tf_op jit(solution)/shard_map/all_to_all | solution.py:332
  156.3 12.4 %collective-permute-start.23 = (bf16[192,512]{1,0:T(8,128)(2,1)S(1)}, bf16[192,512]{1,0:T(8,128)(2,1)S(1)}, u32[]{:S(2)}, u32[]{:S(2)}) collective-permute-start(bf16[192,512]{1,0:T(8,128)(2,1)S(1)} %get-tuple-element.43), channel_id=1, source_target_pairs={{0,32},{32,64},{64,96},{96,0},{1,33},{33,65},{65,97},{97,1},{2,34}... | collective-permute-start | bytes 589832 | tf_op jit(solution)/shard_map/ppermute | solution.py:328
  157.0 12.3 %collective-permute-start.24 = (bf16[192,512]{1,0:T(8,128)(2,1)S(1)}, bf16[192,512]{1,0:T(8,128)(2,1)S(1)}, u32[]{:S(2)}, u32[]{:S(2)}) collective-permute-start(bf16[192,512]{1,0:T(8,128)(2,1)S(1)} %get-tuple-element.45), channel_id=1, source_target_pairs={{0,64},{32,96},{64,0},{96,32},{1,65},{33,97},{65,1},{97,33},{2,66}... | collective-permute-start | bytes 589832 | tf_op jit(solution)/shard_map/ppermute | solution.py:328
  159.3 11.2 %collective-permute-start.25 = (bf16[192,512]{1,0:T(8,128)(2,1)S(1)}, bf16[192,512]{1,0:T(8,128)(2,1)S(1)}, u32[]{:S(2)}, u32[]{:S(2)}) collective-permute-start(bf16[192,512]{1,0:T(8,128)(2,1)S(1)} %get-tuple-element.44), channel_id=1, source_target_pairs={{0,96},{32,0},{64,32},{96,64},{1,97},{33,1},{65,33},{97,65},{2,98}... | collective-permute-start | bytes 589832 | tf_op jit(solution)/shard_map/ppermute | solution.py:328
  162.8 17.3 %collective-permute-start.19 = (bf16[256,512]{1,0:T(8,128)(2,1)}, bf16[256,512]{1,0:T(8,128)(2,1)}, u32[]{:S(2)}, u32[]{:S(2)}) collective-permute-start(bf16[256,512]{1,0:T(8,128)(2,1)} %get-tuple-element.40), channel_id=1, source_target_pairs={{0,32},{32,64},{64,96},{96,0},{1,33},{33,65},{65,97},{97,1},{2,34}... | collective-permute-start | bytes 786440 | tf_op jit(solution)/shard_map/ppermute | solution.py:328
  163.4 16.7 %collective-permute-start.20 = (bf16[256,512]{1,0:T(8,128)(2,1)}, bf16[256,512]{1,0:T(8,128)(2,1)}, u32[]{:S(2)}, u32[]{:S(2)}) collective-permute-start(bf16[256,512]{1,0:T(8,128)(2,1)} %get-tuple-element.42), channel_id=1, source_target_pairs={{0,64},{32,96},{64,0},{96,32},{1,65},{33,97},{65,1},{97,33},{2,66}... | collective-permute-start | bytes 786440 | tf_op jit(solution)/shard_map/ppermute | solution.py:328
  168.7 12.1 %collective-permute-start.21 = (bf16[256,512]{1,0:T(8,128)(2,1)S(1)}, bf16[256,512]{1,0:T(8,128)(2,1)}, u32[]{:S(2)}, u32[]{:S(2)}) collective-permute-start(bf16[256,512]{1,0:T(8,128)(2,1)S(1)} %get-tuple-element.41), channel_id=1, source_target_pairs={{0,96},{32,0},{64,32},{96,64},{1,97},{33,1},{65,33},{97,65},{2,98}... | collective-permute-start | bytes 786440 | tf_op jit(solution)/shard_map/ppermute | solution.py:328
  184.0 12.2 %collective-permute-start.16 = (bf16[64,256]{1,0:T(8,128)(2,1)S(1)}, bf16[64,256]{1,0:T(8,128)(2,1)S(1)}, u32[]{:S(2)}, u32[]{:S(2)}) collective-permute-start(bf16[64,256]{1,0:T(8,128)(2,1)S(1)} %get-tuple-element.46), channel_id=1, source_target_pairs={{8,0},{16,8},{24,16},{32,24},{40,32},{48,40},{56,48},{64,56},{72,6... | collective-permute-start | bytes 98312 | tf_op jit(solution)/shard_map/ppermute | solution.py:30
  186.3 19.9 %all-to-all-start.5 = ((bf16[16,32,512]{2,1,0:T(8,128)(2,1)}), bf16[16,32,512]{2,1,0:T(8,128)(2,1)S(1)}, u32[]{:S(2)}, u32[]{:S(2)}) async-start(bf16[16,32,512]{2,1,0:T(8,128)(2,1)} %fusion.6), calls=%async_computation.5 | async-start | bytes 1048576 | tf_op jit(solution)/shard_map/all_to_all | solution.py:332
  (42 other events, 226.5 us)

commit v4 on v3

v4 whole, which is shorter than its diff:
```python
import functools

import jax
import jax.numpy as jnp
from jax import lax
from jax.experimental import pallas as pl
from jax.experimental.pallas import tpu as pltpu
from jax.sharding import Mesh, PartitionSpec as P

L = 512
BLK = 128
HB = 2
EPSILON = 1e-05

SLAB = ("y", "xl", "c")
LAT = ("xh", "z")
XS = ("xl", "xh")
BF = jnp.bfloat16
F32 = jnp.float32
EDGE_MIB = 16
NODE_MIB = 14
BACK_MIB = 28


def shape_of(shape, dtype):
    return jax.ShapeDtypeStruct(shape, dtype)


def from_behind(value, steps):
    count = lax.axis_size(SLAB)
    first, last = (max(0, -steps), min(count, count - steps))
    return lax.ppermute(value, SLAB, [(source, source + steps) for source in range(first, last)])


def dot(left, right):
    return jnp.dot(left, right, preferred_element_type=F32)


def dot_rows(left, right):
    return lax.dot_general(left, right, (((0,), (0,)), ((), ())), preferred_element_type=F32)


def dot_transpose(left, right):
    return lax.dot_general(left, right, (((1,), (1,)), ((), ())), preferred_element_type=F32)


def one_hot_columns(offsets):
    cells = lax.broadcasted_iota(jnp.int32, (BLK, BLK), 0)
    return (cells == offsets).astype(F32)


def norm_parts(values):
    average = jnp.mean(values, axis=-1, keepdims=True)
    centred = values - average
    variance = jnp.mean(centred * centred, axis=-1, keepdims=True)
    inverse = lax.rsqrt(variance + EPSILON)
    return centred * inverse, inverse


def norm_back(upstream, normed, inverse, gain_vector):
    scaled = upstream * gain_vector
    return inverse * (
        scaled
        - jnp.mean(scaled, axis=-1, keepdims=True)
        - normed * jnp.mean(scaled * normed, axis=-1, keepdims=True)
    )


def split_three(value):
    high = value.astype(BF)
    rest = value - high.astype(F32)
    middle = rest.astype(BF)
    return high, middle, (rest - middle.astype(F32)).astype(BF)


def block_at(number):
    return pl.ds(pl.multiple_of(number * BLK, BLK), BLK)


def copies(pairs, sems):
    made = [pltpu.make_async_copy(src, dst, sems.at[i]) for i, (src, dst) in enumerate(pairs)]
    for one in made:
        one.start()
    return made


def wait_all(made):
    for one in made:
        one.wait()


def weight_pairs(core, y_index, shards, outs, counts):
    total = sum(counts)
    y_count = len(shards) // 2
    pairs = []
    for number, source in enumerate(shards):
        step = number % y_count
        parity = core if number < y_count else 1 - core
        y = lax.rem(y_index - step + y_count, y_count)
        per = source.shape[0] // total
        for x in range(per):
            slab = (y * per + x) * 2 + parity
            at = x * total
            for out, count in zip(outs, counts):
                start = pl.multiple_of(slab * count, 32)
                pairs.append((source.at[pl.ds(at, count), :], out.at[pl.ds(start, count), :]))
                at += count
    return pairs


def pack_grads(core, y_index, grads, keep, send, counts):
    total = sum(counts)
    y_count = keep.shape[0]
    per = keep.shape[1] // total
    for target, parity in ((keep, core), (send, 1 - core)):
        for step in range(y_count):
            y = lax.rem(y_index + step, y_count)
            for x in range(per):
                at = x * total
                for grad, count in zip(grads, counts):
                    start = pl.multiple_of(((y * per + x) * 2 + parity) * count, 32)
                    target[step, pl.ds(at, count), :] = grad[pl.ds(start, count), :].astype(BF)
                    at += count


def prepare(halo, turned, w_edge_in, w_edge_out, w_node_in, w_node_out, up, down, packed):
    for j in range(HB):
        up[:, pl.ds(j * BLK, BLK)] = turned[:, block_at(halo[j])]
        down[:, pl.ds(j * BLK, BLK)] = turned[:, block_at(halo[HB + j])]
    parts = [ref[...].astype(F32) for ref in (w_edge_in, w_edge_out, w_node_in, w_node_out)]
    used = sum(part.shape[0] for part in parts)
    parts.append(jnp.zeros((packed.shape[0] - used, L), F32))
    packed[...] = jnp.concatenate(parts, axis=0).astype(BF)


def assemble(pieces, scal, *refs):
    blocks, (edge_part, node_part, held, edge_rows, node_rows) = refs[:4], refs[4:]
    z_index, x_index = scal[0], scal[1]
    for k, block in enumerate(blocks):
        held[k] = block[...]
    outs = (edge_rows, edge_rows, node_rows, node_rows)
    bases = []
    for number, count in enumerate(pieces):
        bases.append(0 if number % 2 == 0 else bases[-1] + 8 * pieces[number - 1])
    sizes = (8 * (pieces[0] + pieces[1]), 8 * (pieces[2] + pieces[3]))
    for x in range(4):
        x_step = lax.rem(x_index - x + 4, 4)
        for z in range(4):
            z_step = lax.rem(z_index - z + 4, 4)
            shard = held[z_step, pl.ds(pl.multiple_of(x_step * 32, 32), 32), :].astype(F32)
            row, lat = 0, (x % 2) * 4 + z
            for number, count in enumerate(pieces):
                base = (x // 2) * sizes[number // 2] + bases[number] + lat * count
                outs[number][pl.ds(base, count), :] = shard[row : row + count]
                row += count
    edge_part[...] = edge_rows[...].astype(BF)
    node_part[...] = node_rows[...].astype(BF)


def sum_far(pieces, scal, edge_own, e1, e2, e3, node_own, n1, n2, n3, keep, s1, s2, s3, er, nr, sent):
    z_index = scal[0]
    er[...] = sum((ref[...].astype(F32) for ref in (e1, e2, e3)), edge_own[...].astype(F32))
    nr[...] = sum((ref[...].astype(F32) for ref in (n1, n2, n3)), node_own[...].astype(F32))
    ins = (er, er, nr, nr)
    bases = []
    for number, count in enumerate(pieces):
        bases.append(0 if number % 2 == 0 else bases[-1] + 8 * pieces[number - 1])
    sizes = (8 * (pieces[0] + pieces[1]), 8 * (pieces[2] + pieces[3]))
    spare = 32 - sum(pieces)
    for x in range(4):
        for z in range(4):
            lat = (x % 2) * 4 + z
            parts = []
            for number, count in enumerate(pieces):
                base = (x // 2) * sizes[number // 2] + bases[number] + lat * count
                parts.append(ins[number][pl.ds(base, count), :])
            parts.append(jnp.zeros((spare, L), F32))
            sent[z, x] = jnp.concatenate(parts, axis=0)
    keep[...] = sent[z_index]
    for step, out in ((1, s1), (2, s2), (3, s3)):
        out[...] = sent[lax.rem(z_index + step, 4)].astype(BF)


def sum_z(scal, own, r1, r2, r3, keep, s1, s2, s3, held):
    x_index = scal[1]
    held[...] = own[...] + (r1[...].astype(F32) + r2[...].astype(F32) + r3[...].astype(F32))
    keep[...] = held[x_index]
    for step, out in ((1, s1), (2, s2), (3, s3)):
        out[...] = held[lax.rem(x_index + step, 4)].astype(BF)


def sum_x(own, r1, r2, r3, *outs):
    total = own[...] + (r1[...].astype(F32) + r2[...].astype(F32) + r3[...].astype(F32))
    row = 0
    for out in outs:
        count = out.shape[0]
        out[...] = total[row : row + count]
        row += count


def edge_forward(scal, ext_hbm, edges, offsets, *refs):
    shards, refs = refs[:8], refs[8:]
    gain, joined_out, first_out, normed_out, inverse_out, new_edges_out, partial_out = refs[:7]
    ext, joined, first, normed, inverse, new_edges, partial, w_in, w_out, second = refs[7:17]
    sems, out_sems = refs[17:]
    tiles = edges.shape[0] // BLK
    lat_index, core, y_index, count = (scal[2 * tiles + i] for i in range(4))
    slabs = w_in.shape[0] // 3 // 32
    counts = (3 * L // slabs, L // slabs)
    pairs = [(ext_hbm, ext)] + weight_pairs(core, y_index, shards, (w_in, w_out), counts)
    loads = copies(pairs, sems)
    stores = []

    def store(source, target):
        copy = pltpu.make_async_copy(source, target, out_sems.at[len(stores)])
        copy.start()
        stores.append(copy)

    joined[:, pl.ds(0, L)] = edges[...]
    loads[0].wait()
    for t in range(tiles):
        rows = pl.ds(t * BLK, BLK)
        to_src = one_hot_columns(offsets[1, pl.ds(t, 1), :]).T.astype(BF)
        to_dst = one_hot_columns(offsets[0, pl.ds(t, 1), :]).T.astype(BF)
        src, dst = block_at(scal[tiles + t]), block_at(scal[t] + HB)
        joined[rows, pl.ds(L, L)] = dot_transpose(to_src, ext[:, src]).astype(BF)
        joined[rows, pl.ds(2 * L, L)] = dot_transpose(to_dst, ext[:, dst]).astype(BF)
    store(joined, joined_out)
    wait_all(loads[1:])
    for n in range(2):
        columns = pl.ds(n * 256, 256)
        first[:, columns] = jnp.maximum(dot(joined[...], w_in[:, columns]), 0.0).astype(BF)
    store(first, first_out)
    for n in range(2):
        columns = pl.ds(n * 256, 256)
        second[:, columns] = dot(first[...], w_out[:, columns])
    partial[...] = jnp.zeros_like(partial)
    for t in range(tiles):
        rows = pl.ds(t * BLK, BLK)
        live = (lat_index * tiles + t < count).astype(F32)
        values, inv = norm_parts(second[rows, :])
        normed[rows, :] = values
        inverse[rows, :] = jnp.broadcast_to(inv, (BLK, BLK))
        message = values * gain[...] * live
        new_edges[rows, :] = (edges[rows, :].astype(F32) + message).astype(BF)
        second[rows, :] = message
    store(normed, normed_out)
    store(inverse, inverse_out)
    store(new_edges, new_edges_out)
    for t in range(tiles):
        rows = pl.ds(t * BLK, BLK)
        into = one_hot_columns(offsets[0, pl.ds(t, 1), :]).astype(BF)
        high, middle, low = split_three(second[rows, :])
        block = scal[t]
        partial[block] = partial[block] + (dot(into, low) + dot(into, middle) + dot(into, high))
    store(partial, partial_out)
    wait_all(stores)


def node_step(scal, spread, ext_hbm, *refs):
    shards, refs = refs[:8], refs[8:]
    gain, out, d_direct, keep, send = refs[:5]
    own_turned, up_turned, w_in, w_out, joined, first, g_in, g_out, sems = refs[5:]
    lat_index, core, y_index = scal[0], scal[1], scal[2]
    slabs = w_in.shape[0] // 2 // 32
    counts = (2 * L // slabs, L // slabs)
    pairs = [
        (ext_hbm.at[:, block_at(HB + lat_index)], own_turned),
        (ext_hbm.at[:, pl.ds(ext_hbm.shape[1] - BLK, BLK)], up_turned),
    ] + weight_pairs(core, y_index, shards, (w_in, w_out), counts)
    loads = copies(pairs, sems)
    total = spread[0]
    for l in range(1, spread.shape[0]):
        total = total + spread[l]
    joined[:, pl.ds(L, L)] = total.astype(BF)
    wait_all(loads)
    own = own_turned[...].astype(F32).T
    upstream = up_turned[...].astype(F32).T
    joined[:, pl.ds(0, L)] = own.astype(BF)
    first[...] = jnp.maximum(dot(joined[...], w_in[...]), 0.0).astype(BF)
    normed, inverse = norm_parts(dot(first[...], w_out[...]))
    new_rows = (own + normed * gain[...]).T.astype(BF)
    d_second = norm_back(upstream, normed, inverse, gain[...]).astype(BF)
    d_first = dot_transpose(d_second, w_out[...])
    d_first = jnp.where(first[...].astype(F32) > 0, d_first, 0.0).astype(BF)
    d_direct[...] = dot_transpose(w_in[pl.ds(0, L), :], d_first)
    d_agg = dot_transpose(w_in[pl.ds(L, L), :], d_first).astype(BF)
    width = L // out.shape[0]
    for l in range(out.shape[0]):
        out[l, pl.ds(0, L), :] = d_agg
        out[l, pl.ds(L, width), :] = new_rows[l * width : (l + 1) * width, :]
    g_out[...] = dot_rows(first[...], d_second)
    g_in[...] = dot_rows(joined[...], d_first)
    pack_grads(core, y_index, (g_in, g_out), keep, send, counts)


def edge_backward(scal, d_agg, cot, offsets, gain, *refs):
    saved, shards, refs = refs[:5], refs[5:13], refs[13:]
    grad_edges, middle_out, lower, upper, keep, send = refs[:6]
    joined, first, normed, inverse, d_direct, w_in, w_out = refs[6:13]
    d_second, d_first, d_ext, d_turned, g_in, g_out, sems = refs[13:]
    tiles = cot.shape[0] // BLK
    lat_index, core, y_index, count = (scal[2 * tiles + i] for i in range(4))
    slabs = w_in.shape[0] // 3 // 32
    counts = (3 * L // slabs, L // slabs)
    normed_in, inverse_in, first_in, joined_in, direct_in = saved
    pairs = [(normed_in, normed), (inverse_in, inverse)]
    pairs += weight_pairs(core, y_index, shards, (w_in, w_out), counts)
    pairs += [(first_in, first), (joined_in, joined), (direct_in, d_direct)]
    loads = copies(pairs, sems)
    wait_all(loads[:2])
    for t in range(tiles):
        rows = pl.ds(t * BLK, BLK)
        live = (lat_index * tiles + t < count).astype(F32)
        to_dst = one_hot_columns(offsets[0, pl.ds(t, 1), :]).T.astype(BF)
        picked = dot_transpose(to_dst, d_agg[scal[t], pl.ds(0, L), :])
        d_message = (cot[rows, :].astype(F32) + picked) * live
        back = norm_back(d_message, normed[rows, :], inverse[rows, pl.ds(0, 1)], gain[...])
        d_second[rows, :] = back.astype(BF)
    wait_all(loads[2:])
    for n in range(2):
        part = pl.ds(n * 256, 256)
        back = dot_transpose(d_second[...], w_out[part, :])
        d_first[:, part] = jnp.where(first[:, part].astype(F32) > 0, back, 0.0).astype(BF)
    for n in range(4):
        d_turned[pl.ds(n * 256, 256), :] = dot_transpose(
            w_in[pl.ds(L + n * 256, 256), :], d_first[...]
        )
    d_ext[...] = jnp.zeros_like(d_ext)
    for t in range(tiles):
        rows = pl.ds(t * BLK, BLK)
        for row, place, at in ((1, scal[tiles + t], 0), (0, scal[t] + HB, L)):
            into = one_hot_columns(offsets[row, pl.ds(t, 1), :]).T.astype(BF)
            value = d_turned[pl.ds(at, L), rows]
            high = value.astype(BF)
            low = (value - high.astype(F32)).astype(BF)
            d_ext[place] = d_ext[place] + (dot(low, into) + dot(high, into))
    d_ext[HB + lat_index] = d_ext[HB + lat_index] + d_direct[...]
    blocks = middle_out.shape[0]
    for j in range(HB):
        lower[:, pl.ds(j * BLK, BLK)] = d_ext[j].astype(BF)
        upper[:, pl.ds(j * BLK, BLK)] = d_ext[HB + blocks + j].astype(BF)
    middle_out[...] = d_ext[pl.ds(HB, blocks)]
    for n in range(2):
        part = pl.ds(n * 256, 256)
        back = dot_transpose(d_first[...], w_in[part, :])
        grad_edges[:, part] = (cot[:, part].astype(F32) + back).astype(BF)
    for n in range(2):
        part = pl.ds(n * 256, 256)
        g_out[part, :] = dot_rows(first[:, part], d_second[...])
    for n in range(6):
        part = pl.ds(n * 256, 256)
        g_in[part, :] = dot_rows(joined[:, part], d_first[...])
    pack_grads(core, y_index, (g_in, g_out), keep, send, counts)


def add_halo(halo, middle, above, below, columns, held):
    held[...] = middle[...]
    for j in range(HB):
        for place, value in ((halo[j], above), (halo[HB + j], below)):
            held[place] = held[place] + value[:, pl.ds(j * BLK, BLK)].astype(F32)
    width = columns.shape[1]
    for block in range(held.shape[0]):
        for l in range(columns.shape[0]):
            columns[l, :, pl.ds(block * BLK, BLK)] = held[
                block, pl.ds(l * width, width), :
            ].astype(BF)


def finish(arrived, out):
    total = arrived[0].astype(F32)
    for l in range(1, arrived.shape[0]):
        total = total + arrived[l].astype(F32)
    out[...] = total.astype(BF)


def call(kernel, out_shape, scratch, mib, spaces, operands, flops=0, out_spaces="", sems=()):
    moved = sum(x.size * x.dtype.itemsize for x in operands)
    moved += sum(x.size * x.dtype.itemsize for x in out_shape)
    named = {"s": pltpu.SMEM, "v": pltpu.VMEM, "h": pltpu.HBM}
    out_spaces = out_spaces or "v" * len(out_shape)
    return pl.pallas_call(
        kernel,
        out_shape=out_shape,
        in_specs=[pl.BlockSpec(memory_space=named[space]) for space in spaces],
        out_specs=[pl.BlockSpec(memory_space=named[space]) for space in out_spaces],
        scratch_shapes=[pltpu.VMEM(shape, dtype) for shape, dtype in scratch]
        + [pltpu.SemaphoreType.DMA((count,)) for count in sems],
        cost_estimate=pl.CostEstimate(flops=flops, bytes_accessed=moved, transcendentals=0),
        compiler_params=pltpu.CompilerParams(vmem_limit_bytes=mib << 20),
    )(*operands)


def run_edge_forward(scal, ext, edges, offsets, shards, gain, lat_size):
    rows = edges.shape[0]
    outs = [
        shape_of((rows, 3 * L), BF),
        shape_of((rows, L), BF),
        shape_of((rows, L), F32),
        shape_of((rows, BLK), F32),
        shape_of((rows, L), BF),
        shape_of((lat_size, BLK, L), F32),
    ]
    held = [(ext.shape, BF)] + [(out.shape, out.dtype) for out in outs]
    return call(
        edge_forward,
        outs,
        held + [((3 * L, L), BF), ((L, L), BF), ((rows, L), F32)],
        EDGE_MIB,
        "shvv" + "h" * len(shards) + "v",
        (scal, ext, edges, offsets, *shards, gain),
        flops=2 * rows * 4 * L * L,
        out_spaces="h" * len(outs),
        sems=(1 + 4 * len(shards), len(outs)),
    )


def run_node_step(scal, spread, ext, shards, gain):
    lat_size = spread.shape[0]
    chunk = (len(shards) // 2,) + shards[0].shape
    return call(
        node_step,
        [
            shape_of((lat_size, L + L // lat_size, BLK), BF),
            shape_of((L, BLK), F32),
            shape_of(chunk, BF),
            shape_of(chunk, BF),
        ],
        [
            ((L, BLK), BF),
            ((L, BLK), BF),
            ((2 * L, L), BF),
            ((L, L), BF),
            ((BLK, 2 * L), BF),
            ((BLK, L), BF),
            ((2 * L, L), F32),
            ((L, L), F32),
        ],
        NODE_MIB,
        "svh" + "h" * len(shards) + "v",
        (scal, spread, ext, *shards, gain),
        flops=2 * BLK * 9 * L * L,
        sems=(2 + 4 * len(shards),),
    )


def run_edge_backward(scal, d_agg, cot, offsets, gain, saved, shards):
    rows = cot.shape[0]
    lat_size = d_agg.shape[0]
    chunk = (len(shards) // 2,) + shards[0].shape
    normed, inverse, first, joined, d_direct = saved
    return call(
        edge_backward,
        [
            shape_of((rows, L), BF),
            shape_of((lat_size, L, BLK), F32),
            shape_of((L, HB * BLK), BF),
            shape_of((L, HB * BLK), BF),
            shape_of(chunk, BF),
            shape_of(chunk, BF),
        ],
        [
            (joined.shape, BF),
            (first.shape, BF),
            (normed.shape, F32),
            (inverse.shape, F32),
            (d_direct.shape, F32),
            ((3 * L, L), BF),
            ((L, L), BF),
            ((rows, L), BF),
            ((rows, L), BF),
            ((lat_size + 2 * HB, L, BLK), F32),
            ((2 * L, rows), F32),
            ((3 * L, L), F32),
            ((L, L), F32),
        ],
        BACK_MIB,
        "svvvv" + "h" * (len(saved) + len(shards)),
        (scal, d_agg, cot, offsets, gain, *saved, *shards),
        flops=2 * rows * 8 * L * L,
        sems=(5 + 4 * len(shards),),
    )


def swap_cores(value):
    return lax.ppermute(value, "c", [(0, 1), (1, 0)])


def shift(value, axes, step):
    count = lax.axis_size(axes)
    return lax.ppermute(value, axes, [(i, (i + step) % count) for i in range(count)])


def shifts(value, axes):
    return [value] + [shift(value, axes, k) for k in range(1, lax.axis_size(axes))]


def spread_rows(value, axes):
    return lax.all_to_all(value, axes, 0, 0)


def gather_far(value):
    mine = shifts(value, "y")
    return mine + [swap_cores(one) for one in mine]


def reduce_far(keep, send):
    arrived = swap_cores(send)
    both = [(keep[k].astype(F32) + arrived[k].astype(F32)).astype(BF) for k in range(keep.shape[0])]
    return [both[0]] + [shift(both[k], "y", k) for k in range(1, keep.shape[0])]


def per_device(
    nodes,
    edges,
    edge_tiles,
    edge_offsets,
    tile_counts,
    halo_blocks,
    w_edge_in,
    w_edge_out,
    w_node_in,
    w_node_out,
    edge_gain,
    node_gain,
    node_cotangent,
    edge_cotangent,
):
    lat_size = lax.axis_size(LAT)
    place = [lax.axis_index(LAT), lax.axis_index("c"), lax.axis_index("y")]
    slab_rows, width = nodes.shape
    own_rows = slab_rows // lat_size
    halo_rows = HB * BLK
    ext_rows = slab_rows + 2 * halo_rows
    weights = (w_edge_in, w_edge_out, w_node_in, w_node_out)
    pieces = tuple(weight.shape[0] for weight in weights)
    edge_rows = 2 * lat_size * (pieces[0] + pieces[1])
    node_rows = 2 * lat_size * (pieces[2] + pieces[3])

    near_scal = jnp.stack([lax.axis_index("z"), lax.axis_index(XS)]).astype(jnp.int32)
    node_scal = jnp.stack(place).astype(jnp.int32)
    scal = jnp.concatenate([edge_tiles.reshape(-1), node_scal, tile_counts])
    halo = halo_blocks.reshape(-1)
    offsets = edge_offsets.reshape(2, -1, BLK)
    edge_gain_row = edge_gain.reshape(1, L)
    node_gain_row = node_gain.reshape(1, L)

    turned = nodes.T
    up, down, packed = call(
        prepare,
        [
            shape_of((width, halo_rows), BF),
            shape_of((width, halo_rows), BF),
            shape_of((32, L), BF),
        ],
        [],
        4,
        "svvvvv",
        (halo, turned, *weights),
    )
    from_lower = from_behind(up, 1)
    from_upper = from_behind(down, -1)

    near = shifts(jnp.concatenate(shifts(packed, XS), axis=0), "z")
    edge_part, node_part = call(
        functools.partial(assemble, pieces),
        [shape_of((edge_rows, L), BF), shape_of((node_rows, L), BF)],
        [((4, 128, L), BF), ((edge_rows, L), F32), ((node_rows, L), F32)],
        6,
        "svvvv",
        (near_scal, *near),
    )

    table = jnp.concatenate([from_lower, turned, from_upper], axis=1)
    cot = node_cotangent.T.reshape(width, lat_size, own_rows).transpose(1, 0, 2)
    message_out = jnp.concatenate(
        [jnp.broadcast_to(table, (lat_size,) + table.shape), cot], axis=2
    )
    edge_shards = gather_far(edge_part)
    ext = spread_rows(message_out, LAT).reshape(L, ext_rows + own_rows)

    joined, first, normed, inverse, new_edges, partial = run_edge_forward(
        scal, ext, edges, offsets, edge_shards, edge_gain_row, lat_size
    )
    node_shards = gather_far(node_part)
    spread = spread_rows(partial, LAT)
    second_out, d_direct, node_keep, node_send = run_node_step(
        node_scal, spread, ext, node_shards, node_gain_row
    )
    second_in = spread_rows(second_out, LAT)
    new_nodes = second_in[:, L:].transpose(1, 0, 2).reshape(width, slab_rows).T
    node_far = reduce_far(node_keep, node_send)
    second_in, *node_far = lax.optimization_barrier((second_in, *node_far))

    grad_edges, middle, lower, upper, edge_keep, edge_send = run_edge_backward(
        scal, second_in, edge_cotangent, offsets, edge_gain_row,
        (normed, inverse, first, joined, d_direct), edge_shards,
    )
    from_above = from_behind(lower, -1)
    from_below = from_behind(upper, 1)
    (columns,) = call(
        add_halo,
        [shape_of((lat_size, width, slab_rows), BF)],
        [((lat_size, L, BLK), F32)],
        8,
        "svvv",
        (halo, middle, from_above, from_below),
    )
    edge_far = reduce_far(edge_keep, edge_send)
    (grad_slab,) = call(
        finish, [shape_of((width, slab_rows), BF)], [], 4, "v", (spread_rows(columns, LAT),)
    )

    shard = (32, L)
    shards = (4,) + shard
    kept, *sent = call(
        functools.partial(sum_far, pieces),
        [shape_of(shards, F32)] + [shape_of(shards, BF)] * 3,
        [((edge_rows, L), F32), ((node_rows, L), F32), ((4,) + shards, F32)],
        8,
        "s" + "v" * 8,
        (near_scal, *edge_far, *node_far),
    )
    moved = [shift(sent[k - 1], "z", k) for k in range(1, 4)]
    kept, *sent = call(
        sum_z,
        [shape_of(shard, F32)] + [shape_of(shard, BF)] * 3,
        [(shards, F32)],
        4,
        "s" + "v" * 4,
        (near_scal, kept, *moved),
    )
    moved = [shift(sent[k - 1], XS, k) for k in range(1, 4)]
    reduced = call(
        sum_x, [shape_of((count, L), F32) for count in pieces], [], 4, "v" * 4, (kept, *moved)
    )
    return (new_nodes, new_edges, grad_slab.T, grad_edges) + tuple(reduced)


def solution(mesh):
    fine = Mesh(mesh.devices.reshape(4, 2, 2, 2, 4), ("y", "xl", "c", "xh", "z"))
    every = SLAB + LAT
    by_rows = P(every, None)
    split = P(SLAB, LAT)
    placed = (
        split,
        by_rows,
        P(None, every),
        P(None, every),
        P(SLAB),
        P(SLAB, None, None),
        by_rows,
        by_rows,
        by_rows,
        by_rows,
        P(),
        P(),
        split,
        by_rows,
    )
    return jax.shard_map(
        per_device,
        mesh=fine,
        in_specs=placed,
        out_specs=(split, by_rows, split, by_rows, by_rows, by_rows, by_rows, by_rows),
        check_vma=False,
    )
```

time: 210 us -> 233 us (1.11)
  waiting for transfers between devices: 81.1 us -> 95.3 us
  Pallas kernels: 15.3 us -> 28.9 us
  other arithmetic: 14.3 us -> 4.85 us
  starting transfers between devices: 60.2 us -> 69.4 us
  between operations: 4.41 us -> 1.73 us
    ppermute x12 -> x24, waiting for transfers between devices: 29.7 us -> 76.6 us  [shift(): lax.ppermute(value, axes, [(i, (i + step) % count) for i in range(count)])]
    all_to_all x6 -> x4, waiting for transfers between devices: 49.7 us -> 13.3 us  [spread_rows(): return lax.all_to_all(value, axes, 0, 0)]
    ppermute x12 -> x24, starting transfers between devices: 16.7 us -> 40.1 us  [shift(): lax.ppermute(value, axes, [(i, (i + step) % count) for i in range(count)])]
    all_to_all x6 -> x4, starting transfers between devices: 36.5 us -> 21.6 us  [spread_rows(): return lax.all_to_all(value, axes, 0, 0)]
    pallas_call x3 -> x10, Pallas kernels: 15.3 us -> 28.9 us  [call(): pl.pallas_call(kernel, out_shape=out_shape, in_specs=[pl.BlockSpec(memory...]
    unnamed x68 -> x99, local copies, waits for them, and re-layouts: 23 us -> 29 us
    ppermute x4, waiting for transfers between devices: 0.74 us -> 4.71 us  [from_behind(): lax.ppermute(value, SLAB, [(source, source + steps) for source in range(f...]
    slice x16 -> x0, local copies, waits for them, and re-layouts: 3.72 us -> none  [the longest x3 1.83 us: per_device(): out.append(total[at:at + count])]
  transfers between devices with their start and end apart: 32 -> 42, of which waited for: 18 -> 26; matrix products, arithmetic and copies ran while one was open for 9% -> 2% of each run, Pallas kernels for 3% -> 2%
where the time goes in v4:
time: 233 us; the launch traced here: 231 us
  waiting for transfers between devices  95.3 us (41%)
  starting transfers between devices  69.4 us (30%)
  local copies, waits for them, and re-layouts  30.8 us (13%)
  Pallas kernels  28.9 us (12%)
  other arithmetic  4.85 us (2%)
    ppermute x24, waiting for transfers between devices, shift(): lax.ppermute(value, axes, [(i, (i + step) % count) for i in range(count)])  76.6 us
    ppermute x24, starting transfers between devices, shift(): lax.ppermute(value, axes, [(i, (i + step) % count) for i in range(count)])  40.1 us
    unnamed x99, local copies, waits for them, and re-layouts  29 us
    pallas_call x10, Pallas kernels, call(): pl.pallas_call(kernel, out_shape=out_shape, in_specs=[pl.BlockSpec(memory...  28.9 us
    all_to_all x4, starting transfers between devices, spread_rows(): return lax.all_to_all(value, axes, 0, 0)  21.6 us
    all_to_all x4, waiting for transfers between devices, spread_rows(): return lax.all_to_all(value, axes, 0, 0)  13.3 us
    ppermute x4, starting transfers between devices, from_behind(): lax.ppermute(value, SLAB, [(source, source + steps) for source in range(f...  6.92 us
    ppermute x4, waiting for transfers between devices, from_behind(): lax.ppermute(value, SLAB, [(source, source + steps) for source in range(f...  4.71 us
  transfers between devices with their start and end apart: 42, of which 26 were waited for; matrix products, arithmetic and copies ran while one was open for 2% of the time, Pallas kernels for 2%

profile of v4, /device:TPU:0, one launch (start us, length us, event | category | flops | bytes accessed | tf_op | source)
XLA Modules:
  0.0 230.9 jit_solution(12590317786604560199)
XLA Ops:
  8.4 3.6 %collective-permute-done.1 = bf16[64,256]{1,0:T(8,128)(2,1)S(1)} collective-permute-done((bf16[64,256]{1,0:T(8,128)(2,1)S(1)}, bf16[64,256]{1,0:T(8,128)(2,1)S(1)}, u32[]{:S(2)}, u32[]{:S(2)}) %collective-permute-start.1) | collective-permute-done | bytes 32800 | tf_op jit(solution)/shard_map/ppermute | solution.py:32
  14.3 7.6 %all-to-all-start = ((bf16[8,64,1664]{2,1,0:T(8,128)(2,1)}), bf16[8,64,1664]{2,1,0:T(8,128)(2,1)S(1)}, u32[]{:S(2)}, u32[]{:S(2)}) async-start(bf16[8,64,1664]{2,1,0:T(8,128)(2,1)} %pad_maximum_fusion), calls=%async_computation | async-start | bytes 3407872 | tf_op jit(solution)/shard_map/all_to_all | solution.py:499
  22.0 4.6 %collective-permute-start.4 = (bf16[32,512]{1,0:T(8,128)(2,1)S(1)}, bf16[32,512]{1,0:T(8,128)(2,1)S(1)}, u32[]{:S(2)}, u32[]{:S(2)}) collective-permute-start(bf16[32,512]{1,0:T(8,128)(2,1)S(1)} %get-tuple-element.48), channel_id=1, source_target_pairs={{0,20},{4,0},{16,4},{20,16},{1,21},{5,1},{17,5},{21,17},{2,22},{6,... | collective-permute-start | bytes 98312 | tf_op jit(solution)/shard_map/ppermute | solution.py:491
  28.0 18.8 %collective-permute-done.2 = bf16[32,512]{1,0:T(8,128)(2,1)S(1)} collective-permute-done((bf16[32,512]{1,0:T(8,128)(2,1)S(1)}, bf16[32,512]{1,0:T(8,128)(2,1)S(1)}, u32[]{:S(2)}, u32[]{:S(2)}) %collective-permute-start.2) | collective-permute-done | bytes 32800 | tf_op jit(solution)/shard_map/ppermute | solution.py:491
  46.9 2.7 %collective-permute-start.7 = (bf16[128,512]{1,0:T(8,128)(2,1)S(1)}, bf16[128,512]{1,0:T(8,128)(2,1)S(1)}, u32[]{:S(2)}, u32[]{:S(2)}) collective-permute-start(bf16[128,512]{1,0:T(8,128)(2,1)S(1)} %constant_dynamic-update-slice_fusion.refs_0_), channel_id=1, source_target_pairs={{0,3},{1,0},{2,1},{3,2},{4,7},{5,4},{6,5},{7,6},{8,11},{9,8},{10,9... | collective-permute-start | bytes 393224 | tf_op jit(solution)/shard_map/ppermute | solution.py:491
  51.4 4.1 %collective-permute-done.7.refs_3_ = bf16[128,512]{1,0:T(8,128)(2,1)S(1)} collective-permute-done((bf16[128,512]{1,0:T(8,128)(2,1)S(1)}, bf16[128,512]{1,0:T(8,128)(2,1)S(1)}, u32[]{:S(2)}, u32[]{:S(2)}) %collective-permute-start.7) | collective-permute-done | bytes 131104 | tf_op jit(solution)/shard_map/ppermute | solution.py:491
  60.6 3.7 %collective-permute-start.10 = (bf16[256,512]{1,0:T(8,128)(2,1)S(1)}, bf16[256,512]{1,0:T(8,128)(2,1)S(1)}, u32[]{:S(2)}, u32[]{:S(2)}) collective-permute-start(bf16[256,512]{1,0:T(8,128)(2,1)S(1)} %get-tuple-element.49.refs_0_.refs_5_), channel_id=1, source_target_pairs={{0,96},{32,0},{64,32},{96,64},{1,97},{33,1},{65,33},{97,65},{2,98}... | collective-permute-start | bytes 786440 | tf_op jit(solution)/shard_map/ppermute | solution.py:491
  66.1 9.0 %collective-permute-done.10.refs_3_.refs_8_ = bf16[256,512]{1,0:T(8,128)(2,1)S(1)} collective-permute-done((bf16[256,512]{1,0:T(8,128)(2,1)S(1)}, bf16[256,512]{1,0:T(8,128)(2,1)S(1)}, u32[]{:S(2)}, u32[]{:S(2)}) %collective-permute-start.10) | collective-permute-done | bytes 262176 | tf_op jit(solution)/shard_map/ppermute | solution.py:491
  75.6 3.2 %collective-permute-done.8.refs_1_.refs_6_ = bf16[256,512]{1,0:T(8,128)(2,1)S(1)} collective-permute-done((bf16[256,512]{1,0:T(8,128)(2,1)S(1)}, bf16[256,512]{1,0:T(8,128)(2,1)S(1)}, u32[]{:S(2)}, u32[]{:S(2)}) %collective-permute-start.8) | collective-permute-done | bytes 262176 | tf_op jit(solution)/shard_map/ppermute | solution.py:491
  80.4 6.7 %shard_map.199 = (bf16[512,1536]{1,0:T(8,128)(2,1)S(1)}, bf16[512,512]{1,0:T(8,128)(2,1)S(1)}, f32[512,512]{1,0:T(8,128)S(1)}, f32[512,128]{1,0:T(8,128)S(1)}, b...) custom-call(s32[12]{0:T(128)S(1)} %concatenate.13.scal, bf16[512,1664]{1,0:T(8,128)(2,1)S(1)} %bitcast.42, ...), custom_call_target="tpu_custom_call" | custom-call | flops 1073741824 | bytes 10360880 | tf_op jit(solution)/shard_map/pallas_call | solution.py:382
  92.2 4.5 %all-to-all-start.1 = ((f32[8,128,512]{2,1,0:T(8,128)}), f32[8,128,512]{2,1,0:T(8,128)}, u32[]{:S(2)}, u32[]{:S(2)}) async-start(f32[8,128,512]{2,1,0:T(8,128)} %copy-done.1), calls=%async_computation.1 | async-start | bytes 4194304 | tf_op jit(solution)/shard_map/all_to_all | solution.py:499
  99.2 5.3 %collective-permute-done.17.refs_3_ = bf16[192,512]{1,0:T(8,128)(2,1)S(1)} collective-permute-done((bf16[192,512]{1,0:T(8,128)(2,1)S(1)}, bf16[192,512]{1,0:T(8,128)(2,1)S(1)}, u32[]{:S(2)}, u32[]{:S(2)}) %collective-permute-start.17) | collective-permute-done | bytes 196640 | tf_op jit(solution)/shard_map/ppermute | solution.py:491
  106.8 3.1 %collective-permute-done.15.refs_1_ = bf16[192,512]{1,0:T(8,128)(2,1)S(1)} collective-permute-done((bf16[192,512]{1,0:T(8,128)(2,1)S(1)}, bf16[192,512]{1,0:T(8,128)(2,1)S(1)}, u32[]{:S(2)}, u32[]{:S(2)}) %collective-permute-start.15) | collective-permute-done | bytes 196640 | tf_op jit(solution)/shard_map/ppermute | solution.py:491
  112.7 10.9 %all-to-all-done.1.spread = f32[8,128,512]{2,1,0:T(8,128)} async-done(((f32[8,128,512]{2,1,0:T(8,128)}), f32[8,128,512]{2,1,0:T(8,128)}, u32[]{:S(2)}, u32[]{:S(2)}) %all-to-all-start.1) | async-done | bytes 2097184 | tf_op jit(solution)/shard_map/all_to_all | solution.py:499
  127.3 7.6 %shard_map.200 = (bf16[8,576,128]{2,1,0:T(8,128)(2,1)}, f32[512,128]{1,0:T(8,128)S(1)}, bf16[4,192,512]{2,1,0:T(8,128)(2,1)S(1)}, bf16[4,192,512]{2,1,0:T(8,128)(2,1)}) custom-call(s32[3]{0:T(128)S(1)} %pad_add_fusion.scal, f32[8,128,512]{2,1,0:T(8,128)} %all-to-all-done.1.spread, bf16[512,1664]{1,0:T(8,128)(2,1)S(1)} %bitcast.43, ...), custom_call_target="tpu_custom_call" | custom-call | flops 603979776 | bytes 8390668 | tf_op jit(solution)/shard_map/pallas_call | solution.py:382
  135.6 4.8 %all-to-all-start.2 = ((bf16[8,576,128]{2,1,0:T(8,128)(2,1)}), bf16[8,576,128]{2,1,0:T(8,128)(2,1)S(1)}, u32[]{:S(2)}, u32[]{:S(2)}) async-start(bf16[8,576,128]{2,1,0:T(8,128)(2,1)} %get-tuple-element.52), calls=%async_computation.2 | async-start | bytes 2359296 | tf_op jit(solution)/shard_map/all_to_all | solution.py:499
  143.8 5.3 %collective-permute-done.25.n3 = bf16[192,512]{1,0:T(8,128)(2,1)S(1)} collective-permute-done((bf16[192,512]{1,0:T(8,128)(2,1)S(1)}, bf16[192,512]{1,0:T(8,128)(2,1)S(1)}, u32[]{:S(2)}, u32[]{:S(2)}) %collective-permute-start.25) | collective-permute-done | bytes 196640 | tf_op jit(solution)/shard_map/ppermute | solution.py:491
  168.0 8.3 %shard_map.201 = (bf16[512,512]{1,0:T(8,128)(2,1)}, f32[8,512,128]{2,1,0:T(8,128)S(1)}, bf16[512,256]{1,0:T(8,128)(2,1)S(1)}, bf16[512,256]{1,0:T(8,128)(2,1)S(1...) custom-call(s32[12]{0:T(128)S(1)} %concatenate.13.scal, ...), custom_call_target="tpu_custom_call" | custom-call | flops 2147483648 | bytes 12720176 | tf_op jit(solution)/shard_map/pallas_call | solution.py:382
  177.7 3.0 %collective-permute-start.27 = (bf16[512,256]{1,0:T(8,128)(2,1)S(1)}, bf16[512,256]{1,0:T(8,128)(2,1)S(1)}, u32[]{:S(2)}, u32[]{:S(2)}) collective-permute-start(bf16[512,256]{1,0:T(8,128)(2,1)S(1)} %get-tuple-element.64), channel_id=1, source_target_pairs={{0,8},{8,16},{16,24},{24,32},{32,40},{40,48},{48,56},{56,64},{64,7... | collective-permute-start | bytes 786440 | tf_op jit(solution)/shard_map/ppermute | solution.py:32
  183.9 4.8 %all-to-all-start.3 = ((bf16[8,64,1024]{2,1,0:T(8,128)(2,1)}), bf16[8,64,1024]{2,1,0:T(8,128)(2,1)S(1)}, u32[]{:S(2)}, u32[]{:S(2)}) async-start(bf16[8,64,1024]{2,1,0:T(8,128)(2,1)} %shard_map.202), calls=%async_computation.3 | async-start | bytes 2097152 | tf_op jit(solution)/shard_map/all_to_all | solution.py:499
  190.3 7.5 %collective-permute-start.31 = (bf16[256,512]{1,0:T(8,128)(2,1)S(1)}, bf16[256,512]{1,0:T(8,128)(2,1)S(1)}, u32[]{:S(2)}, u32[]{:S(2)}) collective-permute-start(bf16[256,512]{1,0:T(8,128)(2,1)S(1)} %get-tuple-element.84), channel_id=1, source_target_pairs={{0,96},{32,0},{64,32},{96,64},{1,97},{33,1},{65,33},{97,65},{2,98}... | collective-permute-start | bytes 786440 | tf_op jit(solution)/shard_map/ppermute | solution.py:491
  199.7 7.5 %collective-permute-done.31.e3 = bf16[256,512]{1,0:T(8,128)(2,1)S(1)} collective-permute-done((bf16[256,512]{1,0:T(8,128)(2,1)S(1)}, bf16[256,512]{1,0:T(8,128)(2,1)S(1)}, u32[]{:S(2)}, u32[]{:S(2)}) %collective-permute-start.31) | collective-permute-done | bytes 262176 | tf_op jit(solution)/shard_map/ppermute | solution.py:491
  208.0 2.8 %collective-permute-done.29.e1 = bf16[256,512]{1,0:T(8,128)(2,1)S(1)} collective-permute-done((bf16[256,512]{1,0:T(8,128)(2,1)S(1)}, bf16[256,512]{1,0:T(8,128)(2,1)S(1)}, u32[]{:S(2)}, u32[]{:S(2)}) %collective-permute-start.29) | collective-permute-done | bytes 262176 | tf_op jit(solution)/shard_map/ppermute | solution.py:491
  221.9 3.0 %collective-permute-start.35 = (bf16[32,512]{1,0:T(8,128)(2,1)S(1)}, bf16[32,512]{1,0:T(8,128)(2,1)S(1)}, u32[]{:S(2)}, u32[]{:S(2)}) collective-permute-start(bf16[32,512]{1,0:T(8,128)(2,1)S(1)} %get-tuple-element.77), channel_id=1, source_target_pairs={{0,4},{4,16},{16,20},{20,0},{1,5},{5,17},{17,21},{21,1},{2,6},{6,1... | collective-permute-start | bytes 98312 | tf_op jit(solution)/shard_map/ppermute | solution.py:491
  (183 shorter events, 87.1 us)
Async XLA Ops:
  14.3 66.1 %all-to-all-start = ((bf16[8,64,1664]{2,1,0:T(8,128)(2,1)}), bf16[8,64,1664]{2,1,0:T(8,128)(2,1)S(1)}, u32[]{:S(2)}, u32[]{:S(2)}) async-start(bf16[8,64,1664]{2,1,0:T(8,128)(2,1)} %pad_maximum_fusion), calls=%async_computation | async-start | bytes 3407872 | tf_op jit(solution)/shard_map/all_to_all | solution.py:499
  22.0 24.9 %collective-permute-start.4 = (bf16[32,512]{1,0:T(8,128)(2,1)S(1)}, bf16[32,512]{1,0:T(8,128)(2,1)S(1)}, u32[]{:S(2)}, u32[]{:S(2)}) collective-permute-start(bf16[32,512]{1,0:T(8,128)(2,1)S(1)} %get-tuple-element.48), channel_id=1, source_target_pairs={{0,20},{4,0},{16,4},{20,16},{1,21},{5,1},{17,5},{21,17},{2,22},{6,... | collective-permute-start | bytes 98312 | tf_op jit(solution)/shard_map/ppermute | solution.py:491
  26.5 20.3 %collective-permute-start.3 = (bf16[32,512]{1,0:T(8,128)(2,1)S(1)}, bf16[32,512]{1,0:T(8,128)(2,1)S(1)}, u32[]{:S(2)}, u32[]{:S(2)}) collective-permute-start(bf16[32,512]{1,0:T(8,128)(2,1)S(1)} %get-tuple-element.48), channel_id=1, source_target_pairs={{0,16},{4,20},{16,0},{20,4},{1,17},{5,21},{17,1},{21,5},{2,18},{6,... | collective-permute-start | bytes 98312 | tf_op jit(solution)/shard_map/ppermute | solution.py:491
  26.6 20.3 %collective-permute-start.2 = (bf16[32,512]{1,0:T(8,128)(2,1)S(1)}, bf16[32,512]{1,0:T(8,128)(2,1)S(1)}, u32[]{:S(2)}, u32[]{:S(2)}) collective-permute-start(bf16[32,512]{1,0:T(8,128)(2,1)S(1)} %get-tuple-element.48), channel_id=1, source_target_pairs={{0,4},{4,16},{16,20},{20,0},{1,5},{5,17},{17,21},{21,1},{2,6},{6,1... | collective-permute-start | bytes 98312 | tf_op jit(solution)/shard_map/ppermute | solution.py:491
  46.9 8.6 %collective-permute-start.7 = (bf16[128,512]{1,0:T(8,128)(2,1)S(1)}, bf16[128,512]{1,0:T(8,128)(2,1)S(1)}, u32[]{:S(2)}, u32[]{:S(2)}) collective-permute-start(bf16[128,512]{1,0:T(8,128)(2,1)S(1)} %constant_dynamic-update-slice_fusion.refs_0_), channel_id=1, source_target_pairs={{0,3},{1,0},{2,1},{3,2},{4,7},{5,4},{6,5},{7,6},{8,11},{9,8},{10,9... | collective-permute-start | bytes 393224 | tf_op jit(solution)/shard_map/ppermute | solution.py:491
  49.6 7.9 %collective-permute-start.6 = (bf16[128,512]{1,0:T(8,128)(2,1)S(1)}, bf16[128,512]{1,0:T(8,128)(2,1)S(1)}, u32[]{:S(2)}, u32[]{:S(2)}) collective-permute-start(bf16[128,512]{1,0:T(8,128)(2,1)S(1)} %constant_dynamic-update-slice_fusion.refs_0_), channel_id=1, source_target_pairs={{0,2},{1,3},{2,0},{3,1},{4,6},{5,7},{6,4},{7,5},{8,10},{9,11},{10,... | collective-permute-start | bytes 393224 | tf_op jit(solution)/shard_map/ppermute | solution.py:491
  50.5 8.7 %collective-permute-start.5 = (bf16[128,512]{1,0:T(8,128)(2,1)S(1)}, bf16[128,512]{1,0:T(8,128)(2,1)S(1)}, u32[]{:S(2)}, u32[]{:S(2)}) collective-permute-start(bf16[128,512]{1,0:T(8,128)(2,1)S(1)} %constant_dynamic-update-slice_fusion.refs_0_), channel_id=1, source_target_pairs={{0,1},{1,2},{2,3},{3,0},{4,5},{5,6},{6,7},{7,4},{8,9},{9,10},{10,1... | collective-permute-start | bytes 393224 | tf_op jit(solution)/shard_map/ppermute | solution.py:491
  60.6 14.5 %collective-permute-start.10 = (bf16[256,512]{1,0:T(8,128)(2,1)S(1)}, bf16[256,512]{1,0:T(8,128)(2,1)S(1)}, u32[]{:S(2)}, u32[]{:S(2)}) collective-permute-start(bf16[256,512]{1,0:T(8,128)(2,1)S(1)} %get-tuple-element.49.refs_0_.refs_5_), channel_id=1, source_target_pairs={{0,96},{32,0},{64,32},{96,64},{1,97},{33,1},{65,33},{97,65},{2,98}... | collective-permute-start | bytes 786440 | tf_op jit(solution)/shard_map/ppermute | solution.py:491
  64.3 10.8 %collective-permute-start.9 = (bf16[256,512]{1,0:T(8,128)(2,1)S(1)}, bf16[256,512]{1,0:T(8,128)(2,1)S(1)}, u32[]{:S(2)}, u32[]{:S(2)}) collective-permute-start(bf16[256,512]{1,0:T(8,128)(2,1)S(1)} %get-tuple-element.49.refs_0_.refs_5_), channel_id=1, source_target_pairs={{0,64},{32,96},{64,0},{96,32},{1,65},{33,97},{65,1},{97,33},{2,66}... | collective-permute-start | bytes 786440 | tf_op jit(solution)/shard_map/ppermute | solution.py:491
  65.1 13.6 %collective-permute-start.8 = (bf16[256,512]{1,0:T(8,128)(2,1)S(1)}, bf16[256,512]{1,0:T(8,128)(2,1)S(1)}, u32[]{:S(2)}, u32[]{:S(2)}) collective-permute-start(bf16[256,512]{1,0:T(8,128)(2,1)S(1)} %get-tuple-element.49.refs_0_.refs_5_), channel_id=1, source_target_pairs={{0,32},{32,64},{64,96},{96,0},{1,33},{33,65},{65,97},{97,1},{2,34}... | collective-permute-start | bytes 786440 | tf_op jit(solution)/shard_map/ppermute | solution.py:491
  66.1 13.6 %collective-permute-start.11 = (bf16[256,512]{1,0:T(8,128)(2,1)S(1)}, bf16[256,512]{1,0:T(8,128)(2,1)}, u32[]{:S(2)}, u32[]{:S(2)}) collective-permute-start(bf16[256,512]{1,0:T(8,128)(2,1)S(1)} %get-tuple-element.49.refs_0_.refs_5_), channel_id=1, source_target_pairs={{0,8},{8,0},{1,9},{9,1},{2,10},{10,2},{3,11},{11,3},{4,12},{12,4},... | collective-permute-start | bytes 786440 | tf_op jit(solution)/shard_map/ppermute | solution.py:486
  92.2 31.5 %all-to-all-start.1 = ((f32[8,128,512]{2,1,0:T(8,128)}), f32[8,128,512]{2,1,0:T(8,128)}, u32[]{:S(2)}, u32[]{:S(2)}) async-start(f32[8,128,512]{2,1,0:T(8,128)} %copy-done.1), calls=%async_computation.1 | async-start | bytes 4194304 | tf_op jit(solution)/shard_map/all_to_all | solution.py:499
  96.6 7.8 %collective-permute-start.17 = (bf16[192,512]{1,0:T(8,128)(2,1)S(1)}, bf16[192,512]{1,0:T(8,128)(2,1)S(1)}, u32[]{:S(2)}, u32[]{:S(2)}) collective-permute-start(bf16[192,512]{1,0:T(8,128)(2,1)S(1)} %copy-done.14), channel_id=1, source_target_pairs={{0,96},{32,0},{64,32},{96,64},{1,97},{33,1},{65,33},{97,65},{2,98}... | collective-permute-start | bytes 589832 | tf_op jit(solution)/shard_map/ppermute | solution.py:491
  97.4 9.3 %collective-permute-start.16 = (bf16[192,512]{1,0:T(8,128)(2,1)S(1)}, bf16[192,512]{1,0:T(8,128)(2,1)S(1)}, u32[]{:S(2)}, u32[]{:S(2)}) collective-permute-start(bf16[192,512]{1,0:T(8,128)(2,1)S(1)} %copy-done.14), channel_id=1, source_target_pairs={{0,64},{32,96},{64,0},{96,32},{1,65},{33,97},{65,1},{97,33},{2,66}... | collective-permute-start | bytes 589832 | tf_op jit(solution)/shard_map/ppermute | solution.py:491
  98.4 11.5 %collective-permute-start.15 = (bf16[192,512]{1,0:T(8,128)(2,1)S(1)}, bf16[192,512]{1,0:T(8,128)(2,1)S(1)}, u32[]{:S(2)}, u32[]{:S(2)}) collective-permute-start(bf16[192,512]{1,0:T(8,128)(2,1)S(1)} %copy-done.14), channel_id=1, source_target_pairs={{0,32},{32,64},{64,96},{96,0},{1,33},{33,65},{65,97},{97,1},{2,34}... | collective-permute-start | bytes 589832 | tf_op jit(solution)/shard_map/ppermute | solution.py:491
  99.2 10.9 %collective-permute-start.18 = (bf16[192,512]{1,0:T(8,128)(2,1)S(1)}, bf16[192,512]{1,0:T(8,128)(2,1)S(1)}, u32[]{:S(2)}, u32[]{:S(2)}) collective-permute-start(bf16[192,512]{1,0:T(8,128)(2,1)S(1)} %copy-done.14), channel_id=1, source_target_pairs={{0,8},{8,0},{1,9},{9,1},{2,10},{10,2},{3,11},{11,3},{4,12},{12,4},... | collective-permute-start | bytes 589832 | tf_op jit(solution)/shard_map/ppermute | solution.py:486
  135.6 22.0 %all-to-all-start.2 = ((bf16[8,576,128]{2,1,0:T(8,128)(2,1)}), bf16[8,576,128]{2,1,0:T(8,128)(2,1)S(1)}, u32[]{:S(2)}, u32[]{:S(2)}) async-start(bf16[8,576,128]{2,1,0:T(8,128)(2,1)} %get-tuple-element.52), calls=%async_computation.2 | async-start | bytes 2359296 | tf_op jit(solution)/shard_map/all_to_all | solution.py:499
  142.0 9.3 %collective-permute-start.24 = (bf16[192,512]{1,0:T(8,128)(2,1)S(1)}, bf16[192,512]{1,0:T(8,128)(2,1)S(1)}, u32[]{:S(2)}, u32[]{:S(2)}) collective-permute-start(bf16[192,512]{1,0:T(8,128)(2,1)S(1)} %get-tuple-element.89), channel_id=1, source_target_pairs={{0,64},{32,96},{64,0},{96,32},{1,65},{33,97},{65,1},{97,33},{2,66}... | collective-permute-start | bytes 589832 | tf_op jit(solution)/shard_map/ppermute | solution.py:491
  142.9 11.5 %collective-permute-start.23 = (bf16[192,512]{1,0:T(8,128)(2,1)S(1)}, bf16[192,512]{1,0:T(8,128)(2,1)S(1)}, u32[]{:S(2)}, u32[]{:S(2)}) collective-permute-start(bf16[192,512]{1,0:T(8,128)(2,1)S(1)} %get-tuple-element.90), channel_id=1, source_target_pairs={{0,32},{32,64},{64,96},{96,0},{1,33},{33,65},{65,97},{97,1},{2,34}... | collective-permute-start | bytes 589832 | tf_op jit(solution)/shard_map/ppermute | solution.py:491
  176.3 12.4 %collective-permute-start.28 = (bf16[4,256,512]{2,1,0:T(8,128)(2,1)}, bf16[4,256,512]{2,1,0:T(8,128)(2,1)}, u32[]{:S(2)}, u32[]{:S(2)}) collective-permute-start(bf16[4,256,512]{2,1,0:T(8,128)(2,1)} %get-tuple-element.67), channel_id=1, source_target_pairs={{0,8},{8,0},{1,9},{9,1},{2,10},{10,2},{3,11},{11,3},{4,12},{12,4},... | collective-permute-start | bytes 3145736 | tf_op jit(solution)/shard_map/ppermute | solution.py:486
  183.9 42.3 %all-to-all-start.3 = ((bf16[8,64,1024]{2,1,0:T(8,128)(2,1)}), bf16[8,64,1024]{2,1,0:T(8,128)(2,1)S(1)}, u32[]{:S(2)}, u32[]{:S(2)}) async-start(bf16[8,64,1024]{2,1,0:T(8,128)(2,1)} %shard_map.202), calls=%async_computation.3 | async-start | bytes 2097152 | tf_op jit(solution)/shard_map/all_to_all | solution.py:499
  190.3 16.9 %collective-permute-start.31 = (bf16[256,512]{1,0:T(8,128)(2,1)S(1)}, bf16[256,512]{1,0:T(8,128)(2,1)S(1)}, u32[]{:S(2)}, u32[]{:S(2)}) collective-permute-start(bf16[256,512]{1,0:T(8,128)(2,1)S(1)} %get-tuple-element.84), channel_id=1, source_target_pairs={{0,96},{32,0},{64,32},{96,64},{1,97},{33,1},{65,33},{97,65},{2,98}... | collective-permute-start | bytes 786440 | tf_op jit(solution)/shard_map/ppermute | solution.py:491
  197.8 10.2 %collective-permute-start.30 = (bf16[256,512]{1,0:T(8,128)(2,1)S(1)}, bf16[256,512]{1,0:T(8,128)(2,1)S(1)}, u32[]{:S(2)}, u32[]{:S(2)}) collective-permute-start(bf16[256,512]{1,0:T(8,128)(2,1)S(1)} %get-tuple-element.85), channel_id=1, source_target_pairs={{0,64},{32,96},{64,0},{96,32},{1,65},{33,97},{65,1},{97,33},{2,66}... | collective-permute-start | bytes 786440 | tf_op jit(solution)/shard_map/ppermute | solution.py:491
  199.6 11.2 %collective-permute-start.29 = (bf16[256,512]{1,0:T(8,128)(2,1)S(1)}, bf16[256,512]{1,0:T(8,128)(2,1)S(1)}, u32[]{:S(2)}, u32[]{:S(2)}) collective-permute-start(bf16[256,512]{1,0:T(8,128)(2,1)S(1)} %get-tuple-element.86), channel_id=1, source_target_pairs={{0,32},{32,64},{64,96},{96,0},{1,33},{33,65},{65,97},{97,1},{2,34}... | collective-permute-start | bytes 786440 | tf_op jit(solution)/shard_map/ppermute | solution.py:491
  (66 other events, 569.5 us)

commit v5 on v4

--- a/solution.py
+++ b/solution.py
@@ -123,11 +123,15 @@
                     at += count
 
 
-def prepare(halo, turned, w_edge_in, w_edge_out, w_node_in, w_node_out, up, down, packed):
+def prepare(halo, turned, *refs):
+    weights, (up, down, packed), held, sems = refs[:4], refs[4:7], refs[7:-1], refs[-1]
+    pairs = list(zip(weights, held))
     for j in range(HB):
-        up[:, pl.ds(j * BLK, BLK)] = turned[:, block_at(halo[j])]
-        down[:, pl.ds(j * BLK, BLK)] = turned[:, block_at(halo[HB + j])]
-    parts = [ref[...].astype(F32) for ref in (w_edge_in, w_edge_out, w_node_in, w_node_out)]
+        part = pl.ds(j * BLK, BLK)
+        pairs.append((turned.at[:, block_at(halo[j])], up.at[:, part]))
+        pairs.append((turned.at[:, block_at(halo[HB + j])], down.at[:, part]))
+    wait_all(copies(pairs, sems))
+    parts = [ref[...].astype(F32) for ref in held]
     used = sum(part.shape[0] for part in parts)
     parts.append(jnp.zeros((packed.shape[0] - used, L), F32))
     packed[...] = jnp.concatenate(parts, axis=0).astype(BF)
@@ -259,8 +263,8 @@
 
 def node_step(scal, spread, ext_hbm, *refs):
     shards, refs = refs[:8], refs[8:]
-    gain, out, d_direct, keep, send = refs[:5]
-    own_turned, up_turned, w_in, w_out, joined, first, g_in, g_out, sems = refs[5:]
+    gain, out, direct_out, keep, send = refs[:5]
+    own_turned, up_turned, w_in, w_out, joined, first, g_in, g_out, d_direct, sems, out_sems = refs[5:]
     lat_index, core, y_index = scal[0], scal[1], scal[2]
     slabs = w_in.shape[0] // 2 // 32
     counts = (2 * L // slabs, L // slabs)
@@ -284,6 +288,7 @@
     d_first = dot_transpose(d_second, w_out[...])
     d_first = jnp.where(first[...].astype(F32) > 0, d_first, 0.0).astype(BF)
     d_direct[...] = dot_transpose(w_in[pl.ds(0, L), :], d_first)
+    store = copies([(d_direct, direct_out)], out_sems)
     d_agg = dot_transpose(w_in[pl.ds(L, L), :], d_first).astype(BF)
     width = L // out.shape[0]
     for l in range(out.shape[0]):
@@ -292,21 +297,21 @@
     g_out[...] = dot_rows(first[...], d_second)
     g_in[...] = dot_rows(joined[...], d_first)
     pack_grads(core, y_index, (g_in, g_out), keep, send, counts)
+    wait_all(store)
 
 
 def edge_backward(scal, d_agg, cot, offsets, gain, *refs):
-    saved, shards, refs = refs[:5], refs[5:13], refs[13:]
-    grad_edges, middle_out, lower, upper, keep, send = refs[:6]
-    joined, first, normed, inverse, d_direct, w_in, w_out = refs[6:13]
-    d_second, d_first, d_ext, d_turned, g_in, g_out, sems = refs[13:]
+    saved, w_out_shards, refs = refs[:4], refs[4:12], refs[12:]
+    d_first, keep, send = refs[:3]
+    joined, first, normed, inverse, w_in, w_out, d_second, g_in, g_out, sems = refs[3:]
     tiles = cot.shape[0] // BLK
     lat_index, core, y_index, count = (scal[2 * tiles + i] for i in range(4))
     slabs = w_in.shape[0] // 3 // 32
     counts = (3 * L // slabs, L // slabs)
-    normed_in, inverse_in, first_in, joined_in, direct_in = saved
+    normed_in, inverse_in, first_in, joined_in = saved
     pairs = [(normed_in, normed), (inverse_in, inverse)]
-    pairs += weight_pairs(core, y_index, shards, (w_in, w_out), counts)
-    pairs += [(first_in, first), (joined_in, joined), (direct_in, d_direct)]
+    pairs += weight_pairs(core, y_index, w_out_shards, (w_in, w_out), counts)[1::2]
+    pairs += [(first_in, first), (joined_in, joined)]
     loads = copies(pairs, sems)
     wait_all(loads[:2])
     for t in range(tiles):
@@ -322,11 +327,37 @@
         part = pl.ds(n * 256, 256)
         back = dot_transpose(d_second[...], w_out[part, :])
         d_first[:, part] = jnp.where(first[:, part].astype(F32) > 0, back, 0.0).astype(BF)
+    for n in range(2):
+        part = pl.ds(n * 256, 256)
+        g_out[part, :] = dot_rows(first[:, part], d_second[...])
+    for n in range(6):
+        part = pl.ds(n * 256, 256)
+        g_in[part, :] = dot_rows(joined[:, part], d_first[...])
+    pack_grads(core, y_index, (g_in, g_out), keep, send, counts)
+
+
+def edge_inputs(scal, d_first, cot, offsets, direct_in, *refs):
+    shards, refs = refs[:8], refs[8:]
+    grad_out, middle_out, lower, upper = refs[:4]
+    grad_edges, d_direct, w_in, w_out, d_ext, d_turned, sems, out_sems = refs[4:]
+    tiles = cot.shape[0] // BLK
+    lat_index, core, y_index = (scal[2 * tiles + i] for i in range(3))
+    slabs = w_in.shape[0] // 3 // 32
+    counts = (3 * L // slabs, L // slabs)
+    pairs = weight_pairs(core, y_index, shards, (w_in, w_out), counts)[::2]
+    pairs += [(direct_in, d_direct)]
+    loads = copies(pairs, sems)
+    d_ext[...] = jnp.zeros_like(d_ext)
+    wait_all(loads)
     for n in range(4):
         d_turned[pl.ds(n * 256, 256), :] = dot_transpose(
             w_in[pl.ds(L + n * 256, 256), :], d_first[...]
         )
-    d_ext[...] = jnp.zeros_like(d_ext)
+    for n in range(2):
+        part = pl.ds(n * 256, 256)
+        back = dot_transpose(d_first[...], w_in[part, :])
+        grad_edges[:, part] = (cot[:, part].astype(F32) + back).astype(BF)
+    store = copies([(grad_edges, grad_out)], out_sems)
     for t in range(tiles):
         rows = pl.ds(t * BLK, BLK)
         for row, place, at in ((1, scal[tiles + t], 0), (0, scal[t] + HB, L)):
@@ -341,17 +372,7 @@
         lower[:, pl.ds(j * BLK, BLK)] = d_ext[j].astype(BF)
         upper[:, pl.ds(j * BLK, BLK)] = d_ext[HB + blocks + j].astype(BF)
     middle_out[...] = d_ext[pl.ds(HB, blocks)]
-    for n in range(2):
-        part = pl.ds(n * 256, 256)
-        back = dot_transpose(d_first[...], w_in[part, :])
-        grad_edges[:, part] = (cot[:, part].astype(F32) + back).astype(BF)
-    for n in range(2):
-        part = pl.ds(n * 256, 256)
-        g_out[part, :] = dot_rows(first[:, part], d_second[...])
-    for n in range(6):
-        part = pl.ds(n * 256, 256)
-        g_in[part, :] = dot_rows(joined[:, part], d_first[...])
-    pack_grads(core, y_index, (g_in, g_out), keep, send, counts)
+    wait_all(store)
 
 
 def add_halo(halo, middle, above, below, columns, held):
@@ -379,9 +400,17 @@
     moved += sum(x.size * x.dtype.itemsize for x in out_shape)
     named = {"s": pltpu.SMEM, "v": pltpu.VMEM, "h": pltpu.HBM}
     out_spaces = out_spaces or "v" * len(out_shape)
+    operands = [
+        pltpu.with_memory_space_constraint(x, pltpu.HBM) if space == "h" else x
+        for x, space in zip(operands, spaces)
+    ]
+    placed = [
+        pltpu.HBM(x.shape, x.dtype) if space == "h" else x
+        for x, space in zip(out_shape, out_spaces)
+    ]
     return pl.pallas_call(
         kernel,
-        out_shape=out_shape,
+        out_shape=placed,
         in_specs=[pl.BlockSpec(memory_space=named[space]) for space in spaces],
         out_specs=[pl.BlockSpec(memory_space=named[space]) for space in out_spaces],
         scratch_shapes=[pltpu.VMEM(shape, dtype) for shape, dtype in scratch]
@@ -435,50 +464,67 @@
             ((BLK, L), BF),
             ((2 * L, L), F32),
             ((L, L), F32),
+            ((L, BLK), F32),
         ],
         NODE_MIB,
         "svh" + "h" * len(shards) + "v",
         (scal, spread, ext, *shards, gain),
         flops=2 * BLK * 9 * L * L,
-        sems=(2 + 4 * len(shards),),
+        out_spaces="vhvv",
+        sems=(2 + 4 * len(shards), 1),
     )
 
 
 def run_edge_backward(scal, d_agg, cot, offsets, gain, saved, shards):
     rows = cot.shape[0]
-    lat_size = d_agg.shape[0]
     chunk = (len(shards) // 2,) + shards[0].shape
-    normed, inverse, first, joined, d_direct = saved
+    normed, inverse, first, joined = saved
     return call(
         edge_backward,
-        [
-            shape_of((rows, L), BF),
-            shape_of((lat_size, L, BLK), F32),
-            shape_of((L, HB * BLK), BF),
-            shape_of((L, HB * BLK), BF),
-            shape_of(chunk, BF),
-            shape_of(chunk, BF),
-        ],
+        [shape_of((rows, L), BF), shape_of(chunk, BF), shape_of(chunk, BF)],
         [
             (joined.shape, BF),
             (first.shape, BF),
             (normed.shape, F32),
             (inverse.shape, F32),
-            (d_direct.shape, F32),
             ((3 * L, L), BF),
             ((L, L), BF),
             ((rows, L), BF),
-            ((rows, L), BF),
-            ((lat_size + 2 * HB, L, BLK), F32),
-            ((2 * L, rows), F32),
             ((3 * L, L), F32),
             ((L, L), F32),
         ],
         BACK_MIB,
         "svvvv" + "h" * (len(saved) + len(shards)),
         (scal, d_agg, cot, offsets, gain, *saved, *shards),
-        flops=2 * rows * 8 * L * L,
-        sems=(5 + 4 * len(shards),),
+        flops=2 * rows * 5 * L * L,
+        sems=(4 + 2 * len(shards),),
+    )
+
+
+def run_edge_inputs(scal, d_first, cot, offsets, d_direct, shards, lat_size):
+    rows = cot.shape[0]
+    return call(
+        edge_inputs,
+        [
+            shape_of((rows, L), BF),
+            shape_of((lat_size, L, BLK), F32),
+            shape_of((L, HB * BLK), BF),
+            shape_of((L, HB * BLK), BF),
+        ],
+        [
+            ((rows, L), BF),
+            (d_direct.shape, F32),
+            ((3 * L, L), BF),
+            ((L, L), BF),
+            ((lat_size + 2 * HB, L, BLK), F32),
+            ((2 * L, rows), F32),
+        ],
+        EDGE_MIB,
+        "svvvh" + "h" * len(shards),
+        (scal, d_first, cot, offsets, d_direct, *shards),
+        flops=2 * rows * 3 * L * L,
+        out_spaces="hvvv",
+        sems=(1 + 2 * len(shards), 1),
     )
 
 
@@ -553,10 +599,11 @@
             shape_of((width, halo_rows), BF),
             shape_of((32, L), BF),
         ],
-        [],
+        [(weight.shape, BF) for weight in weights],
         4,
-        "svvvvv",
+        "shhhhh",
         (halo, turned, *weights),
+        sems=(4 + 2 * HB,),
     )
     from_lower = from_behind(up, 1)
     from_upper = from_behind(down, -1)
@@ -576,6 +623,9 @@
     message_out = jnp.concatenate(
         [jnp.broadcast_to(table, (lat_size,) + table.shape), cot], axis=2
     )
+    message_out, edge_part, node_part = lax.optimization_barrier(
+        (message_out, edge_part, node_part)
+    )
     edge_shards = gather_far(edge_part)
     ext = spread_rows(message_out, LAT).reshape(L, ext_rows + own_rows)
 
@@ -592,9 +642,12 @@
     node_far = reduce_far(node_keep, node_send)
     second_in, *node_far = lax.optimization_barrier((second_in, *node_far))
 
-    grad_edges, middle, lower, upper, edge_keep, edge_send = run_edge_backward(
+    d_first, edge_keep, edge_send = run_edge_backward(
         scal, second_in, edge_cotangent, offsets, edge_gain_row,
-        (normed, inverse, first, joined, d_direct), edge_shards,
+        (normed, inverse, first, joined), edge_shards,
+    )
+    grad_edges, middle, lower, upper = run_edge_inputs(
+        scal, d_first, edge_cotangent, offsets, d_direct, edge_shards, lat_size
     )
     from_above = from_behind(lower, -1)
     from_below = from_behind(upper, 1)

time: 233 us -> 191 us (0.82)
  local copies, waits for them, and re-layouts: 30.8 us -> 5.3 us
  waiting for transfers between devices: 95.3 us -> 75 us
    unnamed x99 -> x61, local copies, waits for them, and re-layouts: 29 us -> 3.5 us
    ppermute x24, waiting for transfers between devices: 76.6 us -> 53.8 us  [shift(): lax.ppermute(value, axes, [(i, (i + step) % count) for i in range(count)])]
    all_to_all x4, waiting for transfers between devices: 13.3 us -> 19.3 us  [spread_rows(): return lax.all_to_all(value, axes, 0, 0)]
    ppermute x24, starting transfers between devices: 40.1 us -> 43.8 us  [shift(): lax.ppermute(value, axes, [(i, (i + step) % count) for i in range(count)])]
    ppermute x4, waiting for transfers between devices: 4.71 us -> 1.13 us  [from_behind(): lax.ppermute(value, SLAB, [(source, source + steps) for source in range(f...]
    pallas_call x10 -> x11, Pallas kernels: 28.9 us -> 30.5 us  [call(): pl.pallas_call(kernel, out_shape=placed, in_specs=[pl.BlockSpec(memory_sp...]
  transfers between devices with their start and end apart: 42 -> 42, of which waited for: 26 -> 26; matrix products, arithmetic and copies ran while one was open for 2% -> 4% of each run, Pallas kernels for 2% -> 5%
where the time goes in v5:
time: 191 us; the launch traced here: 190 us
  waiting for transfers between devices  75 us (39%)
  starting transfers between devices  71 us (37%)
  Pallas kernels  30.5 us (16%)
  other arithmetic  6.13 us (3%)
  local copies, waits for them, and re-layouts  5.3 us (3%)
    ppermute x24, waiting for transfers between devices, shift(): lax.ppermute(value, axes, [(i, (i + step) % count) for i in range(count)])  53.8 us
    ppermute x24, starting transfers between devices, shift(): lax.ppermute(value, axes, [(i, (i + step) % count) for i in range(count)])  43.8 us
    pallas_call x11, Pallas kernels, call(): pl.pallas_call(kernel, out_shape=placed, in_specs=[pl.BlockSpec(memory_sp...  30.5 us
    all_to_all x4, starting transfers between devices, spread_rows(): return lax.all_to_all(value, axes, 0, 0)  19.4 us
    all_to_all x4, waiting for transfers between devices, spread_rows(): return lax.all_to_all(value, axes, 0, 0)  19.3 us
    ppermute x4, starting transfers between devices, from_behind(): lax.ppermute(value, SLAB, [(source, source + steps) for source in range(f...  6.91 us
  transfers between devices with their start and end apart: 42, of which 26 were waited for; matrix products, arithmetic and copies ran while one was open for 4% of the time, Pallas kernels for 5%

profile of v5, /device:TPU:0, one launch (start us, length us, event | category | flops | bytes accessed | tf_op | source)
XLA Modules:
  0.0 189.8 jit_solution(9812991010313176270)
XLA Ops:
  2.9 2.9 %collective-permute-start.4 = (bf16[32,512]{1,0:T(8,128)(2,1)S(1)}, bf16[32,512]{1,0:T(8,128)(2,1)S(1)}, u32[]{:S(2)}, u32[]{:S(2)}) collective-permute-start(bf16[32,512]{1,0:T(8,128)(2,1)S(1)} %get-tuple-element.52), channel_id=1, source_target_pairs={{0,20},{4,0},{16,4},{20,16},{1,21},{5,1},{17,5},{21,17},{2,22},{6,... | collective-permute-start | bytes 98312 | tf_op jit(solution)/shard_map/ppermute | solution.py:537
  6.1 2.6 %collective-permute-start.2 = (bf16[32,512]{1,0:T(8,128)(2,1)S(1)}, bf16[32,512]{1,0:T(8,128)(2,1)S(1)}, u32[]{:S(2)}, u32[]{:S(2)}) collective-permute-start(bf16[32,512]{1,0:T(8,128)(2,1)S(1)} %get-tuple-element.52), channel_id=1, source_target_pairs={{0,4},{4,16},{16,20},{20,0},{1,5},{5,17},{17,21},{21,1},{2,6},{6,1... | collective-permute-start | bytes 98312 | tf_op jit(solution)/shard_map/ppermute | solution.py:537
  11.5 4.1 %collective-permute-start.7 = (bf16[128,512]{1,0:T(8,128)(2,1)S(1)}, bf16[128,512]{1,0:T(8,128)(2,1)S(1)}, u32[]{:S(2)}, u32[]{:S(2)}) collective-permute-start(bf16[128,512]{1,0:T(8,128)(2,1)S(1)} %constant_dynamic-update-slice_fusion.refs_0_), channel_id=1, source_target_pairs={{0,3},{1,0},{2,1},{3,2},{4,7},{5,4},{6,5},{7,6},{8,11},{9,8},{10,9... | collective-permute-start | bytes 393224 | tf_op jit(solution)/shard_map/ppermute | solution.py:537
  19.3 2.9 %collective-permute-done.7.refs_3_ = bf16[128,512]{1,0:T(8,128)(2,1)S(1)} collective-permute-done((bf16[128,512]{1,0:T(8,128)(2,1)S(1)}, bf16[128,512]{1,0:T(8,128)(2,1)S(1)}, u32[]{:S(2)}, u32[]{:S(2)}) %collective-permute-start.7) | collective-permute-done | bytes 131104 | tf_op jit(solution)/shard_map/ppermute | solution.py:537
  26.6 4.5 %all-to-all-start = ((bf16[8,64,1664]{2,1,0:T(8,128)(2,1)}), bf16[8,64,1664]{2,1,0:T(8,128)(2,1)}, u32[]{:S(2)}, u32[]{:S(2)}) async-start(bf16[8,64,1664]{2,1,0:T(8,128)(2,1)} %pad_maximum_fusion), calls=%async_computation | async-start | bytes 3407872 | tf_op jit(solution)/shard_map/all_to_all | solution.py:545
  31.1 4.3 %collective-permute-start.10 = (bf16[256,512]{1,0:T(8,128)(2,1)S(1)}, bf16[256,512]{1,0:T(8,128)(2,1)S(1)}, u32[]{:S(2)}, u32[]{:S(2)}) collective-permute-start(bf16[256,512]{1,0:T(8,128)(2,1)S(1)} %get-tuple-element.56.refs_0_.refs_4_), channel_id=1, source_target_pairs={{0,96},{32,0},{64,32},{96,64},{1,97},{33,1},{65,33},{97,65},{2,98}... | collective-permute-start | bytes 786440 | tf_op jit(solution)/shard_map/ppermute | solution.py:537
  37.0 7.9 %collective-permute-done.10.refs_3_.refs_7_ = bf16[256,512]{1,0:T(8,128)(2,1)S(1)} collective-permute-done((bf16[256,512]{1,0:T(8,128)(2,1)S(1)}, bf16[256,512]{1,0:T(8,128)(2,1)S(1)}, u32[]{:S(2)}, u32[]{:S(2)}) %collective-permute-start.10) | collective-permute-done | bytes 262176 | tf_op jit(solution)/shard_map/ppermute | solution.py:537
  48.4 5.3 %all-to-all-done = bf16[8,64,1664]{2,1,0:T(8,128)(2,1)} async-done(((bf16[8,64,1664]{2,1,0:T(8,128)(2,1)}), bf16[8,64,1664]{2,1,0:T(8,128)(2,1)}, u32[]{:S(2)}, u32[]{:S(2)}) %all-to-all-start) | async-done | bytes 1703968 | tf_op jit(solution)/shard_map/all_to_all | solution.py:545
  53.8 6.9 %shard_map.199 = (bf16[512,1536]{1,0:T(8,128)(2,1)}, bf16[512,512]{1,0:T(8,128)(2,1)}, f32[512,512]{1,0:T(8,128)}, f32[512,128]{1,0:T(8,128)}, bf16[512,512]{1,0:T(8,128)(2,1)}, /*index=5*/f32[8,128,512]{2,1,0:T(8,128)}) custom-call(s32[12]{0:T(128)S(1)} %concatenate.13.scal, bf16[512,1664]{1,0:T(8,128)(2,1)} %bitcast.8.ext_hbm, ...), custom_call_target="tpu_custom_call" | custom-call | flops 1073741824 | bytes 10360880 | tf_op jit(solution)/shard_map/pallas_call | solution.py:411
  60.7 4.7 %all-to-all-start.1 = ((f32[8,128,512]{2,1,0:T(8,128)}), f32[8,128,512]{2,1,0:T(8,128)S(1)}, u32[]{:S(2)}, u32[]{:S(2)}) async-start(f32[8,128,512]{2,1,0:T(8,128)} %get-tuple-element.57), calls=%async_computation.1 | async-start | bytes 4194304 | tf_op jit(solution)/shard_map/all_to_all | solution.py:545
  67.8 5.5 %collective-permute-done.17.refs_3_ = bf16[192,512]{1,0:T(8,128)(2,1)S(1)} collective-permute-done((bf16[192,512]{1,0:T(8,128)(2,1)S(1)}, bf16[192,512]{1,0:T(8,128)(2,1)S(1)}, u32[]{:S(2)}, u32[]{:S(2)}) %collective-permute-start.17) | collective-permute-done | bytes 196640 | tf_op jit(solution)/shard_map/ppermute | solution.py:537
  79.5 12.6 %all-to-all-done.1.spread = f32[8,128,512]{2,1,0:T(8,128)S(1)} async-done(((f32[8,128,512]{2,1,0:T(8,128)}), f32[8,128,512]{2,1,0:T(8,128)S(1)}, u32[]{:S(2)}, u32[]{:S(2)}) %all-to-all-start.1) | async-done | bytes 2097184 | tf_op jit(solution)/shard_map/all_to_all | solution.py:545
  92.1 6.0 %shard_map.200 = (bf16[8,576,128]{2,1,0:T(8,128)(2,1)}, f32[512,128]{1,0:T(8,128)}, bf16[4,192,512]{2,1,0:T(8,128)(2,1)S(1)}, bf16[4,192,512]{2,1,0:T(8,128)(2,1)}) custom-call(s32[3]{0:T(128)S(1)} %pad_add_fusion.scal, f32[8,128,512]{2,1,0:T(8,128)S(1)} %all-to-all-done.1.spread, bf16[512,1664]{1,0:T(8,128)(2,1)} %bitcast.8.ext_hbm, ...), custom_call_target="tpu_custom_call" | custom-call | flops 603979776 | bytes 8390668 | tf_op jit(solution)/shard_map/pallas_call | solution.py:411
  98.4 4.8 %all-to-all-start.2 = ((bf16[8,576,128]{2,1,0:T(8,128)(2,1)}), bf16[8,576,128]{2,1,0:T(8,128)(2,1)S(1)}, u32[]{:S(2)}, u32[]{:S(2)}) async-start(bf16[8,576,128]{2,1,0:T(8,128)(2,1)} %get-tuple-element.59), calls=%async_computation.2 | async-start | bytes 2359296 | tf_op jit(solution)/shard_map/all_to_all | solution.py:545
  107.4 5.7 %collective-permute-done.25.n3 = bf16[192,512]{1,0:T(8,128)(2,1)S(1)} collective-permute-done((bf16[192,512]{1,0:T(8,128)(2,1)S(1)}, bf16[192,512]{1,0:T(8,128)(2,1)S(1)}, u32[]{:S(2)}, u32[]{:S(2)}) %collective-permute-start.25) | collective-permute-done | bytes 196640 | tf_op jit(solution)/shard_map/ppermute | solution.py:537
  120.4 5.6 %shard_map.201 = (bf16[512,512]{1,0:T(8,128)(2,1)S(1)}, bf16[4,256,512]{2,1,0:T(8,128)(2,1)S(1)}, bf16[4,256,512]{2,1,0:T(8,128)(2,1)}) custom-call(s32[12]{0:T(128)S(1)} %concatenate.13.scal, bf16[8,576,128]{2,1,0:T(8,128)(2,1)S(1)} %all-to-all-done.2.d_agg, bf16[512,512]{1,0:T(8,128)(2,1)S(1)} %copy-done.2, s32[2,4,128]{2,1,0:T(4,128)S(1)} %reshape.76.offsets, ...), custom_call_target="tpu_custom_call" | custom-call | flops 1342177280 | bytes 9836592 | tf_op jit(solution)/shard_map/pallas_call | solution.py:411
  126.1 4.8 %shard_map.202 = (bf16[512,512]{1,0:T(8,128)(2,1)}, f32[8,512,128]{2,1,0:T(8,128)S(1)}, bf16[512,256]{1,0:T(8,128)(2,1)S(1)}, bf16[512,256]{1,0:T(8,128)(2,1)S(1)}) custom-call(s32[12]{0:T(128)S(1)} %concatenate.13.scal, bf16[512,512]{1,0:T(8,128)(2,1)S(1)} %get-tuple-element.68.d_first, bf16[512,512]{1,0:T(8,128)(2,1)S(1)} %copy-done.2, ...), custom_call_target="tpu_custom_call" | custom-call | flops 805306368 | bytes 6557744 | tf_op jit(solution)/shard_map/pallas_call | solution.py:411
  132.1 3.0 %collective-permute-start.27 = (bf16[512,256]{1,0:T(8,128)(2,1)S(1)}, bf16[512,256]{1,0:T(8,128)(2,1)S(1)}, u32[]{:S(2)}, u32[]{:S(2)}) collective-permute-start(bf16[512,256]{1,0:T(8,128)(2,1)S(1)} %get-tuple-element.72), channel_id=1, source_target_pairs={{0,8},{8,16},{16,24},{24,32},{32,40},{40,48},{48,56},{56,64},{64,7... | collective-permute-start | bytes 786440 | tf_op jit(solution)/shard_map/ppermute | solution.py:32
  138.4 5.5 %all-to-all-start.3 = ((bf16[8,64,1024]{2,1,0:T(8,128)(2,1)}), bf16[8,64,1024]{2,1,0:T(8,128)(2,1)S(1)}, u32[]{:S(2)}, u32[]{:S(2)}) async-start(bf16[8,64,1024]{2,1,0:T(8,128)(2,1)} %shard_map.203), calls=%async_computation.3 | async-start | bytes 2097152 | tf_op jit(solution)/shard_map/all_to_all | solution.py:545
  145.4 10.8 %collective-permute-start.31 = (bf16[256,512]{1,0:T(8,128)(2,1)S(1)}, bf16[256,512]{1,0:T(8,128)(2,1)S(1)}, u32[]{:S(2)}, u32[]{:S(2)}) collective-permute-start(bf16[256,512]{1,0:T(8,128)(2,1)S(1)} %get-tuple-element.92), channel_id=1, source_target_pairs={{0,96},{32,0},{64,32},{96,64},{1,97},{33,1},{65,33},{97,65},{2,98}... | collective-permute-start | bytes 786440 | tf_op jit(solution)/shard_map/ppermute | solution.py:537
  158.2 7.3 %collective-permute-done.31.e3 = bf16[256,512]{1,0:T(8,128)(2,1)S(1)} collective-permute-done((bf16[256,512]{1,0:T(8,128)(2,1)S(1)}, bf16[256,512]{1,0:T(8,128)(2,1)S(1)}, u32[]{:S(2)}, u32[]{:S(2)}) %collective-permute-start.31) | collective-permute-done | bytes 262176 | tf_op jit(solution)/shard_map/ppermute | solution.py:537
  166.5 2.8 %collective-permute-done.29.e1 = bf16[256,512]{1,0:T(8,128)(2,1)S(1)} collective-permute-done((bf16[256,512]{1,0:T(8,128)(2,1)S(1)}, bf16[256,512]{1,0:T(8,128)(2,1)S(1)}, u32[]{:S(2)}, u32[]{:S(2)}) %collective-permute-start.29) | collective-permute-done | bytes 262176 | tf_op jit(solution)/shard_map/ppermute | solution.py:537
  172.1 2.7 %collective-permute-start.33 = (bf16[4,32,512]{2,1,0:T(8,128)(2,1)S(1)}, bf16[4,32,512]{2,1,0:T(8,128)(2,1)S(1)}, u32[]{:S(2)}, u32[]{:S(2)}) collective-permute-start(bf16[4,32,512]{2,1,0:T(8,128)(2,1)S(1)} %get-tuple-element.82), channel_id=1, source_target_pairs={{0,2},{1,3},{2,0},{3,1},{4,6},{5,7},{6,4},{7,5},{8,10},{9,11},{10,... | collective-permute-start | bytes 393224 | tf_op jit(solution)/shard_map/ppermute | solution.py:537
  180.7 3.0 %collective-permute-start.35 = (bf16[32,512]{1,0:T(8,128)(2,1)S(1)}, bf16[32,512]{1,0:T(8,128)(2,1)S(1)}, u32[]{:S(2)}, u32[]{:S(2)}) collective-permute-start(bf16[32,512]{1,0:T(8,128)(2,1)S(1)} %get-tuple-element.85), channel_id=1, source_target_pairs={{0,4},{4,16},{16,20},{20,0},{1,5},{5,17},{17,21},{21,1},{2,6},{6,1... | collective-permute-start | bytes 98312 | tf_op jit(solution)/shard_map/ppermute | solution.py:537
  (146 shorter events, 61.9 us)
Async XLA Ops:
  2.9 8.6 %collective-permute-start.4 = (bf16[32,512]{1,0:T(8,128)(2,1)S(1)}, bf16[32,512]{1,0:T(8,128)(2,1)S(1)}, u32[]{:S(2)}, u32[]{:S(2)}) collective-permute-start(bf16[32,512]{1,0:T(8,128)(2,1)S(1)} %get-tuple-element.52), channel_id=1, source_target_pairs={{0,20},{4,0},{16,4},{20,16},{1,21},{5,1},{17,5},{21,17},{2,22},{6,... | collective-permute-start | bytes 98312 | tf_op jit(solution)/shard_map/ppermute | solution.py:537
  8.7 8.2 %collective-permute-start = (bf16[64,256]{1,0:T(8,128)(2,1)S(1)}, bf16[64,256]{1,0:T(8,128)(2,1)S(1)}, u32[]{:S(2)}, u32[]{:S(2)}) collective-permute-start(bf16[64,256]{1,0:T(8,128)(2,1)S(1)} %get-tuple-element.50), channel_id=1, source_target_pairs={{0,8},{8,16},{16,24},{24,32},{32,40},{40,48},{48,56},{56,64},{64,7... | collective-permute-start | bytes 98312 | tf_op jit(solution)/shard_map/ppermute | solution.py:32
  11.5 10.6 %collective-permute-start.7 = (bf16[128,512]{1,0:T(8,128)(2,1)S(1)}, bf16[128,512]{1,0:T(8,128)(2,1)S(1)}, u32[]{:S(2)}, u32[]{:S(2)}) collective-permute-start(bf16[128,512]{1,0:T(8,128)(2,1)S(1)} %constant_dynamic-update-slice_fusion.refs_0_), channel_id=1, source_target_pairs={{0,3},{1,0},{2,1},{3,2},{4,7},{5,4},{6,5},{7,6},{8,11},{9,8},{10,9... | collective-permute-start | bytes 393224 | tf_op jit(solution)/shard_map/ppermute | solution.py:537
  15.6 7.9 %collective-permute-start.6 = (bf16[128,512]{1,0:T(8,128)(2,1)S(1)}, bf16[128,512]{1,0:T(8,128)(2,1)S(1)}, u32[]{:S(2)}, u32[]{:S(2)}) collective-permute-start(bf16[128,512]{1,0:T(8,128)(2,1)S(1)} %constant_dynamic-update-slice_fusion.refs_0_), channel_id=1, source_target_pairs={{0,2},{1,3},{2,0},{3,1},{4,6},{5,7},{6,4},{7,5},{8,10},{9,11},{10,... | collective-permute-start | bytes 393224 | tf_op jit(solution)/shard_map/ppermute | solution.py:537
  15.6 10.3 %collective-permute-start.5 = (bf16[128,512]{1,0:T(8,128)(2,1)S(1)}, bf16[128,512]{1,0:T(8,128)(2,1)S(1)}, u32[]{:S(2)}, u32[]{:S(2)}) collective-permute-start(bf16[128,512]{1,0:T(8,128)(2,1)S(1)} %constant_dynamic-update-slice_fusion.refs_0_), channel_id=1, source_target_pairs={{0,1},{1,2},{2,3},{3,0},{4,5},{5,6},{6,7},{7,4},{8,9},{9,10},{10,1... | collective-permute-start | bytes 393224 | tf_op jit(solution)/shard_map/ppermute | solution.py:537
  26.6 27.1 %all-to-all-start = ((bf16[8,64,1664]{2,1,0:T(8,128)(2,1)}), bf16[8,64,1664]{2,1,0:T(8,128)(2,1)}, u32[]{:S(2)}, u32[]{:S(2)}) async-start(bf16[8,64,1664]{2,1,0:T(8,128)(2,1)} %pad_maximum_fusion), calls=%async_computation | async-start | bytes 3407872 | tf_op jit(solution)/shard_map/all_to_all | solution.py:545
  31.1 13.8 %collective-permute-start.10 = (bf16[256,512]{1,0:T(8,128)(2,1)S(1)}, bf16[256,512]{1,0:T(8,128)(2,1)S(1)}, u32[]{:S(2)}, u32[]{:S(2)}) collective-permute-start(bf16[256,512]{1,0:T(8,128)(2,1)S(1)} %get-tuple-element.56.refs_0_.refs_4_), channel_id=1, source_target_pairs={{0,96},{32,0},{64,32},{96,64},{1,97},{33,1},{65,33},{97,65},{2,98}... | collective-permute-start | bytes 786440 | tf_op jit(solution)/shard_map/ppermute | solution.py:537
  35.4 9.5 %collective-permute-start.9 = (bf16[256,512]{1,0:T(8,128)(2,1)S(1)}, bf16[256,512]{1,0:T(8,128)(2,1)S(1)}, u32[]{:S(2)}, u32[]{:S(2)}) collective-permute-start(bf16[256,512]{1,0:T(8,128)(2,1)S(1)} %get-tuple-element.56.refs_0_.refs_4_), channel_id=1, source_target_pairs={{0,64},{32,96},{64,0},{96,32},{1,65},{33,97},{65,1},{97,33},{2,66}... | collective-permute-start | bytes 786440 | tf_op jit(solution)/shard_map/ppermute | solution.py:537
  36.0 10.9 %collective-permute-start.8 = (bf16[256,512]{1,0:T(8,128)(2,1)S(1)}, bf16[256,512]{1,0:T(8,128)(2,1)S(1)}, u32[]{:S(2)}, u32[]{:S(2)}) collective-permute-start(bf16[256,512]{1,0:T(8,128)(2,1)S(1)} %get-tuple-element.56.refs_0_.refs_4_), channel_id=1, source_target_pairs={{0,32},{32,64},{64,96},{96,0},{1,33},{33,65},{65,97},{97,1},{2,34}... | collective-permute-start | bytes 786440 | tf_op jit(solution)/shard_map/ppermute | solution.py:537
  37.0 10.8 %collective-permute-start.11 = (bf16[256,512]{1,0:T(8,128)(2,1)S(1)}, bf16[256,512]{1,0:T(8,128)(2,1)S(1)}, u32[]{:S(2)}, u32[]{:S(2)}) collective-permute-start(bf16[256,512]{1,0:T(8,128)(2,1)S(1)} %get-tuple-element.56.refs_0_.refs_4_), channel_id=1, source_target_pairs={{0,8},{8,0},{1,9},{9,1},{2,10},{10,2},{3,11},{11,3},{4,12},{12,4},... | collective-permute-start | bytes 786440 | tf_op jit(solution)/shard_map/ppermute | solution.py:532
  60.7 31.3 %all-to-all-start.1 = ((f32[8,128,512]{2,1,0:T(8,128)}), f32[8,128,512]{2,1,0:T(8,128)S(1)}, u32[]{:S(2)}, u32[]{:S(2)}) async-start(f32[8,128,512]{2,1,0:T(8,128)} %get-tuple-element.57), calls=%async_computation.1 | async-start | bytes 4194304 | tf_op jit(solution)/shard_map/all_to_all | solution.py:545
  66.1 9.3 %collective-permute-start.16 = (bf16[192,512]{1,0:T(8,128)(2,1)S(1)}, bf16[192,512]{1,0:T(8,128)(2,1)S(1)}, u32[]{:S(2)}, u32[]{:S(2)}) collective-permute-start(bf16[192,512]{1,0:T(8,128)(2,1)S(1)} %get-tuple-element.58.refs_0_), channel_id=1, source_target_pairs={{0,64},{32,96},{64,0},{96,32},{1,65},{33,97},{65,1},{97,33},{2,66}... | collective-permute-start | bytes 589832 | tf_op jit(solution)/shard_map/ppermute | solution.py:537
  66.8 11.2 %collective-permute-start.15 = (bf16[192,512]{1,0:T(8,128)(2,1)S(1)}, bf16[192,512]{1,0:T(8,128)(2,1)S(1)}, u32[]{:S(2)}, u32[]{:S(2)}) collective-permute-start(bf16[192,512]{1,0:T(8,128)(2,1)S(1)} %get-tuple-element.58.refs_0_), channel_id=1, source_target_pairs={{0,32},{32,64},{64,96},{96,0},{1,33},{33,65},{65,97},{97,1},{2,34}... | collective-permute-start | bytes 589832 | tf_op jit(solution)/shard_map/ppermute | solution.py:537
  67.8 10.3 %collective-permute-start.18 = (bf16[192,512]{1,0:T(8,128)(2,1)S(1)}, bf16[192,512]{1,0:T(8,128)(2,1)S(1)}, u32[]{:S(2)}, u32[]{:S(2)}) collective-permute-start(bf16[192,512]{1,0:T(8,128)(2,1)S(1)} %get-tuple-element.58.refs_0_), channel_id=1, source_target_pairs={{0,8},{8,0},{1,9},{9,1},{2,10},{10,2},{3,11},{11,3},{4,12},{12,4},... | collective-permute-start | bytes 589832 | tf_op jit(solution)/shard_map/ppermute | solution.py:532
  98.4 22.0 %all-to-all-start.2 = ((bf16[8,576,128]{2,1,0:T(8,128)(2,1)}), bf16[8,576,128]{2,1,0:T(8,128)(2,1)S(1)}, u32[]{:S(2)}, u32[]{:S(2)}) async-start(bf16[8,576,128]{2,1,0:T(8,128)(2,1)} %get-tuple-element.59), calls=%async_computation.2 | async-start | bytes 2359296 | tf_op jit(solution)/shard_map/all_to_all | solution.py:545
  105.3 7.8 %collective-permute-start.25 = (bf16[192,512]{1,0:T(8,128)(2,1)S(1)}, bf16[192,512]{1,0:T(8,128)(2,1)S(1)}, u32[]{:S(2)}, u32[]{:S(2)}) collective-permute-start(bf16[192,512]{1,0:T(8,128)(2,1)S(1)} %get-tuple-element.96), channel_id=1, source_target_pairs={{0,96},{32,0},{64,32},{96,64},{1,97},{33,1},{65,33},{97,65},{2,98}... | collective-permute-start | bytes 589832 | tf_op jit(solution)/shard_map/ppermute | solution.py:537
  105.8 9.3 %collective-permute-start.24 = (bf16[192,512]{1,0:T(8,128)(2,1)S(1)}, bf16[192,512]{1,0:T(8,128)(2,1)S(1)}, u32[]{:S(2)}, u32[]{:S(2)}) collective-permute-start(bf16[192,512]{1,0:T(8,128)(2,1)S(1)} %get-tuple-element.97), channel_id=1, source_target_pairs={{0,64},{32,96},{64,0},{96,32},{1,65},{33,97},{65,1},{97,33},{2,66}... | collective-permute-start | bytes 589832 | tf_op jit(solution)/shard_map/ppermute | solution.py:537
  106.4 11.8 %collective-permute-start.23 = (bf16[192,512]{1,0:T(8,128)(2,1)S(1)}, bf16[192,512]{1,0:T(8,128)(2,1)S(1)}, u32[]{:S(2)}, u32[]{:S(2)}) collective-permute-start(bf16[192,512]{1,0:T(8,128)(2,1)S(1)} %get-tuple-element.98), channel_id=1, source_target_pairs={{0,32},{32,64},{64,96},{96,0},{1,33},{33,65},{65,97},{97,1},{2,34}... | collective-permute-start | bytes 589832 | tf_op jit(solution)/shard_map/ppermute | solution.py:537
  126.0 17.9 %collective-permute-start.28 = (bf16[4,256,512]{2,1,0:T(8,128)(2,1)}, bf16[4,256,512]{2,1,0:T(8,128)(2,1)}, u32[]{:S(2)}, u32[]{:S(2)}) collective-permute-start(bf16[4,256,512]{2,1,0:T(8,128)(2,1)} %get-tuple-element.75), channel_id=1, source_target_pairs={{0,8},{8,0},{1,9},{9,1},{2,10},{10,2},{3,11},{11,3},{4,12},{12,4},... | collective-permute-start | bytes 3145736 | tf_op jit(solution)/shard_map/ppermute | solution.py:532
  138.4 46.7 %all-to-all-start.3 = ((bf16[8,64,1024]{2,1,0:T(8,128)(2,1)}), bf16[8,64,1024]{2,1,0:T(8,128)(2,1)S(1)}, u32[]{:S(2)}, u32[]{:S(2)}) async-start(bf16[8,64,1024]{2,1,0:T(8,128)(2,1)} %shard_map.203), calls=%async_computation.3 | async-start | bytes 2097152 | tf_op jit(solution)/shard_map/all_to_all | solution.py:545
  145.4 20.1 %collective-permute-start.31 = (bf16[256,512]{1,0:T(8,128)(2,1)S(1)}, bf16[256,512]{1,0:T(8,128)(2,1)S(1)}, u32[]{:S(2)}, u32[]{:S(2)}) collective-permute-start(bf16[256,512]{1,0:T(8,128)(2,1)S(1)} %get-tuple-element.92), channel_id=1, source_target_pairs={{0,96},{32,0},{64,32},{96,64},{1,97},{33,1},{65,33},{97,65},{2,98}... | collective-permute-start | bytes 786440 | tf_op jit(solution)/shard_map/ppermute | solution.py:537
  156.2 10.2 %collective-permute-start.30 = (bf16[256,512]{1,0:T(8,128)(2,1)S(1)}, bf16[256,512]{1,0:T(8,128)(2,1)S(1)}, u32[]{:S(2)}, u32[]{:S(2)}) collective-permute-start(bf16[256,512]{1,0:T(8,128)(2,1)S(1)} %get-tuple-element.93), channel_id=1, source_target_pairs={{0,64},{32,96},{64,0},{96,32},{1,65},{33,97},{65,1},{97,33},{2,66}... | collective-permute-start | bytes 786440 | tf_op jit(solution)/shard_map/ppermute | solution.py:537
  157.0 12.2 %collective-permute-start.29 = (bf16[256,512]{1,0:T(8,128)(2,1)S(1)}, bf16[256,512]{1,0:T(8,128)(2,1)S(1)}, u32[]{:S(2)}, u32[]{:S(2)}) collective-permute-start(bf16[256,512]{1,0:T(8,128)(2,1)S(1)} %get-tuple-element.94), channel_id=1, source_target_pairs={{0,32},{32,64},{64,96},{96,0},{1,33},{33,65},{65,97},{97,1},{2,34}... | collective-permute-start | bytes 786440 | tf_op jit(solution)/shard_map/ppermute | solution.py:537
  172.1 7.9 %collective-permute-start.33 = (bf16[4,32,512]{2,1,0:T(8,128)(2,1)S(1)}, bf16[4,32,512]{2,1,0:T(8,128)(2,1)S(1)}, u32[]{:S(2)}, u32[]{:S(2)}) collective-permute-start(bf16[4,32,512]{2,1,0:T(8,128)(2,1)S(1)} %get-tuple-element.82), channel_id=1, source_target_pairs={{0,2},{1,3},{2,0},{3,1},{4,6},{5,7},{6,4},{7,5},{8,10},{9,11},{10,... | collective-permute-start | bytes 393224 | tf_op jit(solution)/shard_map/ppermute | solution.py:537
  (47 other events, 506.6 us)

commit v6 on v5

--- a/solution.py
+++ b/solution.py
@@ -6,6 +6,7 @@
 from jax.experimental import pallas as pl
 from jax.experimental.pallas import tpu as pltpu
 from jax.sharding import Mesh, PartitionSpec as P
+
 
 L = 512
 BLK = 128
@@ -202,17 +203,16 @@
         row += count
 
 
-def edge_forward(scal, ext_hbm, edges, offsets, *refs):
+def edge_forward(scal, ext, edges, offsets, *refs):
     shards, refs = refs[:8], refs[8:]
     gain, joined_out, first_out, normed_out, inverse_out, new_edges_out, partial_out = refs[:7]
-    ext, joined, first, normed, inverse, new_edges, partial, w_in, w_out, second = refs[7:17]
-    sems, out_sems = refs[17:]
+    own_out, up_out, refs = refs[7], refs[8], refs[9:]
+    joined, first, normed, inverse, new_edges, partial, w_in, w_out, second, sems, out_sems = refs
     tiles = edges.shape[0] // BLK
     lat_index, core, y_index, count = (scal[2 * tiles + i] for i in range(4))
     slabs = w_in.shape[0] // 3 // 32
     counts = (3 * L // slabs, L // slabs)
-    pairs = [(ext_hbm, ext)] + weight_pairs(core, y_index, shards, (w_in, w_out), counts)
-    loads = copies(pairs, sems)
+    loads = copies(weight_pairs(core, y_index, shards, (w_in, w_out), counts), sems)
     stores = []
 
     def store(source, target):
@@ -220,8 +220,9 @@
         copy.start()
         stores.append(copy)
 
+    store(ext.at[:, block_at(HB + lat_index)], own_out)
+    store(ext.at[:, pl.ds(ext.shape[1] - BLK, BLK)], up_out)
     joined[:, pl.ds(0, L)] = edges[...]
-    loads[0].wait()
     for t in range(tiles):
         rows = pl.ds(t * BLK, BLK)
         to_src = one_hot_columns(offsets[1, pl.ds(t, 1), :]).T.astype(BF)
@@ -230,7 +231,7 @@
         joined[rows, pl.ds(L, L)] = dot_transpose(to_src, ext[:, src]).astype(BF)
         joined[rows, pl.ds(2 * L, L)] = dot_transpose(to_dst, ext[:, dst]).astype(BF)
     store(joined, joined_out)
-    wait_all(loads[1:])
+    wait_all(loads)
     for n in range(2):
         columns = pl.ds(n * 256, 256)
         first[:, columns] = jnp.maximum(dot(joined[...], w_in[:, columns]), 0.0).astype(BF)
@@ -261,43 +262,52 @@
     wait_all(stores)
 
 
-def node_step(scal, spread, ext_hbm, *refs):
+def node_step(scal, spread, own_hbm, up_hbm, *refs):
     shards, refs = refs[:8], refs[8:]
-    gain, out, direct_out, keep, send = refs[:5]
-    own_turned, up_turned, w_in, w_out, joined, first, g_in, g_out, d_direct, sems, out_sems = refs[5:]
-    lat_index, core, y_index = scal[0], scal[1], scal[2]
+    gain, out, direct_out, joined_out, first_out, d_second_out, d_first_out = refs[:7]
+    own_turned, up_turned, w_in, w_out, joined, first, d_second, d_first, d_direct = refs[7:16]
+    sems, out_sems = refs[16:]
+    core, y_index = scal[1], scal[2]
     slabs = w_in.shape[0] // 2 // 32
     counts = (2 * L // slabs, L // slabs)
-    pairs = [
-        (ext_hbm.at[:, block_at(HB + lat_index)], own_turned),
-        (ext_hbm.at[:, pl.ds(ext_hbm.shape[1] - BLK, BLK)], up_turned),
-    ] + weight_pairs(core, y_index, shards, (w_in, w_out), counts)
+    pairs = [(own_hbm, own_turned), (up_hbm, up_turned)]
+    pairs += weight_pairs(core, y_index, shards, (w_in, w_out), counts)
     loads = copies(pairs, sems)
+    wait_all(loads[:2])
+    own = own_turned[...].astype(F32).T
+    upstream = up_turned[...].astype(F32).T
+    joined[:, pl.ds(0, L)] = own.astype(BF)
     total = spread[0]
     for l in range(1, spread.shape[0]):
         total = total + spread[l]
     joined[:, pl.ds(L, L)] = total.astype(BF)
-    wait_all(loads)
-    own = own_turned[...].astype(F32).T
-    upstream = up_turned[...].astype(F32).T
-    joined[:, pl.ds(0, L)] = own.astype(BF)
+    wait_all(loads[2:])
     first[...] = jnp.maximum(dot(joined[...], w_in[...]), 0.0).astype(BF)
     normed, inverse = norm_parts(dot(first[...], w_out[...]))
+    d_second[...] = norm_back(upstream, normed, inverse, gain[...]).astype(BF)
+    back = dot_transpose(d_second[...], w_out[...])
+    d_first[...] = jnp.where(first[...].astype(F32) > 0, back, 0.0).astype(BF)
+    d_agg = dot_transpose(w_in[pl.ds(L, L), :], d_first[...]).astype(BF)
     new_rows = (own + normed * gain[...]).T.astype(BF)
-    d_second = norm_back(upstream, normed, inverse, gain[...]).astype(BF)
-    d_first = dot_transpose(d_second, w_out[...])
-    d_first = jnp.where(first[...].astype(F32) > 0, d_first, 0.0).astype(BF)
-    d_direct[...] = dot_transpose(w_in[pl.ds(0, L), :], d_first)
-    store = copies([(d_direct, direct_out)], out_sems)
-    d_agg = dot_transpose(w_in[pl.ds(L, L), :], d_first).astype(BF)
     width = L // out.shape[0]
     for l in range(out.shape[0]):
         out[l, pl.ds(0, L), :] = d_agg
         out[l, pl.ds(L, width), :] = new_rows[l * width : (l + 1) * width, :]
-    g_out[...] = dot_rows(first[...], d_second)
-    g_in[...] = dot_rows(joined[...], d_first)
-    pack_grads(core, y_index, (g_in, g_out), keep, send, counts)
-    wait_all(store)
+    d_direct[...] = dot_transpose(w_in[pl.ds(0, L), :], d_first[...])
+    held = (d_direct, joined, first, d_second, d_first)
+    outs = (direct_out, joined_out, first_out, d_second_out, d_first_out)
+    wait_all(copies(zip(held, outs), out_sems))
+
+
+def node_grads(scal, *refs):
+    saved, (keep, send), refs = refs[:4], refs[4:6], refs[6:]
+    held, (g_in, g_out, sems) = refs[:4], refs[4:]
+    wait_all(copies(zip(saved, held), sems))
+    joined, first, d_second, d_first = held
+    g_out[...] = dot_rows(first[...], d_second[...])
+    g_in[...] = dot_rows(joined[...], d_first[...])
+    slabs = g_in.shape[0] // 2 // 32
+    pack_grads(scal[1], scal[2], (g_in, g_out), keep, send, (2 * L // slabs, L // slabs))
 
 
 def edge_backward(scal, d_agg, cot, offsets, gain, *refs):
@@ -430,48 +440,50 @@
         shape_of((rows, L), BF),
         shape_of((lat_size, BLK, L), F32),
     ]
-    held = [(ext.shape, BF)] + [(out.shape, out.dtype) for out in outs]
+    held = [(out.shape, out.dtype) for out in outs]
+    outs += [shape_of((L, BLK), BF)] * 2
     return call(
         edge_forward,
         outs,
         held + [((3 * L, L), BF), ((L, L), BF), ((rows, L), F32)],
         EDGE_MIB,
-        "shvv" + "h" * len(shards) + "v",
+        "svvv" + "h" * len(shards) + "v",
         (scal, ext, edges, offsets, *shards, gain),
         flops=2 * rows * 4 * L * L,
         out_spaces="h" * len(outs),
-        sems=(1 + 4 * len(shards), len(outs)),
-    )
-
-
-def run_node_step(scal, spread, ext, shards, gain):
+        sems=(4 * len(shards), len(outs)),
+    )
+
+
+def run_node_step(scal, spread, own, up, shards, gain):
     lat_size = spread.shape[0]
-    chunk = (len(shards) // 2,) + shards[0].shape
+    rows = [((BLK, 2 * L), BF), ((BLK, L), BF), ((BLK, L), BF), ((BLK, L), BF)]
     return call(
         node_step,
-        [
-            shape_of((lat_size, L + L // lat_size, BLK), BF),
-            shape_of((L, BLK), F32),
-            shape_of(chunk, BF),
-            shape_of(chunk, BF),
-        ],
-        [
-            ((L, BLK), BF),
-            ((L, BLK), BF),
-            ((2 * L, L), BF),
-            ((L, L), BF),
-            ((BLK, 2 * L), BF),
-            ((BLK, L), BF),
-            ((2 * L, L), F32),
-            ((L, L), F32),
-            ((L, BLK), F32),
-        ],
+        [shape_of((lat_size, L + L // lat_size, BLK), BF), shape_of((L, BLK), F32)]
+        + [shape_of(*row) for row in rows],
+        [((L, BLK), BF), ((L, BLK), BF), ((2 * L, L), BF), ((L, L), BF)]
+        + rows
+        + [((L, BLK), F32)],
         NODE_MIB,
-        "svh" + "h" * len(shards) + "v",
-        (scal, spread, ext, *shards, gain),
-        flops=2 * BLK * 9 * L * L,
-        out_spaces="vhvv",
-        sems=(2 + 4 * len(shards), 1),
+        "svhh" + "h" * len(shards) + "v",
+        (scal, spread, own, up, *shards, gain),
+        flops=2 * BLK * 6 * L * L,
+        out_spaces="vhhhhh",
+        sems=(2 + 4 * len(shards), 5),
+    )
+
+
+def run_node_grads(scal, saved, shard, y_count):
+    return call(
+        node_grads,
+        [shape_of((y_count,) + shard.shape, BF)] * 2,
+        [(one.shape, BF) for one in saved] + [((2 * L, L), F32), ((L, L), F32)],
+        NODE_MIB,
+        "shhhh",
+        (scal, *saved),
+        flops=2 * BLK * 3 * L * L,
+        sems=(4,),
     )
 
 
@@ -608,7 +620,13 @@
     from_lower = from_behind(up, 1)
     from_upper = from_behind(down, -1)
 
-    near = shifts(jnp.concatenate(shifts(packed, XS), axis=0), "z")
+    table = jnp.concatenate([from_lower, turned, from_upper], axis=1)
+    cot = node_cotangent.T.reshape(width, lat_size, own_rows).transpose(1, 0, 2)
+    message_out = jnp.concatenate(
+        [jnp.broadcast_to(table, (lat_size,) + table.shape), cot], axis=2
+    )
+    by_x = jnp.concatenate(shifts(packed, XS), axis=0)
+    near = shifts(by_x, "z")
     edge_part, node_part = call(
         functools.partial(assemble, pieces),
         [shape_of((edge_rows, L), BF), shape_of((node_rows, L), BF)],
@@ -618,24 +636,19 @@
         (near_scal, *near),
     )
 
-    table = jnp.concatenate([from_lower, turned, from_upper], axis=1)
-    cot = node_cotangent.T.reshape(width, lat_size, own_rows).transpose(1, 0, 2)
-    message_out = jnp.concatenate(
-        [jnp.broadcast_to(table, (lat_size,) + table.shape), cot], axis=2
-    )
-    message_out, edge_part, node_part = lax.optimization_barrier(
-        (message_out, edge_part, node_part)
-    )
     edge_shards = gather_far(edge_part)
     ext = spread_rows(message_out, LAT).reshape(L, ext_rows + own_rows)
 
-    joined, first, normed, inverse, new_edges, partial = run_edge_forward(
+    joined, first, normed, inverse, new_edges, partial, own, node_up = run_edge_forward(
         scal, ext, edges, offsets, edge_shards, edge_gain_row, lat_size
     )
     node_shards = gather_far(node_part)
     spread = spread_rows(partial, LAT)
-    second_out, d_direct, node_keep, node_send = run_node_step(
-        node_scal, spread, ext, node_shards, node_gain_row
+    second_out, d_direct, *node_saved = run_node_step(
+        node_scal, spread, own, node_up, node_shards, node_gain_row
+    )
+    node_keep, node_send = run_node_grads(
+        node_scal, node_saved, node_part, lax.axis_size("y")
     )
     second_in = spread_rows(second_out, LAT)
     new_nodes = second_in[:, L:].transpose(1, 0, 2).reshape(width, slab_rows).T
@@ -651,6 +664,7 @@
     )
     from_above = from_behind(lower, -1)
     from_below = from_behind(upper, 1)
+    edge_far = reduce_far(edge_keep, edge_send)
     (columns,) = call(
         add_halo,
         [shape_of((lat_size, width, slab_rows), BF)],
@@ -659,10 +673,8 @@
         "svvv",
         (halo, middle, from_above, from_below),
     )
-    edge_far = reduce_far(edge_keep, edge_send)
-    (grad_slab,) = call(
-        finish, [shape_of((width, slab_rows), BF)], [], 4, "v", (spread_rows(columns, LAT),)
-    )
+    columns = spread_rows(columns, LAT)
+    (grad_slab,) = call(finish, [shape_of((width, slab_rows), BF)], [], 4, "v", (columns,))
 
     shard = (32, L)
     shards = (4,) + shard
@@ -711,6 +723,7 @@
         split,
         by_rows,
     )
+
     return jax.shard_map(
         per_device,
         mesh=fine,

time: 191 us -> 211 us (1.10)
  starting transfers between devices: 71 us -> 81.1 us
  waiting for transfers between devices: 75 us -> 82.9 us
  Pallas kernels: 30.5 us -> 34.2 us
    ppermute x24, waiting for transfers between devices: 53.8 us -> 62.3 us  [shift(): lax.ppermute(value, axes, [(i, (i + step) % count) for i in range(count)])]
    ppermute x24, starting transfers between devices: 43.8 us -> 51.1 us  [shift(): lax.ppermute(value, axes, [(i, (i + step) % count) for i in range(count)])]
    all_to_all x4, waiting for transfers between devices: 19.3 us -> 14.1 us  [spread_rows(): return lax.all_to_all(value, axes, 0, 0)]
    pallas_call x11 -> x12, Pallas kernels: 30.5 us -> 34.2 us  [call(): pl.pallas_call(kernel, out_shape=placed, in_specs=[pl.BlockSpec(memory_sp...]
    ppermute x4, waiting for transfers between devices: 1.13 us -> 4.71 us  [from_behind(): lax.ppermute(value, SLAB, [(source, source + steps) for source in range(f...]
    all_to_all x4, starting transfers between devices: 19.4 us -> 21.9 us  [spread_rows(): return lax.all_to_all(value, axes, 0, 0)]
  transfers between devices with their start and end apart: 42 -> 42, of which waited for: 26 -> 24; matrix products, arithmetic and copies ran while one was open for 4% -> 2% of each run, Pallas kernels for 5% -> 5%
where the time goes in v6:
time: 211 us; the launch traced here: 209 us
  waiting for transfers between devices  82.9 us (39%)
  starting transfers between devices  81.1 us (38%)
  Pallas kernels  34.2 us (16%)
  other arithmetic  4.87 us (2%)
  local copies, waits for them, and re-layouts  4.62 us (2%)
    ppermute x24, waiting for transfers between devices, shift(): lax.ppermute(value, axes, [(i, (i + step) % count) for i in range(count)])  62.3 us
    ppermute x24, starting transfers between devices, shift(): lax.ppermute(value, axes, [(i, (i + step) % count) for i in range(count)])  51.1 us
    pallas_call x12, Pallas kernels, call(): pl.pallas_call(kernel, out_shape=placed, in_specs=[pl.BlockSpec(memory_sp...  34.2 us
    all_to_all x4, starting transfers between devices, spread_rows(): return lax.all_to_all(value, axes, 0, 0)  21.9 us
    all_to_all x4, waiting for transfers between devices, spread_rows(): return lax.all_to_all(value, axes, 0, 0)  14.1 us
    ppermute x4, starting transfers between devices, from_behind(): lax.ppermute(value, SLAB, [(source, source + steps) for source in range(f...  6.92 us
    ppermute x4, waiting for transfers between devices, from_behind(): lax.ppermute(value, SLAB, [(source, source + steps) for source in range(f...  4.71 us
  transfers between devices with their start and end apart: 42, of which 24 were waited for; matrix products, arithmetic and copies ran while one was open for 2% of the time, Pallas kernels for 5%

profile of v6, /device:TPU:0, one launch (start us, length us, event | category | flops | bytes accessed | tf_op | source)
XLA Modules:
  0.0 209.3 jit_solution(9710271444328460016)
XLA Ops:
  5.6 3.6 %collective-permute-done.1 = bf16[64,256]{1,0:T(8,128)(2,1)S(1)} collective-permute-done((bf16[64,256]{1,0:T(8,128)(2,1)S(1)}, bf16[64,256]{1,0:T(8,128)(2,1)S(1)}, u32[]{:S(2)}, u32[]{:S(2)}) %collective-permute-start.1) | collective-permute-done | bytes 32800 | tf_op jit(solution)/shard_map/ppermute | solution.py:33
  11.6 7.6 %all-to-all-start = ((bf16[8,64,1664]{2,1,0:T(8,128)(2,1)}), bf16[8,64,1664]{2,1,0:T(8,128)(2,1)S(1)}, u32[]{:S(2)}, u32[]{:S(2)}) async-start(bf16[8,64,1664]{2,1,0:T(8,128)(2,1)} %pad_maximum_fusion), calls=%async_computation | async-start | bytes 3407872 | tf_op jit(solution)/shard_map/all_to_all | solution.py:557
  19.2 3.5 %collective-permute-start.2 = (bf16[32,512]{1,0:T(8,128)(2,1)S(1)}, bf16[32,512]{1,0:T(8,128)(2,1)S(1)}, u32[]{:S(2)}, u32[]{:S(2)}) collective-permute-start(bf16[32,512]{1,0:T(8,128)(2,1)S(1)} %get-tuple-element.55), channel_id=1, source_target_pairs={{0,4},{4,16},{16,20},{20,0},{1,5},{5,17},{17,21},{21,1},{2,6},{6,1... | collective-permute-start | bytes 98312 | tf_op jit(solution)/shard_map/ppermute | solution.py:549
  24.6 19.0 %collective-permute-done.2 = bf16[32,512]{1,0:T(8,128)(2,1)S(1)} collective-permute-done((bf16[32,512]{1,0:T(8,128)(2,1)S(1)}, bf16[32,512]{1,0:T(8,128)(2,1)S(1)}, u32[]{:S(2)}, u32[]{:S(2)}) %collective-permute-start.2) | collective-permute-done | bytes 32800 | tf_op jit(solution)/shard_map/ppermute | solution.py:549
  50.6 3.7 %collective-permute-done.6.refs_2_ = bf16[128,512]{1,0:T(8,128)(2,1)S(1)} collective-permute-done((bf16[128,512]{1,0:T(8,128)(2,1)S(1)}, bf16[128,512]{1,0:T(8,128)(2,1)S(1)}, u32[]{:S(2)}, u32[]{:S(2)}) %collective-permute-start.6) | collective-permute-done | bytes 131104 | tf_op jit(solution)/shard_map/ppermute | solution.py:549
  62.1 3.4 %collective-permute-done.8.refs_1_.refs_5_ = bf16[256,512]{1,0:T(8,128)(2,1)S(1)} collective-permute-done((bf16[256,512]{1,0:T(8,128)(2,1)S(1)}, bf16[256,512]{1,0:T(8,128)(2,1)S(1)}, u32[]{:S(2)}, u32[]{:S(2)}) %collective-permute-start.8) | collective-permute-done | bytes 262176 | tf_op jit(solution)/shard_map/ppermute | solution.py:549
  65.6 5.9 %collective-permute-done.9.refs_2_.refs_6_ = bf16[256,512]{1,0:T(8,128)(2,1)} collective-permute-done((bf16[256,512]{1,0:T(8,128)(2,1)S(1)}, bf16[256,512]{1,0:T(8,128)(2,1)}, u32[]{:S(2)}, u32[]{:S(2)}) %collective-permute-start.9) | collective-permute-done | bytes 262176 | tf_op jit(solution)/shard_map/ppermute | solution.py:549
  73.7 7.4 %shard_map.199 = (bf16[512,1536]{1,0:T(8,128)(2,1)}, bf16[512,512]{1,0:T(8,128)(2,1)}, f32[512,512]{1,0:T(8,128)}, f32[512,128]{1,0:T(8,128)}, bf16[512,512]{1,0...) custom-call(s32[12]{0:T(128)S(1)} %concatenate.13.scal, ...), custom_call_target="tpu_custom_call" | custom-call | flops 1073741824 | bytes 10623024 | tf_op jit(solution)/shard_map/pallas_call | solution.py:421
  81.2 4.6 %all-to-all-start.1 = ((f32[8,128,512]{2,1,0:T(8,128)}), f32[8,128,512]{2,1,0:T(8,128)S(1)}, u32[]{:S(2)}, u32[]{:S(2)}) async-start(f32[8,128,512]{2,1,0:T(8,128)} %get-tuple-element.57), calls=%async_computation.1 | async-start | bytes 4194304 | tf_op jit(solution)/shard_map/all_to_all | solution.py:557
  94.3 4.0 %collective-permute-done.16.refs_2_ = bf16[192,512]{1,0:T(8,128)(2,1)S(1)} collective-permute-done((bf16[192,512]{1,0:T(8,128)(2,1)S(1)}, bf16[192,512]{1,0:T(8,128)(2,1)S(1)}, u32[]{:S(2)}, u32[]{:S(2)}) %collective-permute-start.16) | collective-permute-done | bytes 196640 | tf_op jit(solution)/shard_map/ppermute | solution.py:549
  100.4 12.1 %all-to-all-done.1.spread = f32[8,128,512]{2,1,0:T(8,128)S(1)} async-done(((f32[8,128,512]{2,1,0:T(8,128)}), f32[8,128,512]{2,1,0:T(8,128)S(1)}, u32[]{:S(2)}, u32[]{:S(2)}) %all-to-all-start.1) | async-done | bytes 2097184 | tf_op jit(solution)/shard_map/all_to_all | solution.py:557
  112.5 5.8 %shard_map.200 = (bf16[8,576,128]{2,1,0:T(8,128)(2,1)}, f32[512,128]{1,0:T(8,128)}, bf16[128,1024]{1,0:T(8,128)(2,1)}, bf16[128,512]{1,0:T(8,128)(2,1)}, bf16[12...) custom-call(s32[3]{0:T(128)S(1)} %pad_add_fusion.scal, f32[8,128,512]{2,1,0:T(8,128)S(1)} %all-to-all-done.1.spread, ...), custom_call_target="tpu_custom_call" | custom-call | flops 402653184 | bytes 6031372 | tf_op jit(solution)/shard_map/pallas_call | solution.py:421
  118.3 3.3 %shard_map.201 = (bf16[4,192,512]{2,1,0:T(8,128)(2,1)S(1)}, bf16[4,192,512]{2,1,0:T(8,128)(2,1)}) custom-call(s32[3]{0:T(128)S(1)} %pad_add_fusion.scal, bf16[128,1024]{1,0:T(8,128)(2,1)} %get-tuple-element.63.refs_0_, bf16[128,512]{1,0:T(8,128)(2,1)} %get-tuple-element.64.refs_1_, bf16[128,512]{1,0:T(8,128)(2,1)} %get-tuple-element.65.refs_2_, ...), custom_call_target="tpu_custom_call" | custom-call | flops 201326592 | bytes 2228236 | tf_op jit(solution)/shard_map/pallas_call | solution.py:421
  121.9 4.8 %all-to-all-start.2 = ((bf16[8,576,128]{2,1,0:T(8,128)(2,1)}), bf16[8,576,128]{2,1,0:T(8,128)(2,1)S(1)}, u32[]{:S(2)}, u32[]{:S(2)}) async-start(bf16[8,576,128]{2,1,0:T(8,128)(2,1)} %get-tuple-element.61), calls=%async_computation.2 | async-start | bytes 2359296 | tf_op jit(solution)/shard_map/all_to_all | solution.py:557
  136.8 3.7 %collective-permute-done.24.n2 = bf16[192,512]{1,0:T(8,128)(2,1)S(1)} collective-permute-done((bf16[192,512]{1,0:T(8,128)(2,1)S(1)}, bf16[192,512]{1,0:T(8,128)(2,1)S(1)}, u32[]{:S(2)}, u32[]{:S(2)}) %collective-permute-start.24) | collective-permute-done | bytes 196640 | tf_op jit(solution)/shard_map/ppermute | solution.py:549
  143.9 5.6 %shard_map.202 = (bf16[512,512]{1,0:T(8,128)(2,1)S(1)}, bf16[4,256,512]{2,1,0:T(8,128)(2,1)S(1)}, bf16[4,256,512]{2,1,0:T(8,128)(2,1)}) custom-call(s32[12]{0:T(128)S(1)} %concatenate.13.scal, bf16[8,576,128]{2,1,0:T(8,128)(2,1)S(1)} %all-to-all-done.2.d_agg, bf16[512,512]{1,0:T(8,128)(2,1)S(1)} %copy-done.2, s32[2,4,128]{2,1,0:T(4,128)S(1)} %reshape.76.offsets, ...), custom_call_target="tpu_custom_call" | custom-call | flops 1342177280 | bytes 9836592 | tf_op jit(solution)/shard_map/pallas_call | solution.py:421
  149.6 4.8 %shard_map.203 = (bf16[512,512]{1,0:T(8,128)(2,1)}, f32[8,512,128]{2,1,0:T(8,128)S(1)}, bf16[512,256]{1,0:T(8,128)(2,1)S(1)}, bf16[512,256]{1,0:T(8,128)(2,1)S(1)}) custom-call(s32[12]{0:T(128)S(1)} %concatenate.13.scal, bf16[512,512]{1,0:T(8,128)(2,1)S(1)} %get-tuple-element.74.d_first, bf16[512,512]{1,0:T(8,128)(2,1)S(1)} %copy-done.2, ...), custom_call_target="tpu_custom_call" | custom-call | flops 805306368 | bytes 6557744 | tf_op jit(solution)/shard_map/pallas_call | solution.py:421
  155.7 3.0 %collective-permute-start.27 = (bf16[512,256]{1,0:T(8,128)(2,1)S(1)}, bf16[512,256]{1,0:T(8,128)(2,1)S(1)}, u32[]{:S(2)}, u32[]{:S(2)}) collective-permute-start(bf16[512,256]{1,0:T(8,128)(2,1)S(1)} %get-tuple-element.78), channel_id=1, source_target_pairs={{0,8},{8,16},{16,24},{24,32},{32,40},{40,48},{48,56},{56,64},{64,7... | collective-permute-start | bytes 786440 | tf_op jit(solution)/shard_map/ppermute | solution.py:33
  161.9 4.9 %all-to-all-start.3 = ((bf16[8,64,1024]{2,1,0:T(8,128)(2,1)}), bf16[8,64,1024]{2,1,0:T(8,128)(2,1)S(1)}, u32[]{:S(2)}, u32[]{:S(2)}) async-start(bf16[8,64,1024]{2,1,0:T(8,128)(2,1)} %shard_map.204), calls=%async_computation.3 | async-start | bytes 2097152 | tf_op jit(solution)/shard_map/all_to_all | solution.py:557
  168.4 7.8 %collective-permute-start.29 = (bf16[256,512]{1,0:T(8,128)(2,1)S(1)}, bf16[256,512]{1,0:T(8,128)(2,1)S(1)}, u32[]{:S(2)}, u32[]{:S(2)}) collective-permute-start(bf16[256,512]{1,0:T(8,128)(2,1)S(1)} %get-tuple-element.100), channel_id=1, source_target_pairs={{0,32},{32,64},{64,96},{96,0},{1,33},{33,65},{65,97},{97,1},{2,34}... | collective-permute-start | bytes 786440 | tf_op jit(solution)/shard_map/ppermute | solution.py:549
  176.2 3.0 %collective-permute-start.30 = (bf16[256,512]{1,0:T(8,128)(2,1)S(1)}, bf16[256,512]{1,0:T(8,128)(2,1)S(1)}, u32[]{:S(2)}, u32[]{:S(2)}) collective-permute-start(bf16[256,512]{1,0:T(8,128)(2,1)S(1)} %get-tuple-element.99), channel_id=1, source_target_pairs={{0,64},{32,96},{64,0},{96,32},{1,65},{33,97},{65,1},{97,33},{2,66}... | collective-permute-start | bytes 786440 | tf_op jit(solution)/shard_map/ppermute | solution.py:549
  180.1 3.9 %collective-permute-done.29.e1 = bf16[256,512]{1,0:T(8,128)(2,1)S(1)} collective-permute-done((bf16[256,512]{1,0:T(8,128)(2,1)S(1)}, bf16[256,512]{1,0:T(8,128)(2,1)S(1)}, u32[]{:S(2)}, u32[]{:S(2)}) %collective-permute-start.29) | collective-permute-done | bytes 262176 | tf_op jit(solution)/shard_map/ppermute | solution.py:549
  184.0 4.9 %collective-permute-done.30.e2 = bf16[256,512]{1,0:T(8,128)(2,1)S(1)} collective-permute-done((bf16[256,512]{1,0:T(8,128)(2,1)S(1)}, bf16[256,512]{1,0:T(8,128)(2,1)S(1)}, u32[]{:S(2)}, u32[]{:S(2)}) %collective-permute-start.30) | collective-permute-done | bytes 262176 | tf_op jit(solution)/shard_map/ppermute | solution.py:549
  200.0 3.0 %collective-permute-start.35 = (bf16[32,512]{1,0:T(8,128)(2,1)S(1)}, bf16[32,512]{1,0:T(8,128)(2,1)S(1)}, u32[]{:S(2)}, u32[]{:S(2)}) collective-permute-start(bf16[32,512]{1,0:T(8,128)(2,1)S(1)} %get-tuple-element.91), channel_id=1, source_target_pairs={{0,4},{4,16},{16,20},{20,0},{1,5},{5,17},{17,21},{21,1},{2,6},{6,1... | collective-permute-start | bytes 98312 | tf_op jit(solution)/shard_map/ppermute | solution.py:549
  (135 shorter events, 74.4 us)
Async XLA Ops:
  11.6 62.1 %all-to-all-start = ((bf16[8,64,1664]{2,1,0:T(8,128)(2,1)}), bf16[8,64,1664]{2,1,0:T(8,128)(2,1)S(1)}, u32[]{:S(2)}, u32[]{:S(2)}) async-start(bf16[8,64,1664]{2,1,0:T(8,128)(2,1)} %pad_maximum_fusion), calls=%async_computation | async-start | bytes 3407872 | tf_op jit(solution)/shard_map/all_to_all | solution.py:557
  19.2 24.5 %collective-permute-start.2 = (bf16[32,512]{1,0:T(8,128)(2,1)S(1)}, bf16[32,512]{1,0:T(8,128)(2,1)S(1)}, u32[]{:S(2)}, u32[]{:S(2)}) collective-permute-start(bf16[32,512]{1,0:T(8,128)(2,1)S(1)} %get-tuple-element.55), channel_id=1, source_target_pairs={{0,4},{4,16},{16,20},{20,0},{1,5},{5,17},{17,21},{21,1},{2,6},{6,1... | collective-permute-start | bytes 98312 | tf_op jit(solution)/shard_map/ppermute | solution.py:549
  22.7 21.0 %collective-permute-start.3 = (bf16[32,512]{1,0:T(8,128)(2,1)S(1)}, bf16[32,512]{1,0:T(8,128)(2,1)S(1)}, u32[]{:S(2)}, u32[]{:S(2)}) collective-permute-start(bf16[32,512]{1,0:T(8,128)(2,1)S(1)} %get-tuple-element.55), channel_id=1, source_target_pairs={{0,16},{4,20},{16,0},{20,4},{1,17},{5,21},{17,1},{21,5},{2,18},{6,... | collective-permute-start | bytes 98312 | tf_op jit(solution)/shard_map/ppermute | solution.py:549
  24.6 19.1 %collective-permute-start.4 = (bf16[32,512]{1,0:T(8,128)(2,1)S(1)}, bf16[32,512]{1,0:T(8,128)(2,1)S(1)}, u32[]{:S(2)}, u32[]{:S(2)}) collective-permute-start(bf16[32,512]{1,0:T(8,128)(2,1)S(1)} %get-tuple-element.55), channel_id=1, source_target_pairs={{0,20},{4,0},{16,4},{20,16},{1,21},{5,1},{17,5},{21,17},{2,22},{6,... | collective-permute-start | bytes 98312 | tf_op jit(solution)/shard_map/ppermute | solution.py:549
  45.2 9.1 %collective-permute-start.6 = (bf16[128,512]{1,0:T(8,128)(2,1)S(1)}, bf16[128,512]{1,0:T(8,128)(2,1)S(1)}, u32[]{:S(2)}, u32[]{:S(2)}) collective-permute-start(bf16[128,512]{1,0:T(8,128)(2,1)S(1)} %constant_dynamic-update-slice_fusion.refs_0_), channel_id=1, source_target_pairs={{0,2},{1,3},{2,0},{3,1},{4,6},{5,7},{6,4},{7,5},{8,10},{9,11},{10,... | collective-permute-start | bytes 393224 | tf_op jit(solution)/shard_map/ppermute | solution.py:549
  55.0 10.5 %collective-permute-start.8 = (bf16[256,512]{1,0:T(8,128)(2,1)S(1)}, bf16[256,512]{1,0:T(8,128)(2,1)S(1)}, u32[]{:S(2)}, u32[]{:S(2)}) collective-permute-start(bf16[256,512]{1,0:T(8,128)(2,1)S(1)} %get-tuple-element.56.refs_0_.refs_4_), channel_id=1, source_target_pairs={{0,32},{32,64},{64,96},{96,0},{1,33},{33,65},{65,97},{97,1},{2,34}... | collective-permute-start | bytes 786440 | tf_op jit(solution)/shard_map/ppermute | solution.py:549
  57.9 13.6 %collective-permute-start.9 = (bf16[256,512]{1,0:T(8,128)(2,1)S(1)}, bf16[256,512]{1,0:T(8,128)(2,1)}, u32[]{:S(2)}, u32[]{:S(2)}) collective-permute-start(bf16[256,512]{1,0:T(8,128)(2,1)S(1)} %get-tuple-element.56.refs_0_.refs_4_), channel_id=1, source_target_pairs={{0,64},{32,96},{64,0},{96,32},{1,65},{33,97},{65,1},{97,33},{2,66}... | collective-permute-start | bytes 786440 | tf_op jit(solution)/shard_map/ppermute | solution.py:549
  60.8 10.7 %collective-permute-start.10 = (bf16[256,512]{1,0:T(8,128)(2,1)S(1)}, bf16[256,512]{1,0:T(8,128)(2,1)}, u32[]{:S(2)}, u32[]{:S(2)}) collective-permute-start(bf16[256,512]{1,0:T(8,128)(2,1)S(1)} %get-tuple-element.56.refs_0_.refs_4_), channel_id=1, source_target_pairs={{0,96},{32,0},{64,32},{96,64},{1,97},{33,1},{65,33},{97,65},{2,98}... | collective-permute-start | bytes 786440 | tf_op jit(solution)/shard_map/ppermute | solution.py:549
  62.1 10.7 %collective-permute-start.11 = (bf16[256,512]{1,0:T(8,128)(2,1)S(1)}, bf16[256,512]{1,0:T(8,128)(2,1)}, u32[]{:S(2)}, u32[]{:S(2)}) collective-permute-start(bf16[256,512]{1,0:T(8,128)(2,1)S(1)} %get-tuple-element.56.refs_0_.refs_4_), channel_id=1, source_target_pairs={{0,8},{8,0},{1,9},{9,1},{2,10},{10,2},{3,11},{11,3},{4,12},{12,4},... | collective-permute-start | bytes 786440 | tf_op jit(solution)/shard_map/ppermute | solution.py:544
  65.6 7.2 %collective-permute-start.12 = (bf16[256,512]{1,0:T(8,128)(2,1)S(1)}, bf16[256,512]{1,0:T(8,128)(2,1)}, u32[]{:S(2)}, u32[]{:S(2)}) collective-permute-start(bf16[256,512]{1,0:T(8,128)(2,1)S(1)} %collective-permute-done.8.refs_1_.refs_5_), channel_id=1, source_target_pairs={{0,8},{8,0},{1,9},{9,1},{2,10},{10,2},{3,11},{11,3},{4,12},{12,4},... | collective-permute-start | bytes 786440 | tf_op jit(solution)/shard_map/ppermute | solution.py:544
  81.2 31.3 %all-to-all-start.1 = ((f32[8,128,512]{2,1,0:T(8,128)}), f32[8,128,512]{2,1,0:T(8,128)S(1)}, u32[]{:S(2)}, u32[]{:S(2)}) async-start(f32[8,128,512]{2,1,0:T(8,128)} %get-tuple-element.57), calls=%async_computation.1 | async-start | bytes 4194304 | tf_op jit(solution)/shard_map/all_to_all | solution.py:557
  85.8 8.5 %collective-permute-start.15 = (bf16[192,512]{1,0:T(8,128)(2,1)S(1)}, bf16[192,512]{1,0:T(8,128)(2,1)S(1)}, u32[]{:S(2)}, u32[]{:S(2)}) collective-permute-start(bf16[192,512]{1,0:T(8,128)(2,1)S(1)} %get-tuple-element.60.refs_0_), channel_id=1, source_target_pairs={{0,32},{32,64},{64,96},{96,0},{1,33},{33,65},{65,97},{97,1},{2,34}... | collective-permute-start | bytes 589832 | tf_op jit(solution)/shard_map/ppermute | solution.py:549
  87.1 11.2 %collective-permute-start.16 = (bf16[192,512]{1,0:T(8,128)(2,1)S(1)}, bf16[192,512]{1,0:T(8,128)(2,1)S(1)}, u32[]{:S(2)}, u32[]{:S(2)}) collective-permute-start(bf16[192,512]{1,0:T(8,128)(2,1)S(1)} %get-tuple-element.60.refs_0_), channel_id=1, source_target_pairs={{0,64},{32,96},{64,0},{96,32},{1,65},{33,97},{65,1},{97,33},{2,66}... | collective-permute-start | bytes 589832 | tf_op jit(solution)/shard_map/ppermute | solution.py:549
  89.5 9.0 %collective-permute-start.17 = (bf16[192,512]{1,0:T(8,128)(2,1)S(1)}, bf16[192,512]{1,0:T(8,128)(2,1)S(1)}, u32[]{:S(2)}, u32[]{:S(2)}) collective-permute-start(bf16[192,512]{1,0:T(8,128)(2,1)S(1)} %get-tuple-element.60.refs_0_), channel_id=1, source_target_pairs={{0,96},{32,0},{64,32},{96,64},{1,97},{33,1},{65,33},{97,65},{2,98}... | collective-permute-start | bytes 589832 | tf_op jit(solution)/shard_map/ppermute | solution.py:549
  91.6 7.3 %collective-permute-start.18 = (bf16[192,512]{1,0:T(8,128)(2,1)S(1)}, bf16[192,512]{1,0:T(8,128)(2,1)S(1)}, u32[]{:S(2)}, u32[]{:S(2)}) collective-permute-start(bf16[192,512]{1,0:T(8,128)(2,1)S(1)} %get-tuple-element.60.refs_0_), channel_id=1, source_target_pairs={{0,8},{8,0},{1,9},{9,1},{2,10},{10,2},{3,11},{11,3},{4,12},{12,4},... | collective-permute-start | bytes 589832 | tf_op jit(solution)/shard_map/ppermute | solution.py:544
  121.9 22.0 %all-to-all-start.2 = ((bf16[8,576,128]{2,1,0:T(8,128)(2,1)}), bf16[8,576,128]{2,1,0:T(8,128)(2,1)S(1)}, u32[]{:S(2)}, u32[]{:S(2)}) async-start(bf16[8,576,128]{2,1,0:T(8,128)(2,1)} %get-tuple-element.61), calls=%async_computation.2 | async-start | bytes 2359296 | tf_op jit(solution)/shard_map/all_to_all | solution.py:557
  127.5 8.5 %collective-permute-start.23 = (bf16[192,512]{1,0:T(8,128)(2,1)S(1)}, bf16[192,512]{1,0:T(8,128)(2,1)S(1)}, u32[]{:S(2)}, u32[]{:S(2)}) collective-permute-start(bf16[192,512]{1,0:T(8,128)(2,1)S(1)} %get-tuple-element.104), channel_id=1, source_target_pairs={{0,32},{32,64},{64,96},{96,0},{1,33},{33,65},{65,97},{97,1},{2,34}... | collective-permute-start | bytes 589832 | tf_op jit(solution)/shard_map/ppermute | solution.py:549
  128.9 11.6 %collective-permute-start.24 = (bf16[192,512]{1,0:T(8,128)(2,1)S(1)}, bf16[192,512]{1,0:T(8,128)(2,1)S(1)}, u32[]{:S(2)}, u32[]{:S(2)}) collective-permute-start(bf16[192,512]{1,0:T(8,128)(2,1)S(1)} %get-tuple-element.103), channel_id=1, source_target_pairs={{0,64},{32,96},{64,0},{96,32},{1,65},{33,97},{65,1},{97,33},{2,66}... | collective-permute-start | bytes 589832 | tf_op jit(solution)/shard_map/ppermute | solution.py:549
  131.2 9.9 %collective-permute-start.25 = (bf16[192,512]{1,0:T(8,128)(2,1)S(1)}, bf16[192,512]{1,0:T(8,128)(2,1)S(1)}, u32[]{:S(2)}, u32[]{:S(2)}) collective-permute-start(bf16[192,512]{1,0:T(8,128)(2,1)S(1)} %get-tuple-element.102), channel_id=1, source_target_pairs={{0,96},{32,0},{64,32},{96,64},{1,97},{33,1},{65,33},{97,65},{2,98}... | collective-permute-start | bytes 589832 | tf_op jit(solution)/shard_map/ppermute | solution.py:549
  149.5 17.4 %collective-permute-start.28 = (bf16[4,256,512]{2,1,0:T(8,128)(2,1)}, bf16[4,256,512]{2,1,0:T(8,128)(2,1)}, u32[]{:S(2)}, u32[]{:S(2)}) collective-permute-start(bf16[4,256,512]{2,1,0:T(8,128)(2,1)} %get-tuple-element.81), channel_id=1, source_target_pairs={{0,8},{8,0},{1,9},{9,1},{2,10},{10,2},{3,11},{11,3},{4,12},{12,4},... | collective-permute-start | bytes 3145736 | tf_op jit(solution)/shard_map/ppermute | solution.py:544
  161.9 42.5 %all-to-all-start.3 = ((bf16[8,64,1024]{2,1,0:T(8,128)(2,1)}), bf16[8,64,1024]{2,1,0:T(8,128)(2,1)S(1)}, u32[]{:S(2)}, u32[]{:S(2)}) async-start(bf16[8,64,1024]{2,1,0:T(8,128)(2,1)} %shard_map.204), calls=%async_computation.3 | async-start | bytes 2097152 | tf_op jit(solution)/shard_map/all_to_all | solution.py:557
  168.4 15.6 %collective-permute-start.29 = (bf16[256,512]{1,0:T(8,128)(2,1)S(1)}, bf16[256,512]{1,0:T(8,128)(2,1)S(1)}, u32[]{:S(2)}, u32[]{:S(2)}) collective-permute-start(bf16[256,512]{1,0:T(8,128)(2,1)S(1)} %get-tuple-element.100), channel_id=1, source_target_pairs={{0,32},{32,64},{64,96},{96,0},{1,33},{33,65},{65,97},{97,1},{2,34}... | collective-permute-start | bytes 786440 | tf_op jit(solution)/shard_map/ppermute | solution.py:549
  176.2 12.7 %collective-permute-start.30 = (bf16[256,512]{1,0:T(8,128)(2,1)S(1)}, bf16[256,512]{1,0:T(8,128)(2,1)S(1)}, u32[]{:S(2)}, u32[]{:S(2)}) collective-permute-start(bf16[256,512]{1,0:T(8,128)(2,1)S(1)} %get-tuple-element.99), channel_id=1, source_target_pairs={{0,64},{32,96},{64,0},{96,32},{1,65},{33,97},{65,1},{97,33},{2,66}... | collective-permute-start | bytes 786440 | tf_op jit(solution)/shard_map/ppermute | solution.py:549
  179.2 9.7 %collective-permute-start.31 = (bf16[256,512]{1,0:T(8,128)(2,1)S(1)}, bf16[256,512]{1,0:T(8,128)(2,1)S(1)}, u32[]{:S(2)}, u32[]{:S(2)}) collective-permute-start(bf16[256,512]{1,0:T(8,128)(2,1)S(1)} %get-tuple-element.98), channel_id=1, source_target_pairs={{0,96},{32,0},{64,32},{96,64},{1,97},{33,1},{65,33},{97,65},{2,98}... | collective-permute-start | bytes 786440 | tf_op jit(solution)/shard_map/ppermute | solution.py:549
  (41 other events, 594.7 us)

commit v7 on v6

--- a/solution.py
+++ b/solution.py
@@ -109,6 +109,11 @@
     return pairs
 
 
+def unpack_weights(core, y_index, shards, outs, counts):
+    for source, target in weight_pairs(core, y_index, shards, outs, counts):
+        target[...] = source[...]
+
+
 def pack_grads(core, y_index, grads, keep, send, counts):
     total = sum(counts)
     y_count = keep.shape[0]
@@ -129,13 +134,27 @@
     pairs = list(zip(weights, held))
     for j in range(HB):
         part = pl.ds(j * BLK, BLK)
-        pairs.append((turned.at[:, block_at(halo[j])], up.at[:, part]))
-        pairs.append((turned.at[:, block_at(halo[HB + j])], down.at[:, part]))
+        pairs.append((turned.at[:, block_at(halo[0, 0, j])], up.at[:, part]))
+        pairs.append((turned.at[:, block_at(halo[0, 1, j])], down.at[:, part]))
     wait_all(copies(pairs, sems))
     parts = [ref[...].astype(F32) for ref in held]
     used = sum(part.shape[0] for part in parts)
     parts.append(jnp.zeros((packed.shape[0] - used, L), F32))
     packed[...] = jnp.concatenate(parts, axis=0).astype(BF)
+
+
+def fill_message(lower, turned, upper, cot, out, table, held, in_sems, sems):
+    rows, halo_rows = turned.shape[1], lower.shape[1]
+    loads = copies([(turned, table.at[:, pl.ds(halo_rows, rows)]), (cot, held)], in_sems)
+    table[:, pl.ds(0, halo_rows)] = lower[...]
+    table[:, pl.ds(halo_rows + rows, halo_rows)] = upper[...]
+    wait_all(loads)
+    pairs = []
+    for l in range(out.shape[0]):
+        pairs.append((table, out.at[l, :, pl.ds(0, table.shape[1])]))
+        part = out.at[l, :, pl.ds(table.shape[1], BLK)]
+        pairs.append((held.at[:, pl.ds(l * BLK, BLK)], part))
+    wait_all(copies(pairs, sems))
 
 
 def assemble(pieces, scal, *refs):
@@ -212,7 +231,6 @@
     lat_index, core, y_index, count = (scal[2 * tiles + i] for i in range(4))
     slabs = w_in.shape[0] // 3 // 32
     counts = (3 * L // slabs, L // slabs)
-    loads = copies(weight_pairs(core, y_index, shards, (w_in, w_out), counts), sems)
     stores = []
 
     def store(source, target):
@@ -222,7 +240,7 @@
 
     store(ext.at[:, block_at(HB + lat_index)], own_out)
     store(ext.at[:, pl.ds(ext.shape[1] - BLK, BLK)], up_out)
-    joined[:, pl.ds(0, L)] = edges[...]
+    loads = copies([(edges, joined.at[:, pl.ds(0, L)])], sems)
     for t in range(tiles):
         rows = pl.ds(t * BLK, BLK)
         to_src = one_hot_columns(offsets[1, pl.ds(t, 1), :]).T.astype(BF)
@@ -230,8 +248,9 @@
         src, dst = block_at(scal[tiles + t]), block_at(scal[t] + HB)
         joined[rows, pl.ds(L, L)] = dot_transpose(to_src, ext[:, src]).astype(BF)
         joined[rows, pl.ds(2 * L, L)] = dot_transpose(to_dst, ext[:, dst]).astype(BF)
+    wait_all(loads)
     store(joined, joined_out)
-    wait_all(loads)
+    unpack_weights(core, y_index, shards, (w_in, w_out), counts)
     for n in range(2):
         columns = pl.ds(n * 256, 256)
         first[:, columns] = jnp.maximum(dot(joined[...], w_in[:, columns]), 0.0).astype(BF)
@@ -247,7 +266,7 @@
         normed[rows, :] = values
         inverse[rows, :] = jnp.broadcast_to(inv, (BLK, BLK))
         message = values * gain[...] * live
-        new_edges[rows, :] = (edges[rows, :].astype(F32) + message).astype(BF)
+        new_edges[rows, :] = (joined[rows, pl.ds(0, L)].astype(F32) + message).astype(BF)
         second[rows, :] = message
     store(normed, normed_out)
     store(inverse, inverse_out)
@@ -270,10 +289,9 @@
     core, y_index = scal[1], scal[2]
     slabs = w_in.shape[0] // 2 // 32
     counts = (2 * L // slabs, L // slabs)
-    pairs = [(own_hbm, own_turned), (up_hbm, up_turned)]
-    pairs += weight_pairs(core, y_index, shards, (w_in, w_out), counts)
-    loads = copies(pairs, sems)
-    wait_all(loads[:2])
+    loads = copies([(own_hbm, own_turned), (up_hbm, up_turned)], sems)
+    unpack_weights(core, y_index, shards, (w_in, w_out), counts)
+    wait_all(loads)
     own = own_turned[...].astype(F32).T
     upstream = up_turned[...].astype(F32).T
     joined[:, pl.ds(0, L)] = own.astype(BF)
@@ -281,7 +299,6 @@
     for l in range(1, spread.shape[0]):
         total = total + spread[l]
     joined[:, pl.ds(L, L)] = total.astype(BF)
-    wait_all(loads[2:])
     first[...] = jnp.maximum(dot(joined[...], w_in[...]), 0.0).astype(BF)
     normed, inverse = norm_parts(dot(first[...], w_out[...]))
     d_second[...] = norm_back(upstream, normed, inverse, gain[...]).astype(BF)
@@ -388,7 +405,7 @@
 def add_halo(halo, middle, above, below, columns, held):
     held[...] = middle[...]
     for j in range(HB):
-        for place, value in ((halo[j], above), (halo[HB + j], below)):
+        for place, value in ((halo[0, 0, j], above), (halo[0, 1, j], below)):
             held[place] = held[place] + value[:, pl.ds(j * BLK, BLK)].astype(F32)
     width = columns.shape[1]
     for block in range(held.shape[0]):
@@ -447,11 +464,11 @@
         outs,
         held + [((3 * L, L), BF), ((L, L), BF), ((rows, L), F32)],
         EDGE_MIB,
-        "svvv" + "h" * len(shards) + "v",
+        "svhv" + "v" * len(shards) + "v",
         (scal, ext, edges, offsets, *shards, gain),
         flops=2 * rows * 4 * L * L,
         out_spaces="h" * len(outs),
-        sems=(4 * len(shards), len(outs)),
+        sems=(1, len(outs)),
     )
 
 
@@ -466,11 +483,11 @@
         + rows
         + [((L, BLK), F32)],
         NODE_MIB,
-        "svhh" + "h" * len(shards) + "v",
+        "svhh" + "v" * len(shards) + "v",
         (scal, spread, own, up, *shards, gain),
         flops=2 * BLK * 6 * L * L,
         out_spaces="vhhhhh",
-        sems=(2 + 4 * len(shards), 5),
+        sems=(2, 5),
     )
 
 
@@ -598,7 +615,7 @@
     near_scal = jnp.stack([lax.axis_index("z"), lax.axis_index(XS)]).astype(jnp.int32)
     node_scal = jnp.stack(place).astype(jnp.int32)
     scal = jnp.concatenate([edge_tiles.reshape(-1), node_scal, tile_counts])
-    halo = halo_blocks.reshape(-1)
+    halo = halo_blocks
     offsets = edge_offsets.reshape(2, -1, BLK)
     edge_gain_row = edge_gain.reshape(1, L)
     node_gain_row = node_gain.reshape(1, L)
@@ -620,10 +637,15 @@
     from_lower = from_behind(up, 1)
     from_upper = from_behind(down, -1)
 
-    table = jnp.concatenate([from_lower, turned, from_upper], axis=1)
-    cot = node_cotangent.T.reshape(width, lat_size, own_rows).transpose(1, 0, 2)
-    message_out = jnp.concatenate(
-        [jnp.broadcast_to(table, (lat_size,) + table.shape), cot], axis=2
+    (message_out,) = call(
+        fill_message,
+        [shape_of((lat_size, width, ext_rows + own_rows), BF)],
+        [((width, ext_rows), BF), ((width, slab_rows), BF)],
+        4,
+        "vhvh",
+        (from_lower, turned, from_upper, node_cotangent.T),
+        out_spaces="h",
+        sems=(2, 2 * lat_size),
     )
     by_x = jnp.concatenate(shifts(packed, XS), axis=0)
     near = shifts(by_x, "z")
@@ -653,7 +675,6 @@
     second_in = spread_rows(second_out, LAT)
     new_nodes = second_in[:, L:].transpose(1, 0, 2).reshape(width, slab_rows).T
     node_far = reduce_far(node_keep, node_send)
-    second_in, *node_far = lax.optimization_barrier((second_in, *node_far))
 
     d_first, edge_keep, edge_send = run_edge_backward(
         scal, second_in, edge_cotangent, offsets, edge_gain_row,

time: 211 us -> 221 us (1.047)
  blocking collectives: 0 us -> 23.5 us
  starting transfers between devices: 81.1 us -> 73.3 us
  waiting for transfers between devices: 82.9 us -> 79.8 us
    all_to_all x0 -> x1, blocking collectives: none -> 23.5 us  [spread_rows(): return lax.all_to_all(value, axes, 0, 0)]
    all_to_all x4 -> x3, starting transfers between devices: 21.9 us -> 15.8 us  [spread_rows(): return lax.all_to_all(value, axes, 0, 0)]
    all_to_all x4 -> x3, waiting for transfers between devices: 14.1 us -> 11.8 us  [spread_rows(): return lax.all_to_all(value, axes, 0, 0)]
    concatenate x2 -> x0, other arithmetic: 2.28 us -> none  [the longest x1 1.36 us: per_device(): jnp.concatenate([jnp.broadcast_to(table, (lat_size,) + table.shape), cot]...]
    pallas_call x12 -> x13, Pallas kernels: 34.2 us -> 33.7 us  [call(): pl.pallas_call(kernel, out_shape=placed, in_specs=[pl.BlockSpec(memory_sp...]
  transfers between devices with their start and end apart: 42 -> 41, of which waited for: 24 -> 22; matrix products, arithmetic and copies ran while one was open for 2% -> 2% of each run, Pallas kernels for 5% -> 6%
where the time goes in v7:
time: 221 us; the launch traced here: 219 us
  waiting for transfers between devices  79.8 us (36%)
  starting transfers between devices  73.3 us (33%)
  Pallas kernels  33.7 us (15%)
  blocking collectives  23.5 us (11%)
  local copies, waits for them, and re-layouts  4.09 us (2%)
  other arithmetic  3.3 us (1%)
    ppermute x24, waiting for transfers between devices, shift(): lax.ppermute(value, axes, [(i, (i + step) % count) for i in range(count)])  61.5 us
    ppermute x24, starting transfers between devices, shift(): lax.ppermute(value, axes, [(i, (i + step) % count) for i in range(count)])  49.1 us
    pallas_call x13, Pallas kernels, call(): pl.pallas_call(kernel, out_shape=placed, in_specs=[pl.BlockSpec(memory_sp...  33.7 us
    all_to_all x1, blocking collectives, spread_rows(): return lax.all_to_all(value, axes, 0, 0)  23.5 us
    all_to_all x3, starting transfers between devices, spread_rows(): return lax.all_to_all(value, axes, 0, 0)  15.8 us
    all_to_all x3, waiting for transfers between devices, spread_rows(): return lax.all_to_all(value, axes, 0, 0)  11.8 us
    ppermute x4, starting transfers between devices, from_behind(): lax.ppermute(value, SLAB, [(source, source + steps) for source in range(f...  6.92 us
    ppermute x4, waiting for transfers between devices, from_behind(): lax.ppermute(value, SLAB, [(source, source + steps) for source in range(f...  4.75 us
  transfers between devices with their start and end apart: 41, of which 22 were waited for; matrix products, arithmetic and copies ran while one was open for 2% of the time, Pallas kernels for 6%

profile of v7, /device:TPU:0, one launch (start us, length us, event | category | flops | bytes accessed | tf_op | source)
XLA Modules:
  0.0 219.3 jit_solution(2685470399463718387)
XLA Ops:
  5.4 3.6 %collective-permute-done.1.upper = bf16[64,256]{1,0:T(8,128)(2,1)S(1)} collective-permute-done((bf16[64,256]{1,0:T(8,128)(2,1)S(1)}, bf16[64,256]{1,0:T(8,128)(2,1)S(1)}, u32[]{:S(2)}, u32[]{:S(2)}) %collective-permute-start.1) | collective-permute-done | bytes 32800 | tf_op jit(solution)/shard_map/ppermute | solution.py:33
  11.4 7.6 %all-to-all-start = ((bf16[8,64,1664]{2,1,0:T(8,128)(2,1)}), bf16[8,64,1664]{2,1,0:T(8,128)(2,1)S(1)}, u32[]{:S(2)}, u32[]{:S(2)}) async-start(bf16[8,64,1664]{2,1,0:T(8,128)(2,1)} %shard_map.198), calls=%async_computation | async-start | bytes 3407872 | tf_op jit(solution)/shard_map/all_to_all | solution.py:574
  19.0 3.5 %collective-permute-start.2 = (bf16[32,512]{1,0:T(8,128)(2,1)S(1)}, bf16[32,512]{1,0:T(8,128)(2,1)S(1)}, u32[]{:S(2)}, u32[]{:S(2)}) collective-permute-start(bf16[32,512]{1,0:T(8,128)(2,1)S(1)} %get-tuple-element.50), channel_id=1, source_target_pairs={{0,4},{4,16},{16,20},{20,0},{1,5},{5,17},{17,21},{21,1},{2,6},{6,1... | collective-permute-start | bytes 98312 | tf_op jit(solution)/shard_map/ppermute | solution.py:566
  24.5 19.0 %collective-permute-done.2 = bf16[32,512]{1,0:T(8,128)(2,1)S(1)} collective-permute-done((bf16[32,512]{1,0:T(8,128)(2,1)S(1)}, bf16[32,512]{1,0:T(8,128)(2,1)S(1)}, u32[]{:S(2)}, u32[]{:S(2)}) %collective-permute-start.2) | collective-permute-done | bytes 32800 | tf_op jit(solution)/shard_map/ppermute | solution.py:566
  50.5 3.7 %collective-permute-done.6.refs_2_ = bf16[128,512]{1,0:T(8,128)(2,1)S(1)} collective-permute-done((bf16[128,512]{1,0:T(8,128)(2,1)S(1)}, bf16[128,512]{1,0:T(8,128)(2,1)S(1)}, u32[]{:S(2)}, u32[]{:S(2)}) %collective-permute-start.6) | collective-permute-done | bytes 131104 | tf_op jit(solution)/shard_map/ppermute | solution.py:566
  54.9 2.8 %collective-permute-start.8 = (bf16[256,512]{1,0:T(8,128)(2,1)S(1)}, bf16[256,512]{1,0:T(8,128)(2,1)S(1)}, u32[]{:S(2)}, u32[]{:S(2)}) collective-permute-start(bf16[256,512]{1,0:T(8,128)(2,1)S(1)} %get-tuple-element.51.refs_0_.refs_4_), channel_id=1, source_target_pairs={{0,32},{32,64},{64,96},{96,0},{1,33},{33,65},{65,97},{97,1},{2,34}... | collective-permute-start | bytes 786440 | tf_op jit(solution)/shard_map/ppermute | solution.py:566
  57.7 2.9 %collective-permute-start.9 = (bf16[256,512]{1,0:T(8,128)(2,1)S(1)}, bf16[256,512]{1,0:T(8,128)(2,1)S(1)}, u32[]{:S(2)}, u32[]{:S(2)}) collective-permute-start(bf16[256,512]{1,0:T(8,128)(2,1)S(1)} %get-tuple-element.51.refs_0_.refs_4_), channel_id=1, source_target_pairs={{0,64},{32,96},{64,0},{96,32},{1,65},{33,97},{65,1},{97,33},{2,66}... | collective-permute-start | bytes 786440 | tf_op jit(solution)/shard_map/ppermute | solution.py:566
  61.9 3.4 %collective-permute-done.8.refs_1_.refs_5_ = bf16[256,512]{1,0:T(8,128)(2,1)S(1)} collective-permute-done((bf16[256,512]{1,0:T(8,128)(2,1)S(1)}, bf16[256,512]{1,0:T(8,128)(2,1)S(1)}, u32[]{:S(2)}, u32[]{:S(2)}) %collective-permute-start.8) | collective-permute-done | bytes 262176 | tf_op jit(solution)/shard_map/ppermute | solution.py:566
  65.4 5.8 %collective-permute-done.9.refs_2_.refs_6_ = bf16[256,512]{1,0:T(8,128)(2,1)S(1)} collective-permute-done((bf16[256,512]{1,0:T(8,128)(2,1)S(1)}, bf16[256,512]{1,0:T(8,128)(2,1)S(1)}, u32[]{:S(2)}, u32[]{:S(2)}) %collective-permute-start.9) | collective-permute-done | bytes 262176 | tf_op jit(solution)/shard_map/ppermute | solution.py:566
  73.2 6.3 %shard_map.200 = (bf16[512,1536]{1,0:T(8,128)(2,1)}, bf16[512,512]{1,0:T(8,128)(2,1)}, f32[512,512]{1,0:T(8,128)}, f32[512,128]{1,0:T(8,128)}, bf16[512,512]{1,0...) custom-call(s32[12]{0:T(128)S(1)} %concatenate.7.scal, ...), custom_call_target="tpu_custom_call" | custom-call | flops 1073741824 | bytes 10623024 | tf_op jit(solution)/shard_map/pallas_call | solution.py:438
  79.6 4.6 %all-to-all-start.1 = ((f32[8,128,512]{2,1,0:T(8,128)}), f32[8,128,512]{2,1,0:T(8,128)S(1)}, u32[]{:S(2)}, u32[]{:S(2)}) async-start(f32[8,128,512]{2,1,0:T(8,128)} %get-tuple-element.52), calls=%async_computation.1 | async-start | bytes 4194304 | tf_op jit(solution)/shard_map/all_to_all | solution.py:574
  92.7 4.0 %collective-permute-done.16.refs_2_ = bf16[192,512]{1,0:T(8,128)(2,1)S(1)} collective-permute-done((bf16[192,512]{1,0:T(8,128)(2,1)S(1)}, bf16[192,512]{1,0:T(8,128)(2,1)S(1)}, u32[]{:S(2)}, u32[]{:S(2)}) %collective-permute-start.16) | collective-permute-done | bytes 196640 | tf_op jit(solution)/shard_map/ppermute | solution.py:566
  99.1 11.8 %all-to-all-done.1.spread = f32[8,128,512]{2,1,0:T(8,128)S(1)} async-done(((f32[8,128,512]{2,1,0:T(8,128)}), f32[8,128,512]{2,1,0:T(8,128)S(1)}, u32[]{:S(2)}, u32[]{:S(2)}) %all-to-all-start.1) | async-done | bytes 2097184 | tf_op jit(solution)/shard_map/all_to_all | solution.py:574
  111.8 4.0 %shard_map.201 = (bf16[8,576,128]{2,1,0:T(8,128)(2,1)S(1)}, f32[512,128]{1,0:T(8,128)}, bf16[128,1024]{1,0:T(8,128)(2,1)}, bf16[128,512]{1,0:T(8,128)(2,1)}, bf1...) custom-call(s32[3]{0:T(128)S(1)} %pad_add_fusion.scal, f32[8,128,512]{2,1,0:T(8,128)S(1)} %all-to-all-done.1.spread, ...), custom_call_target="tpu_custom_call" | custom-call | flops 402653184 | bytes 6031372 | tf_op jit(solution)/shard_map/pallas_call | solution.py:438
  115.9 23.5 %all_to_all.20.d_agg = bf16[8,576,128]{2,1,0:T(8,128)(2,1)S(1)} all-to-all(bf16[8,576,128]{2,1,0:T(8,128)(2,1)S(1)} %get-tuple-element.56), channel_id=1, replica_groups=mesh['y'=4,'xl'=2,'c'=2,'xh'=2,'z'=4] {'xh','z'}, dimensions={0} | all-to-all | bytes 2359296 | tf_op jit(solution)/shard_map/all_to_all | solution.py:574
  139.4 5.7 %shard_map.202 = (bf16[512,512]{1,0:T(8,128)(2,1)S(1)}, bf16[4,256,512]{2,1,0:T(8,128)(2,1)S(1)}, bf16[4,256,512]{2,1,0:T(8,128)(2,1)}) custom-call(s32[12]{0:T(128)S(1)} %concatenate.7.scal, bf16[8,576,128]{2,1,0:T(8,128)(2,1)S(1)} %all_to_all.20.d_agg, bf16[512,512]{1,0:T(8,128)(2,1)S(1)} %copy-done.6, s32[2,4,128]{2,1,0:T(4,128)S(1)} %reshape.68.offsets, ...), custom_call_target="tpu_custom_call" | custom-call | flops 1342177280 | bytes 9836592 | tf_op jit(solution)/shard_map/pallas_call | solution.py:438
  145.1 3.3 %shard_map.206 = (bf16[4,192,512]{2,1,0:T(8,128)(2,1)S(1)}, bf16[4,192,512]{2,1,0:T(8,128)(2,1)}) custom-call(s32[3]{0:T(128)S(1)} %pad_add_fusion.scal, bf16[128,1024]{1,0:T(8,128)(2,1)} %get-tuple-element.70.refs_0_, bf16[128,512]{1,0:T(8,128)(2,1)} %get-tuple-element.71.refs_1_, bf16[128,512]{1,0:T(8,128)(2,1)} %get-tuple-element.72.refs_2_, ...), custom_call_target="tpu_custom_call" | custom-call | flops 201326592 | bytes 2228236 | tf_op jit(solution)/shard_map/pallas_call | solution.py:438
  149.8 4.8 %shard_map.203 = (bf16[512,512]{1,0:T(8,128)(2,1)}, f32[8,512,128]{2,1,0:T(8,128)S(1)}, bf16[512,256]{1,0:T(8,128)(2,1)S(1)}, bf16[512,256]{1,0:T(8,128)(2,1)S(1)}) custom-call(s32[12]{0:T(128)S(1)} %concatenate.7.scal, bf16[512,512]{1,0:T(8,128)(2,1)S(1)} %get-tuple-element.62.d_first, bf16[512,512]{1,0:T(8,128)(2,1)S(1)} %copy-done.6, ...), custom_call_target="tpu_custom_call" | custom-call | flops 805306368 | bytes 6557744 | tf_op jit(solution)/shard_map/pallas_call | solution.py:438
  155.9 3.0 %collective-permute-start.23 = (bf16[512,256]{1,0:T(8,128)(2,1)S(1)}, bf16[512,256]{1,0:T(8,128)(2,1)S(1)}, u32[]{:S(2)}, u32[]{:S(2)}) collective-permute-start(bf16[512,256]{1,0:T(8,128)(2,1)S(1)} %get-tuple-element.66), channel_id=1, source_target_pairs={{0,8},{8,16},{16,24},{24,32},{32,40},{40,48},{48,56},{56,64},{64,7... | collective-permute-start | bytes 786440 | tf_op jit(solution)/shard_map/ppermute | solution.py:33
  162.1 3.6 %all-to-all-start.3 = ((bf16[8,64,1024]{2,1,0:T(8,128)(2,1)}), bf16[8,64,1024]{2,1,0:T(8,128)(2,1)S(1)}, u32[]{:S(2)}, u32[]{:S(2)}) async-start(bf16[8,64,1024]{2,1,0:T(8,128)(2,1)} %shard_map.204), calls=%async_computation.3 | async-start | bytes 2097152 | tf_op jit(solution)/shard_map/all_to_all | solution.py:574
  167.4 6.7 %collective-permute-start.29 = (bf16[192,512]{1,0:T(8,128)(2,1)S(1)}, bf16[192,512]{1,0:T(8,128)(2,1)S(1)}, u32[]{:S(2)}, u32[]{:S(2)}) collective-permute-start(bf16[192,512]{1,0:T(8,128)(2,1)S(1)} %get-tuple-element.94), channel_id=1, source_target_pairs={{0,32},{32,64},{64,96},{96,0},{1,33},{33,65},{65,97},{97,1},{2,34}... | collective-permute-start | bytes 589832 | tf_op jit(solution)/shard_map/ppermute | solution.py:566
  183.7 12.1 %collective-permute-done.30.n2 = bf16[192,512]{1,0:T(8,128)(2,1)S(1)} collective-permute-done((bf16[192,512]{1,0:T(8,128)(2,1)S(1)}, bf16[192,512]{1,0:T(8,128)(2,1)S(1)}, u32[]{:S(2)}, u32[]{:S(2)}) %collective-permute-start.30) | collective-permute-done | bytes 196640 | tf_op jit(solution)/shard_map/ppermute | solution.py:566
  208.7 3.1 %collective-permute-start.35 = (bf16[32,512]{1,0:T(8,128)(2,1)S(1)}, bf16[32,512]{1,0:T(8,128)(2,1)S(1)}, u32[]{:S(2)}, u32[]{:S(2)}) collective-permute-start(bf16[32,512]{1,0:T(8,128)(2,1)S(1)} %get-tuple-element.81), channel_id=1, source_target_pairs={{0,4},{4,16},{16,20},{20,0},{1,5},{5,17},{17,21},{21,1},{2,6},{6,1... | collective-permute-start | bytes 98312 | tf_op jit(solution)/shard_map/ppermute | solution.py:566
  215.6 3.0 %collective-permute-done.37.r3 = bf16[32,512]{1,0:T(8,128)(2,1)S(1)} collective-permute-done((bf16[32,512]{1,0:T(8,128)(2,1)S(1)}, bf16[32,512]{1,0:T(8,128)(2,1)S(1)}, u32[]{:S(2)}, u32[]{:S(2)}) %collective-permute-start.37) | collective-permute-done | bytes 32800 | tf_op jit(solution)/shard_map/ppermute | solution.py:566
  (116 shorter events, 65.8 us)
Async XLA Ops:
  11.4 61.8 %all-to-all-start = ((bf16[8,64,1664]{2,1,0:T(8,128)(2,1)}), bf16[8,64,1664]{2,1,0:T(8,128)(2,1)S(1)}, u32[]{:S(2)}, u32[]{:S(2)}) async-start(bf16[8,64,1664]{2,1,0:T(8,128)(2,1)} %shard_map.198), calls=%async_computation | async-start | bytes 3407872 | tf_op jit(solution)/shard_map/all_to_all | solution.py:574
  19.0 24.5 %collective-permute-start.2 = (bf16[32,512]{1,0:T(8,128)(2,1)S(1)}, bf16[32,512]{1,0:T(8,128)(2,1)S(1)}, u32[]{:S(2)}, u32[]{:S(2)}) collective-permute-start(bf16[32,512]{1,0:T(8,128)(2,1)S(1)} %get-tuple-element.50), channel_id=1, source_target_pairs={{0,4},{4,16},{16,20},{20,0},{1,5},{5,17},{17,21},{21,1},{2,6},{6,1... | collective-permute-start | bytes 98312 | tf_op jit(solution)/shard_map/ppermute | solution.py:566
  22.6 21.0 %collective-permute-start.3 = (bf16[32,512]{1,0:T(8,128)(2,1)S(1)}, bf16[32,512]{1,0:T(8,128)(2,1)S(1)}, u32[]{:S(2)}, u32[]{:S(2)}) collective-permute-start(bf16[32,512]{1,0:T(8,128)(2,1)S(1)} %get-tuple-element.50), channel_id=1, source_target_pairs={{0,16},{4,20},{16,0},{20,4},{1,17},{5,21},{17,1},{21,5},{2,18},{6,... | collective-permute-start | bytes 98312 | tf_op jit(solution)/shard_map/ppermute | solution.py:566
  24.5 19.1 %collective-permute-start.4 = (bf16[32,512]{1,0:T(8,128)(2,1)S(1)}, bf16[32,512]{1,0:T(8,128)(2,1)S(1)}, u32[]{:S(2)}, u32[]{:S(2)}) collective-permute-start(bf16[32,512]{1,0:T(8,128)(2,1)S(1)} %get-tuple-element.50), channel_id=1, source_target_pairs={{0,20},{4,0},{16,4},{20,16},{1,21},{5,1},{17,5},{21,17},{2,22},{6,... | collective-permute-start | bytes 98312 | tf_op jit(solution)/shard_map/ppermute | solution.py:566
  45.1 9.1 %collective-permute-start.6 = (bf16[128,512]{1,0:T(8,128)(2,1)S(1)}, bf16[128,512]{1,0:T(8,128)(2,1)S(1)}, u32[]{:S(2)}, u32[]{:S(2)}) collective-permute-start(bf16[128,512]{1,0:T(8,128)(2,1)S(1)} %constant_dynamic-update-slice_fusion.refs_0_), channel_id=1, source_target_pairs={{0,2},{1,3},{2,0},{3,1},{4,6},{5,7},{6,4},{7,5},{8,10},{9,11},{10,... | collective-permute-start | bytes 393224 | tf_op jit(solution)/shard_map/ppermute | solution.py:566
  54.9 10.5 %collective-permute-start.8 = (bf16[256,512]{1,0:T(8,128)(2,1)S(1)}, bf16[256,512]{1,0:T(8,128)(2,1)S(1)}, u32[]{:S(2)}, u32[]{:S(2)}) collective-permute-start(bf16[256,512]{1,0:T(8,128)(2,1)S(1)} %get-tuple-element.51.refs_0_.refs_4_), channel_id=1, source_target_pairs={{0,32},{32,64},{64,96},{96,0},{1,33},{33,65},{65,97},{97,1},{2,34}... | collective-permute-start | bytes 786440 | tf_op jit(solution)/shard_map/ppermute | solution.py:566
  57.7 13.5 %collective-permute-start.9 = (bf16[256,512]{1,0:T(8,128)(2,1)S(1)}, bf16[256,512]{1,0:T(8,128)(2,1)S(1)}, u32[]{:S(2)}, u32[]{:S(2)}) collective-permute-start(bf16[256,512]{1,0:T(8,128)(2,1)S(1)} %get-tuple-element.51.refs_0_.refs_4_), channel_id=1, source_target_pairs={{0,64},{32,96},{64,0},{96,32},{1,65},{33,97},{65,1},{97,33},{2,66}... | collective-permute-start | bytes 786440 | tf_op jit(solution)/shard_map/ppermute | solution.py:566
  60.6 10.6 %collective-permute-start.10 = (bf16[256,512]{1,0:T(8,128)(2,1)S(1)}, bf16[256,512]{1,0:T(8,128)(2,1)S(1)}, u32[]{:S(2)}, u32[]{:S(2)}) collective-permute-start(bf16[256,512]{1,0:T(8,128)(2,1)S(1)} %get-tuple-element.51.refs_0_.refs_4_), channel_id=1, source_target_pairs={{0,96},{32,0},{64,32},{96,64},{1,97},{33,1},{65,33},{97,65},{2,98}... | collective-permute-start | bytes 786440 | tf_op jit(solution)/shard_map/ppermute | solution.py:566
  61.9 10.6 %collective-permute-start.11 = (bf16[256,512]{1,0:T(8,128)(2,1)S(1)}, bf16[256,512]{1,0:T(8,128)(2,1)S(1)}, u32[]{:S(2)}, u32[]{:S(2)}) collective-permute-start(bf16[256,512]{1,0:T(8,128)(2,1)S(1)} %get-tuple-element.51.refs_0_.refs_4_), channel_id=1, source_target_pairs={{0,8},{8,0},{1,9},{9,1},{2,10},{10,2},{3,11},{11,3},{4,12},{12,4},... | collective-permute-start | bytes 786440 | tf_op jit(solution)/shard_map/ppermute | solution.py:561
  65.4 7.1 %collective-permute-start.12 = (bf16[256,512]{1,0:T(8,128)(2,1)S(1)}, bf16[256,512]{1,0:T(8,128)(2,1)S(1)}, u32[]{:S(2)}, u32[]{:S(2)}) collective-permute-start(bf16[256,512]{1,0:T(8,128)(2,1)S(1)} %collective-permute-done.8.refs_1_.refs_5_), channel_id=1, source_target_pairs={{0,8},{8,0},{1,9},{9,1},{2,10},{10,2},{3,11},{11,3},{4,12},{12,4},... | collective-permute-start | bytes 786440 | tf_op jit(solution)/shard_map/ppermute | solution.py:561
  79.6 31.3 %all-to-all-start.1 = ((f32[8,128,512]{2,1,0:T(8,128)}), f32[8,128,512]{2,1,0:T(8,128)S(1)}, u32[]{:S(2)}, u32[]{:S(2)}) async-start(f32[8,128,512]{2,1,0:T(8,128)} %get-tuple-element.52), calls=%async_computation.1 | async-start | bytes 4194304 | tf_op jit(solution)/shard_map/all_to_all | solution.py:574
  84.2 8.5 %collective-permute-start.15 = (bf16[192,512]{1,0:T(8,128)(2,1)S(1)}, bf16[192,512]{1,0:T(8,128)(2,1)S(1)}, u32[]{:S(2)}, u32[]{:S(2)}) collective-permute-start(bf16[192,512]{1,0:T(8,128)(2,1)S(1)} %get-tuple-element.55.refs_0_), channel_id=1, source_target_pairs={{0,32},{32,64},{64,96},{96,0},{1,33},{33,65},{65,97},{97,1},{2,34}... | collective-permute-start | bytes 589832 | tf_op jit(solution)/shard_map/ppermute | solution.py:566
  85.5 11.2 %collective-permute-start.16 = (bf16[192,512]{1,0:T(8,128)(2,1)S(1)}, bf16[192,512]{1,0:T(8,128)(2,1)S(1)}, u32[]{:S(2)}, u32[]{:S(2)}) collective-permute-start(bf16[192,512]{1,0:T(8,128)(2,1)S(1)} %get-tuple-element.55.refs_0_), channel_id=1, source_target_pairs={{0,64},{32,96},{64,0},{96,32},{1,65},{33,97},{65,1},{97,33},{2,66}... | collective-permute-start | bytes 589832 | tf_op jit(solution)/shard_map/ppermute | solution.py:566
  87.9 9.0 %collective-permute-start.17 = (bf16[192,512]{1,0:T(8,128)(2,1)S(1)}, bf16[192,512]{1,0:T(8,128)(2,1)S(1)}, u32[]{:S(2)}, u32[]{:S(2)}) collective-permute-start(bf16[192,512]{1,0:T(8,128)(2,1)S(1)} %get-tuple-element.55.refs_0_), channel_id=1, source_target_pairs={{0,96},{32,0},{64,32},{96,64},{1,97},{33,1},{65,33},{97,65},{2,98}... | collective-permute-start | bytes 589832 | tf_op jit(solution)/shard_map/ppermute | solution.py:566
  90.0 7.4 %collective-permute-start.18 = (bf16[192,512]{1,0:T(8,128)(2,1)S(1)}, bf16[192,512]{1,0:T(8,128)(2,1)S(1)}, u32[]{:S(2)}, u32[]{:S(2)}) collective-permute-start(bf16[192,512]{1,0:T(8,128)(2,1)S(1)} %get-tuple-element.55.refs_0_), channel_id=1, source_target_pairs={{0,8},{8,0},{1,9},{9,1},{2,10},{10,2},{3,11},{11,3},{4,12},{12,4},... | collective-permute-start | bytes 589832 | tf_op jit(solution)/shard_map/ppermute | solution.py:561
  145.0 29.1 %collective-permute-start.24 = (bf16[4,256,512]{2,1,0:T(8,128)(2,1)}, bf16[4,256,512]{2,1,0:T(8,128)(2,1)}, u32[]{:S(2)}, u32[]{:S(2)}) collective-permute-start(bf16[4,256,512]{2,1,0:T(8,128)(2,1)} %get-tuple-element.69), channel_id=1, source_target_pairs={{0,8},{8,0},{1,9},{9,1},{2,10},{10,2},{3,11},{11,3},{4,12},{12,4},... | collective-permute-start | bytes 3145736 | tf_op jit(solution)/shard_map/ppermute | solution.py:561
  149.3 16.4 %collective-permute-start.28 = (bf16[4,192,512]{2,1,0:T(8,128)(2,1)}, bf16[4,192,512]{2,1,0:T(8,128)(2,1)}, u32[]{:S(2)}, u32[]{:S(2)}) collective-permute-start(bf16[4,192,512]{2,1,0:T(8,128)(2,1)} %get-tuple-element.75), channel_id=1, source_target_pairs={{0,8},{8,0},{1,9},{9,1},{2,10},{10,2},{3,11},{11,3},{4,12},{12,4},... | collective-permute-start | bytes 2359304 | tf_op jit(solution)/shard_map/ppermute | solution.py:561
  162.1 51.8 %all-to-all-start.3 = ((bf16[8,64,1024]{2,1,0:T(8,128)(2,1)}), bf16[8,64,1024]{2,1,0:T(8,128)(2,1)S(1)}, u32[]{:S(2)}, u32[]{:S(2)}) async-start(bf16[8,64,1024]{2,1,0:T(8,128)(2,1)} %shard_map.204), calls=%async_computation.3 | async-start | bytes 2097152 | tf_op jit(solution)/shard_map/all_to_all | solution.py:574
  167.4 14.5 %collective-permute-start.29 = (bf16[192,512]{1,0:T(8,128)(2,1)S(1)}, bf16[192,512]{1,0:T(8,128)(2,1)S(1)}, u32[]{:S(2)}, u32[]{:S(2)}) collective-permute-start(bf16[192,512]{1,0:T(8,128)(2,1)S(1)} %get-tuple-element.94), channel_id=1, source_target_pairs={{0,32},{32,64},{64,96},{96,0},{1,33},{33,65},{65,97},{97,1},{2,34}... | collective-permute-start | bytes 589832 | tf_op jit(solution)/shard_map/ppermute | solution.py:566
  175.6 22.0 %collective-permute-start.25 = (bf16[256,512]{1,0:T(8,128)(2,1)S(1)}, bf16[256,512]{1,0:T(8,128)(2,1)S(1)}, u32[]{:S(2)}, u32[]{:S(2)}) collective-permute-start(bf16[256,512]{1,0:T(8,128)(2,1)S(1)} %get-tuple-element.90), channel_id=1, source_target_pairs={{0,32},{32,64},{64,96},{96,0},{1,33},{33,65},{65,97},{97,1},{2,34}... | collective-permute-start | bytes 786440 | tf_op jit(solution)/shard_map/ppermute | solution.py:566
  177.2 20.5 %collective-permute-start.26 = (bf16[256,512]{1,0:T(8,128)(2,1)S(1)}, bf16[256,512]{1,0:T(8,128)(2,1)S(1)}, u32[]{:S(2)}, u32[]{:S(2)}) collective-permute-start(bf16[256,512]{1,0:T(8,128)(2,1)S(1)} %get-tuple-element.89), channel_id=1, source_target_pairs={{0,64},{32,96},{64,0},{96,32},{1,65},{33,97},{65,1},{97,33},{2,66}... | collective-permute-start | bytes 786440 | tf_op jit(solution)/shard_map/ppermute | solution.py:566
  178.9 18.7 %collective-permute-start.27 = (bf16[256,512]{1,0:T(8,128)(2,1)S(1)}, bf16[256,512]{1,0:T(8,128)(2,1)S(1)}, u32[]{:S(2)}, u32[]{:S(2)}) collective-permute-start(bf16[256,512]{1,0:T(8,128)(2,1)S(1)} %get-tuple-element.88), channel_id=1, source_target_pairs={{0,96},{32,0},{64,32},{96,64},{1,97},{33,1},{65,33},{97,65},{2,98}... | collective-permute-start | bytes 786440 | tf_op jit(solution)/shard_map/ppermute | solution.py:566
  181.5 14.2 %collective-permute-start.30 = (bf16[192,512]{1,0:T(8,128)(2,1)S(1)}, bf16[192,512]{1,0:T(8,128)(2,1)S(1)}, u32[]{:S(2)}, u32[]{:S(2)}) collective-permute-start(bf16[192,512]{1,0:T(8,128)(2,1)S(1)} %get-tuple-element.93), channel_id=1, source_target_pairs={{0,64},{32,96},{64,0},{96,32},{1,65},{33,97},{65,1},{97,33},{2,66}... | collective-permute-start | bytes 589832 | tf_op jit(solution)/shard_map/ppermute | solution.py:566
  181.9 15.8 %collective-permute-start.31 = (bf16[192,512]{1,0:T(8,128)(2,1)S(1)}, bf16[192,512]{1,0:T(8,128)(2,1)S(1)}, u32[]{:S(2)}, u32[]{:S(2)}) collective-permute-start(bf16[192,512]{1,0:T(8,128)(2,1)S(1)} %get-tuple-element.92), channel_id=1, source_target_pairs={{0,96},{32,0},{64,32},{96,64},{1,97},{33,1},{65,33},{97,65},{2,98}... | collective-permute-start | bytes 589832 | tf_op jit(solution)/shard_map/ppermute | solution.py:566
  (33 other events, 396.2 us)

commit v8 on v7

--- a/solution.py
+++ b/solution.py
@@ -328,18 +328,19 @@
 
 
 def edge_backward(scal, d_agg, cot, offsets, gain, *refs):
-    saved, w_out_shards, refs = refs[:4], refs[4:12], refs[12:]
-    d_first, keep, send = refs[:3]
-    joined, first, normed, inverse, w_in, w_out, d_second, g_in, g_out, sems = refs[3:]
+    saved, shards, refs = refs[:4], refs[4:12], refs[12:]
+    d_first, d_second, middle_out, lower, upper = refs[:5]
+    first, normed, inverse, d_direct, w_in, w_out, d_ext, d_turned, sems = refs[5:]
     tiles = cot.shape[0] // BLK
     lat_index, core, y_index, count = (scal[2 * tiles + i] for i in range(4))
     slabs = w_in.shape[0] // 3 // 32
     counts = (3 * L // slabs, L // slabs)
-    normed_in, inverse_in, first_in, joined_in = saved
-    pairs = [(normed_in, normed), (inverse_in, inverse)]
-    pairs += weight_pairs(core, y_index, w_out_shards, (w_in, w_out), counts)[1::2]
-    pairs += [(first_in, first), (joined_in, joined)]
-    loads = copies(pairs, sems)
+    normed_in, inverse_in, first_in, direct_in = saved
+    weights = weight_pairs(core, y_index, shards, (w_in, w_out), counts)
+    pairs = [(normed_in, normed), (inverse_in, inverse)] + weights[1::2] + [(first_in, first)]
+    early = len(pairs)
+    loads = copies(pairs + weights[::2] + [(direct_in, d_direct)], sems)
+    d_ext[...] = jnp.zeros_like(d_ext)
     wait_all(loads[:2])
     for t in range(tiles):
         rows = pl.ds(t * BLK, BLK)
@@ -349,42 +350,16 @@
         d_message = (cot[rows, :].astype(F32) + picked) * live
         back = norm_back(d_message, normed[rows, :], inverse[rows, pl.ds(0, 1)], gain[...])
         d_second[rows, :] = back.astype(BF)
-    wait_all(loads[2:])
+    wait_all(loads[2:early])
     for n in range(2):
         part = pl.ds(n * 256, 256)
         back = dot_transpose(d_second[...], w_out[part, :])
         d_first[:, part] = jnp.where(first[:, part].astype(F32) > 0, back, 0.0).astype(BF)
-    for n in range(2):
-        part = pl.ds(n * 256, 256)
-        g_out[part, :] = dot_rows(first[:, part], d_second[...])
-    for n in range(6):
-        part = pl.ds(n * 256, 256)
-        g_in[part, :] = dot_rows(joined[:, part], d_first[...])
-    pack_grads(core, y_index, (g_in, g_out), keep, send, counts)
-
-
-def edge_inputs(scal, d_first, cot, offsets, direct_in, *refs):
-    shards, refs = refs[:8], refs[8:]
-    grad_out, middle_out, lower, upper = refs[:4]
-    grad_edges, d_direct, w_in, w_out, d_ext, d_turned, sems, out_sems = refs[4:]
-    tiles = cot.shape[0] // BLK
-    lat_index, core, y_index = (scal[2 * tiles + i] for i in range(3))
-    slabs = w_in.shape[0] // 3 // 32
-    counts = (3 * L // slabs, L // slabs)
-    pairs = weight_pairs(core, y_index, shards, (w_in, w_out), counts)[::2]
-    pairs += [(direct_in, d_direct)]
-    loads = copies(pairs, sems)
-    d_ext[...] = jnp.zeros_like(d_ext)
-    wait_all(loads)
+    wait_all(loads[early:])
     for n in range(4):
         d_turned[pl.ds(n * 256, 256), :] = dot_transpose(
             w_in[pl.ds(L + n * 256, 256), :], d_first[...]
         )
-    for n in range(2):
-        part = pl.ds(n * 256, 256)
-        back = dot_transpose(d_first[...], w_in[part, :])
-        grad_edges[:, part] = (cot[:, part].astype(F32) + back).astype(BF)
-    store = copies([(grad_edges, grad_out)], out_sems)
     for t in range(tiles):
         rows = pl.ds(t * BLK, BLK)
         for row, place, at in ((1, scal[tiles + t], 0), (0, scal[t] + HB, L)):
@@ -399,7 +374,35 @@
         lower[:, pl.ds(j * BLK, BLK)] = d_ext[j].astype(BF)
         upper[:, pl.ds(j * BLK, BLK)] = d_ext[HB + blocks + j].astype(BF)
     middle_out[...] = d_ext[pl.ds(HB, blocks)]
-    wait_all(store)
+
+
+def edge_grads(scal, d_first, d_second, cot, *refs):
+    saved, shards, refs = refs[:2], refs[2:10], refs[10:]
+    grad_out, keep, send, first, joined, grad_edges, w_in, w_out, g_in, g_out = refs[:10]
+    sems, out_sems = refs[10:]
+    tiles = cot.shape[0] // BLK
+    core, y_index = scal[2 * tiles + 1], scal[2 * tiles + 2]
+    slabs = w_in.shape[0] // 3 // 32
+    counts = (3 * L // slabs, L // slabs)
+    first_in, joined_in = saved
+    pairs = [(first_in, first), (joined_in, joined)]
+    pairs += weight_pairs(core, y_index, shards, (w_in, w_out), counts)[::2]
+    loads = copies(pairs, sems)
+    loads[0].wait()
+    for n in range(2):
+        part = pl.ds(n * 256, 256)
+        g_out[part, :] = dot_rows(first[:, part], d_second[...])
+    loads[1].wait()
+    for n in range(6):
+        part = pl.ds(n * 256, 256)
+        g_in[part, :] = dot_rows(joined[:, part], d_first[...])
+    pack_grads(core, y_index, (g_in, g_out), keep, send, counts)
+    wait_all(loads[2:])
+    for n in range(2):
+        part = pl.ds(n * 256, 256)
+        back = dot_transpose(d_first[...], w_in[part, :])
+        grad_edges[:, part] = (cot[:, part].astype(F32) + back).astype(BF)
+    wait_all(copies([(grad_edges, grad_out)], out_sems))
 
 
 def add_halo(halo, middle, above, below, columns, held):
@@ -506,35 +509,11 @@
 
 def run_edge_backward(scal, d_agg, cot, offsets, gain, saved, shards):
     rows = cot.shape[0]
-    chunk = (len(shards) // 2,) + shards[0].shape
-    normed, inverse, first, joined = saved
+    lat_size = d_agg.shape[0]
     return call(
         edge_backward,
-        [shape_of((rows, L), BF), shape_of(chunk, BF), shape_of(chunk, BF)],
         [
-            (joined.shape, BF),
-            (first.shape, BF),
-            (normed.shape, F32),
-            (inverse.shape, F32),
-            ((3 * L, L), BF),
-            ((L, L), BF),
-            ((rows, L), BF),
-            ((3 * L, L), F32),
-            ((L, L), F32),
-        ],
-        BACK_MIB,
-        "svvvv" + "h" * (len(saved) + len(shards)),
-        (scal, d_agg, cot, offsets, gain, *saved, *shards),
-        flops=2 * rows * 5 * L * L,
-        sems=(4 + 2 * len(shards),),
-    )
-
-
-def run_edge_inputs(scal, d_first, cot, offsets, d_direct, shards, lat_size):
-    rows = cot.shape[0]
-    return call(
-        edge_inputs,
-        [
+            shape_of((rows, L), BF),
             shape_of((rows, L), BF),
             shape_of((lat_size, L, BLK), F32),
             shape_of((L, HB * BLK), BF),
@@ -542,18 +521,36 @@
         ],
         [
             ((rows, L), BF),
-            (d_direct.shape, F32),
+            ((rows, L), F32),
+            ((rows, BLK), F32),
+            ((L, BLK), F32),
             ((3 * L, L), BF),
             ((L, L), BF),
             ((lat_size + 2 * HB, L, BLK), F32),
             ((2 * L, rows), F32),
         ],
-        EDGE_MIB,
-        "svvvh" + "h" * len(shards),
-        (scal, d_first, cot, offsets, d_direct, *shards),
-        flops=2 * rows * 3 * L * L,
-        out_spaces="hvvv",
-        sems=(1 + 2 * len(shards), 1),
+        BACK_MIB,
+        "svvvv" + "h" * (len(saved) + len(shards)),
+        (scal, d_agg, cot, offsets, gain, *saved, *shards),
+        flops=2 * rows * 4 * L * L,
+        sems=(4 + 4 * len(shards),),
+    )
+
+
+def run_edge_grads(scal, d_first, d_second, cot, saved, shards):
+    rows = cot.shape[0]
+    chunk = (len(shards) // 2,) + shards[0].shape
+    return call(
+        edge_grads,
+        [shape_of((rows, L), BF), shape_of(chunk, BF), shape_of(chunk, BF)],
+        [(one.shape, BF) for one in saved]
+        + [((rows, L), BF), ((3 * L, L), BF), ((L, L), BF), ((3 * L, L), F32), ((L, L), F32)],
+        BACK_MIB,
+        "svvv" + "h" * (len(saved) + len(shards)),
+        (scal, d_first, d_second, cot, *saved, *shards),
+        flops=2 * rows * 5 * L * L,
+        out_spaces="hvv",
+        sems=(2 + 2 * len(shards), 1),
     )
 
 
@@ -579,8 +576,7 @@
     return mine + [swap_cores(one) for one in mine]
 
 
-def reduce_far(keep, send):
-    arrived = swap_cores(send)
+def reduce_far(keep, arrived):
     both = [(keep[k].astype(F32) + arrived[k].astype(F32)).astype(BF) for k in range(keep.shape[0])]
     return [both[0]] + [shift(both[k], "y", k) for k in range(1, keep.shape[0])]
 
@@ -674,18 +670,19 @@
     )
     second_in = spread_rows(second_out, LAT)
     new_nodes = second_in[:, L:].transpose(1, 0, 2).reshape(width, slab_rows).T
-    node_far = reduce_far(node_keep, node_send)
-
-    d_first, edge_keep, edge_send = run_edge_backward(
+    node_far = reduce_far(node_keep, swap_cores(node_send))
+
+    d_first, d_second, middle, lower, upper = run_edge_backward(
         scal, second_in, edge_cotangent, offsets, edge_gain_row,
-        (normed, inverse, first, joined), edge_shards,
-    )
-    grad_edges, middle, lower, upper = run_edge_inputs(
-        scal, d_first, edge_cotangent, offsets, d_direct, edge_shards, lat_size
+        (normed, inverse, first, d_direct), edge_shards,
     )
     from_above = from_behind(lower, -1)
     from_below = from_behind(upper, 1)
-    edge_far = reduce_far(edge_keep, edge_send)
+    grad_edges, edge_keep, edge_send = run_edge_grads(
+        scal, d_first, d_second, edge_cotangent, (first, joined), edge_shards
+    )
+    edge_arrived = swap_cores(edge_send)
+    edge_far = reduce_far(edge_keep, edge_arrived)
     (columns,) = call(
         add_halo,
         [shape_of((lat_size, width, slab_rows), BF)],

time: 221 us -> 221 us (level)
  transfers between devices with their start and end apart: 41 -> 41, of which waited for: 22 -> 22; matrix products, arithmetic and copies ran while one was open for 2% -> 2% of each run, Pallas kernels for 6% -> 4%
where the time goes in v8:
time: 221 us; the launch traced here: 220 us
  waiting for transfers between devices  79.7 us (36%)
  starting transfers between devices  73.3 us (33%)
  Pallas kernels  33.9 us (15%)
  blocking collectives  23.5 us (11%)
  local copies, waits for them, and re-layouts  4.11 us (2%)
  other arithmetic  3.3 us (1%)
    ppermute x24, waiting for transfers between devices, shift(): lax.ppermute(value, axes, [(i, (i + step) % count) for i in range(count)])  61.4 us
    ppermute x24, starting transfers between devices, shift(): lax.ppermute(value, axes, [(i, (i + step) % count) for i in range(count)])  49.2 us
    pallas_call x13, Pallas kernels, call(): pl.pallas_call(kernel, out_shape=placed, in_specs=[pl.BlockSpec(memory_sp...  33.9 us
    all_to_all x1, blocking collectives, spread_rows(): return lax.all_to_all(value, axes, 0, 0)  23.5 us
    all_to_all x3, starting transfers between devices, spread_rows(): return lax.all_to_all(value, axes, 0, 0)  15.8 us
    all_to_all x3, waiting for transfers between devices, spread_rows(): return lax.all_to_all(value, axes, 0, 0)  11.8 us
    ppermute x4, starting transfers between devices, from_behind(): lax.ppermute(value, SLAB, [(source, source + steps) for source in range(f...  6.91 us
    ppermute x4, waiting for transfers between devices, from_behind(): lax.ppermute(value, SLAB, [(source, source + steps) for source in range(f...  4.75 us
  transfers between devices with their start and end apart: 41, of which 22 were waited for; matrix products, arithmetic and copies ran while one was open for 2% of the time, Pallas kernels for 4%

profile of v8, /device:TPU:0, one launch (start us, length us, event | category | flops | bytes accessed | tf_op | source)
XLA Modules:
  0.0 219.5 jit_solution(8469200289616689281)
XLA Ops:
  5.4 3.6 %collective-permute-done.1.upper = bf16[64,256]{1,0:T(8,128)(2,1)S(1)} collective-permute-done((bf16[64,256]{1,0:T(8,128)(2,1)S(1)}, bf16[64,256]{1,0:T(8,128)(2,1)S(1)}, u32[]{:S(2)}, u32[]{:S(2)}) %collective-permute-start.1) | collective-permute-done | bytes 32800 | tf_op jit(solution)/shard_map/ppermute | solution.py:33
  11.4 7.6 %all-to-all-start = ((bf16[8,64,1664]{2,1,0:T(8,128)(2,1)}), bf16[8,64,1664]{2,1,0:T(8,128)(2,1)S(1)}, u32[]{:S(2)}, u32[]{:S(2)}) async-start(bf16[8,64,1664]{2,1,0:T(8,128)(2,1)} %shard_map.198), calls=%async_computation | async-start | bytes 3407872 | tf_op jit(solution)/shard_map/all_to_all | solution.py:571
  19.0 3.5 %collective-permute-start.2 = (bf16[32,512]{1,0:T(8,128)(2,1)S(1)}, bf16[32,512]{1,0:T(8,128)(2,1)S(1)}, u32[]{:S(2)}, u32[]{:S(2)}) collective-permute-start(bf16[32,512]{1,0:T(8,128)(2,1)S(1)} %get-tuple-element.51), channel_id=1, source_target_pairs={{0,4},{4,16},{16,20},{20,0},{1,5},{5,17},{17,21},{21,1},{2,6},{6,1... | collective-permute-start | bytes 98312 | tf_op jit(solution)/shard_map/ppermute | solution.py:563
  24.5 19.0 %collective-permute-done.2 = bf16[32,512]{1,0:T(8,128)(2,1)S(1)} collective-permute-done((bf16[32,512]{1,0:T(8,128)(2,1)S(1)}, bf16[32,512]{1,0:T(8,128)(2,1)S(1)}, u32[]{:S(2)}, u32[]{:S(2)}) %collective-permute-start.2) | collective-permute-done | bytes 32800 | tf_op jit(solution)/shard_map/ppermute | solution.py:563
  50.5 3.7 %collective-permute-done.6.refs_2_ = bf16[128,512]{1,0:T(8,128)(2,1)S(1)} collective-permute-done((bf16[128,512]{1,0:T(8,128)(2,1)S(1)}, bf16[128,512]{1,0:T(8,128)(2,1)S(1)}, u32[]{:S(2)}, u32[]{:S(2)}) %collective-permute-start.6) | collective-permute-done | bytes 131104 | tf_op jit(solution)/shard_map/ppermute | solution.py:563
  54.9 2.8 %collective-permute-start.8 = (bf16[256,512]{1,0:T(8,128)(2,1)S(1)}, bf16[256,512]{1,0:T(8,128)(2,1)S(1)}, u32[]{:S(2)}, u32[]{:S(2)}) collective-permute-start(bf16[256,512]{1,0:T(8,128)(2,1)S(1)} %get-tuple-element.52.refs_0_.refs_4_.refs_2_), channel_id=1, source_target_pairs={{0,32},{32,64},{64,96},{96,0},{1,33},{33,65},{65,97},{97,1},{2,34}... | collective-permute-start | bytes 786440 | tf_op jit(solution)/shard_map/ppermute | solution.py:563
  57.7 2.9 %collective-permute-start.9 = (bf16[256,512]{1,0:T(8,128)(2,1)S(1)}, bf16[256,512]{1,0:T(8,128)(2,1)S(1)}, u32[]{:S(2)}, u32[]{:S(2)}) collective-permute-start(bf16[256,512]{1,0:T(8,128)(2,1)S(1)} %get-tuple-element.52.refs_0_.refs_4_.refs_2_), channel_id=1, source_target_pairs={{0,64},{32,96},{64,0},{96,32},{1,65},{33,97},{65,1},{97,33},{2,66}... | collective-permute-start | bytes 786440 | tf_op jit(solution)/shard_map/ppermute | solution.py:563
  61.9 3.4 %collective-permute-done.8.refs_1_.refs_5_.refs_3_ = bf16[256,512]{1,0:T(8,128)(2,1)S(1)} collective-permute-done((bf16[256,512]{1,0:T(8,128)(2,1)S(1)}, bf16[256,512]{1,0:T(8,128)(2,1)S(1)}, u32[]{:S(2)}, u32[]{:S(2)}) %collective-permute-start.8) | collective-permute-done | bytes 262176 | tf_op jit(solution)/shard_map/ppermute | solution.py:563
  65.4 5.8 %collective-permute-done.9.refs_2_.refs_6_.refs_4_ = bf16[256,512]{1,0:T(8,128)(2,1)S(1)} collective-permute-done((bf16[256,512]{1,0:T(8,128)(2,1)S(1)}, bf16[256,512]{1,0:T(8,128)(2,1)S(1)}, u32[]{:S(2)}, u32[]{:S(2)}) %collective-permute-start.9) | collective-permute-done | bytes 262176 | tf_op jit(solution)/shard_map/ppermute | solution.py:563
  73.2 6.3 %shard_map.200 = (bf16[512,1536]{1,0:T(8,128)(2,1)}, bf16[512,512]{1,0:T(8,128)(2,1)}, f32[512,512]{1,0:T(8,128)}, f32[512,128]{1,0:T(8,128)}, bf16[512,512]{1,0...) custom-call(s32[12]{0:T(128)S(1)} %concatenate.7.scal, ...), custom_call_target="tpu_custom_call" | custom-call | flops 1073741824 | bytes 10623024 | tf_op jit(solution)/shard_map/pallas_call | solution.py:441
  79.6 4.6 %all-to-all-start.1 = ((f32[8,128,512]{2,1,0:T(8,128)}), f32[8,128,512]{2,1,0:T(8,128)S(1)}, u32[]{:S(2)}, u32[]{:S(2)}) async-start(f32[8,128,512]{2,1,0:T(8,128)} %get-tuple-element.53), calls=%async_computation.1 | async-start | bytes 4194304 | tf_op jit(solution)/shard_map/all_to_all | solution.py:571
  92.7 4.0 %collective-permute-done.16.refs_2_ = bf16[192,512]{1,0:T(8,128)(2,1)S(1)} collective-permute-done((bf16[192,512]{1,0:T(8,128)(2,1)S(1)}, bf16[192,512]{1,0:T(8,128)(2,1)S(1)}, u32[]{:S(2)}, u32[]{:S(2)}) %collective-permute-start.16) | collective-permute-done | bytes 196640 | tf_op jit(solution)/shard_map/ppermute | solution.py:563
  99.2 11.8 %all-to-all-done.1.spread = f32[8,128,512]{2,1,0:T(8,128)S(1)} async-done(((f32[8,128,512]{2,1,0:T(8,128)}), f32[8,128,512]{2,1,0:T(8,128)S(1)}, u32[]{:S(2)}, u32[]{:S(2)}) %all-to-all-start.1) | async-done | bytes 2097184 | tf_op jit(solution)/shard_map/all_to_all | solution.py:571
  111.9 4.0 %shard_map.201 = (bf16[8,576,128]{2,1,0:T(8,128)(2,1)S(1)}, f32[512,128]{1,0:T(8,128)}, bf16[128,1024]{1,0:T(8,128)(2,1)}, bf16[128,512]{1,0:T(8,128)(2,1)}, bf1...) custom-call(s32[3]{0:T(128)S(1)} %pad_add_fusion.scal, f32[8,128,512]{2,1,0:T(8,128)S(1)} %all-to-all-done.1.spread, ...), custom_call_target="tpu_custom_call" | custom-call | flops 402653184 | bytes 6031372 | tf_op jit(solution)/shard_map/pallas_call | solution.py:441
  115.9 23.5 %all_to_all.20.d_agg = bf16[8,576,128]{2,1,0:T(8,128)(2,1)S(1)} all-to-all(bf16[8,576,128]{2,1,0:T(8,128)(2,1)S(1)} %get-tuple-element.57), channel_id=1, replica_groups=mesh['y'=4,'xl'=2,'c'=2,'xh'=2,'z'=4] {'xh','z'}, dimensions={0} | all-to-all | bytes 2359296 | tf_op jit(solution)/shard_map/all_to_all | solution.py:571
  139.4 4.9 %shard_map.202 = (bf16[512,512]{1,0:T(8,128)(2,1)S(1)}, bf16[512,512]{1,0:T(8,128)(2,1)S(1)}, f32[8,512,128]{2,1,0:T(8,128)S(1)}, bf16[512,256]{1,0:T(8,128)(2,1)S(1)}, bf16[512,256]{1,0:T(8,128)(2,1)S(1)}) custom-call(s32[12]{0:T(128)S(1)} %concatenate.7.scal, bf16[8,576,128]{2,1,0:T(8,128)(2,1)S(1)} %all_to_all.20.d_agg, bf16[512,512]{1,0:T(8,128)(2,1)S(1)} %copy-done.6, ...), custom_call_target="tpu_custom_call" | custom-call | flops 1073741824 | bytes 9574448 | tf_op jit(solution)/shard_map/pallas_call | solution.py:441
  144.3 5.8 %shard_map.205 = (bf16[512,512]{1,0:T(8,128)(2,1)}, bf16[4,256,512]{2,1,0:T(8,128)(2,1)S(1)}, bf16[4,256,512]{2,1,0:T(8,128)(2,1)}) custom-call(s32[12]{0:T(128)S(1)} %concatenate.7.scal, bf16[512,512]{1,0:T(8,128)(2,1)S(1)} %get-tuple-element.66.d_first, bf16[512,512]{1,0:T(8,128)(2,1)S(1)} %get-tuple-element.67.d_second, bf16[512,512]{1,0:T(8,128)(2,1)S(1)} %copy-done.6, ...), custom_call_target="tpu_custom_call" | custom-call | flops 1342177280 | bytes 8388656 | tf_op jit(solution)/shard_map/pallas_call | solution.py:441
  150.2 3.3 %shard_map.206 = (bf16[4,192,512]{2,1,0:T(8,128)(2,1)S(1)}, bf16[4,192,512]{2,1,0:T(8,128)(2,1)}) custom-call(s32[3]{0:T(128)S(1)} %pad_add_fusion.scal, bf16[128,1024]{1,0:T(8,128)(2,1)} %get-tuple-element.72.refs_0_, bf16[128,512]{1,0:T(8,128)(2,1)} %get-tuple-element.73.refs_1_, bf16[128,512]{1,0:T(8,128)(2,1)} %get-tuple-element.74.refs_2_, ...), custom_call_target="tpu_custom_call" | custom-call | flops 201326592 | bytes 2228236 | tf_op jit(solution)/shard_map/pallas_call | solution.py:441
  156.1 3.0 %collective-permute-start.23 = (bf16[512,256]{1,0:T(8,128)(2,1)S(1)}, bf16[512,256]{1,0:T(8,128)(2,1)S(1)}, u32[]{:S(2)}, u32[]{:S(2)}) collective-permute-start(bf16[512,256]{1,0:T(8,128)(2,1)S(1)} %get-tuple-element.65), channel_id=1, source_target_pairs={{0,8},{8,16},{16,24},{24,32},{32,40},{40,48},{48,56},{56,64},{64,7... | collective-permute-start | bytes 786440 | tf_op jit(solution)/shard_map/ppermute | solution.py:33
  162.4 3.6 %all-to-all-start.3 = ((bf16[8,64,1024]{2,1,0:T(8,128)(2,1)}), bf16[8,64,1024]{2,1,0:T(8,128)(2,1)S(1)}, u32[]{:S(2)}, u32[]{:S(2)}) async-start(bf16[8,64,1024]{2,1,0:T(8,128)(2,1)} %shard_map.203), calls=%async_computation.3 | async-start | bytes 2097152 | tf_op jit(solution)/shard_map/all_to_all | solution.py:571
  167.6 6.7 %collective-permute-start.29 = (bf16[192,512]{1,0:T(8,128)(2,1)S(1)}, bf16[192,512]{1,0:T(8,128)(2,1)S(1)}, u32[]{:S(2)}, u32[]{:S(2)}) collective-permute-start(bf16[192,512]{1,0:T(8,128)(2,1)S(1)} %get-tuple-element.96), channel_id=1, source_target_pairs={{0,32},{32,64},{64,96},{96,0},{1,33},{33,65},{65,97},{97,1},{2,34}... | collective-permute-start | bytes 589832 | tf_op jit(solution)/shard_map/ppermute | solution.py:563
  183.9 12.1 %collective-permute-done.30.n2 = bf16[192,512]{1,0:T(8,128)(2,1)S(1)} collective-permute-done((bf16[192,512]{1,0:T(8,128)(2,1)S(1)}, bf16[192,512]{1,0:T(8,128)(2,1)S(1)}, u32[]{:S(2)}, u32[]{:S(2)}) %collective-permute-start.30) | collective-permute-done | bytes 196640 | tf_op jit(solution)/shard_map/ppermute | solution.py:563
  208.9 3.1 %collective-permute-start.35 = (bf16[32,512]{1,0:T(8,128)(2,1)S(1)}, bf16[32,512]{1,0:T(8,128)(2,1)S(1)}, u32[]{:S(2)}, u32[]{:S(2)}) collective-permute-start(bf16[32,512]{1,0:T(8,128)(2,1)S(1)} %get-tuple-element.83), channel_id=1, source_target_pairs={{0,4},{4,16},{16,20},{20,0},{1,5},{5,17},{17,21},{21,1},{2,6},{6,1... | collective-permute-start | bytes 98312 | tf_op jit(solution)/shard_map/ppermute | solution.py:563
  215.8 3.0 %collective-permute-done.37.r3 = bf16[32,512]{1,0:T(8,128)(2,1)S(1)} collective-permute-done((bf16[32,512]{1,0:T(8,128)(2,1)S(1)}, bf16[32,512]{1,0:T(8,128)(2,1)S(1)}, u32[]{:S(2)}, u32[]{:S(2)}) %collective-permute-start.37) | collective-permute-done | bytes 32800 | tf_op jit(solution)/shard_map/ppermute | solution.py:563
  (116 shorter events, 65.8 us)
Async XLA Ops:
  11.4 61.8 %all-to-all-start = ((bf16[8,64,1664]{2,1,0:T(8,128)(2,1)}), bf16[8,64,1664]{2,1,0:T(8,128)(2,1)S(1)}, u32[]{:S(2)}, u32[]{:S(2)}) async-start(bf16[8,64,1664]{2,1,0:T(8,128)(2,1)} %shard_map.198), calls=%async_computation | async-start | bytes 3407872 | tf_op jit(solution)/shard_map/all_to_all | solution.py:571
  19.0 24.5 %collective-permute-start.2 = (bf16[32,512]{1,0:T(8,128)(2,1)S(1)}, bf16[32,512]{1,0:T(8,128)(2,1)S(1)}, u32[]{:S(2)}, u32[]{:S(2)}) collective-permute-start(bf16[32,512]{1,0:T(8,128)(2,1)S(1)} %get-tuple-element.51), channel_id=1, source_target_pairs={{0,4},{4,16},{16,20},{20,0},{1,5},{5,17},{17,21},{21,1},{2,6},{6,1... | collective-permute-start | bytes 98312 | tf_op jit(solution)/shard_map/ppermute | solution.py:563
  22.5 21.0 %collective-permute-start.3 = (bf16[32,512]{1,0:T(8,128)(2,1)S(1)}, bf16[32,512]{1,0:T(8,128)(2,1)S(1)}, u32[]{:S(2)}, u32[]{:S(2)}) collective-permute-start(bf16[32,512]{1,0:T(8,128)(2,1)S(1)} %get-tuple-element.51), channel_id=1, source_target_pairs={{0,16},{4,20},{16,0},{20,4},{1,17},{5,21},{17,1},{21,5},{2,18},{6,... | collective-permute-start | bytes 98312 | tf_op jit(solution)/shard_map/ppermute | solution.py:563
  24.5 19.1 %collective-permute-start.4 = (bf16[32,512]{1,0:T(8,128)(2,1)S(1)}, bf16[32,512]{1,0:T(8,128)(2,1)S(1)}, u32[]{:S(2)}, u32[]{:S(2)}) collective-permute-start(bf16[32,512]{1,0:T(8,128)(2,1)S(1)} %get-tuple-element.51), channel_id=1, source_target_pairs={{0,20},{4,0},{16,4},{20,16},{1,21},{5,1},{17,5},{21,17},{2,22},{6,... | collective-permute-start | bytes 98312 | tf_op jit(solution)/shard_map/ppermute | solution.py:563
  45.1 9.1 %collective-permute-start.6 = (bf16[128,512]{1,0:T(8,128)(2,1)S(1)}, bf16[128,512]{1,0:T(8,128)(2,1)S(1)}, u32[]{:S(2)}, u32[]{:S(2)}) collective-permute-start(bf16[128,512]{1,0:T(8,128)(2,1)S(1)} %constant_dynamic-update-slice_fusion.refs_0_), channel_id=1, source_target_pairs={{0,2},{1,3},{2,0},{3,1},{4,6},{5,7},{6,4},{7,5},{8,10},{9,11},{10,... | collective-permute-start | bytes 393224 | tf_op jit(solution)/shard_map/ppermute | solution.py:563
  54.9 10.5 %collective-permute-start.8 = (bf16[256,512]{1,0:T(8,128)(2,1)S(1)}, bf16[256,512]{1,0:T(8,128)(2,1)S(1)}, u32[]{:S(2)}, u32[]{:S(2)}) collective-permute-start(bf16[256,512]{1,0:T(8,128)(2,1)S(1)} %get-tuple-element.52.refs_0_.refs_4_.refs_2_), channel_id=1, source_target_pairs={{0,32},{32,64},{64,96},{96,0},{1,33},{33,65},{65,97},{97,1},{2,34}... | collective-permute-start | bytes 786440 | tf_op jit(solution)/shard_map/ppermute | solution.py:563
  57.7 13.5 %collective-permute-start.9 = (bf16[256,512]{1,0:T(8,128)(2,1)S(1)}, bf16[256,512]{1,0:T(8,128)(2,1)S(1)}, u32[]{:S(2)}, u32[]{:S(2)}) collective-permute-start(bf16[256,512]{1,0:T(8,128)(2,1)S(1)} %get-tuple-element.52.refs_0_.refs_4_.refs_2_), channel_id=1, source_target_pairs={{0,64},{32,96},{64,0},{96,32},{1,65},{33,97},{65,1},{97,33},{2,66}... | collective-permute-start | bytes 786440 | tf_op jit(solution)/shard_map/ppermute | solution.py:563
  60.6 10.6 %collective-permute-start.10 = (bf16[256,512]{1,0:T(8,128)(2,1)S(1)}, bf16[256,512]{1,0:T(8,128)(2,1)S(1)}, u32[]{:S(2)}, u32[]{:S(2)}) collective-permute-start(bf16[256,512]{1,0:T(8,128)(2,1)S(1)} %get-tuple-element.52.refs_0_.refs_4_.refs_2_), channel_id=1, source_target_pairs={{0,96},{32,0},{64,32},{96,64},{1,97},{33,1},{65,33},{97,65},{2,98}... | collective-permute-start | bytes 786440 | tf_op jit(solution)/shard_map/ppermute | solution.py:563
  61.9 10.6 %collective-permute-start.11 = (bf16[256,512]{1,0:T(8,128)(2,1)S(1)}, bf16[256,512]{1,0:T(8,128)(2,1)S(1)}, u32[]{:S(2)}, u32[]{:S(2)}) collective-permute-start(bf16[256,512]{1,0:T(8,128)(2,1)S(1)} %get-tuple-element.52.refs_0_.refs_4_.refs_2_), channel_id=1, source_target_pairs={{0,8},{8,0},{1,9},{9,1},{2,10},{10,2},{3,11},{11,3},{4,12},{12,4},... | collective-permute-start | bytes 786440 | tf_op jit(solution)/shard_map/ppermute | solution.py:558
  65.4 7.1 %collective-permute-start.12 = (bf16[256,512]{1,0:T(8,128)(2,1)S(1)}, bf16[256,512]{1,0:T(8,128)(2,1)S(1)}, u32[]{:S(2)}, u32[]{:S(2)}) collective-permute-start(bf16[256,512]{1,0:T(8,128)(2,1)S(1)} %collective-permute-done.8.refs_1_.refs_5_.refs_3_), channel_id=1, source_target_pairs={{0,8},{8,0},{1,9},{9,1},{2,10},{10,2},{3,11},{11,3},{4,12},{12,4},... | collective-permute-start | bytes 786440 | tf_op jit(solution)/shard_map/ppermute | solution.py:558
  79.6 31.3 %all-to-all-start.1 = ((f32[8,128,512]{2,1,0:T(8,128)}), f32[8,128,512]{2,1,0:T(8,128)S(1)}, u32[]{:S(2)}, u32[]{:S(2)}) async-start(f32[8,128,512]{2,1,0:T(8,128)} %get-tuple-element.53), calls=%async_computation.1 | async-start | bytes 4194304 | tf_op jit(solution)/shard_map/all_to_all | solution.py:571
  84.2 8.5 %collective-permute-start.15 = (bf16[192,512]{1,0:T(8,128)(2,1)S(1)}, bf16[192,512]{1,0:T(8,128)(2,1)S(1)}, u32[]{:S(2)}, u32[]{:S(2)}) collective-permute-start(bf16[192,512]{1,0:T(8,128)(2,1)S(1)} %get-tuple-element.56.refs_0_), channel_id=1, source_target_pairs={{0,32},{32,64},{64,96},{96,0},{1,33},{33,65},{65,97},{97,1},{2,34}... | collective-permute-start | bytes 589832 | tf_op jit(solution)/shard_map/ppermute | solution.py:563
  85.5 11.2 %collective-permute-start.16 = (bf16[192,512]{1,0:T(8,128)(2,1)S(1)}, bf16[192,512]{1,0:T(8,128)(2,1)S(1)}, u32[]{:S(2)}, u32[]{:S(2)}) collective-permute-start(bf16[192,512]{1,0:T(8,128)(2,1)S(1)} %get-tuple-element.56.refs_0_), channel_id=1, source_target_pairs={{0,64},{32,96},{64,0},{96,32},{1,65},{33,97},{65,1},{97,33},{2,66}... | collective-permute-start | bytes 589832 | tf_op jit(solution)/shard_map/ppermute | solution.py:563
  87.9 9.0 %collective-permute-start.17 = (bf16[192,512]{1,0:T(8,128)(2,1)S(1)}, bf16[192,512]{1,0:T(8,128)(2,1)S(1)}, u32[]{:S(2)}, u32[]{:S(2)}) collective-permute-start(bf16[192,512]{1,0:T(8,128)(2,1)S(1)} %get-tuple-element.56.refs_0_), channel_id=1, source_target_pairs={{0,96},{32,0},{64,32},{96,64},{1,97},{33,1},{65,33},{97,65},{2,98}... | collective-permute-start | bytes 589832 | tf_op jit(solution)/shard_map/ppermute | solution.py:563
  90.0 7.4 %collective-permute-start.18 = (bf16[192,512]{1,0:T(8,128)(2,1)S(1)}, bf16[192,512]{1,0:T(8,128)(2,1)S(1)}, u32[]{:S(2)}, u32[]{:S(2)}) collective-permute-start(bf16[192,512]{1,0:T(8,128)(2,1)S(1)} %get-tuple-element.56.refs_0_), channel_id=1, source_target_pairs={{0,8},{8,0},{1,9},{9,1},{2,10},{10,2},{3,11},{11,3},{4,12},{12,4},... | collective-permute-start | bytes 589832 | tf_op jit(solution)/shard_map/ppermute | solution.py:558
  150.1 24.3 %collective-permute-start.24 = (bf16[4,256,512]{2,1,0:T(8,128)(2,1)}, bf16[4,256,512]{2,1,0:T(8,128)(2,1)}, u32[]{:S(2)}, u32[]{:S(2)}) collective-permute-start(bf16[4,256,512]{2,1,0:T(8,128)(2,1)} %get-tuple-element.71), channel_id=1, source_target_pairs={{0,8},{8,0},{1,9},{9,1},{2,10},{10,2},{3,11},{11,3},{4,12},{12,4},... | collective-permute-start | bytes 3145736 | tf_op jit(solution)/shard_map/ppermute | solution.py:558
  154.4 11.6 %collective-permute-start.28 = (bf16[4,192,512]{2,1,0:T(8,128)(2,1)}, bf16[4,192,512]{2,1,0:T(8,128)(2,1)}, u32[]{:S(2)}, u32[]{:S(2)}) collective-permute-start(bf16[4,192,512]{2,1,0:T(8,128)(2,1)} %get-tuple-element.77), channel_id=1, source_target_pairs={{0,8},{8,0},{1,9},{9,1},{2,10},{10,2},{3,11},{11,3},{4,12},{12,4},... | collective-permute-start | bytes 2359304 | tf_op jit(solution)/shard_map/ppermute | solution.py:558
  162.4 51.8 %all-to-all-start.3 = ((bf16[8,64,1024]{2,1,0:T(8,128)(2,1)}), bf16[8,64,1024]{2,1,0:T(8,128)(2,1)S(1)}, u32[]{:S(2)}, u32[]{:S(2)}) async-start(bf16[8,64,1024]{2,1,0:T(8,128)(2,1)} %shard_map.203), calls=%async_computation.3 | async-start | bytes 2097152 | tf_op jit(solution)/shard_map/all_to_all | solution.py:571
  167.6 14.5 %collective-permute-start.29 = (bf16[192,512]{1,0:T(8,128)(2,1)S(1)}, bf16[192,512]{1,0:T(8,128)(2,1)S(1)}, u32[]{:S(2)}, u32[]{:S(2)}) collective-permute-start(bf16[192,512]{1,0:T(8,128)(2,1)S(1)} %get-tuple-element.96), channel_id=1, source_target_pairs={{0,32},{32,64},{64,96},{96,0},{1,33},{33,65},{65,97},{97,1},{2,34}... | collective-permute-start | bytes 589832 | tf_op jit(solution)/shard_map/ppermute | solution.py:563
  175.8 22.0 %collective-permute-start.25 = (bf16[256,512]{1,0:T(8,128)(2,1)S(1)}, bf16[256,512]{1,0:T(8,128)(2,1)S(1)}, u32[]{:S(2)}, u32[]{:S(2)}) collective-permute-start(bf16[256,512]{1,0:T(8,128)(2,1)S(1)} %get-tuple-element.92), channel_id=1, source_target_pairs={{0,32},{32,64},{64,96},{96,0},{1,33},{33,65},{65,97},{97,1},{2,34}... | collective-permute-start | bytes 786440 | tf_op jit(solution)/shard_map/ppermute | solution.py:563
  177.4 20.5 %collective-permute-start.26 = (bf16[256,512]{1,0:T(8,128)(2,1)S(1)}, bf16[256,512]{1,0:T(8,128)(2,1)S(1)}, u32[]{:S(2)}, u32[]{:S(2)}) collective-permute-start(bf16[256,512]{1,0:T(8,128)(2,1)S(1)} %get-tuple-element.91), channel_id=1, source_target_pairs={{0,64},{32,96},{64,0},{96,32},{1,65},{33,97},{65,1},{97,33},{2,66}... | collective-permute-start | bytes 786440 | tf_op jit(solution)/shard_map/ppermute | solution.py:563
  179.2 18.7 %collective-permute-start.27 = (bf16[256,512]{1,0:T(8,128)(2,1)S(1)}, bf16[256,512]{1,0:T(8,128)(2,1)S(1)}, u32[]{:S(2)}, u32[]{:S(2)}) collective-permute-start(bf16[256,512]{1,0:T(8,128)(2,1)S(1)} %get-tuple-element.90), channel_id=1, source_target_pairs={{0,96},{32,0},{64,32},{96,64},{1,97},{33,1},{65,33},{97,65},{2,98}... | collective-permute-start | bytes 786440 | tf_op jit(solution)/shard_map/ppermute | solution.py:563
  181.7 14.2 %collective-permute-start.30 = (bf16[192,512]{1,0:T(8,128)(2,1)S(1)}, bf16[192,512]{1,0:T(8,128)(2,1)S(1)}, u32[]{:S(2)}, u32[]{:S(2)}) collective-permute-start(bf16[192,512]{1,0:T(8,128)(2,1)S(1)} %get-tuple-element.95), channel_id=1, source_target_pairs={{0,64},{32,96},{64,0},{96,32},{1,65},{33,97},{65,1},{97,33},{2,66}... | collective-permute-start | bytes 589832 | tf_op jit(solution)/shard_map/ppermute | solution.py:563
  182.1 15.8 %collective-permute-start.31 = (bf16[192,512]{1,0:T(8,128)(2,1)S(1)}, bf16[192,512]{1,0:T(8,128)(2,1)S(1)}, u32[]{:S(2)}, u32[]{:S(2)}) collective-permute-start(bf16[192,512]{1,0:T(8,128)(2,1)S(1)} %get-tuple-element.94), channel_id=1, source_target_pairs={{0,96},{32,0},{64,32},{96,64},{1,97},{33,1},{65,33},{97,65},{2,98}... | collective-permute-start | bytes 589832 | tf_op jit(solution)/shard_map/ppermute | solution.py:563
  (33 other events, 401.5 us)

commit v9 on v7

--- a/solution.py
+++ b/solution.py
@@ -283,14 +283,16 @@
 
 def node_step(scal, spread, own_hbm, up_hbm, *refs):
     shards, refs = refs[:8], refs[8:]
-    gain, out, direct_out, joined_out, first_out, d_second_out, d_first_out = refs[:7]
-    own_turned, up_turned, w_in, w_out, joined, first, d_second, d_first, d_direct = refs[7:16]
-    sems, out_sems = refs[16:]
+    gain, out, rows_out, direct_out, joined_out, first_out, d_second_out, d_first_out = refs[:8]
+    own_turned, up_turned, w_in, w_out, joined, first, d_second, d_first = refs[8:16]
+    d_direct, new_rows, sems, out_sems = refs[16:]
     core, y_index = scal[1], scal[2]
     slabs = w_in.shape[0] // 2 // 32
     counts = (2 * L // slabs, L // slabs)
-    loads = copies([(own_hbm, own_turned), (up_hbm, up_turned)], sems)
-    unpack_weights(core, y_index, shards, (w_in, w_out), counts)
+    pairs = weight_pairs(core, y_index, shards, (w_in, w_out), counts)
+    loads = copies([(own_hbm, own_turned), (up_hbm, up_turned)] + pairs[:4], sems)
+    for source, target in pairs[4:]:
+        target[...] = source[...]
     wait_all(loads)
     own = own_turned[...].astype(F32).T
     upstream = up_turned[...].astype(F32).T
@@ -305,14 +307,12 @@
     back = dot_transpose(d_second[...], w_out[...])
     d_first[...] = jnp.where(first[...].astype(F32) > 0, back, 0.0).astype(BF)
     d_agg = dot_transpose(w_in[pl.ds(L, L), :], d_first[...]).astype(BF)
-    new_rows = (own + normed * gain[...]).T.astype(BF)
-    width = L // out.shape[0]
     for l in range(out.shape[0]):
-        out[l, pl.ds(0, L), :] = d_agg
-        out[l, pl.ds(L, width), :] = new_rows[l * width : (l + 1) * width, :]
+        out[l] = d_agg
+    new_rows[...] = (own + normed * gain[...]).T.astype(BF)
     d_direct[...] = dot_transpose(w_in[pl.ds(0, L), :], d_first[...])
-    held = (d_direct, joined, first, d_second, d_first)
-    outs = (direct_out, joined_out, first_out, d_second_out, d_first_out)
+    held = (new_rows, d_direct, joined, first, d_second, d_first)
+    outs = (rows_out, direct_out, joined_out, first_out, d_second_out, d_first_out)
     wait_all(copies(zip(held, outs), out_sems))
 
 
@@ -345,7 +345,7 @@
         rows = pl.ds(t * BLK, BLK)
         live = (lat_index * tiles + t < count).astype(F32)
         to_dst = one_hot_columns(offsets[0, pl.ds(t, 1), :]).T.astype(BF)
-        picked = dot_transpose(to_dst, d_agg[scal[t], pl.ds(0, L), :])
+        picked = dot_transpose(to_dst, d_agg[scal[t]])
         d_message = (cot[rows, :].astype(F32) + picked) * live
         back = norm_back(d_message, normed[rows, :], inverse[rows, pl.ds(0, 1)], gain[...])
         d_second[rows, :] = back.astype(BF)
@@ -363,11 +363,10 @@
     pack_grads(core, y_index, (g_in, g_out), keep, send, counts)
 
 
-def edge_inputs(scal, d_first, cot, offsets, direct_in, *refs):
+def edge_inputs(scal, d_first, offsets, direct_in, *refs):
     shards, refs = refs[:8], refs[8:]
-    grad_out, middle_out, lower, upper = refs[:4]
-    grad_edges, d_direct, w_in, w_out, d_ext, d_turned, sems, out_sems = refs[4:]
-    tiles = cot.shape[0] // BLK
+    middle_out, lower, upper, d_direct, w_in, w_out, d_ext, d_turned, sems = refs
+    tiles = d_first.shape[0] // BLK
     lat_index, core, y_index = (scal[2 * tiles + i] for i in range(3))
     slabs = w_in.shape[0] // 3 // 32
     counts = (3 * L // slabs, L // slabs)
@@ -380,11 +379,6 @@
         d_turned[pl.ds(n * 256, 256), :] = dot_transpose(
             w_in[pl.ds(L + n * 256, 256), :], d_first[...]
         )
-    for n in range(2):
-        part = pl.ds(n * 256, 256)
-        back = dot_transpose(d_first[...], w_in[part, :])
-        grad_edges[:, part] = (cot[:, part].astype(F32) + back).astype(BF)
-    store = copies([(grad_edges, grad_out)], out_sems)
     for t in range(tiles):
         rows = pl.ds(t * BLK, BLK)
         for row, place, at in ((1, scal[tiles + t], 0), (0, scal[t] + HB, L)):
@@ -399,10 +393,24 @@
         lower[:, pl.ds(j * BLK, BLK)] = d_ext[j].astype(BF)
         upper[:, pl.ds(j * BLK, BLK)] = d_ext[HB + blocks + j].astype(BF)
     middle_out[...] = d_ext[pl.ds(HB, blocks)]
-    wait_all(store)
-
-
-def add_halo(halo, middle, above, below, columns, held):
+
+
+def edge_grads(scal, d_first, cot_in, *refs):
+    shards, (grad_out, grad_edges, cot, w_in, w_out, sems, out_sems) = refs[:8], refs[8:]
+    tiles = cot.shape[0] // BLK
+    core, y_index = scal[2 * tiles + 1], scal[2 * tiles + 2]
+    slabs = w_in.shape[0] // 3 // 32
+    counts = (3 * L // slabs, L // slabs)
+    pairs = weight_pairs(core, y_index, shards, (w_in, w_out), counts)[::2]
+    wait_all(copies(pairs + [(cot_in, cot)], sems))
+    for n in range(2):
+        part = pl.ds(n * 256, 256)
+        back = dot_transpose(d_first[...], w_in[part, :])
+        grad_edges[:, part] = (cot[:, part].astype(F32) + back).astype(BF)
+    wait_all(copies([(grad_edges, grad_out)], out_sems))
+
+
+def add_halo(halo, middle, above, below, new_rows, columns, held):
     held[...] = middle[...]
     for j in range(HB):
         for place, value in ((halo[0, 0, j], above), (halo[0, 1, j], below)):
@@ -413,13 +421,19 @@
             columns[l, :, pl.ds(block * BLK, BLK)] = held[
                 block, pl.ds(l * width, width), :
             ].astype(BF)
-
-
-def finish(arrived, out):
-    total = arrived[0].astype(F32)
+    last = pl.ds(held.shape[0] * BLK, BLK)
+    for l in range(columns.shape[0]):
+        columns[l, :, last] = new_rows[pl.ds(l * width, width), :]
+
+
+def finish(arrived, out, new_nodes):
+    cells = pl.ds(0, out.shape[1])
+    total = arrived[0, :, cells].astype(F32)
     for l in range(1, arrived.shape[0]):
-        total = total + arrived[l].astype(F32)
+        total = total + arrived[l, :, cells].astype(F32)
     out[...] = total.astype(BF)
+    for l in range(arrived.shape[0]):
+        new_nodes[:, pl.ds(l * BLK, BLK)] = arrived[l, :, pl.ds(out.shape[1], BLK)]
 
 
 def call(kernel, out_shape, scratch, mib, spaces, operands, flops=0, out_spaces="", sems=()):
@@ -477,17 +491,17 @@
     rows = [((BLK, 2 * L), BF), ((BLK, L), BF), ((BLK, L), BF), ((BLK, L), BF)]
     return call(
         node_step,
-        [shape_of((lat_size, L + L // lat_size, BLK), BF), shape_of((L, BLK), F32)]
+        [shape_of((lat_size, L, BLK), BF), shape_of((L, BLK), BF), shape_of((L, BLK), F32)]
         + [shape_of(*row) for row in rows],
         [((L, BLK), BF), ((L, BLK), BF), ((2 * L, L), BF), ((L, L), BF)]
         + rows
-        + [((L, BLK), F32)],
+        + [((L, BLK), F32), ((L, BLK), BF)],
         NODE_MIB,
-        "svhh" + "v" * len(shards) + "v",
+        "svhhh" + "v" * (len(shards) - 1) + "v",
         (scal, spread, own, up, *shards, gain),
         flops=2 * BLK * 6 * L * L,
-        out_spaces="vhhhhh",
-        sems=(2, 5),
+        out_spaces="vhhhhhh",
+        sems=(2 + 4, 6),
     )
 
 
@@ -530,18 +544,16 @@
     )
 
 
-def run_edge_inputs(scal, d_first, cot, offsets, d_direct, shards, lat_size):
-    rows = cot.shape[0]
+def run_edge_inputs(scal, d_first, offsets, d_direct, shards, lat_size):
+    rows = d_first.shape[0]
     return call(
         edge_inputs,
         [
-            shape_of((rows, L), BF),
             shape_of((lat_size, L, BLK), F32),
             shape_of((L, HB * BLK), BF),
             shape_of((L, HB * BLK), BF),
         ],
         [
-            ((rows, L), BF),
             (d_direct.shape, F32),
             ((3 * L, L), BF),
             ((L, L), BF),
@@ -549,10 +561,24 @@
             ((2 * L, rows), F32),
         ],
         EDGE_MIB,
-        "svvvh" + "h" * len(shards),
-        (scal, d_first, cot, offsets, d_direct, *shards),
-        flops=2 * rows * 3 * L * L,
-        out_spaces="hvvv",
+        "svvh" + "h" * len(shards),
+        (scal, d_first, offsets, d_direct, *shards),
+        flops=2 * rows * 2 * L * L,
+        sems=(1 + 2 * len(shards),),
+    )
+
+
+def run_edge_grads(scal, d_first, cot, shards):
+    rows = cot.shape[0]
+    return call(
+        edge_grads,
+        [shape_of((rows, L), BF)],
+        [((rows, L), BF), ((rows, L), BF), ((3 * L, L), BF), ((L, L), BF)],
+        EDGE_MIB,
+        "svh" + "h" * len(shards),
+        (scal, d_first, cot, *shards),
+        flops=2 * rows * L * L,
+        out_spaces="h",
         sems=(1 + 2 * len(shards), 1),
     )
 
@@ -666,36 +692,38 @@
     )
     node_shards = gather_far(node_part)
     spread = spread_rows(partial, LAT)
-    second_out, d_direct, *node_saved = run_node_step(
+    second_out, new_rows, d_direct, *node_saved = run_node_step(
         node_scal, spread, own, node_up, node_shards, node_gain_row
     )
     node_keep, node_send = run_node_grads(
         node_scal, node_saved, node_part, lax.axis_size("y")
     )
     second_in = spread_rows(second_out, LAT)
-    new_nodes = second_in[:, L:].transpose(1, 0, 2).reshape(width, slab_rows).T
     node_far = reduce_far(node_keep, node_send)
 
     d_first, edge_keep, edge_send = run_edge_backward(
         scal, second_in, edge_cotangent, offsets, edge_gain_row,
         (normed, inverse, first, joined), edge_shards,
     )
-    grad_edges, middle, lower, upper = run_edge_inputs(
-        scal, d_first, edge_cotangent, offsets, d_direct, edge_shards, lat_size
+    middle, lower, upper = run_edge_inputs(
+        scal, d_first, offsets, d_direct, edge_shards, lat_size
     )
     from_above = from_behind(lower, -1)
     from_below = from_behind(upper, 1)
+    (grad_edges,) = run_edge_grads(scal, d_first, edge_cotangent, edge_shards)
     edge_far = reduce_far(edge_keep, edge_send)
     (columns,) = call(
         add_halo,
-        [shape_of((lat_size, width, slab_rows), BF)],
+        [shape_of((lat_size, width, slab_rows + own_rows), BF)],
         [((lat_size, L, BLK), F32)],
         8,
-        "svvv",
-        (halo, middle, from_above, from_below),
+        "svvvv",
+        (halo, middle, from_above, from_below, new_rows),
     )
     columns = spread_rows(columns, LAT)
-    (grad_slab,) = call(finish, [shape_of((width, slab_rows), BF)], [], 4, "v", (columns,))
+    grad_slab, new_nodes = call(
+        finish, [shape_of((width, slab_rows), BF)] * 2, [], 6, "v", (columns,)
+    )
 
     shard = (32, L)
     shards = (4,) + shard
@@ -720,7 +748,7 @@
     reduced = call(
         sum_x, [shape_of((count, L), F32) for count in pieces], [], 4, "v" * 4, (kept, *moved)
     )
-    return (new_nodes, new_edges, grad_slab.T, grad_edges) + tuple(reduced)
+    return (new_nodes.T, new_edges, grad_slab.T, grad_edges) + tuple(reduced)
 
 
 def solution(mesh):

time: 221 us -> 217 us (0.982)
  waiting for transfers between devices: 79.8 us -> 76.8 us
  Pallas kernels: 33.7 us -> 36.3 us
    ppermute x24, waiting for transfers between devices: 61.5 us -> 58.5 us  [shift(): lax.ppermute(value, axes, [(i, (i + step) % count) for i in range(count)])]
    pallas_call x13 -> x14, Pallas kernels: 33.7 us -> 36.3 us  [call(): pl.pallas_call(kernel, out_shape=placed, in_specs=[pl.BlockSpec(memory_sp...]
  transfers between devices with their start and end apart: 41 -> 41, of which waited for: 22 -> 21; matrix products, arithmetic and copies ran while one was open for 2% -> 2% of each run, Pallas kernels for 6% -> 7%
where the time goes in v9:
time: 217 us; the launch traced here: 216 us
  waiting for transfers between devices  76.8 us (35%)
  starting transfers between devices  73.4 us (34%)
  Pallas kernels  36.3 us (17%)
  blocking collectives  22 us (10%)
  other arithmetic  3.06 us (1%)
  local copies, waits for them, and re-layouts  2.54 us (1%)
    ppermute x24, waiting for transfers between devices, shift(): lax.ppermute(value, axes, [(i, (i + step) % count) for i in range(count)])  58.5 us
    ppermute x24, starting transfers between devices, shift(): lax.ppermute(value, axes, [(i, (i + step) % count) for i in range(count)])  49.2 us
    pallas_call x14, Pallas kernels, call(): pl.pallas_call(kernel, out_shape=placed, in_specs=[pl.BlockSpec(memory_sp...  36.3 us
    all_to_all x1, blocking collectives, spread_rows(): return lax.all_to_all(value, axes, 0, 0)  22 us
    all_to_all x3, starting transfers between devices, spread_rows(): return lax.all_to_all(value, axes, 0, 0)  15.8 us
    all_to_all x3, waiting for transfers between devices, spread_rows(): return lax.all_to_all(value, axes, 0, 0)  11.8 us
    ppermute x4, starting transfers between devices, from_behind(): lax.ppermute(value, SLAB, [(source, source + steps) for source in range(f...  6.92 us
    ppermute x4, waiting for transfers between devices, from_behind(): lax.ppermute(value, SLAB, [(source, source + steps) for source in range(f...  4.75 us
  transfers between devices with their start and end apart: 41, of which 21 were waited for; matrix products, arithmetic and copies ran while one was open for 2% of the time, Pallas kernels for 7%

profile of v9, /device:TPU:0, one launch (start us, length us, event | category | flops | bytes accessed | tf_op | source)
XLA Modules:
  0.0 215.9 jit_solution(8186624861691291452)
XLA Ops:
  5.4 3.6 %collective-permute-done.1.upper = bf16[64,256]{1,0:T(8,128)(2,1)S(1)} collective-permute-done((bf16[64,256]{1,0:T(8,128)(2,1)S(1)}, bf16[64,256]{1,0:T(8,128)(2,1)S(1)}, u32[]{:S(2)}, u32[]{:S(2)}) %collective-permute-start.1) | collective-permute-done | bytes 32800 | tf_op jit(solution)/shard_map/ppermute | solution.py:33
  11.4 7.6 %all-to-all-start = ((bf16[8,64,1664]{2,1,0:T(8,128)(2,1)}), bf16[8,64,1664]{2,1,0:T(8,128)(2,1)S(1)}, u32[]{:S(2)}, u32[]{:S(2)}) async-start(bf16[8,64,1664]{2,1,0:T(8,128)(2,1)} %shard_map.198), calls=%async_computation | async-start | bytes 3407872 | tf_op jit(solution)/shard_map/all_to_all | solution.py:600
  19.0 3.5 %collective-permute-start.2 = (bf16[32,512]{1,0:T(8,128)(2,1)S(1)}, bf16[32,512]{1,0:T(8,128)(2,1)S(1)}, u32[]{:S(2)}, u32[]{:S(2)}) collective-permute-start(bf16[32,512]{1,0:T(8,128)(2,1)S(1)} %get-tuple-element.52), channel_id=1, source_target_pairs={{0,4},{4,16},{16,20},{20,0},{1,5},{5,17},{17,21},{21,1},{2,6},{6,1... | collective-permute-start | bytes 98312 | tf_op jit(solution)/shard_map/ppermute | solution.py:592
  24.5 19.0 %collective-permute-done.2 = bf16[32,512]{1,0:T(8,128)(2,1)S(1)} collective-permute-done((bf16[32,512]{1,0:T(8,128)(2,1)S(1)}, bf16[32,512]{1,0:T(8,128)(2,1)S(1)}, u32[]{:S(2)}, u32[]{:S(2)}) %collective-permute-start.2) | collective-permute-done | bytes 32800 | tf_op jit(solution)/shard_map/ppermute | solution.py:592
  50.5 3.7 %collective-permute-done.6.refs_2_ = bf16[128,512]{1,0:T(8,128)(2,1)S(1)} collective-permute-done((bf16[128,512]{1,0:T(8,128)(2,1)S(1)}, bf16[128,512]{1,0:T(8,128)(2,1)S(1)}, u32[]{:S(2)}, u32[]{:S(2)}) %collective-permute-start.6) | collective-permute-done | bytes 131104 | tf_op jit(solution)/shard_map/ppermute | solution.py:592
  54.9 2.8 %collective-permute-start.8 = (bf16[256,512]{1,0:T(8,128)(2,1)S(1)}, bf16[256,512]{1,0:T(8,128)(2,1)S(1)}, u32[]{:S(2)}, u32[]{:S(2)}) collective-permute-start(bf16[256,512]{1,0:T(8,128)(2,1)S(1)} %get-tuple-element.53.refs_0_.refs_4_), channel_id=1, source_target_pairs={{0,32},{32,64},{64,96},{96,0},{1,33},{33,65},{65,97},{97,1},{2,34}... | collective-permute-start | bytes 786440 | tf_op jit(solution)/shard_map/ppermute | solution.py:592
  57.7 2.9 %collective-permute-start.9 = (bf16[256,512]{1,0:T(8,128)(2,1)S(1)}, bf16[256,512]{1,0:T(8,128)(2,1)S(1)}, u32[]{:S(2)}, u32[]{:S(2)}) collective-permute-start(bf16[256,512]{1,0:T(8,128)(2,1)S(1)} %get-tuple-element.53.refs_0_.refs_4_), channel_id=1, source_target_pairs={{0,64},{32,96},{64,0},{96,32},{1,65},{33,97},{65,1},{97,33},{2,66}... | collective-permute-start | bytes 786440 | tf_op jit(solution)/shard_map/ppermute | solution.py:592
  61.9 3.4 %collective-permute-done.8.refs_1_.refs_5_ = bf16[256,512]{1,0:T(8,128)(2,1)S(1)} collective-permute-done((bf16[256,512]{1,0:T(8,128)(2,1)S(1)}, bf16[256,512]{1,0:T(8,128)(2,1)S(1)}, u32[]{:S(2)}, u32[]{:S(2)}) %collective-permute-start.8) | collective-permute-done | bytes 262176 | tf_op jit(solution)/shard_map/ppermute | solution.py:592
  65.4 5.8 %collective-permute-done.9.refs_2_.refs_6_ = bf16[256,512]{1,0:T(8,128)(2,1)S(1)} collective-permute-done((bf16[256,512]{1,0:T(8,128)(2,1)S(1)}, bf16[256,512]{1,0:T(8,128)(2,1)S(1)}, u32[]{:S(2)}, u32[]{:S(2)}) %collective-permute-start.9) | collective-permute-done | bytes 262176 | tf_op jit(solution)/shard_map/ppermute | solution.py:592
  73.2 6.3 %shard_map.200 = (bf16[512,1536]{1,0:T(8,128)(2,1)}, bf16[512,512]{1,0:T(8,128)(2,1)}, f32[512,512]{1,0:T(8,128)}, f32[512,128]{1,0:T(8,128)}, bf16[512,512]{1,0...) custom-call(s32[12]{0:T(128)S(1)} %concatenate.7.scal, ...), custom_call_target="tpu_custom_call" | custom-call | flops 1073741824 | bytes 10623024 | tf_op jit(solution)/shard_map/pallas_call | solution.py:452
  79.6 4.6 %all-to-all-start.1 = ((f32[8,128,512]{2,1,0:T(8,128)}), f32[8,128,512]{2,1,0:T(8,128)S(1)}, u32[]{:S(2)}, u32[]{:S(2)}) async-start(f32[8,128,512]{2,1,0:T(8,128)} %get-tuple-element.54), calls=%async_computation.1 | async-start | bytes 4194304 | tf_op jit(solution)/shard_map/all_to_all | solution.py:600
  92.7 4.0 %collective-permute-done.16.refs_2_ = bf16[192,512]{1,0:T(8,128)(2,1)S(1)} collective-permute-done((bf16[192,512]{1,0:T(8,128)(2,1)S(1)}, bf16[192,512]{1,0:T(8,128)(2,1)S(1)}, u32[]{:S(2)}, u32[]{:S(2)}) %collective-permute-start.16) | collective-permute-done | bytes 196640 | tf_op jit(solution)/shard_map/ppermute | solution.py:592
  99.1 11.8 %all-to-all-done.1.spread = f32[8,128,512]{2,1,0:T(8,128)S(1)} async-done(((f32[8,128,512]{2,1,0:T(8,128)}), f32[8,128,512]{2,1,0:T(8,128)S(1)}, u32[]{:S(2)}, u32[]{:S(2)}) %all-to-all-start.1) | async-done | bytes 2097184 | tf_op jit(solution)/shard_map/all_to_all | solution.py:600
  111.8 4.1 %shard_map.201 = (bf16[8,512,128]{2,1,0:T(8,128)(2,1)S(1)}, bf16[512,128]{1,0:T(8,128)(2,1)}, f32[512,128]{1,0:T(8,128)}, bf16[128,1024]{1,0:T(8,128)(2,1)}, bf1...) custom-call(s32[3]{0:T(128)S(1)} %pad_add_fusion.scal, ...), custom_call_target="tpu_custom_call" | custom-call | flops 402653184 | bytes 6031372 | tf_op jit(solution)/shard_map/pallas_call | solution.py:452
  116.0 22.0 %all_to_all.20.d_agg = bf16[8,512,128]{2,1,0:T(8,128)(2,1)S(1)} all-to-all(bf16[8,512,128]{2,1,0:T(8,128)(2,1)S(1)} %get-tuple-element.58), channel_id=1, replica_groups=mesh['y'=4,'xl'=2,'c'=2,'xh'=2,'z'=4] {'xh','z'}, dimensions={0} | all-to-all | bytes 2097152 | tf_op jit(solution)/shard_map/all_to_all | solution.py:600
  138.0 5.6 %shard_map.202 = (bf16[512,512]{1,0:T(8,128)(2,1)S(1)}, bf16[4,256,512]{2,1,0:T(8,128)(2,1)S(1)}, bf16[4,256,512]{2,1,0:T(8,128)(2,1)}) custom-call(s32[12]{0:T(128)S(1)} %concatenate.7.scal, bf16[8,512,128]{2,1,0:T(8,128)(2,1)S(1)} %all_to_all.20.d_agg, bf16[512,512]{1,0:T(8,128)(2,1)S(1)} %copy-done.6, s32[2,4,128]{2,1,0:T(4,128)S(1)} %reshape.65.offsets, ...), custom_call_target="tpu_custom_call" | custom-call | flops 1342177280 | bytes 9705520 | tf_op jit(solution)/shard_map/pallas_call | solution.py:452
  143.8 3.3 %shard_map.207 = (bf16[4,192,512]{2,1,0:T(8,128)(2,1)S(1)}, bf16[4,192,512]{2,1,0:T(8,128)(2,1)}) custom-call(s32[3]{0:T(128)S(1)} %pad_add_fusion.scal, bf16[128,1024]{1,0:T(8,128)(2,1)} %get-tuple-element.74.refs_0_, bf16[128,512]{1,0:T(8,128)(2,1)} %get-tuple-element.75.refs_1_, bf16[128,512]{1,0:T(8,128)(2,1)} %get-tuple-element.76.refs_2_, ...), custom_call_target="tpu_custom_call" | custom-call | flops 201326592 | bytes 2228236 | tf_op jit(solution)/shard_map/pallas_call | solution.py:452
  147.6 3.8 %shard_map.203 = (f32[8,512,128]{2,1,0:T(8,128)S(1)}, bf16[512,256]{1,0:T(8,128)(2,1)S(1)}, bf16[512,256]{1,0:T(8,128)(2,1)S(1)}) custom-call(s32[12]{0:T(128)S(1)} %concatenate.7.scal, bf16[512,512]{1,0:T(8,128)(2,1)S(1)} %get-tuple-element.63.d_first, s32[2,4,128]{2,1,0:T(4,128)S(1)} %reshape.65.offsets, f32[512,128]{1,0:T(8,128)} %get-tuple-element.64.direct_in, ...), custom_call_target="tpu_custom_call" | custom-call | flops 536870912 | bytes 5509168 | tf_op jit(solution)/shard_map/pallas_call | solution.py:452
  152.7 3.0 %collective-permute-start.23 = (bf16[512,256]{1,0:T(8,128)(2,1)S(1)}, bf16[512,256]{1,0:T(8,128)(2,1)S(1)}, u32[]{:S(2)}, u32[]{:S(2)}) collective-permute-start(bf16[512,256]{1,0:T(8,128)(2,1)S(1)} %get-tuple-element.67), channel_id=1, source_target_pairs={{0,8},{8,16},{16,24},{24,32},{32,40},{40,48},{48,56},{56,64},{64,7... | collective-permute-start | bytes 786440 | tf_op jit(solution)/shard_map/ppermute | solution.py:33
  158.9 3.6 %all-to-all-start.3 = ((bf16[8,64,1152]{2,1,0:T(8,128)(2,1)}), bf16[8,64,1152]{2,1,0:T(8,128)(2,1)S(1)}, u32[]{:S(2)}, u32[]{:S(2)}) async-start(bf16[8,64,1152]{2,1,0:T(8,128)(2,1)} %shard_map.204), calls=%async_computation.3 | async-start | bytes 2359296 | tf_op jit(solution)/shard_map/all_to_all | solution.py:600
  164.0 6.8 %collective-permute-start.29 = (bf16[192,512]{1,0:T(8,128)(2,1)S(1)}, bf16[192,512]{1,0:T(8,128)(2,1)S(1)}, u32[]{:S(2)}, u32[]{:S(2)}) collective-permute-start(bf16[192,512]{1,0:T(8,128)(2,1)S(1)} %get-tuple-element.98), channel_id=1, source_target_pairs={{0,32},{32,64},{64,96},{96,0},{1,33},{33,65},{65,97},{97,1},{2,34}... | collective-permute-start | bytes 589832 | tf_op jit(solution)/shard_map/ppermute | solution.py:592
  180.2 12.1 %collective-permute-done.30.n2 = bf16[192,512]{1,0:T(8,128)(2,1)S(1)} collective-permute-done((bf16[192,512]{1,0:T(8,128)(2,1)S(1)}, bf16[192,512]{1,0:T(8,128)(2,1)S(1)}, u32[]{:S(2)}, u32[]{:S(2)}) %collective-permute-start.30) | collective-permute-done | bytes 196640 | tf_op jit(solution)/shard_map/ppermute | solution.py:592
  205.2 3.1 %collective-permute-start.35 = (bf16[32,512]{1,0:T(8,128)(2,1)S(1)}, bf16[32,512]{1,0:T(8,128)(2,1)S(1)}, u32[]{:S(2)}, u32[]{:S(2)}) collective-permute-start(bf16[32,512]{1,0:T(8,128)(2,1)S(1)} %get-tuple-element.85), channel_id=1, source_target_pairs={{0,4},{4,16},{16,20},{20,0},{1,5},{5,17},{17,21},{21,1},{2,6},{6,1... | collective-permute-start | bytes 98312 | tf_op jit(solution)/shard_map/ppermute | solution.py:592
  209.8 3.6 %shard_map.206 = bf16[512,512]{1,0:T(8,128)(2,1)} custom-call(s32[12]{0:T(128)S(1)} %concatenate.7.scal, bf16[512,512]{1,0:T(8,128)(2,1)S(1)} %get-tuple-element.63.d_first, bf16[512,512]{1,0:T(8,128)(2,1)} %cot_in.1, bf16[256,512]{1,0:T(8,128)(2,1)} %copy-done, bf16[256,512]{1,0:T(8,128)(2,1)} %copy-done.1, bf16[256,512]{1,0:T(8,128)(2,1)} %copy-done.2, ...), custom_call_target="tpu_custom_call" | custom-call | flops 268435456 | bytes 3670064 | tf_op jit(solution)/shard_map/pallas_call | solution.py:452
  (118 shorter events, 64.1 us)
Async XLA Ops:
  11.4 61.8 %all-to-all-start = ((bf16[8,64,1664]{2,1,0:T(8,128)(2,1)}), bf16[8,64,1664]{2,1,0:T(8,128)(2,1)S(1)}, u32[]{:S(2)}, u32[]{:S(2)}) async-start(bf16[8,64,1664]{2,1,0:T(8,128)(2,1)} %shard_map.198), calls=%async_computation | async-start | bytes 3407872 | tf_op jit(solution)/shard_map/all_to_all | solution.py:600
  19.0 24.5 %collective-permute-start.2 = (bf16[32,512]{1,0:T(8,128)(2,1)S(1)}, bf16[32,512]{1,0:T(8,128)(2,1)S(1)}, u32[]{:S(2)}, u32[]{:S(2)}) collective-permute-start(bf16[32,512]{1,0:T(8,128)(2,1)S(1)} %get-tuple-element.52), channel_id=1, source_target_pairs={{0,4},{4,16},{16,20},{20,0},{1,5},{5,17},{17,21},{21,1},{2,6},{6,1... | collective-permute-start | bytes 98312 | tf_op jit(solution)/shard_map/ppermute | solution.py:592
  22.5 21.0 %collective-permute-start.3 = (bf16[32,512]{1,0:T(8,128)(2,1)S(1)}, bf16[32,512]{1,0:T(8,128)(2,1)S(1)}, u32[]{:S(2)}, u32[]{:S(2)}) collective-permute-start(bf16[32,512]{1,0:T(8,128)(2,1)S(1)} %get-tuple-element.52), channel_id=1, source_target_pairs={{0,16},{4,20},{16,0},{20,4},{1,17},{5,21},{17,1},{21,5},{2,18},{6,... | collective-permute-start | bytes 98312 | tf_op jit(solution)/shard_map/ppermute | solution.py:592
  24.5 19.1 %collective-permute-start.4 = (bf16[32,512]{1,0:T(8,128)(2,1)S(1)}, bf16[32,512]{1,0:T(8,128)(2,1)S(1)}, u32[]{:S(2)}, u32[]{:S(2)}) collective-permute-start(bf16[32,512]{1,0:T(8,128)(2,1)S(1)} %get-tuple-element.52), channel_id=1, source_target_pairs={{0,20},{4,0},{16,4},{20,16},{1,21},{5,1},{17,5},{21,17},{2,22},{6,... | collective-permute-start | bytes 98312 | tf_op jit(solution)/shard_map/ppermute | solution.py:592
  45.1 9.1 %collective-permute-start.6 = (bf16[128,512]{1,0:T(8,128)(2,1)S(1)}, bf16[128,512]{1,0:T(8,128)(2,1)S(1)}, u32[]{:S(2)}, u32[]{:S(2)}) collective-permute-start(bf16[128,512]{1,0:T(8,128)(2,1)S(1)} %constant_dynamic-update-slice_fusion.refs_0_), channel_id=1, source_target_pairs={{0,2},{1,3},{2,0},{3,1},{4,6},{5,7},{6,4},{7,5},{8,10},{9,11},{10,... | collective-permute-start | bytes 393224 | tf_op jit(solution)/shard_map/ppermute | solution.py:592
  54.9 10.5 %collective-permute-start.8 = (bf16[256,512]{1,0:T(8,128)(2,1)S(1)}, bf16[256,512]{1,0:T(8,128)(2,1)S(1)}, u32[]{:S(2)}, u32[]{:S(2)}) collective-permute-start(bf16[256,512]{1,0:T(8,128)(2,1)S(1)} %get-tuple-element.53.refs_0_.refs_4_), channel_id=1, source_target_pairs={{0,32},{32,64},{64,96},{96,0},{1,33},{33,65},{65,97},{97,1},{2,34}... | collective-permute-start | bytes 786440 | tf_op jit(solution)/shard_map/ppermute | solution.py:592
  57.7 13.5 %collective-permute-start.9 = (bf16[256,512]{1,0:T(8,128)(2,1)S(1)}, bf16[256,512]{1,0:T(8,128)(2,1)S(1)}, u32[]{:S(2)}, u32[]{:S(2)}) collective-permute-start(bf16[256,512]{1,0:T(8,128)(2,1)S(1)} %get-tuple-element.53.refs_0_.refs_4_), channel_id=1, source_target_pairs={{0,64},{32,96},{64,0},{96,32},{1,65},{33,97},{65,1},{97,33},{2,66}... | collective-permute-start | bytes 786440 | tf_op jit(solution)/shard_map/ppermute | solution.py:592
  60.6 10.6 %collective-permute-start.10 = (bf16[256,512]{1,0:T(8,128)(2,1)S(1)}, bf16[256,512]{1,0:T(8,128)(2,1)S(1)}, u32[]{:S(2)}, u32[]{:S(2)}) collective-permute-start(bf16[256,512]{1,0:T(8,128)(2,1)S(1)} %get-tuple-element.53.refs_0_.refs_4_), channel_id=1, source_target_pairs={{0,96},{32,0},{64,32},{96,64},{1,97},{33,1},{65,33},{97,65},{2,98}... | collective-permute-start | bytes 786440 | tf_op jit(solution)/shard_map/ppermute | solution.py:592
  61.9 10.6 %collective-permute-start.11 = (bf16[256,512]{1,0:T(8,128)(2,1)S(1)}, bf16[256,512]{1,0:T(8,128)(2,1)S(1)}, u32[]{:S(2)}, u32[]{:S(2)}) collective-permute-start(bf16[256,512]{1,0:T(8,128)(2,1)S(1)} %get-tuple-element.53.refs_0_.refs_4_), channel_id=1, source_target_pairs={{0,8},{8,0},{1,9},{9,1},{2,10},{10,2},{3,11},{11,3},{4,12},{12,4},... | collective-permute-start | bytes 786440 | tf_op jit(solution)/shard_map/ppermute | solution.py:587
  79.6 31.3 %all-to-all-start.1 = ((f32[8,128,512]{2,1,0:T(8,128)}), f32[8,128,512]{2,1,0:T(8,128)S(1)}, u32[]{:S(2)}, u32[]{:S(2)}) async-start(f32[8,128,512]{2,1,0:T(8,128)} %get-tuple-element.54), calls=%async_computation.1 | async-start | bytes 4194304 | tf_op jit(solution)/shard_map/all_to_all | solution.py:600
  84.2 8.5 %collective-permute-start.15 = (bf16[192,512]{1,0:T(8,128)(2,1)S(1)}, bf16[192,512]{1,0:T(8,128)(2,1)S(1)}, u32[]{:S(2)}, u32[]{:S(2)}) collective-permute-start(bf16[192,512]{1,0:T(8,128)(2,1)S(1)} %get-tuple-element.57.refs_0_), channel_id=1, source_target_pairs={{0,32},{32,64},{64,96},{96,0},{1,33},{33,65},{65,97},{97,1},{2,34}... | collective-permute-start | bytes 589832 | tf_op jit(solution)/shard_map/ppermute | solution.py:592
  85.5 11.2 %collective-permute-start.16 = (bf16[192,512]{1,0:T(8,128)(2,1)S(1)}, bf16[192,512]{1,0:T(8,128)(2,1)S(1)}, u32[]{:S(2)}, u32[]{:S(2)}) collective-permute-start(bf16[192,512]{1,0:T(8,128)(2,1)S(1)} %get-tuple-element.57.refs_0_), channel_id=1, source_target_pairs={{0,64},{32,96},{64,0},{96,32},{1,65},{33,97},{65,1},{97,33},{2,66}... | collective-permute-start | bytes 589832 | tf_op jit(solution)/shard_map/ppermute | solution.py:592
  87.9 9.0 %collective-permute-start.17 = (bf16[192,512]{1,0:T(8,128)(2,1)S(1)}, bf16[192,512]{1,0:T(8,128)(2,1)S(1)}, u32[]{:S(2)}, u32[]{:S(2)}) collective-permute-start(bf16[192,512]{1,0:T(8,128)(2,1)S(1)} %get-tuple-element.57.refs_0_), channel_id=1, source_target_pairs={{0,96},{32,0},{64,32},{96,64},{1,97},{33,1},{65,33},{97,65},{2,98}... | collective-permute-start | bytes 589832 | tf_op jit(solution)/shard_map/ppermute | solution.py:592
  90.0 7.4 %collective-permute-start.18 = (bf16[192,512]{1,0:T(8,128)(2,1)S(1)}, bf16[192,512]{1,0:T(8,128)(2,1)S(1)}, u32[]{:S(2)}, u32[]{:S(2)}) collective-permute-start(bf16[192,512]{1,0:T(8,128)(2,1)S(1)} %get-tuple-element.57.refs_0_), channel_id=1, source_target_pairs={{0,8},{8,0},{1,9},{9,1},{2,10},{10,2},{3,11},{11,3},{4,12},{12,4},... | collective-permute-start | bytes 589832 | tf_op jit(solution)/shard_map/ppermute | solution.py:587
  143.6 27.1 %collective-permute-start.24 = (bf16[4,256,512]{2,1,0:T(8,128)(2,1)}, bf16[4,256,512]{2,1,0:T(8,128)(2,1)}, u32[]{:S(2)}, u32[]{:S(2)}) collective-permute-start(bf16[4,256,512]{2,1,0:T(8,128)(2,1)} %get-tuple-element.73), channel_id=1, source_target_pairs={{0,8},{8,0},{1,9},{9,1},{2,10},{10,2},{3,11},{11,3},{4,12},{12,4},... | collective-permute-start | bytes 3145736 | tf_op jit(solution)/shard_map/ppermute | solution.py:587
  147.1 15.5 %collective-permute-start.28 = (bf16[4,192,512]{2,1,0:T(8,128)(2,1)}, bf16[4,192,512]{2,1,0:T(8,128)(2,1)}, u32[]{:S(2)}, u32[]{:S(2)}) collective-permute-start(bf16[4,192,512]{2,1,0:T(8,128)(2,1)} %get-tuple-element.79), channel_id=1, source_target_pairs={{0,8},{8,0},{1,9},{9,1},{2,10},{10,2},{3,11},{11,3},{4,12},{12,4},... | collective-permute-start | bytes 2359304 | tf_op jit(solution)/shard_map/ppermute | solution.py:587
  158.9 54.5 %all-to-all-start.3 = ((bf16[8,64,1152]{2,1,0:T(8,128)(2,1)}), bf16[8,64,1152]{2,1,0:T(8,128)(2,1)S(1)}, u32[]{:S(2)}, u32[]{:S(2)}) async-start(bf16[8,64,1152]{2,1,0:T(8,128)(2,1)} %shard_map.204), calls=%async_computation.3 | async-start | bytes 2359296 | tf_op jit(solution)/shard_map/all_to_all | solution.py:600
  164.0 14.5 %collective-permute-start.29 = (bf16[192,512]{1,0:T(8,128)(2,1)S(1)}, bf16[192,512]{1,0:T(8,128)(2,1)S(1)}, u32[]{:S(2)}, u32[]{:S(2)}) collective-permute-start(bf16[192,512]{1,0:T(8,128)(2,1)S(1)} %get-tuple-element.98), channel_id=1, source_target_pairs={{0,32},{32,64},{64,96},{96,0},{1,33},{33,65},{65,97},{97,1},{2,34}... | collective-permute-start | bytes 589832 | tf_op jit(solution)/shard_map/ppermute | solution.py:592
  172.2 22.0 %collective-permute-start.25 = (bf16[256,512]{1,0:T(8,128)(2,1)S(1)}, bf16[256,512]{1,0:T(8,128)(2,1)S(1)}, u32[]{:S(2)}, u32[]{:S(2)}) collective-permute-start(bf16[256,512]{1,0:T(8,128)(2,1)S(1)} %get-tuple-element.94), channel_id=1, source_target_pairs={{0,32},{32,64},{64,96},{96,0},{1,33},{33,65},{65,97},{97,1},{2,34}... | collective-permute-start | bytes 786440 | tf_op jit(solution)/shard_map/ppermute | solution.py:592
  173.7 20.5 %collective-permute-start.26 = (bf16[256,512]{1,0:T(8,128)(2,1)S(1)}, bf16[256,512]{1,0:T(8,128)(2,1)S(1)}, u32[]{:S(2)}, u32[]{:S(2)}) collective-permute-start(bf16[256,512]{1,0:T(8,128)(2,1)S(1)} %get-tuple-element.93), channel_id=1, source_target_pairs={{0,64},{32,96},{64,0},{96,32},{1,65},{33,97},{65,1},{97,33},{2,66}... | collective-permute-start | bytes 786440 | tf_op jit(solution)/shard_map/ppermute | solution.py:592
  175.5 18.7 %collective-permute-start.27 = (bf16[256,512]{1,0:T(8,128)(2,1)S(1)}, bf16[256,512]{1,0:T(8,128)(2,1)S(1)}, u32[]{:S(2)}, u32[]{:S(2)}) collective-permute-start(bf16[256,512]{1,0:T(8,128)(2,1)S(1)} %get-tuple-element.92), channel_id=1, source_target_pairs={{0,96},{32,0},{64,32},{96,64},{1,97},{33,1},{65,33},{97,65},{2,98}... | collective-permute-start | bytes 786440 | tf_op jit(solution)/shard_map/ppermute | solution.py:592
  178.1 14.2 %collective-permute-start.30 = (bf16[192,512]{1,0:T(8,128)(2,1)S(1)}, bf16[192,512]{1,0:T(8,128)(2,1)S(1)}, u32[]{:S(2)}, u32[]{:S(2)}) collective-permute-start(bf16[192,512]{1,0:T(8,128)(2,1)S(1)} %get-tuple-element.97), channel_id=1, source_target_pairs={{0,64},{32,96},{64,0},{96,32},{1,65},{33,97},{65,1},{97,33},{2,66}... | collective-permute-start | bytes 589832 | tf_op jit(solution)/shard_map/ppermute | solution.py:592
  178.4 15.8 %collective-permute-start.31 = (bf16[192,512]{1,0:T(8,128)(2,1)S(1)}, bf16[192,512]{1,0:T(8,128)(2,1)S(1)}, u32[]{:S(2)}, u32[]{:S(2)}) collective-permute-start(bf16[192,512]{1,0:T(8,128)(2,1)S(1)} %get-tuple-element.96), channel_id=1, source_target_pairs={{0,96},{32,0},{64,32},{96,64},{1,97},{33,1},{65,33},{97,65},{2,98}... | collective-permute-start | bytes 589832 | tf_op jit(solution)/shard_map/ppermute | solution.py:592
  205.2 9.0 %collective-permute-start.35 = (bf16[32,512]{1,0:T(8,128)(2,1)S(1)}, bf16[32,512]{1,0:T(8,128)(2,1)S(1)}, u32[]{:S(2)}, u32[]{:S(2)}) collective-permute-start(bf16[32,512]{1,0:T(8,128)(2,1)S(1)} %get-tuple-element.85), channel_id=1, source_target_pairs={{0,4},{4,16},{16,20},{20,0},{1,5},{5,17},{17,21},{21,1},{2,6},{6,1... | collective-permute-start | bytes 98312 | tf_op jit(solution)/shard_map/ppermute | solution.py:592
  (34 other events, 448.2 us)

commit v10 on v9

--- a/solution.py
+++ b/solution.py
@@ -329,8 +329,8 @@
 
 def edge_backward(scal, d_agg, cot, offsets, gain, *refs):
     saved, w_out_shards, refs = refs[:4], refs[4:12], refs[12:]
-    d_first, keep, send = refs[:3]
-    joined, first, normed, inverse, w_in, w_out, d_second, g_in, g_out, sems = refs[3:]
+    d_first, d_first_out, keep, send = refs[:4]
+    joined, first, normed, inverse, w_in, w_out, d_second, g_in, g_out, sems, out_sems = refs[4:]
     tiles = cot.shape[0] // BLK
     lat_index, core, y_index, count = (scal[2 * tiles + i] for i in range(4))
     slabs = w_in.shape[0] // 3 // 32
@@ -354,6 +354,7 @@
         part = pl.ds(n * 256, 256)
         back = dot_transpose(d_second[...], w_out[part, :])
         d_first[:, part] = jnp.where(first[:, part].astype(F32) > 0, back, 0.0).astype(BF)
+    store = copies([(d_first, d_first_out)], out_sems)
     for n in range(2):
         part = pl.ds(n * 256, 256)
         g_out[part, :] = dot_rows(first[:, part], d_second[...])
@@ -361,6 +362,7 @@
         part = pl.ds(n * 256, 256)
         g_in[part, :] = dot_rows(joined[:, part], d_first[...])
     pack_grads(core, y_index, (g_in, g_out), keep, send, counts)
+    wait_all(store)
 
 
 def edge_inputs(scal, d_first, offsets, direct_in, *refs):
@@ -395,14 +397,15 @@
     middle_out[...] = d_ext[pl.ds(HB, blocks)]
 
 
-def edge_grads(scal, d_first, cot_in, *refs):
-    shards, (grad_out, grad_edges, cot, w_in, w_out, sems, out_sems) = refs[:8], refs[8:]
+def edge_grads(scal, d_first_in, cot_in, *refs):
+    shards, refs = refs[:8], refs[8:]
+    grad_out, grad_edges, cot, d_first, w_in, w_out, sems, out_sems = refs
     tiles = cot.shape[0] // BLK
     core, y_index = scal[2 * tiles + 1], scal[2 * tiles + 2]
     slabs = w_in.shape[0] // 3 // 32
     counts = (3 * L // slabs, L // slabs)
     pairs = weight_pairs(core, y_index, shards, (w_in, w_out), counts)[::2]
-    wait_all(copies(pairs + [(cot_in, cot)], sems))
+    wait_all(copies(pairs + [(cot_in, cot), (d_first_in, d_first)], sems))
     for n in range(2):
         part = pl.ds(n * 256, 256)
         back = dot_transpose(d_first[...], w_in[part, :])
@@ -524,7 +527,7 @@
     normed, inverse, first, joined = saved
     return call(
         edge_backward,
-        [shape_of((rows, L), BF), shape_of(chunk, BF), shape_of(chunk, BF)],
+        [shape_of((rows, L), BF)] * 2 + [shape_of(chunk, BF)] * 2,
         [
             (joined.shape, BF),
             (first.shape, BF),
@@ -540,7 +543,8 @@
         "svvvv" + "h" * (len(saved) + len(shards)),
         (scal, d_agg, cot, offsets, gain, *saved, *shards),
         flops=2 * rows * 5 * L * L,
-        sems=(4 + 2 * len(shards),),
+        out_spaces="vhvv",
+        sems=(4 + 2 * len(shards), 1),
     )
 
 
@@ -573,13 +577,13 @@
     return call(
         edge_grads,
         [shape_of((rows, L), BF)],
-        [((rows, L), BF), ((rows, L), BF), ((3 * L, L), BF), ((L, L), BF)],
+        [((rows, L), BF)] * 3 + [((3 * L, L), BF), ((L, L), BF)],
         EDGE_MIB,
-        "svh" + "h" * len(shards),
+        "shh" + "h" * len(shards),
         (scal, d_first, cot, *shards),
         flops=2 * rows * L * L,
         out_spaces="h",
-        sems=(1 + 2 * len(shards), 1),
+        sems=(2 + 2 * len(shards), 1),
     )
 
 
@@ -701,7 +705,7 @@
     second_in = spread_rows(second_out, LAT)
     node_far = reduce_far(node_keep, node_send)
 
-    d_first, edge_keep, edge_send = run_edge_backward(
+    d_first, d_first_kept, edge_keep, edge_send = run_edge_backward(
         scal, second_in, edge_cotangent, offsets, edge_gain_row,
         (normed, inverse, first, joined), edge_shards,
     )
@@ -710,7 +714,7 @@
     )
     from_above = from_behind(lower, -1)
     from_below = from_behind(upper, 1)
-    (grad_edges,) = run_edge_grads(scal, d_first, edge_cotangent, edge_shards)
+    (grad_edges,) = run_edge_grads(scal, d_first_kept, edge_cotangent, edge_shards)
     edge_far = reduce_far(edge_keep, edge_send)
     (columns,) = call(
         add_halo,

time: 217 us -> 219 us (level)
  transfers between devices with their start and end apart: 41 -> 41, of which waited for: 21 -> 21; matrix products, arithmetic and copies ran while one was open for 2% -> 1% of each run, Pallas kernels for 7% -> 7%
where the time goes in v10:
time: 219 us; the launch traced here: 217 us
  waiting for transfers between devices  76.6 us (35%)
  starting transfers between devices  73.5 us (34%)
  Pallas kernels  37.3 us (17%)
  blocking collectives  22 us (10%)
  local copies, waits for them, and re-layouts  3.21 us (1%)
  other arithmetic  3.06 us (1%)
    ppermute x24, waiting for transfers between devices, shift(): lax.ppermute(value, axes, [(i, (i + step) % count) for i in range(count)])  58.3 us
    ppermute x24, starting transfers between devices, shift(): lax.ppermute(value, axes, [(i, (i + step) % count) for i in range(count)])  49.2 us
    pallas_call x14, Pallas kernels, call(): pl.pallas_call(kernel, out_shape=placed, in_specs=[pl.BlockSpec(memory_sp...  37.3 us
    all_to_all x1, blocking collectives, spread_rows(): return lax.all_to_all(value, axes, 0, 0)  22 us
    all_to_all x3, starting transfers between devices, spread_rows(): return lax.all_to_all(value, axes, 0, 0)  15.9 us
    all_to_all x3, waiting for transfers between devices, spread_rows(): return lax.all_to_all(value, axes, 0, 0)  11.7 us
    ppermute x4, starting transfers between devices, from_behind(): lax.ppermute(value, SLAB, [(source, source + steps) for source in range(f...  6.92 us
    ppermute x4, waiting for transfers between devices, from_behind(): lax.ppermute(value, SLAB, [(source, source + steps) for source in range(f...  4.75 us
  transfers between devices with their start and end apart: 41, of which 21 were waited for; matrix products, arithmetic and copies ran while one was open for 1% of the time, Pallas kernels for 7%

profile of v10, /device:TPU:0, one launch (start us, length us, event | category | flops | bytes accessed | tf_op | source)
XLA Modules:
  0.0 217.3 jit_solution(854673387991173107)
XLA Ops:
  5.4 3.6 %collective-permute-done.1.upper = bf16[64,256]{1,0:T(8,128)(2,1)S(1)} collective-permute-done((bf16[64,256]{1,0:T(8,128)(2,1)S(1)}, bf16[64,256]{1,0:T(8,128)(2,1)S(1)}, u32[]{:S(2)}, u32[]{:S(2)}) %collective-permute-start.1) | collective-permute-done | bytes 32800 | tf_op jit(solution)/shard_map/ppermute | solution.py:33
  11.4 7.6 %all-to-all-start = ((bf16[8,64,1664]{2,1,0:T(8,128)(2,1)}), bf16[8,64,1664]{2,1,0:T(8,128)(2,1)S(1)}, u32[]{:S(2)}, u32[]{:S(2)}) async-start(bf16[8,64,1664]{2,1,0:T(8,128)(2,1)} %shard_map.198), calls=%async_computation | async-start | bytes 3407872 | tf_op jit(solution)/shard_map/all_to_all | solution.py:604
  19.0 3.5 %collective-permute-start.2 = (bf16[32,512]{1,0:T(8,128)(2,1)S(1)}, bf16[32,512]{1,0:T(8,128)(2,1)S(1)}, u32[]{:S(2)}, u32[]{:S(2)}) collective-permute-start(bf16[32,512]{1,0:T(8,128)(2,1)S(1)} %get-tuple-element.53), channel_id=1, source_target_pairs={{0,4},{4,16},{16,20},{20,0},{1,5},{5,17},{17,21},{21,1},{2,6},{6,1... | collective-permute-start | bytes 98312 | tf_op jit(solution)/shard_map/ppermute | solution.py:596
  24.5 19.0 %collective-permute-done.2 = bf16[32,512]{1,0:T(8,128)(2,1)S(1)} collective-permute-done((bf16[32,512]{1,0:T(8,128)(2,1)S(1)}, bf16[32,512]{1,0:T(8,128)(2,1)S(1)}, u32[]{:S(2)}, u32[]{:S(2)}) %collective-permute-start.2) | collective-permute-done | bytes 32800 | tf_op jit(solution)/shard_map/ppermute | solution.py:596
  50.5 3.7 %collective-permute-done.6.refs_2_ = bf16[128,512]{1,0:T(8,128)(2,1)S(1)} collective-permute-done((bf16[128,512]{1,0:T(8,128)(2,1)S(1)}, bf16[128,512]{1,0:T(8,128)(2,1)S(1)}, u32[]{:S(2)}, u32[]{:S(2)}) %collective-permute-start.6) | collective-permute-done | bytes 131104 | tf_op jit(solution)/shard_map/ppermute | solution.py:596
  55.5 2.7 %collective-permute-start.8 = (bf16[256,512]{1,0:T(8,128)(2,1)S(1)}, bf16[256,512]{1,0:T(8,128)(2,1)S(1)}, u32[]{:S(2)}, u32[]{:S(2)}) collective-permute-start(bf16[256,512]{1,0:T(8,128)(2,1)S(1)} %get-tuple-element.54.refs_0_.refs_4_), channel_id=1, source_target_pairs={{0,32},{32,64},{64,96},{96,0},{1,33},{33,65},{65,97},{97,1},{2,34}... | collective-permute-start | bytes 786440 | tf_op jit(solution)/shard_map/ppermute | solution.py:596
  58.3 2.9 %collective-permute-start.9 = (bf16[256,512]{1,0:T(8,128)(2,1)S(1)}, bf16[256,512]{1,0:T(8,128)(2,1)S(1)}, u32[]{:S(2)}, u32[]{:S(2)}) collective-permute-start(bf16[256,512]{1,0:T(8,128)(2,1)S(1)} %get-tuple-element.54.refs_0_.refs_4_), channel_id=1, source_target_pairs={{0,64},{32,96},{64,0},{96,32},{1,65},{33,97},{65,1},{97,33},{2,66}... | collective-permute-start | bytes 786440 | tf_op jit(solution)/shard_map/ppermute | solution.py:596
  62.5 3.4 %collective-permute-done.8.refs_1_.refs_5_ = bf16[256,512]{1,0:T(8,128)(2,1)S(1)} collective-permute-done((bf16[256,512]{1,0:T(8,128)(2,1)S(1)}, bf16[256,512]{1,0:T(8,128)(2,1)S(1)}, u32[]{:S(2)}, u32[]{:S(2)}) %collective-permute-start.8) | collective-permute-done | bytes 262176 | tf_op jit(solution)/shard_map/ppermute | solution.py:596
  66.0 5.8 %collective-permute-done.9.refs_2_.refs_6_ = bf16[256,512]{1,0:T(8,128)(2,1)S(1)} collective-permute-done((bf16[256,512]{1,0:T(8,128)(2,1)S(1)}, bf16[256,512]{1,0:T(8,128)(2,1)S(1)}, u32[]{:S(2)}, u32[]{:S(2)}) %collective-permute-start.9) | collective-permute-done | bytes 262176 | tf_op jit(solution)/shard_map/ppermute | solution.py:596
  73.8 6.3 %shard_map.200 = (bf16[512,1536]{1,0:T(8,128)(2,1)}, bf16[512,512]{1,0:T(8,128)(2,1)}, f32[512,512]{1,0:T(8,128)}, f32[512,128]{1,0:T(8,128)}, bf16[512,512]{1,0...) custom-call(s32[12]{0:T(128)S(1)} %concatenate.7.scal, ...), custom_call_target="tpu_custom_call" | custom-call | flops 1073741824 | bytes 10623024 | tf_op jit(solution)/shard_map/pallas_call | solution.py:455
  80.2 4.7 %all-to-all-start.1 = ((f32[8,128,512]{2,1,0:T(8,128)}), f32[8,128,512]{2,1,0:T(8,128)S(1)}, u32[]{:S(2)}, u32[]{:S(2)}) async-start(f32[8,128,512]{2,1,0:T(8,128)} %get-tuple-element.55), calls=%async_computation.1 | async-start | bytes 4194304 | tf_op jit(solution)/shard_map/all_to_all | solution.py:604
  93.5 4.0 %collective-permute-done.16.refs_2_ = bf16[192,512]{1,0:T(8,128)(2,1)S(1)} collective-permute-done((bf16[192,512]{1,0:T(8,128)(2,1)S(1)}, bf16[192,512]{1,0:T(8,128)(2,1)S(1)}, u32[]{:S(2)}, u32[]{:S(2)}) %collective-permute-start.16) | collective-permute-done | bytes 196640 | tf_op jit(solution)/shard_map/ppermute | solution.py:596
  99.9 11.7 %all-to-all-done.1.spread = f32[8,128,512]{2,1,0:T(8,128)S(1)} async-done(((f32[8,128,512]{2,1,0:T(8,128)}), f32[8,128,512]{2,1,0:T(8,128)S(1)}, u32[]{:S(2)}, u32[]{:S(2)}) %all-to-all-start.1) | async-done | bytes 2097184 | tf_op jit(solution)/shard_map/all_to_all | solution.py:604
  112.6 4.2 %shard_map.201 = (bf16[8,512,128]{2,1,0:T(8,128)(2,1)S(1)}, bf16[512,128]{1,0:T(8,128)(2,1)}, f32[512,128]{1,0:T(8,128)}, bf16[128,1024]{1,0:T(8,128)(2,1)}, bf1...) custom-call(s32[3]{0:T(128)S(1)} %pad_add_fusion.scal, ...), custom_call_target="tpu_custom_call" | custom-call | flops 402653184 | bytes 6031372 | tf_op jit(solution)/shard_map/pallas_call | solution.py:455
  116.7 22.0 %all_to_all.20.d_agg = bf16[8,512,128]{2,1,0:T(8,128)(2,1)S(1)} all-to-all(bf16[8,512,128]{2,1,0:T(8,128)(2,1)S(1)} %get-tuple-element.59), channel_id=1, replica_groups=mesh['y'=4,'xl'=2,'c'=2,'xh'=2,'z'=4] {'xh','z'}, dimensions={0} | all-to-all | bytes 2097152 | tf_op jit(solution)/shard_map/all_to_all | solution.py:604
  138.8 6.3 %shard_map.202 = (bf16[512,512]{1,0:T(8,128)(2,1)S(1)}, bf16[512,512]{1,0:T(8,128)(2,1)}, bf16[4,256,512]{2,1,0:T(8,128)(2,1)S(1)}, bf16[4,256,512]{2,1,0:T(8,128)(2,1)}) custom-call(s32[12]{0:T(128)S(1)} %concatenate.7.scal, bf16[8,512,128]{2,1,0:T(8,128)(2,1)S(1)} %all_to_all.20.d_agg, bf16[512,512]{1,0:T(8,128)(2,1)S(1)} %copy-done.6, ...), custom_call_target="tpu_custom_call" | custom-call | flops 1342177280 | bytes 10229808 | tf_op jit(solution)/shard_map/pallas_call | solution.py:455
  145.2 3.3 %shard_map.207 = (bf16[4,192,512]{2,1,0:T(8,128)(2,1)S(1)}, bf16[4,192,512]{2,1,0:T(8,128)(2,1)}) custom-call(s32[3]{0:T(128)S(1)} %pad_add_fusion.scal, bf16[128,1024]{1,0:T(8,128)(2,1)} %get-tuple-element.76.refs_0_, bf16[128,512]{1,0:T(8,128)(2,1)} %get-tuple-element.77.refs_1_, bf16[128,512]{1,0:T(8,128)(2,1)} %get-tuple-element.78.refs_2_, ...), custom_call_target="tpu_custom_call" | custom-call | flops 201326592 | bytes 2228236 | tf_op jit(solution)/shard_map/pallas_call | solution.py:455
  149.1 3.8 %shard_map.203 = (f32[8,512,128]{2,1,0:T(8,128)S(1)}, bf16[512,256]{1,0:T(8,128)(2,1)S(1)}, bf16[512,256]{1,0:T(8,128)(2,1)S(1)}) custom-call(s32[12]{0:T(128)S(1)} %concatenate.7.scal, bf16[512,512]{1,0:T(8,128)(2,1)S(1)} %get-tuple-element.64.d_first, s32[2,4,128]{2,1,0:T(4,128)S(1)} %reshape.65.offsets, f32[512,128]{1,0:T(8,128)} %get-tuple-element.65.direct_in, ...), custom_call_target="tpu_custom_call" | custom-call | flops 536870912 | bytes 5509168 | tf_op jit(solution)/shard_map/pallas_call | solution.py:455
  154.2 3.0 %collective-permute-start.23 = (bf16[512,256]{1,0:T(8,128)(2,1)S(1)}, bf16[512,256]{1,0:T(8,128)(2,1)S(1)}, u32[]{:S(2)}, u32[]{:S(2)}) collective-permute-start(bf16[512,256]{1,0:T(8,128)(2,1)S(1)} %get-tuple-element.68), channel_id=1, source_target_pairs={{0,8},{8,16},{16,24},{24,32},{32,40},{40,48},{48,56},{56,64},{64,7... | collective-permute-start | bytes 786440 | tf_op jit(solution)/shard_map/ppermute | solution.py:33
  160.4 3.6 %all-to-all-start.3 = ((bf16[8,64,1152]{2,1,0:T(8,128)(2,1)}), bf16[8,64,1152]{2,1,0:T(8,128)(2,1)S(1)}, u32[]{:S(2)}, u32[]{:S(2)}) async-start(bf16[8,64,1152]{2,1,0:T(8,128)(2,1)} %shard_map.204), calls=%async_computation.3 | async-start | bytes 2359296 | tf_op jit(solution)/shard_map/all_to_all | solution.py:604
  165.4 6.8 %collective-permute-start.29 = (bf16[192,512]{1,0:T(8,128)(2,1)S(1)}, bf16[192,512]{1,0:T(8,128)(2,1)S(1)}, u32[]{:S(2)}, u32[]{:S(2)}) collective-permute-start(bf16[192,512]{1,0:T(8,128)(2,1)S(1)} %get-tuple-element.100), channel_id=1, source_target_pairs={{0,32},{32,64},{64,96},{96,0},{1,33},{33,65},{65,97},{97,1},{2,34}... | collective-permute-start | bytes 589832 | tf_op jit(solution)/shard_map/ppermute | solution.py:596
  181.7 12.1 %collective-permute-done.30.n2 = bf16[192,512]{1,0:T(8,128)(2,1)S(1)} collective-permute-done((bf16[192,512]{1,0:T(8,128)(2,1)S(1)}, bf16[192,512]{1,0:T(8,128)(2,1)S(1)}, u32[]{:S(2)}, u32[]{:S(2)}) %collective-permute-start.30) | collective-permute-done | bytes 196640 | tf_op jit(solution)/shard_map/ppermute | solution.py:596
  206.7 3.1 %collective-permute-start.35 = (bf16[32,512]{1,0:T(8,128)(2,1)S(1)}, bf16[32,512]{1,0:T(8,128)(2,1)S(1)}, u32[]{:S(2)}, u32[]{:S(2)}) collective-permute-start(bf16[32,512]{1,0:T(8,128)(2,1)S(1)} %get-tuple-element.87), channel_id=1, source_target_pairs={{0,4},{4,16},{16,20},{20,0},{1,5},{5,17},{17,21},{21,1},{2,6},{6,1... | collective-permute-start | bytes 98312 | tf_op jit(solution)/shard_map/ppermute | solution.py:596
  211.3 3.8 %shard_map.206 = bf16[512,512]{1,0:T(8,128)(2,1)} custom-call(s32[12]{0:T(128)S(1)} %concatenate.7.scal, bf16[512,512]{1,0:T(8,128)(2,1)} %get-tuple-element.73.d_first_in, bf16[512,512]{1,0:T(8,128)(2,1)} %cot_in.1, bf16[256,512]{1,0:T(8,128)(2,1)} %copy-done, bf16[256,512]{1,0:T(8,128)(2,1)} %copy-done.1, bf16[256,512]{1,0:T(8,128)(2,1)} %copy-done.2, ...), custom_call_target="tpu_custom_call" | custom-call | flops 268435456 | bytes 3670064 | tf_op jit(solution)/shard_map/pallas_call | solution.py:455
  (120 shorter events, 64.7 us)
Async XLA Ops:
  11.4 62.4 %all-to-all-start = ((bf16[8,64,1664]{2,1,0:T(8,128)(2,1)}), bf16[8,64,1664]{2,1,0:T(8,128)(2,1)S(1)}, u32[]{:S(2)}, u32[]{:S(2)}) async-start(bf16[8,64,1664]{2,1,0:T(8,128)(2,1)} %shard_map.198), calls=%async_computation | async-start | bytes 3407872 | tf_op jit(solution)/shard_map/all_to_all | solution.py:604
  19.0 24.5 %collective-permute-start.2 = (bf16[32,512]{1,0:T(8,128)(2,1)S(1)}, bf16[32,512]{1,0:T(8,128)(2,1)S(1)}, u32[]{:S(2)}, u32[]{:S(2)}) collective-permute-start(bf16[32,512]{1,0:T(8,128)(2,1)S(1)} %get-tuple-element.53), channel_id=1, source_target_pairs={{0,4},{4,16},{16,20},{20,0},{1,5},{5,17},{17,21},{21,1},{2,6},{6,1... | collective-permute-start | bytes 98312 | tf_op jit(solution)/shard_map/ppermute | solution.py:596
  22.6 21.0 %collective-permute-start.3 = (bf16[32,512]{1,0:T(8,128)(2,1)S(1)}, bf16[32,512]{1,0:T(8,128)(2,1)S(1)}, u32[]{:S(2)}, u32[]{:S(2)}) collective-permute-start(bf16[32,512]{1,0:T(8,128)(2,1)S(1)} %get-tuple-element.53), channel_id=1, source_target_pairs={{0,16},{4,20},{16,0},{20,4},{1,17},{5,21},{17,1},{21,5},{2,18},{6,... | collective-permute-start | bytes 98312 | tf_op jit(solution)/shard_map/ppermute | solution.py:596
  24.5 19.1 %collective-permute-start.4 = (bf16[32,512]{1,0:T(8,128)(2,1)S(1)}, bf16[32,512]{1,0:T(8,128)(2,1)S(1)}, u32[]{:S(2)}, u32[]{:S(2)}) collective-permute-start(bf16[32,512]{1,0:T(8,128)(2,1)S(1)} %get-tuple-element.53), channel_id=1, source_target_pairs={{0,20},{4,0},{16,4},{20,16},{1,21},{5,1},{17,5},{21,17},{2,22},{6,... | collective-permute-start | bytes 98312 | tf_op jit(solution)/shard_map/ppermute | solution.py:596
  45.1 9.1 %collective-permute-start.6 = (bf16[128,512]{1,0:T(8,128)(2,1)S(1)}, bf16[128,512]{1,0:T(8,128)(2,1)S(1)}, u32[]{:S(2)}, u32[]{:S(2)}) collective-permute-start(bf16[128,512]{1,0:T(8,128)(2,1)S(1)} %constant_dynamic-update-slice_fusion.refs_0_), channel_id=1, source_target_pairs={{0,2},{1,3},{2,0},{3,1},{4,6},{5,7},{6,4},{7,5},{8,10},{9,11},{10,... | collective-permute-start | bytes 393224 | tf_op jit(solution)/shard_map/ppermute | solution.py:596
  55.5 10.4 %collective-permute-start.8 = (bf16[256,512]{1,0:T(8,128)(2,1)S(1)}, bf16[256,512]{1,0:T(8,128)(2,1)S(1)}, u32[]{:S(2)}, u32[]{:S(2)}) collective-permute-start(bf16[256,512]{1,0:T(8,128)(2,1)S(1)} %get-tuple-element.54.refs_0_.refs_4_), channel_id=1, source_target_pairs={{0,32},{32,64},{64,96},{96,0},{1,33},{33,65},{65,97},{97,1},{2,34}... | collective-permute-start | bytes 786440 | tf_op jit(solution)/shard_map/ppermute | solution.py:596
  58.3 13.5 %collective-permute-start.9 = (bf16[256,512]{1,0:T(8,128)(2,1)S(1)}, bf16[256,512]{1,0:T(8,128)(2,1)S(1)}, u32[]{:S(2)}, u32[]{:S(2)}) collective-permute-start(bf16[256,512]{1,0:T(8,128)(2,1)S(1)} %get-tuple-element.54.refs_0_.refs_4_), channel_id=1, source_target_pairs={{0,64},{32,96},{64,0},{96,32},{1,65},{33,97},{65,1},{97,33},{2,66}... | collective-permute-start | bytes 786440 | tf_op jit(solution)/shard_map/ppermute | solution.py:596
  61.2 10.6 %collective-permute-start.10 = (bf16[256,512]{1,0:T(8,128)(2,1)S(1)}, bf16[256,512]{1,0:T(8,128)(2,1)S(1)}, u32[]{:S(2)}, u32[]{:S(2)}) collective-permute-start(bf16[256,512]{1,0:T(8,128)(2,1)S(1)} %get-tuple-element.54.refs_0_.refs_4_), channel_id=1, source_target_pairs={{0,96},{32,0},{64,32},{96,64},{1,97},{33,1},{65,33},{97,65},{2,98}... | collective-permute-start | bytes 786440 | tf_op jit(solution)/shard_map/ppermute | solution.py:596
  62.5 10.6 %collective-permute-start.11 = (bf16[256,512]{1,0:T(8,128)(2,1)S(1)}, bf16[256,512]{1,0:T(8,128)(2,1)S(1)}, u32[]{:S(2)}, u32[]{:S(2)}) collective-permute-start(bf16[256,512]{1,0:T(8,128)(2,1)S(1)} %get-tuple-element.54.refs_0_.refs_4_), channel_id=1, source_target_pairs={{0,8},{8,0},{1,9},{9,1},{2,10},{10,2},{3,11},{11,3},{4,12},{12,4},... | collective-permute-start | bytes 786440 | tf_op jit(solution)/shard_map/ppermute | solution.py:591
  80.2 31.4 %all-to-all-start.1 = ((f32[8,128,512]{2,1,0:T(8,128)}), f32[8,128,512]{2,1,0:T(8,128)S(1)}, u32[]{:S(2)}, u32[]{:S(2)}) async-start(f32[8,128,512]{2,1,0:T(8,128)} %get-tuple-element.55), calls=%async_computation.1 | async-start | bytes 4194304 | tf_op jit(solution)/shard_map/all_to_all | solution.py:604
  84.9 8.6 %collective-permute-start.15 = (bf16[192,512]{1,0:T(8,128)(2,1)S(1)}, bf16[192,512]{1,0:T(8,128)(2,1)S(1)}, u32[]{:S(2)}, u32[]{:S(2)}) collective-permute-start(bf16[192,512]{1,0:T(8,128)(2,1)S(1)} %copy-done.8), channel_id=1, source_target_pairs={{0,32},{32,64},{64,96},{96,0},{1,33},{33,65},{65,97},{97,1},{2,34}... | collective-permute-start | bytes 589832 | tf_op jit(solution)/shard_map/ppermute | solution.py:596
  86.3 11.3 %collective-permute-start.16 = (bf16[192,512]{1,0:T(8,128)(2,1)S(1)}, bf16[192,512]{1,0:T(8,128)(2,1)S(1)}, u32[]{:S(2)}, u32[]{:S(2)}) collective-permute-start(bf16[192,512]{1,0:T(8,128)(2,1)S(1)} %copy-done.8), channel_id=1, source_target_pairs={{0,64},{32,96},{64,0},{96,32},{1,65},{33,97},{65,1},{97,33},{2,66}... | collective-permute-start | bytes 589832 | tf_op jit(solution)/shard_map/ppermute | solution.py:596
  88.7 9.0 %collective-permute-start.17 = (bf16[192,512]{1,0:T(8,128)(2,1)S(1)}, bf16[192,512]{1,0:T(8,128)(2,1)S(1)}, u32[]{:S(2)}, u32[]{:S(2)}) collective-permute-start(bf16[192,512]{1,0:T(8,128)(2,1)S(1)} %copy-done.8), channel_id=1, source_target_pairs={{0,96},{32,0},{64,32},{96,64},{1,97},{33,1},{65,33},{97,65},{2,98}... | collective-permute-start | bytes 589832 | tf_op jit(solution)/shard_map/ppermute | solution.py:596
  90.8 7.4 %collective-permute-start.18 = (bf16[192,512]{1,0:T(8,128)(2,1)S(1)}, bf16[192,512]{1,0:T(8,128)(2,1)S(1)}, u32[]{:S(2)}, u32[]{:S(2)}) collective-permute-start(bf16[192,512]{1,0:T(8,128)(2,1)S(1)} %copy-done.8), channel_id=1, source_target_pairs={{0,8},{8,0},{1,9},{9,1},{2,10},{10,2},{3,11},{11,3},{4,12},{12,4},... | collective-permute-start | bytes 589832 | tf_op jit(solution)/shard_map/ppermute | solution.py:591
  145.1 27.1 %collective-permute-start.24 = (bf16[4,256,512]{2,1,0:T(8,128)(2,1)}, bf16[4,256,512]{2,1,0:T(8,128)(2,1)}, u32[]{:S(2)}, u32[]{:S(2)}) collective-permute-start(bf16[4,256,512]{2,1,0:T(8,128)(2,1)} %get-tuple-element.75), channel_id=1, source_target_pairs={{0,8},{8,0},{1,9},{9,1},{2,10},{10,2},{3,11},{11,3},{4,12},{12,4},... | collective-permute-start | bytes 3145736 | tf_op jit(solution)/shard_map/ppermute | solution.py:591
  148.5 15.5 %collective-permute-start.28 = (bf16[4,192,512]{2,1,0:T(8,128)(2,1)}, bf16[4,192,512]{2,1,0:T(8,128)(2,1)}, u32[]{:S(2)}, u32[]{:S(2)}) collective-permute-start(bf16[4,192,512]{2,1,0:T(8,128)(2,1)} %get-tuple-element.81), channel_id=1, source_target_pairs={{0,8},{8,0},{1,9},{9,1},{2,10},{10,2},{3,11},{11,3},{4,12},{12,4},... | collective-permute-start | bytes 2359304 | tf_op jit(solution)/shard_map/ppermute | solution.py:591
  160.4 54.7 %all-to-all-start.3 = ((bf16[8,64,1152]{2,1,0:T(8,128)(2,1)}), bf16[8,64,1152]{2,1,0:T(8,128)(2,1)S(1)}, u32[]{:S(2)}, u32[]{:S(2)}) async-start(bf16[8,64,1152]{2,1,0:T(8,128)(2,1)} %shard_map.204), calls=%async_computation.3 | async-start | bytes 2359296 | tf_op jit(solution)/shard_map/all_to_all | solution.py:604
  165.4 14.5 %collective-permute-start.29 = (bf16[192,512]{1,0:T(8,128)(2,1)S(1)}, bf16[192,512]{1,0:T(8,128)(2,1)S(1)}, u32[]{:S(2)}, u32[]{:S(2)}) collective-permute-start(bf16[192,512]{1,0:T(8,128)(2,1)S(1)} %get-tuple-element.100), channel_id=1, source_target_pairs={{0,32},{32,64},{64,96},{96,0},{1,33},{33,65},{65,97},{97,1},{2,34}... | collective-permute-start | bytes 589832 | tf_op jit(solution)/shard_map/ppermute | solution.py:596
  173.7 22.0 %collective-permute-start.25 = (bf16[256,512]{1,0:T(8,128)(2,1)S(1)}, bf16[256,512]{1,0:T(8,128)(2,1)S(1)}, u32[]{:S(2)}, u32[]{:S(2)}) collective-permute-start(bf16[256,512]{1,0:T(8,128)(2,1)S(1)} %get-tuple-element.96), channel_id=1, source_target_pairs={{0,32},{32,64},{64,96},{96,0},{1,33},{33,65},{65,97},{97,1},{2,34}... | collective-permute-start | bytes 786440 | tf_op jit(solution)/shard_map/ppermute | solution.py:596
  175.2 20.5 %collective-permute-start.26 = (bf16[256,512]{1,0:T(8,128)(2,1)S(1)}, bf16[256,512]{1,0:T(8,128)(2,1)S(1)}, u32[]{:S(2)}, u32[]{:S(2)}) collective-permute-start(bf16[256,512]{1,0:T(8,128)(2,1)S(1)} %get-tuple-element.95), channel_id=1, source_target_pairs={{0,64},{32,96},{64,0},{96,32},{1,65},{33,97},{65,1},{97,33},{2,66}... | collective-permute-start | bytes 786440 | tf_op jit(solution)/shard_map/ppermute | solution.py:596
  177.0 18.7 %collective-permute-start.27 = (bf16[256,512]{1,0:T(8,128)(2,1)S(1)}, bf16[256,512]{1,0:T(8,128)(2,1)S(1)}, u32[]{:S(2)}, u32[]{:S(2)}) collective-permute-start(bf16[256,512]{1,0:T(8,128)(2,1)S(1)} %get-tuple-element.94), channel_id=1, source_target_pairs={{0,96},{32,0},{64,32},{96,64},{1,97},{33,1},{65,33},{97,65},{2,98}... | collective-permute-start | bytes 786440 | tf_op jit(solution)/shard_map/ppermute | solution.py:596
  179.5 14.2 %collective-permute-start.30 = (bf16[192,512]{1,0:T(8,128)(2,1)S(1)}, bf16[192,512]{1,0:T(8,128)(2,1)S(1)}, u32[]{:S(2)}, u32[]{:S(2)}) collective-permute-start(bf16[192,512]{1,0:T(8,128)(2,1)S(1)} %get-tuple-element.99), channel_id=1, source_target_pairs={{0,64},{32,96},{64,0},{96,32},{1,65},{33,97},{65,1},{97,33},{2,66}... | collective-permute-start | bytes 589832 | tf_op jit(solution)/shard_map/ppermute | solution.py:596
  179.9 15.8 %collective-permute-start.31 = (bf16[192,512]{1,0:T(8,128)(2,1)S(1)}, bf16[192,512]{1,0:T(8,128)(2,1)S(1)}, u32[]{:S(2)}, u32[]{:S(2)}) collective-permute-start(bf16[192,512]{1,0:T(8,128)(2,1)S(1)} %get-tuple-element.98), channel_id=1, source_target_pairs={{0,96},{32,0},{64,32},{96,64},{1,97},{33,1},{65,33},{97,65},{2,98}... | collective-permute-start | bytes 589832 | tf_op jit(solution)/shard_map/ppermute | solution.py:596
  206.7 9.2 %collective-permute-start.35 = (bf16[32,512]{1,0:T(8,128)(2,1)S(1)}, bf16[32,512]{1,0:T(8,128)(2,1)S(1)}, u32[]{:S(2)}, u32[]{:S(2)}) collective-permute-start(bf16[32,512]{1,0:T(8,128)(2,1)S(1)} %get-tuple-element.87), channel_id=1, source_target_pairs={{0,4},{4,16},{16,20},{20,0},{1,5},{5,17},{17,21},{21,1},{2,6},{6,1... | collective-permute-start | bytes 98312 | tf_op jit(solution)/shard_map/ppermute | solution.py:596
  (35 other events, 420.5 us)

commit v11 on v10

--- a/solution.py
+++ b/solution.py
@@ -290,8 +290,8 @@
     slabs = w_in.shape[0] // 2 // 32
     counts = (2 * L // slabs, L // slabs)
     pairs = weight_pairs(core, y_index, shards, (w_in, w_out), counts)
-    loads = copies([(own_hbm, own_turned), (up_hbm, up_turned)] + pairs[:4], sems)
-    for source, target in pairs[4:]:
+    loads = copies([(own_hbm, own_turned), (up_hbm, up_turned)] + pairs[-4:], sems)
+    for source, target in pairs[:-4]:
         target[...] = source[...]
     wait_all(loads)
     own = own_turned[...].astype(F32).T
@@ -500,7 +500,7 @@
         + rows
         + [((L, BLK), F32), ((L, BLK), BF)],
         NODE_MIB,
-        "svhhh" + "v" * (len(shards) - 1) + "v",
+        "svhh" + "v" * (len(shards) - 1) + "hv",
         (scal, spread, own, up, *shards, gain),
         flops=2 * BLK * 6 * L * L,
         out_spaces="vhhhhhh",
@@ -609,8 +609,7 @@
     return mine + [swap_cores(one) for one in mine]
 
 
-def reduce_far(keep, send):
-    arrived = swap_cores(send)
+def reduce_far(keep, arrived):
     both = [(keep[k].astype(F32) + arrived[k].astype(F32)).astype(BF) for k in range(keep.shape[0])]
     return [both[0]] + [shift(both[k], "y", k) for k in range(1, keep.shape[0])]
 
@@ -703,19 +702,18 @@
         node_scal, node_saved, node_part, lax.axis_size("y")
     )
     second_in = spread_rows(second_out, LAT)
-    node_far = reduce_far(node_keep, node_send)
+    node_far = reduce_far(node_keep, swap_cores(node_send))
 
     d_first, d_first_kept, edge_keep, edge_send = run_edge_backward(
         scal, second_in, edge_cotangent, offsets, edge_gain_row,
         (normed, inverse, first, joined), edge_shards,
     )
-    middle, lower, upper = run_edge_inputs(
-        scal, d_first, offsets, d_direct, edge_shards, lat_size
-    )
+    middle, lower, upper = run_edge_inputs(scal, d_first, offsets, d_direct, edge_shards, lat_size)
     from_above = from_behind(lower, -1)
     from_below = from_behind(upper, 1)
     (grad_edges,) = run_edge_grads(scal, d_first_kept, edge_cotangent, edge_shards)
-    edge_far = reduce_far(edge_keep, edge_send)
+    edge_arrived = swap_cores(edge_send)
+    edge_far = reduce_far(edge_keep, edge_arrived)
     (columns,) = call(
         add_halo,
         [shape_of((lat_size, width, slab_rows + own_rows), BF)],

time: 219 us -> 218 us (level)
  transfers between devices with their start and end apart: 41 -> 41, of which waited for: 21 -> 21; matrix products, arithmetic and copies ran while one was open for 1% -> 2% of each run, Pallas kernels for 7% -> 7%
where the time goes in v11:
time: 218 us; the launch traced here: 216 us
  waiting for transfers between devices  77.3 us (35%)
  starting transfers between devices  73.5 us (34%)
  Pallas kernels  37.3 us (17%)
  blocking collectives  22 us (10%)
  other arithmetic  3.06 us (1%)
    ppermute x24, waiting for transfers between devices, shift(): lax.ppermute(value, axes, [(i, (i + step) % count) for i in range(count)])  58.3 us
    ppermute x24, starting transfers between devices, shift(): lax.ppermute(value, axes, [(i, (i + step) % count) for i in range(count)])  49.2 us
    pallas_call x14, Pallas kernels, call(): pl.pallas_call(kernel, out_shape=placed, in_specs=[pl.BlockSpec(memory_sp...  37.3 us
    all_to_all x1, blocking collectives, spread_rows(): return lax.all_to_all(value, axes, 0, 0)  22 us
    all_to_all x3, starting transfers between devices, spread_rows(): return lax.all_to_all(value, axes, 0, 0)  15.9 us
    all_to_all x3, waiting for transfers between devices, spread_rows(): return lax.all_to_all(value, axes, 0, 0)  12.3 us
    ppermute x4, starting transfers between devices, from_behind(): lax.ppermute(value, SLAB, [(source, source + steps) for source in range(f...  6.92 us
    ppermute x4, waiting for transfers between devices, from_behind(): lax.ppermute(value, SLAB, [(source, source + steps) for source in range(f...  4.75 us
  transfers between devices with their start and end apart: 41, of which 21 were waited for; matrix products, arithmetic and copies ran while one was open for 2% of the time, Pallas kernels for 7%

profile of v11, /device:TPU:0, one launch (start us, length us, event | category | flops | bytes accessed | tf_op | source)
XLA Modules:
  0.0 216.4 jit_solution(6799111333223900129)
XLA Ops:
  5.4 3.6 %collective-permute-done.1.upper = bf16[64,256]{1,0:T(8,128)(2,1)S(1)} collective-permute-done((bf16[64,256]{1,0:T(8,128)(2,1)S(1)}, bf16[64,256]{1,0:T(8,128)(2,1)S(1)}, u32[]{:S(2)}, u32[]{:S(2)}) %collective-permute-start.1) | collective-permute-done | bytes 32800 | tf_op jit(solution)/shard_map/ppermute | solution.py:33
  11.4 7.6 %all-to-all-start = ((bf16[8,64,1664]{2,1,0:T(8,128)(2,1)}), bf16[8,64,1664]{2,1,0:T(8,128)(2,1)S(1)}, u32[]{:S(2)}, u32[]{:S(2)}) async-start(bf16[8,64,1664]{2,1,0:T(8,128)(2,1)} %shard_map.198), calls=%async_computation | async-start | bytes 3407872 | tf_op jit(solution)/shard_map/all_to_all | solution.py:604
  19.0 3.5 %collective-permute-start.2 = (bf16[32,512]{1,0:T(8,128)(2,1)S(1)}, bf16[32,512]{1,0:T(8,128)(2,1)S(1)}, u32[]{:S(2)}, u32[]{:S(2)}) collective-permute-start(bf16[32,512]{1,0:T(8,128)(2,1)S(1)} %get-tuple-element.53), channel_id=1, source_target_pairs={{0,4},{4,16},{16,20},{20,0},{1,5},{5,17},{17,21},{21,1},{2,6},{6,1... | collective-permute-start | bytes 98312 | tf_op jit(solution)/shard_map/ppermute | solution.py:596
  24.5 19.0 %collective-permute-done.2 = bf16[32,512]{1,0:T(8,128)(2,1)S(1)} collective-permute-done((bf16[32,512]{1,0:T(8,128)(2,1)S(1)}, bf16[32,512]{1,0:T(8,128)(2,1)S(1)}, u32[]{:S(2)}, u32[]{:S(2)}) %collective-permute-start.2) | collective-permute-done | bytes 32800 | tf_op jit(solution)/shard_map/ppermute | solution.py:596
  50.5 3.7 %collective-permute-done.6.refs_2_ = bf16[128,512]{1,0:T(8,128)(2,1)S(1)} collective-permute-done((bf16[128,512]{1,0:T(8,128)(2,1)S(1)}, bf16[128,512]{1,0:T(8,128)(2,1)S(1)}, u32[]{:S(2)}, u32[]{:S(2)}) %collective-permute-start.6) | collective-permute-done | bytes 131104 | tf_op jit(solution)/shard_map/ppermute | solution.py:596
  58.3 2.9 %collective-permute-start.9 = (bf16[256,512]{1,0:T(8,128)(2,1)S(1)}, bf16[256,512]{1,0:T(8,128)(2,1)S(1)}, u32[]{:S(2)}, u32[]{:S(2)}) collective-permute-start(bf16[256,512]{1,0:T(8,128)(2,1)S(1)} %get-tuple-element.54.refs_0_.refs_4_), channel_id=1, source_target_pairs={{0,64},{32,96},{64,0},{96,32},{1,65},{33,97},{65,1},{97,33},{2,66}... | collective-permute-start | bytes 786440 | tf_op jit(solution)/shard_map/ppermute | solution.py:596
  62.5 3.4 %collective-permute-done.8.refs_1_.refs_5_ = bf16[256,512]{1,0:T(8,128)(2,1)S(1)} collective-permute-done((bf16[256,512]{1,0:T(8,128)(2,1)S(1)}, bf16[256,512]{1,0:T(8,128)(2,1)S(1)}, u32[]{:S(2)}, u32[]{:S(2)}) %collective-permute-start.8) | collective-permute-done | bytes 262176 | tf_op jit(solution)/shard_map/ppermute | solution.py:596
  66.0 5.8 %collective-permute-done.9.refs_2_.refs_6_ = bf16[256,512]{1,0:T(8,128)(2,1)S(1)} collective-permute-done((bf16[256,512]{1,0:T(8,128)(2,1)S(1)}, bf16[256,512]{1,0:T(8,128)(2,1)S(1)}, u32[]{:S(2)}, u32[]{:S(2)}) %collective-permute-start.9) | collective-permute-done | bytes 262176 | tf_op jit(solution)/shard_map/ppermute | solution.py:596
  73.8 6.3 %shard_map.200 = (bf16[512,1536]{1,0:T(8,128)(2,1)}, bf16[512,512]{1,0:T(8,128)(2,1)}, f32[512,512]{1,0:T(8,128)}, f32[512,128]{1,0:T(8,128)}, bf16[512,512]{1,0...) custom-call(s32[12]{0:T(128)S(1)} %concatenate.7.scal, ...), custom_call_target="tpu_custom_call" | custom-call | flops 1073741824 | bytes 10623024 | tf_op jit(solution)/shard_map/pallas_call | solution.py:455
  80.2 4.7 %all-to-all-start.1 = ((f32[8,128,512]{2,1,0:T(8,128)}), f32[8,128,512]{2,1,0:T(8,128)S(1)}, u32[]{:S(2)}, u32[]{:S(2)}) async-start(f32[8,128,512]{2,1,0:T(8,128)} %get-tuple-element.55), calls=%async_computation.1 | async-start | bytes 4194304 | tf_op jit(solution)/shard_map/all_to_all | solution.py:604
  90.8 2.8 %collective-permute-done.15.refs_1_ = bf16[192,512]{1,0:T(8,128)(2,1)S(1)} collective-permute-done((bf16[192,512]{1,0:T(8,128)(2,1)S(1)}, bf16[192,512]{1,0:T(8,128)(2,1)S(1)}, u32[]{:S(2)}, u32[]{:S(2)}) %collective-permute-start.15) | collective-permute-done | bytes 196640 | tf_op jit(solution)/shard_map/ppermute | solution.py:596
  93.6 4.0 %collective-permute-done.16.refs_2_ = bf16[192,512]{1,0:T(8,128)(2,1)S(1)} collective-permute-done((bf16[192,512]{1,0:T(8,128)(2,1)S(1)}, bf16[192,512]{1,0:T(8,128)(2,1)S(1)}, u32[]{:S(2)}, u32[]{:S(2)}) %collective-permute-start.16) | collective-permute-done | bytes 196640 | tf_op jit(solution)/shard_map/ppermute | solution.py:596
  99.4 12.3 %all-to-all-done.1.spread = f32[8,128,512]{2,1,0:T(8,128)S(1)} async-done(((f32[8,128,512]{2,1,0:T(8,128)}), f32[8,128,512]{2,1,0:T(8,128)S(1)}, u32[]{:S(2)}, u32[]{:S(2)}) %all-to-all-start.1) | async-done | bytes 2097184 | tf_op jit(solution)/shard_map/all_to_all | solution.py:604
  111.7 4.1 %shard_map.201 = (bf16[8,512,128]{2,1,0:T(8,128)(2,1)S(1)}, bf16[512,128]{1,0:T(8,128)(2,1)}, f32[512,128]{1,0:T(8,128)}, bf16[128,1024]{1,0:T(8,128)(2,1)}, bf1...) custom-call(s32[3]{0:T(128)S(1)} %pad_add_fusion.scal, ...), custom_call_target="tpu_custom_call" | custom-call | flops 402653184 | bytes 6031372 | tf_op jit(solution)/shard_map/pallas_call | solution.py:455
  115.8 22.0 %all_to_all.20.d_agg = bf16[8,512,128]{2,1,0:T(8,128)(2,1)S(1)} all-to-all(bf16[8,512,128]{2,1,0:T(8,128)(2,1)S(1)} %get-tuple-element.59), channel_id=1, replica_groups=mesh['y'=4,'xl'=2,'c'=2,'xh'=2,'z'=4] {'xh','z'}, dimensions={0} | all-to-all | bytes 2097152 | tf_op jit(solution)/shard_map/all_to_all | solution.py:604
  137.8 6.3 %shard_map.202 = (bf16[512,512]{1,0:T(8,128)(2,1)S(1)}, bf16[512,512]{1,0:T(8,128)(2,1)}, bf16[4,256,512]{2,1,0:T(8,128)(2,1)S(1)}, bf16[4,256,512]{2,1,0:T(8,128)(2,1)}) custom-call(s32[12]{0:T(128)S(1)} %concatenate.7.scal, bf16[8,512,128]{2,1,0:T(8,128)(2,1)S(1)} %all_to_all.20.d_agg, bf16[512,512]{1,0:T(8,128)(2,1)S(1)} %copy-done.6, ...), custom_call_target="tpu_custom_call" | custom-call | flops 1342177280 | bytes 10229808 | tf_op jit(solution)/shard_map/pallas_call | solution.py:455
  144.3 3.3 %shard_map.207 = (bf16[4,192,512]{2,1,0:T(8,128)(2,1)S(1)}, bf16[4,192,512]{2,1,0:T(8,128)(2,1)}) custom-call(s32[3]{0:T(128)S(1)} %pad_add_fusion.scal, bf16[128,1024]{1,0:T(8,128)(2,1)} %get-tuple-element.76.refs_0_, bf16[128,512]{1,0:T(8,128)(2,1)} %get-tuple-element.77.refs_1_, bf16[128,512]{1,0:T(8,128)(2,1)} %get-tuple-element.78.refs_2_, ...), custom_call_target="tpu_custom_call" | custom-call | flops 201326592 | bytes 2228236 | tf_op jit(solution)/shard_map/pallas_call | solution.py:455
  148.2 3.8 %shard_map.203 = (f32[8,512,128]{2,1,0:T(8,128)S(1)}, bf16[512,256]{1,0:T(8,128)(2,1)S(1)}, bf16[512,256]{1,0:T(8,128)(2,1)S(1)}) custom-call(s32[12]{0:T(128)S(1)} %concatenate.7.scal, bf16[512,512]{1,0:T(8,128)(2,1)S(1)} %get-tuple-element.64.d_first, s32[2,4,128]{2,1,0:T(4,128)S(1)} %reshape.65.offsets, f32[512,128]{1,0:T(8,128)} %get-tuple-element.65.direct_in, ...), custom_call_target="tpu_custom_call" | custom-call | flops 536870912 | bytes 5509168 | tf_op jit(solution)/shard_map/pallas_call | solution.py:455
  153.3 3.0 %collective-permute-start.23 = (bf16[512,256]{1,0:T(8,128)(2,1)S(1)}, bf16[512,256]{1,0:T(8,128)(2,1)S(1)}, u32[]{:S(2)}, u32[]{:S(2)}) collective-permute-start(bf16[512,256]{1,0:T(8,128)(2,1)S(1)} %get-tuple-element.68), channel_id=1, source_target_pairs={{0,8},{8,16},{16,24},{24,32},{32,40},{40,48},{48,56},{56,64},{64,7... | collective-permute-start | bytes 786440 | tf_op jit(solution)/shard_map/ppermute | solution.py:33
  159.5 3.6 %all-to-all-start.3 = ((bf16[8,64,1152]{2,1,0:T(8,128)(2,1)}), bf16[8,64,1152]{2,1,0:T(8,128)(2,1)S(1)}, u32[]{:S(2)}, u32[]{:S(2)}) async-start(bf16[8,64,1152]{2,1,0:T(8,128)(2,1)} %shard_map.204), calls=%async_computation.3 | async-start | bytes 2359296 | tf_op jit(solution)/shard_map/all_to_all | solution.py:604
  164.5 6.8 %collective-permute-start.29 = (bf16[192,512]{1,0:T(8,128)(2,1)S(1)}, bf16[192,512]{1,0:T(8,128)(2,1)S(1)}, u32[]{:S(2)}, u32[]{:S(2)}) collective-permute-start(bf16[192,512]{1,0:T(8,128)(2,1)S(1)} %get-tuple-element.100), channel_id=1, source_target_pairs={{0,32},{32,64},{64,96},{96,0},{1,33},{33,65},{65,97},{97,1},{2,34}... | collective-permute-start | bytes 589832 | tf_op jit(solution)/shard_map/ppermute | solution.py:596
  180.8 12.1 %collective-permute-done.30.n2 = bf16[192,512]{1,0:T(8,128)(2,1)S(1)} collective-permute-done((bf16[192,512]{1,0:T(8,128)(2,1)S(1)}, bf16[192,512]{1,0:T(8,128)(2,1)S(1)}, u32[]{:S(2)}, u32[]{:S(2)}) %collective-permute-start.30) | collective-permute-done | bytes 196640 | tf_op jit(solution)/shard_map/ppermute | solution.py:596
  205.8 3.1 %collective-permute-start.35 = (bf16[32,512]{1,0:T(8,128)(2,1)S(1)}, bf16[32,512]{1,0:T(8,128)(2,1)S(1)}, u32[]{:S(2)}, u32[]{:S(2)}) collective-permute-start(bf16[32,512]{1,0:T(8,128)(2,1)S(1)} %get-tuple-element.87), channel_id=1, source_target_pairs={{0,4},{4,16},{16,20},{20,0},{1,5},{5,17},{17,21},{21,1},{2,6},{6,1... | collective-permute-start | bytes 98312 | tf_op jit(solution)/shard_map/ppermute | solution.py:596
  210.4 3.8 %shard_map.206 = bf16[512,512]{1,0:T(8,128)(2,1)} custom-call(s32[12]{0:T(128)S(1)} %concatenate.7.scal, bf16[512,512]{1,0:T(8,128)(2,1)} %get-tuple-element.73.d_first_in, bf16[512,512]{1,0:T(8,128)(2,1)} %cot_in.1, bf16[256,512]{1,0:T(8,128)(2,1)} %copy-done, bf16[256,512]{1,0:T(8,128)(2,1)} %copy-done.1, bf16[256,512]{1,0:T(8,128)(2,1)} %copy-done.2, ...), custom_call_target="tpu_custom_call" | custom-call | flops 268435456 | bytes 3670064 | tf_op jit(solution)/shard_map/pallas_call | solution.py:455
  (116 shorter events, 63.2 us)
Async XLA Ops:
  11.4 62.4 %all-to-all-start = ((bf16[8,64,1664]{2,1,0:T(8,128)(2,1)}), bf16[8,64,1664]{2,1,0:T(8,128)(2,1)S(1)}, u32[]{:S(2)}, u32[]{:S(2)}) async-start(bf16[8,64,1664]{2,1,0:T(8,128)(2,1)} %shard_map.198), calls=%async_computation | async-start | bytes 3407872 | tf_op jit(solution)/shard_map/all_to_all | solution.py:604
  19.0 24.5 %collective-permute-start.2 = (bf16[32,512]{1,0:T(8,128)(2,1)S(1)}, bf16[32,512]{1,0:T(8,128)(2,1)S(1)}, u32[]{:S(2)}, u32[]{:S(2)}) collective-permute-start(bf16[32,512]{1,0:T(8,128)(2,1)S(1)} %get-tuple-element.53), channel_id=1, source_target_pairs={{0,4},{4,16},{16,20},{20,0},{1,5},{5,17},{17,21},{21,1},{2,6},{6,1... | collective-permute-start | bytes 98312 | tf_op jit(solution)/shard_map/ppermute | solution.py:596
  22.6 21.0 %collective-permute-start.3 = (bf16[32,512]{1,0:T(8,128)(2,1)S(1)}, bf16[32,512]{1,0:T(8,128)(2,1)S(1)}, u32[]{:S(2)}, u32[]{:S(2)}) collective-permute-start(bf16[32,512]{1,0:T(8,128)(2,1)S(1)} %get-tuple-element.53), channel_id=1, source_target_pairs={{0,16},{4,20},{16,0},{20,4},{1,17},{5,21},{17,1},{21,5},{2,18},{6,... | collective-permute-start | bytes 98312 | tf_op jit(solution)/shard_map/ppermute | solution.py:596
  24.5 19.1 %collective-permute-start.4 = (bf16[32,512]{1,0:T(8,128)(2,1)S(1)}, bf16[32,512]{1,0:T(8,128)(2,1)S(1)}, u32[]{:S(2)}, u32[]{:S(2)}) collective-permute-start(bf16[32,512]{1,0:T(8,128)(2,1)S(1)} %get-tuple-element.53), channel_id=1, source_target_pairs={{0,20},{4,0},{16,4},{20,16},{1,21},{5,1},{17,5},{21,17},{2,22},{6,... | collective-permute-start | bytes 98312 | tf_op jit(solution)/shard_map/ppermute | solution.py:596
  45.1 9.1 %collective-permute-start.6 = (bf16[128,512]{1,0:T(8,128)(2,1)S(1)}, bf16[128,512]{1,0:T(8,128)(2,1)S(1)}, u32[]{:S(2)}, u32[]{:S(2)}) collective-permute-start(bf16[128,512]{1,0:T(8,128)(2,1)S(1)} %constant_dynamic-update-slice_fusion.refs_0_), channel_id=1, source_target_pairs={{0,2},{1,3},{2,0},{3,1},{4,6},{5,7},{6,4},{7,5},{8,10},{9,11},{10,... | collective-permute-start | bytes 393224 | tf_op jit(solution)/shard_map/ppermute | solution.py:596
  55.5 10.4 %collective-permute-start.8 = (bf16[256,512]{1,0:T(8,128)(2,1)S(1)}, bf16[256,512]{1,0:T(8,128)(2,1)S(1)}, u32[]{:S(2)}, u32[]{:S(2)}) collective-permute-start(bf16[256,512]{1,0:T(8,128)(2,1)S(1)} %get-tuple-element.54.refs_0_.refs_4_), channel_id=1, source_target_pairs={{0,32},{32,64},{64,96},{96,0},{1,33},{33,65},{65,97},{97,1},{2,34}... | collective-permute-start | bytes 786440 | tf_op jit(solution)/shard_map/ppermute | solution.py:596
  58.3 13.5 %collective-permute-start.9 = (bf16[256,512]{1,0:T(8,128)(2,1)S(1)}, bf16[256,512]{1,0:T(8,128)(2,1)S(1)}, u32[]{:S(2)}, u32[]{:S(2)}) collective-permute-start(bf16[256,512]{1,0:T(8,128)(2,1)S(1)} %get-tuple-element.54.refs_0_.refs_4_), channel_id=1, source_target_pairs={{0,64},{32,96},{64,0},{96,32},{1,65},{33,97},{65,1},{97,33},{2,66}... | collective-permute-start | bytes 786440 | tf_op jit(solution)/shard_map/ppermute | solution.py:596
  61.2 10.6 %collective-permute-start.10 = (bf16[256,512]{1,0:T(8,128)(2,1)S(1)}, bf16[256,512]{1,0:T(8,128)(2,1)S(1)}, u32[]{:S(2)}, u32[]{:S(2)}) collective-permute-start(bf16[256,512]{1,0:T(8,128)(2,1)S(1)} %get-tuple-element.54.refs_0_.refs_4_), channel_id=1, source_target_pairs={{0,96},{32,0},{64,32},{96,64},{1,97},{33,1},{65,33},{97,65},{2,98}... | collective-permute-start | bytes 786440 | tf_op jit(solution)/shard_map/ppermute | solution.py:596
  62.5 10.6 %collective-permute-start.11 = (bf16[256,512]{1,0:T(8,128)(2,1)S(1)}, bf16[256,512]{1,0:T(8,128)(2,1)S(1)}, u32[]{:S(2)}, u32[]{:S(2)}) collective-permute-start(bf16[256,512]{1,0:T(8,128)(2,1)S(1)} %get-tuple-element.54.refs_0_.refs_4_), channel_id=1, source_target_pairs={{0,8},{8,0},{1,9},{9,1},{2,10},{10,2},{3,11},{11,3},{4,12},{12,4},... | collective-permute-start | bytes 786440 | tf_op jit(solution)/shard_map/ppermute | solution.py:591
  80.2 31.4 %all-to-all-start.1 = ((f32[8,128,512]{2,1,0:T(8,128)}), f32[8,128,512]{2,1,0:T(8,128)S(1)}, u32[]{:S(2)}, u32[]{:S(2)}) async-start(f32[8,128,512]{2,1,0:T(8,128)} %get-tuple-element.55), calls=%async_computation.1 | async-start | bytes 4194304 | tf_op jit(solution)/shard_map/all_to_all | solution.py:604
  84.9 8.6 %collective-permute-start.15 = (bf16[192,512]{1,0:T(8,128)(2,1)S(1)}, bf16[192,512]{1,0:T(8,128)(2,1)S(1)}, u32[]{:S(2)}, u32[]{:S(2)}) collective-permute-start(bf16[192,512]{1,0:T(8,128)(2,1)S(1)} %copy-done.8), channel_id=1, source_target_pairs={{0,32},{32,64},{64,96},{96,0},{1,33},{33,65},{65,97},{97,1},{2,34}... | collective-permute-start | bytes 589832 | tf_op jit(solution)/shard_map/ppermute | solution.py:596
  86.3 11.2 %collective-permute-start.16 = (bf16[192,512]{1,0:T(8,128)(2,1)S(1)}, bf16[192,512]{1,0:T(8,128)(2,1)S(1)}, u32[]{:S(2)}, u32[]{:S(2)}) collective-permute-start(bf16[192,512]{1,0:T(8,128)(2,1)S(1)} %copy-done.8), channel_id=1, source_target_pairs={{0,64},{32,96},{64,0},{96,32},{1,65},{33,97},{65,1},{97,33},{2,66}... | collective-permute-start | bytes 589832 | tf_op jit(solution)/shard_map/ppermute | solution.py:596
  88.7 9.0 %collective-permute-start.17 = (bf16[192,512]{1,0:T(8,128)(2,1)S(1)}, bf16[192,512]{1,0:T(8,128)(2,1)S(1)}, u32[]{:S(2)}, u32[]{:S(2)}) collective-permute-start(bf16[192,512]{1,0:T(8,128)(2,1)S(1)} %copy-done.8), channel_id=1, source_target_pairs={{0,96},{32,0},{64,32},{96,64},{1,97},{33,1},{65,33},{97,65},{2,98}... | collective-permute-start | bytes 589832 | tf_op jit(solution)/shard_map/ppermute | solution.py:596
  90.8 7.3 %collective-permute-start.18 = (bf16[192,512]{1,0:T(8,128)(2,1)S(1)}, bf16[192,512]{1,0:T(8,128)(2,1)S(1)}, u32[]{:S(2)}, u32[]{:S(2)}) collective-permute-start(bf16[192,512]{1,0:T(8,128)(2,1)S(1)} %copy-done.8), channel_id=1, source_target_pairs={{0,8},{8,0},{1,9},{9,1},{2,10},{10,2},{3,11},{11,3},{4,12},{12,4},... | collective-permute-start | bytes 589832 | tf_op jit(solution)/shard_map/ppermute | solution.py:591
  144.2 27.1 %collective-permute-start.24 = (bf16[4,256,512]{2,1,0:T(8,128)(2,1)}, bf16[4,256,512]{2,1,0:T(8,128)(2,1)}, u32[]{:S(2)}, u32[]{:S(2)}) collective-permute-start(bf16[4,256,512]{2,1,0:T(8,128)(2,1)} %get-tuple-element.75), channel_id=1, source_target_pairs={{0,8},{8,0},{1,9},{9,1},{2,10},{10,2},{3,11},{11,3},{4,12},{12,4},... | collective-permute-start | bytes 3145736 | tf_op jit(solution)/shard_map/ppermute | solution.py:591
  147.6 15.5 %collective-permute-start.28 = (bf16[4,192,512]{2,1,0:T(8,128)(2,1)}, bf16[4,192,512]{2,1,0:T(8,128)(2,1)}, u32[]{:S(2)}, u32[]{:S(2)}) collective-permute-start(bf16[4,192,512]{2,1,0:T(8,128)(2,1)} %get-tuple-element.81), channel_id=1, source_target_pairs={{0,8},{8,0},{1,9},{9,1},{2,10},{10,2},{3,11},{11,3},{4,12},{12,4},... | collective-permute-start | bytes 2359304 | tf_op jit(solution)/shard_map/ppermute | solution.py:591
  159.5 54.7 %all-to-all-start.3 = ((bf16[8,64,1152]{2,1,0:T(8,128)(2,1)}), bf16[8,64,1152]{2,1,0:T(8,128)(2,1)S(1)}, u32[]{:S(2)}, u32[]{:S(2)}) async-start(bf16[8,64,1152]{2,1,0:T(8,128)(2,1)} %shard_map.204), calls=%async_computation.3 | async-start | bytes 2359296 | tf_op jit(solution)/shard_map/all_to_all | solution.py:604
  164.5 14.5 %collective-permute-start.29 = (bf16[192,512]{1,0:T(8,128)(2,1)S(1)}, bf16[192,512]{1,0:T(8,128)(2,1)S(1)}, u32[]{:S(2)}, u32[]{:S(2)}) collective-permute-start(bf16[192,512]{1,0:T(8,128)(2,1)S(1)} %get-tuple-element.100), channel_id=1, source_target_pairs={{0,32},{32,64},{64,96},{96,0},{1,33},{33,65},{65,97},{97,1},{2,34}... | collective-permute-start | bytes 589832 | tf_op jit(solution)/shard_map/ppermute | solution.py:596
  172.7 22.0 %collective-permute-start.25 = (bf16[256,512]{1,0:T(8,128)(2,1)S(1)}, bf16[256,512]{1,0:T(8,128)(2,1)S(1)}, u32[]{:S(2)}, u32[]{:S(2)}) collective-permute-start(bf16[256,512]{1,0:T(8,128)(2,1)S(1)} %get-tuple-element.96), channel_id=1, source_target_pairs={{0,32},{32,64},{64,96},{96,0},{1,33},{33,65},{65,97},{97,1},{2,34}... | collective-permute-start | bytes 786440 | tf_op jit(solution)/shard_map/ppermute | solution.py:596
  174.3 20.5 %collective-permute-start.26 = (bf16[256,512]{1,0:T(8,128)(2,1)S(1)}, bf16[256,512]{1,0:T(8,128)(2,1)S(1)}, u32[]{:S(2)}, u32[]{:S(2)}) collective-permute-start(bf16[256,512]{1,0:T(8,128)(2,1)S(1)} %get-tuple-element.95), channel_id=1, source_target_pairs={{0,64},{32,96},{64,0},{96,32},{1,65},{33,97},{65,1},{97,33},{2,66}... | collective-permute-start | bytes 786440 | tf_op jit(solution)/shard_map/ppermute | solution.py:596
  176.1 18.7 %collective-permute-start.27 = (bf16[256,512]{1,0:T(8,128)(2,1)S(1)}, bf16[256,512]{1,0:T(8,128)(2,1)S(1)}, u32[]{:S(2)}, u32[]{:S(2)}) collective-permute-start(bf16[256,512]{1,0:T(8,128)(2,1)S(1)} %get-tuple-element.94), channel_id=1, source_target_pairs={{0,96},{32,0},{64,32},{96,64},{1,97},{33,1},{65,33},{97,65},{2,98}... | collective-permute-start | bytes 786440 | tf_op jit(solution)/shard_map/ppermute | solution.py:596
  178.6 14.2 %collective-permute-start.30 = (bf16[192,512]{1,0:T(8,128)(2,1)S(1)}, bf16[192,512]{1,0:T(8,128)(2,1)S(1)}, u32[]{:S(2)}, u32[]{:S(2)}) collective-permute-start(bf16[192,512]{1,0:T(8,128)(2,1)S(1)} %get-tuple-element.99), channel_id=1, source_target_pairs={{0,64},{32,96},{64,0},{96,32},{1,65},{33,97},{65,1},{97,33},{2,66}... | collective-permute-start | bytes 589832 | tf_op jit(solution)/shard_map/ppermute | solution.py:596
  179.0 15.8 %collective-permute-start.31 = (bf16[192,512]{1,0:T(8,128)(2,1)S(1)}, bf16[192,512]{1,0:T(8,128)(2,1)S(1)}, u32[]{:S(2)}, u32[]{:S(2)}) collective-permute-start(bf16[192,512]{1,0:T(8,128)(2,1)S(1)} %get-tuple-element.98), channel_id=1, source_target_pairs={{0,96},{32,0},{64,32},{96,64},{1,97},{33,1},{65,33},{97,65},{2,98}... | collective-permute-start | bytes 589832 | tf_op jit(solution)/shard_map/ppermute | solution.py:596
  205.8 9.2 %collective-permute-start.35 = (bf16[32,512]{1,0:T(8,128)(2,1)S(1)}, bf16[32,512]{1,0:T(8,128)(2,1)S(1)}, u32[]{:S(2)}, u32[]{:S(2)}) collective-permute-start(bf16[32,512]{1,0:T(8,128)(2,1)S(1)} %get-tuple-element.87), channel_id=1, source_target_pairs={{0,4},{4,16},{16,20},{20,0},{1,5},{5,17},{17,21},{21,1},{2,6},{6,1... | collective-permute-start | bytes 98312 | tf_op jit(solution)/shard_map/ppermute | solution.py:596
  (33 other events, 419.1 us)

commit v12 on v10

--- a/solution.py
+++ b/solution.py
@@ -290,8 +290,8 @@
     slabs = w_in.shape[0] // 2 // 32
     counts = (2 * L // slabs, L // slabs)
     pairs = weight_pairs(core, y_index, shards, (w_in, w_out), counts)
-    loads = copies([(own_hbm, own_turned), (up_hbm, up_turned)] + pairs[:4], sems)
-    for source, target in pairs[4:]:
+    loads = copies([(own_hbm, own_turned), (up_hbm, up_turned)] + pairs[-4:], sems)
+    for source, target in pairs[:-4]:
         target[...] = source[...]
     wait_all(loads)
     own = own_turned[...].astype(F32).T
@@ -500,7 +500,7 @@
         + rows
         + [((L, BLK), F32), ((L, BLK), BF)],
         NODE_MIB,
-        "svhhh" + "v" * (len(shards) - 1) + "v",
+        "svhh" + "v" * (len(shards) - 1) + "hv",
         (scal, spread, own, up, *shards, gain),
         flops=2 * BLK * 6 * L * L,
         out_spaces="vhhhhhh",

time: 219 us -> 218 us (level)
  transfers between devices with their start and end apart: 41 -> 41, of which waited for: 21 -> 21; matrix products, arithmetic and copies ran while one was open for 1% -> 2% of each run, Pallas kernels for 7% -> 7%
where the time goes in v12:
time: 218 us; the launch traced here: 216 us
  waiting for transfers between devices  77.3 us (35%)
  starting transfers between devices  73.5 us (34%)
  Pallas kernels  37.3 us (17%)
  blocking collectives  22 us (10%)
  other arithmetic  3.06 us (1%)
    ppermute x24, waiting for transfers between devices, shift(): lax.ppermute(value, axes, [(i, (i + step) % count) for i in range(count)])  58.3 us
    ppermute x24, starting transfers between devices, shift(): lax.ppermute(value, axes, [(i, (i + step) % count) for i in range(count)])  49.2 us
    pallas_call x14, Pallas kernels, call(): pl.pallas_call(kernel, out_shape=placed, in_specs=[pl.BlockSpec(memory_sp...  37.3 us
    all_to_all x1, blocking collectives, spread_rows(): return lax.all_to_all(value, axes, 0, 0)  22 us
    all_to_all x3, starting transfers between devices, spread_rows(): return lax.all_to_all(value, axes, 0, 0)  15.9 us
    all_to_all x3, waiting for transfers between devices, spread_rows(): return lax.all_to_all(value, axes, 0, 0)  12.3 us
    ppermute x4, starting transfers between devices, from_behind(): lax.ppermute(value, SLAB, [(source, source + steps) for source in range(f...  6.92 us
    ppermute x4, waiting for transfers between devices, from_behind(): lax.ppermute(value, SLAB, [(source, source + steps) for source in range(f...  4.75 us
  transfers between devices with their start and end apart: 41, of which 21 were waited for; matrix products, arithmetic and copies ran while one was open for 2% of the time, Pallas kernels for 7%

profile of v12, /device:TPU:0, one launch (start us, length us, event | category | flops | bytes accessed | tf_op | source)
XLA Modules:
  0.0 216.4 jit_solution(6799111333223900129)
XLA Ops:
  5.4 3.6 %collective-permute-done.1.upper = bf16[64,256]{1,0:T(8,128)(2,1)S(1)} collective-permute-done((bf16[64,256]{1,0:T(8,128)(2,1)S(1)}, bf16[64,256]{1,0:T(8,128)(2,1)S(1)}, u32[]{:S(2)}, u32[]{:S(2)}) %collective-permute-start.1) | collective-permute-done | bytes 32800 | tf_op jit(solution)/shard_map/ppermute | solution.py:33
  11.4 7.6 %all-to-all-start = ((bf16[8,64,1664]{2,1,0:T(8,128)(2,1)}), bf16[8,64,1664]{2,1,0:T(8,128)(2,1)S(1)}, u32[]{:S(2)}, u32[]{:S(2)}) async-start(bf16[8,64,1664]{2,1,0:T(8,128)(2,1)} %shard_map.198), calls=%async_computation | async-start | bytes 3407872 | tf_op jit(solution)/shard_map/all_to_all | solution.py:604
  19.0 3.5 %collective-permute-start.2 = (bf16[32,512]{1,0:T(8,128)(2,1)S(1)}, bf16[32,512]{1,0:T(8,128)(2,1)S(1)}, u32[]{:S(2)}, u32[]{:S(2)}) collective-permute-start(bf16[32,512]{1,0:T(8,128)(2,1)S(1)} %get-tuple-element.53), channel_id=1, source_target_pairs={{0,4},{4,16},{16,20},{20,0},{1,5},{5,17},{17,21},{21,1},{2,6},{6,1... | collective-permute-start | bytes 98312 | tf_op jit(solution)/shard_map/ppermute | solution.py:596
  24.5 19.0 %collective-permute-done.2 = bf16[32,512]{1,0:T(8,128)(2,1)S(1)} collective-permute-done((bf16[32,512]{1,0:T(8,128)(2,1)S(1)}, bf16[32,512]{1,0:T(8,128)(2,1)S(1)}, u32[]{:S(2)}, u32[]{:S(2)}) %collective-permute-start.2) | collective-permute-done | bytes 32800 | tf_op jit(solution)/shard_map/ppermute | solution.py:596
  50.5 3.7 %collective-permute-done.6.refs_2_ = bf16[128,512]{1,0:T(8,128)(2,1)S(1)} collective-permute-done((bf16[128,512]{1,0:T(8,128)(2,1)S(1)}, bf16[128,512]{1,0:T(8,128)(2,1)S(1)}, u32[]{:S(2)}, u32[]{:S(2)}) %collective-permute-start.6) | collective-permute-done | bytes 131104 | tf_op jit(solution)/shard_map/ppermute | solution.py:596
  58.3 2.9 %collective-permute-start.9 = (bf16[256,512]{1,0:T(8,128)(2,1)S(1)}, bf16[256,512]{1,0:T(8,128)(2,1)S(1)}, u32[]{:S(2)}, u32[]{:S(2)}) collective-permute-start(bf16[256,512]{1,0:T(8,128)(2,1)S(1)} %get-tuple-element.54.refs_0_.refs_4_), channel_id=1, source_target_pairs={{0,64},{32,96},{64,0},{96,32},{1,65},{33,97},{65,1},{97,33},{2,66}... | collective-permute-start | bytes 786440 | tf_op jit(solution)/shard_map/ppermute | solution.py:596
  62.5 3.4 %collective-permute-done.8.refs_1_.refs_5_ = bf16[256,512]{1,0:T(8,128)(2,1)S(1)} collective-permute-done((bf16[256,512]{1,0:T(8,128)(2,1)S(1)}, bf16[256,512]{1,0:T(8,128)(2,1)S(1)}, u32[]{:S(2)}, u32[]{:S(2)}) %collective-permute-start.8) | collective-permute-done | bytes 262176 | tf_op jit(solution)/shard_map/ppermute | solution.py:596
  66.0 5.8 %collective-permute-done.9.refs_2_.refs_6_ = bf16[256,512]{1,0:T(8,128)(2,1)S(1)} collective-permute-done((bf16[256,512]{1,0:T(8,128)(2,1)S(1)}, bf16[256,512]{1,0:T(8,128)(2,1)S(1)}, u32[]{:S(2)}, u32[]{:S(2)}) %collective-permute-start.9) | collective-permute-done | bytes 262176 | tf_op jit(solution)/shard_map/ppermute | solution.py:596
  73.8 6.3 %shard_map.200 = (bf16[512,1536]{1,0:T(8,128)(2,1)}, bf16[512,512]{1,0:T(8,128)(2,1)}, f32[512,512]{1,0:T(8,128)}, f32[512,128]{1,0:T(8,128)}, bf16[512,512]{1,0...) custom-call(s32[12]{0:T(128)S(1)} %concatenate.7.scal, ...), custom_call_target="tpu_custom_call" | custom-call | flops 1073741824 | bytes 10623024 | tf_op jit(solution)/shard_map/pallas_call | solution.py:455
  80.2 4.7 %all-to-all-start.1 = ((f32[8,128,512]{2,1,0:T(8,128)}), f32[8,128,512]{2,1,0:T(8,128)S(1)}, u32[]{:S(2)}, u32[]{:S(2)}) async-start(f32[8,128,512]{2,1,0:T(8,128)} %get-tuple-element.55), calls=%async_computation.1 | async-start | bytes 4194304 | tf_op jit(solution)/shard_map/all_to_all | solution.py:604
  90.8 2.8 %collective-permute-done.15.refs_1_ = bf16[192,512]{1,0:T(8,128)(2,1)S(1)} collective-permute-done((bf16[192,512]{1,0:T(8,128)(2,1)S(1)}, bf16[192,512]{1,0:T(8,128)(2,1)S(1)}, u32[]{:S(2)}, u32[]{:S(2)}) %collective-permute-start.15) | collective-permute-done | bytes 196640 | tf_op jit(solution)/shard_map/ppermute | solution.py:596
  93.6 4.0 %collective-permute-done.16.refs_2_ = bf16[192,512]{1,0:T(8,128)(2,1)S(1)} collective-permute-done((bf16[192,512]{1,0:T(8,128)(2,1)S(1)}, bf16[192,512]{1,0:T(8,128)(2,1)S(1)}, u32[]{:S(2)}, u32[]{:S(2)}) %collective-permute-start.16) | collective-permute-done | bytes 196640 | tf_op jit(solution)/shard_map/ppermute | solution.py:596
  99.4 12.3 %all-to-all-done.1.spread = f32[8,128,512]{2,1,0:T(8,128)S(1)} async-done(((f32[8,128,512]{2,1,0:T(8,128)}), f32[8,128,512]{2,1,0:T(8,128)S(1)}, u32[]{:S(2)}, u32[]{:S(2)}) %all-to-all-start.1) | async-done | bytes 2097184 | tf_op jit(solution)/shard_map/all_to_all | solution.py:604
  111.7 4.1 %shard_map.201 = (bf16[8,512,128]{2,1,0:T(8,128)(2,1)S(1)}, bf16[512,128]{1,0:T(8,128)(2,1)}, f32[512,128]{1,0:T(8,128)}, bf16[128,1024]{1,0:T(8,128)(2,1)}, bf1...) custom-call(s32[3]{0:T(128)S(1)} %pad_add_fusion.scal, ...), custom_call_target="tpu_custom_call" | custom-call | flops 402653184 | bytes 6031372 | tf_op jit(solution)/shard_map/pallas_call | solution.py:455
  115.8 22.0 %all_to_all.20.d_agg = bf16[8,512,128]{2,1,0:T(8,128)(2,1)S(1)} all-to-all(bf16[8,512,128]{2,1,0:T(8,128)(2,1)S(1)} %get-tuple-element.59), channel_id=1, replica_groups=mesh['y'=4,'xl'=2,'c'=2,'xh'=2,'z'=4] {'xh','z'}, dimensions={0} | all-to-all | bytes 2097152 | tf_op jit(solution)/shard_map/all_to_all | solution.py:604
  137.8 6.3 %shard_map.202 = (bf16[512,512]{1,0:T(8,128)(2,1)S(1)}, bf16[512,512]{1,0:T(8,128)(2,1)}, bf16[4,256,512]{2,1,0:T(8,128)(2,1)S(1)}, bf16[4,256,512]{2,1,0:T(8,128)(2,1)}) custom-call(s32[12]{0:T(128)S(1)} %concatenate.7.scal, bf16[8,512,128]{2,1,0:T(8,128)(2,1)S(1)} %all_to_all.20.d_agg, bf16[512,512]{1,0:T(8,128)(2,1)S(1)} %copy-done.6, ...), custom_call_target="tpu_custom_call" | custom-call | flops 1342177280 | bytes 10229808 | tf_op jit(solution)/shard_map/pallas_call | solution.py:455
  144.3 3.3 %shard_map.207 = (bf16[4,192,512]{2,1,0:T(8,128)(2,1)S(1)}, bf16[4,192,512]{2,1,0:T(8,128)(2,1)}) custom-call(s32[3]{0:T(128)S(1)} %pad_add_fusion.scal, bf16[128,1024]{1,0:T(8,128)(2,1)} %get-tuple-element.76.refs_0_, bf16[128,512]{1,0:T(8,128)(2,1)} %get-tuple-element.77.refs_1_, bf16[128,512]{1,0:T(8,128)(2,1)} %get-tuple-element.78.refs_2_, ...), custom_call_target="tpu_custom_call" | custom-call | flops 201326592 | bytes 2228236 | tf_op jit(solution)/shard_map/pallas_call | solution.py:455
  148.2 3.8 %shard_map.203 = (f32[8,512,128]{2,1,0:T(8,128)S(1)}, bf16[512,256]{1,0:T(8,128)(2,1)S(1)}, bf16[512,256]{1,0:T(8,128)(2,1)S(1)}) custom-call(s32[12]{0:T(128)S(1)} %concatenate.7.scal, bf16[512,512]{1,0:T(8,128)(2,1)S(1)} %get-tuple-element.64.d_first, s32[2,4,128]{2,1,0:T(4,128)S(1)} %reshape.65.offsets, f32[512,128]{1,0:T(8,128)} %get-tuple-element.65.direct_in, ...), custom_call_target="tpu_custom_call" | custom-call | flops 536870912 | bytes 5509168 | tf_op jit(solution)/shard_map/pallas_call | solution.py:455
  153.3 3.0 %collective-permute-start.23 = (bf16[512,256]{1,0:T(8,128)(2,1)S(1)}, bf16[512,256]{1,0:T(8,128)(2,1)S(1)}, u32[]{:S(2)}, u32[]{:S(2)}) collective-permute-start(bf16[512,256]{1,0:T(8,128)(2,1)S(1)} %get-tuple-element.68), channel_id=1, source_target_pairs={{0,8},{8,16},{16,24},{24,32},{32,40},{40,48},{48,56},{56,64},{64,7... | collective-permute-start | bytes 786440 | tf_op jit(solution)/shard_map/ppermute | solution.py:33
  159.5 3.6 %all-to-all-start.3 = ((bf16[8,64,1152]{2,1,0:T(8,128)(2,1)}), bf16[8,64,1152]{2,1,0:T(8,128)(2,1)S(1)}, u32[]{:S(2)}, u32[]{:S(2)}) async-start(bf16[8,64,1152]{2,1,0:T(8,128)(2,1)} %shard_map.204), calls=%async_computation.3 | async-start | bytes 2359296 | tf_op jit(solution)/shard_map/all_to_all | solution.py:604
  164.5 6.8 %collective-permute-start.29 = (bf16[192,512]{1,0:T(8,128)(2,1)S(1)}, bf16[192,512]{1,0:T(8,128)(2,1)S(1)}, u32[]{:S(2)}, u32[]{:S(2)}) collective-permute-start(bf16[192,512]{1,0:T(8,128)(2,1)S(1)} %get-tuple-element.100), channel_id=1, source_target_pairs={{0,32},{32,64},{64,96},{96,0},{1,33},{33,65},{65,97},{97,1},{2,34}... | collective-permute-start | bytes 589832 | tf_op jit(solution)/shard_map/ppermute | solution.py:596
  180.8 12.1 %collective-permute-done.30.n2 = bf16[192,512]{1,0:T(8,128)(2,1)S(1)} collective-permute-done((bf16[192,512]{1,0:T(8,128)(2,1)S(1)}, bf16[192,512]{1,0:T(8,128)(2,1)S(1)}, u32[]{:S(2)}, u32[]{:S(2)}) %collective-permute-start.30) | collective-permute-done | bytes 196640 | tf_op jit(solution)/shard_map/ppermute | solution.py:596
  205.8 3.1 %collective-permute-start.35 = (bf16[32,512]{1,0:T(8,128)(2,1)S(1)}, bf16[32,512]{1,0:T(8,128)(2,1)S(1)}, u32[]{:S(2)}, u32[]{:S(2)}) collective-permute-start(bf16[32,512]{1,0:T(8,128)(2,1)S(1)} %get-tuple-element.87), channel_id=1, source_target_pairs={{0,4},{4,16},{16,20},{20,0},{1,5},{5,17},{17,21},{21,1},{2,6},{6,1... | collective-permute-start | bytes 98312 | tf_op jit(solution)/shard_map/ppermute | solution.py:596
  210.4 3.8 %shard_map.206 = bf16[512,512]{1,0:T(8,128)(2,1)} custom-call(s32[12]{0:T(128)S(1)} %concatenate.7.scal, bf16[512,512]{1,0:T(8,128)(2,1)} %get-tuple-element.73.d_first_in, bf16[512,512]{1,0:T(8,128)(2,1)} %cot_in.1, bf16[256,512]{1,0:T(8,128)(2,1)} %copy-done, bf16[256,512]{1,0:T(8,128)(2,1)} %copy-done.1, bf16[256,512]{1,0:T(8,128)(2,1)} %copy-done.2, ...), custom_call_target="tpu_custom_call" | custom-call | flops 268435456 | bytes 3670064 | tf_op jit(solution)/shard_map/pallas_call | solution.py:455
  (116 shorter events, 63.2 us)
Async XLA Ops:
  11.4 62.4 %all-to-all-start = ((bf16[8,64,1664]{2,1,0:T(8,128)(2,1)}), bf16[8,64,1664]{2,1,0:T(8,128)(2,1)S(1)}, u32[]{:S(2)}, u32[]{:S(2)}) async-start(bf16[8,64,1664]{2,1,0:T(8,128)(2,1)} %shard_map.198), calls=%async_computation | async-start | bytes 3407872 | tf_op jit(solution)/shard_map/all_to_all | solution.py:604
  19.0 24.5 %collective-permute-start.2 = (bf16[32,512]{1,0:T(8,128)(2,1)S(1)}, bf16[32,512]{1,0:T(8,128)(2,1)S(1)}, u32[]{:S(2)}, u32[]{:S(2)}) collective-permute-start(bf16[32,512]{1,0:T(8,128)(2,1)S(1)} %get-tuple-element.53), channel_id=1, source_target_pairs={{0,4},{4,16},{16,20},{20,0},{1,5},{5,17},{17,21},{21,1},{2,6},{6,1... | collective-permute-start | bytes 98312 | tf_op jit(solution)/shard_map/ppermute | solution.py:596
  22.6 21.0 %collective-permute-start.3 = (bf16[32,512]{1,0:T(8,128)(2,1)S(1)}, bf16[32,512]{1,0:T(8,128)(2,1)S(1)}, u32[]{:S(2)}, u32[]{:S(2)}) collective-permute-start(bf16[32,512]{1,0:T(8,128)(2,1)S(1)} %get-tuple-element.53), channel_id=1, source_target_pairs={{0,16},{4,20},{16,0},{20,4},{1,17},{5,21},{17,1},{21,5},{2,18},{6,... | collective-permute-start | bytes 98312 | tf_op jit(solution)/shard_map/ppermute | solution.py:596
  24.5 19.1 %collective-permute-start.4 = (bf16[32,512]{1,0:T(8,128)(2,1)S(1)}, bf16[32,512]{1,0:T(8,128)(2,1)S(1)}, u32[]{:S(2)}, u32[]{:S(2)}) collective-permute-start(bf16[32,512]{1,0:T(8,128)(2,1)S(1)} %get-tuple-element.53), channel_id=1, source_target_pairs={{0,20},{4,0},{16,4},{20,16},{1,21},{5,1},{17,5},{21,17},{2,22},{6,... | collective-permute-start | bytes 98312 | tf_op jit(solution)/shard_map/ppermute | solution.py:596
  45.1 9.1 %collective-permute-start.6 = (bf16[128,512]{1,0:T(8,128)(2,1)S(1)}, bf16[128,512]{1,0:T(8,128)(2,1)S(1)}, u32[]{:S(2)}, u32[]{:S(2)}) collective-permute-start(bf16[128,512]{1,0:T(8,128)(2,1)S(1)} %constant_dynamic-update-slice_fusion.refs_0_), channel_id=1, source_target_pairs={{0,2},{1,3},{2,0},{3,1},{4,6},{5,7},{6,4},{7,5},{8,10},{9,11},{10,... | collective-permute-start | bytes 393224 | tf_op jit(solution)/shard_map/ppermute | solution.py:596
  55.5 10.4 %collective-permute-start.8 = (bf16[256,512]{1,0:T(8,128)(2,1)S(1)}, bf16[256,512]{1,0:T(8,128)(2,1)S(1)}, u32[]{:S(2)}, u32[]{:S(2)}) collective-permute-start(bf16[256,512]{1,0:T(8,128)(2,1)S(1)} %get-tuple-element.54.refs_0_.refs_4_), channel_id=1, source_target_pairs={{0,32},{32,64},{64,96},{96,0},{1,33},{33,65},{65,97},{97,1},{2,34}... | collective-permute-start | bytes 786440 | tf_op jit(solution)/shard_map/ppermute | solution.py:596
  58.3 13.5 %collective-permute-start.9 = (bf16[256,512]{1,0:T(8,128)(2,1)S(1)}, bf16[256,512]{1,0:T(8,128)(2,1)S(1)}, u32[]{:S(2)}, u32[]{:S(2)}) collective-permute-start(bf16[256,512]{1,0:T(8,128)(2,1)S(1)} %get-tuple-element.54.refs_0_.refs_4_), channel_id=1, source_target_pairs={{0,64},{32,96},{64,0},{96,32},{1,65},{33,97},{65,1},{97,33},{2,66}... | collective-permute-start | bytes 786440 | tf_op jit(solution)/shard_map/ppermute | solution.py:596
  61.2 10.6 %collective-permute-start.10 = (bf16[256,512]{1,0:T(8,128)(2,1)S(1)}, bf16[256,512]{1,0:T(8,128)(2,1)S(1)}, u32[]{:S(2)}, u32[]{:S(2)}) collective-permute-start(bf16[256,512]{1,0:T(8,128)(2,1)S(1)} %get-tuple-element.54.refs_0_.refs_4_), channel_id=1, source_target_pairs={{0,96},{32,0},{64,32},{96,64},{1,97},{33,1},{65,33},{97,65},{2,98}... | collective-permute-start | bytes 786440 | tf_op jit(solution)/shard_map/ppermute | solution.py:596
  62.5 10.6 %collective-permute-start.11 = (bf16[256,512]{1,0:T(8,128)(2,1)S(1)}, bf16[256,512]{1,0:T(8,128)(2,1)S(1)}, u32[]{:S(2)}, u32[]{:S(2)}) collective-permute-start(bf16[256,512]{1,0:T(8,128)(2,1)S(1)} %get-tuple-element.54.refs_0_.refs_4_), channel_id=1, source_target_pairs={{0,8},{8,0},{1,9},{9,1},{2,10},{10,2},{3,11},{11,3},{4,12},{12,4},... | collective-permute-start | bytes 786440 | tf_op jit(solution)/shard_map/ppermute | solution.py:591
  80.2 31.4 %all-to-all-start.1 = ((f32[8,128,512]{2,1,0:T(8,128)}), f32[8,128,512]{2,1,0:T(8,128)S(1)}, u32[]{:S(2)}, u32[]{:S(2)}) async-start(f32[8,128,512]{2,1,0:T(8,128)} %get-tuple-element.55), calls=%async_computation.1 | async-start | bytes 4194304 | tf_op jit(solution)/shard_map/all_to_all | solution.py:604
  84.9 8.6 %collective-permute-start.15 = (bf16[192,512]{1,0:T(8,128)(2,1)S(1)}, bf16[192,512]{1,0:T(8,128)(2,1)S(1)}, u32[]{:S(2)}, u32[]{:S(2)}) collective-permute-start(bf16[192,512]{1,0:T(8,128)(2,1)S(1)} %copy-done.8), channel_id=1, source_target_pairs={{0,32},{32,64},{64,96},{96,0},{1,33},{33,65},{65,97},{97,1},{2,34}... | collective-permute-start | bytes 589832 | tf_op jit(solution)/shard_map/ppermute | solution.py:596
  86.3 11.2 %collective-permute-start.16 = (bf16[192,512]{1,0:T(8,128)(2,1)S(1)}, bf16[192,512]{1,0:T(8,128)(2,1)S(1)}, u32[]{:S(2)}, u32[]{:S(2)}) collective-permute-start(bf16[192,512]{1,0:T(8,128)(2,1)S(1)} %copy-done.8), channel_id=1, source_target_pairs={{0,64},{32,96},{64,0},{96,32},{1,65},{33,97},{65,1},{97,33},{2,66}... | collective-permute-start | bytes 589832 | tf_op jit(solution)/shard_map/ppermute | solution.py:596
  88.7 9.0 %collective-permute-start.17 = (bf16[192,512]{1,0:T(8,128)(2,1)S(1)}, bf16[192,512]{1,0:T(8,128)(2,1)S(1)}, u32[]{:S(2)}, u32[]{:S(2)}) collective-permute-start(bf16[192,512]{1,0:T(8,128)(2,1)S(1)} %copy-done.8), channel_id=1, source_target_pairs={{0,96},{32,0},{64,32},{96,64},{1,97},{33,1},{65,33},{97,65},{2,98}... | collective-permute-start | bytes 589832 | tf_op jit(solution)/shard_map/ppermute | solution.py:596
  90.8 7.3 %collective-permute-start.18 = (bf16[192,512]{1,0:T(8,128)(2,1)S(1)}, bf16[192,512]{1,0:T(8,128)(2,1)S(1)}, u32[]{:S(2)}, u32[]{:S(2)}) collective-permute-start(bf16[192,512]{1,0:T(8,128)(2,1)S(1)} %copy-done.8), channel_id=1, source_target_pairs={{0,8},{8,0},{1,9},{9,1},{2,10},{10,2},{3,11},{11,3},{4,12},{12,4},... | collective-permute-start | bytes 589832 | tf_op jit(solution)/shard_map/ppermute | solution.py:591
  144.2 27.1 %collective-permute-start.24 = (bf16[4,256,512]{2,1,0:T(8,128)(2,1)}, bf16[4,256,512]{2,1,0:T(8,128)(2,1)}, u32[]{:S(2)}, u32[]{:S(2)}) collective-permute-start(bf16[4,256,512]{2,1,0:T(8,128)(2,1)} %get-tuple-element.75), channel_id=1, source_target_pairs={{0,8},{8,0},{1,9},{9,1},{2,10},{10,2},{3,11},{11,3},{4,12},{12,4},... | collective-permute-start | bytes 3145736 | tf_op jit(solution)/shard_map/ppermute | solution.py:591
  147.6 15.5 %collective-permute-start.28 = (bf16[4,192,512]{2,1,0:T(8,128)(2,1)}, bf16[4,192,512]{2,1,0:T(8,128)(2,1)}, u32[]{:S(2)}, u32[]{:S(2)}) collective-permute-start(bf16[4,192,512]{2,1,0:T(8,128)(2,1)} %get-tuple-element.81), channel_id=1, source_target_pairs={{0,8},{8,0},{1,9},{9,1},{2,10},{10,2},{3,11},{11,3},{4,12},{12,4},... | collective-permute-start | bytes 2359304 | tf_op jit(solution)/shard_map/ppermute | solution.py:591
  159.5 54.7 %all-to-all-start.3 = ((bf16[8,64,1152]{2,1,0:T(8,128)(2,1)}), bf16[8,64,1152]{2,1,0:T(8,128)(2,1)S(1)}, u32[]{:S(2)}, u32[]{:S(2)}) async-start(bf16[8,64,1152]{2,1,0:T(8,128)(2,1)} %shard_map.204), calls=%async_computation.3 | async-start | bytes 2359296 | tf_op jit(solution)/shard_map/all_to_all | solution.py:604
  164.5 14.5 %collective-permute-start.29 = (bf16[192,512]{1,0:T(8,128)(2,1)S(1)}, bf16[192,512]{1,0:T(8,128)(2,1)S(1)}, u32[]{:S(2)}, u32[]{:S(2)}) collective-permute-start(bf16[192,512]{1,0:T(8,128)(2,1)S(1)} %get-tuple-element.100), channel_id=1, source_target_pairs={{0,32},{32,64},{64,96},{96,0},{1,33},{33,65},{65,97},{97,1},{2,34}... | collective-permute-start | bytes 589832 | tf_op jit(solution)/shard_map/ppermute | solution.py:596
  172.7 22.0 %collective-permute-start.25 = (bf16[256,512]{1,0:T(8,128)(2,1)S(1)}, bf16[256,512]{1,0:T(8,128)(2,1)S(1)}, u32[]{:S(2)}, u32[]{:S(2)}) collective-permute-start(bf16[256,512]{1,0:T(8,128)(2,1)S(1)} %get-tuple-element.96), channel_id=1, source_target_pairs={{0,32},{32,64},{64,96},{96,0},{1,33},{33,65},{65,97},{97,1},{2,34}... | collective-permute-start | bytes 786440 | tf_op jit(solution)/shard_map/ppermute | solution.py:596
  174.3 20.5 %collective-permute-start.26 = (bf16[256,512]{1,0:T(8,128)(2,1)S(1)}, bf16[256,512]{1,0:T(8,128)(2,1)S(1)}, u32[]{:S(2)}, u32[]{:S(2)}) collective-permute-start(bf16[256,512]{1,0:T(8,128)(2,1)S(1)} %get-tuple-element.95), channel_id=1, source_target_pairs={{0,64},{32,96},{64,0},{96,32},{1,65},{33,97},{65,1},{97,33},{2,66}... | collective-permute-start | bytes 786440 | tf_op jit(solution)/shard_map/ppermute | solution.py:596
  176.1 18.7 %collective-permute-start.27 = (bf16[256,512]{1,0:T(8,128)(2,1)S(1)}, bf16[256,512]{1,0:T(8,128)(2,1)S(1)}, u32[]{:S(2)}, u32[]{:S(2)}) collective-permute-start(bf16[256,512]{1,0:T(8,128)(2,1)S(1)} %get-tuple-element.94), channel_id=1, source_target_pairs={{0,96},{32,0},{64,32},{96,64},{1,97},{33,1},{65,33},{97,65},{2,98}... | collective-permute-start | bytes 786440 | tf_op jit(solution)/shard_map/ppermute | solution.py:596
  178.6 14.2 %collective-permute-start.30 = (bf16[192,512]{1,0:T(8,128)(2,1)S(1)}, bf16[192,512]{1,0:T(8,128)(2,1)S(1)}, u32[]{:S(2)}, u32[]{:S(2)}) collective-permute-start(bf16[192,512]{1,0:T(8,128)(2,1)S(1)} %get-tuple-element.99), channel_id=1, source_target_pairs={{0,64},{32,96},{64,0},{96,32},{1,65},{33,97},{65,1},{97,33},{2,66}... | collective-permute-start | bytes 589832 | tf_op jit(solution)/shard_map/ppermute | solution.py:596
  179.0 15.8 %collective-permute-start.31 = (bf16[192,512]{1,0:T(8,128)(2,1)S(1)}, bf16[192,512]{1,0:T(8,128)(2,1)S(1)}, u32[]{:S(2)}, u32[]{:S(2)}) collective-permute-start(bf16[192,512]{1,0:T(8,128)(2,1)S(1)} %get-tuple-element.98), channel_id=1, source_target_pairs={{0,96},{32,0},{64,32},{96,64},{1,97},{33,1},{65,33},{97,65},{2,98}... | collective-permute-start | bytes 589832 | tf_op jit(solution)/shard_map/ppermute | solution.py:596
  205.8 9.2 %collective-permute-start.35 = (bf16[32,512]{1,0:T(8,128)(2,1)S(1)}, bf16[32,512]{1,0:T(8,128)(2,1)S(1)}, u32[]{:S(2)}, u32[]{:S(2)}) collective-permute-start(bf16[32,512]{1,0:T(8,128)(2,1)S(1)} %get-tuple-element.87), channel_id=1, source_target_pairs={{0,4},{4,16},{16,20},{20,0},{1,5},{5,17},{17,21},{21,1},{2,6},{6,1... | collective-permute-start | bytes 98312 | tf_op jit(solution)/shard_map/ppermute | solution.py:596
  (33 other events, 419.1 us)

commit v13 on v12

--- a/solution.py
+++ b/solution.py
@@ -301,19 +301,23 @@
     for l in range(1, spread.shape[0]):
         total = total + spread[l]
     joined[:, pl.ds(L, L)] = total.astype(BF)
+    stores = copies([(joined, joined_out)], out_sems)
     first[...] = jnp.maximum(dot(joined[...], w_in[...]), 0.0).astype(BF)
+    stores += copies([(first, first_out)], out_sems.at[pl.ds(1, 1)])
     normed, inverse = norm_parts(dot(first[...], w_out[...]))
     d_second[...] = norm_back(upstream, normed, inverse, gain[...]).astype(BF)
     back = dot_transpose(d_second[...], w_out[...])
     d_first[...] = jnp.where(first[...].astype(F32) > 0, back, 0.0).astype(BF)
+    pairs = [(d_second, d_second_out), (d_first, d_first_out)]
+    stores += copies(pairs, out_sems.at[pl.ds(2, 2)])
+    d_direct[...] = dot_transpose(w_in[pl.ds(0, L), :], d_first[...])
+    new_rows[...] = (own + normed * gain[...]).T.astype(BF)
+    pairs = [(d_direct, direct_out), (new_rows, rows_out)]
+    stores += copies(pairs, out_sems.at[pl.ds(4, 2)])
     d_agg = dot_transpose(w_in[pl.ds(L, L), :], d_first[...]).astype(BF)
     for l in range(out.shape[0]):
         out[l] = d_agg
-    new_rows[...] = (own + normed * gain[...]).T.astype(BF)
-    d_direct[...] = dot_transpose(w_in[pl.ds(0, L), :], d_first[...])
-    held = (new_rows, d_direct, joined, first, d_second, d_first)
-    outs = (rows_out, direct_out, joined_out, first_out, d_second_out, d_first_out)
-    wait_all(copies(zip(held, outs), out_sems))
+    wait_all(stores)
 
 
 def node_grads(scal, *refs):

time: 218 us -> 218 us (level)
  no operation moved by 1% of the time
where the time goes in v13:
time: 218 us; the launch traced here: 216 us
  waiting for transfers between devices  77.3 us (35%)
  starting transfers between devices  73.5 us (34%)
  Pallas kernels  37.1 us (17%)
  blocking collectives  22 us (10%)
  other arithmetic  3.06 us (1%)
    ppermute x24, waiting for transfers between devices, shift(): lax.ppermute(value, axes, [(i, (i + step) % count) for i in range(count)])  58.3 us
    ppermute x24, starting transfers between devices, shift(): lax.ppermute(value, axes, [(i, (i + step) % count) for i in range(count)])  49.2 us
    pallas_call x14, Pallas kernels, call(): pl.pallas_call(kernel, out_shape=placed, in_specs=[pl.BlockSpec(memory_sp...  37.1 us
    all_to_all x1, blocking collectives, spread_rows(): return lax.all_to_all(value, axes, 0, 0)  22 us
    all_to_all x3, starting transfers between devices, spread_rows(): return lax.all_to_all(value, axes, 0, 0)  15.9 us
    all_to_all x3, waiting for transfers between devices, spread_rows(): return lax.all_to_all(value, axes, 0, 0)  12.3 us
    ppermute x4, starting transfers between devices, from_behind(): lax.ppermute(value, SLAB, [(source, source + steps) for source in range(f...  6.92 us
    ppermute x4, waiting for transfers between devices, from_behind(): lax.ppermute(value, SLAB, [(source, source + steps) for source in range(f...  4.75 us
  transfers between devices with their start and end apart: 41, of which 21 were waited for; matrix products, arithmetic and copies ran while one was open for 2% of the time, Pallas kernels for 7%

profile of v13, /device:TPU:0, one launch (start us, length us, event | category | flops | bytes accessed | tf_op | source)
XLA Modules:
  0.0 216.2 jit_solution(13713537062281610876)
XLA Ops:
  5.4 3.6 %collective-permute-done.1.upper = bf16[64,256]{1,0:T(8,128)(2,1)S(1)} collective-permute-done((bf16[64,256]{1,0:T(8,128)(2,1)S(1)}, bf16[64,256]{1,0:T(8,128)(2,1)S(1)}, u32[]{:S(2)}, u32[]{:S(2)}) %collective-permute-start.1) | collective-permute-done | bytes 32800 | tf_op jit(solution)/shard_map/ppermute | solution.py:33
  11.4 7.6 %all-to-all-start = ((bf16[8,64,1664]{2,1,0:T(8,128)(2,1)}), bf16[8,64,1664]{2,1,0:T(8,128)(2,1)S(1)}, u32[]{:S(2)}, u32[]{:S(2)}) async-start(bf16[8,64,1664]{2,1,0:T(8,128)(2,1)} %shard_map.198), calls=%async_computation | async-start | bytes 3407872 | tf_op jit(solution)/shard_map/all_to_all | solution.py:608
  19.0 3.5 %collective-permute-start.2 = (bf16[32,512]{1,0:T(8,128)(2,1)S(1)}, bf16[32,512]{1,0:T(8,128)(2,1)S(1)}, u32[]{:S(2)}, u32[]{:S(2)}) collective-permute-start(bf16[32,512]{1,0:T(8,128)(2,1)S(1)} %get-tuple-element.53), channel_id=1, source_target_pairs={{0,4},{4,16},{16,20},{20,0},{1,5},{5,17},{17,21},{21,1},{2,6},{6,1... | collective-permute-start | bytes 98312 | tf_op jit(solution)/shard_map/ppermute | solution.py:600
  24.5 19.0 %collective-permute-done.2 = bf16[32,512]{1,0:T(8,128)(2,1)S(1)} collective-permute-done((bf16[32,512]{1,0:T(8,128)(2,1)S(1)}, bf16[32,512]{1,0:T(8,128)(2,1)S(1)}, u32[]{:S(2)}, u32[]{:S(2)}) %collective-permute-start.2) | collective-permute-done | bytes 32800 | tf_op jit(solution)/shard_map/ppermute | solution.py:600
  50.5 3.7 %collective-permute-done.6.refs_2_ = bf16[128,512]{1,0:T(8,128)(2,1)S(1)} collective-permute-done((bf16[128,512]{1,0:T(8,128)(2,1)S(1)}, bf16[128,512]{1,0:T(8,128)(2,1)S(1)}, u32[]{:S(2)}, u32[]{:S(2)}) %collective-permute-start.6) | collective-permute-done | bytes 131104 | tf_op jit(solution)/shard_map/ppermute | solution.py:600
  58.3 2.9 %collective-permute-start.9 = (bf16[256,512]{1,0:T(8,128)(2,1)S(1)}, bf16[256,512]{1,0:T(8,128)(2,1)S(1)}, u32[]{:S(2)}, u32[]{:S(2)}) collective-permute-start(bf16[256,512]{1,0:T(8,128)(2,1)S(1)} %get-tuple-element.54.refs_0_.refs_4_), channel_id=1, source_target_pairs={{0,64},{32,96},{64,0},{96,32},{1,65},{33,97},{65,1},{97,33},{2,66}... | collective-permute-start | bytes 786440 | tf_op jit(solution)/shard_map/ppermute | solution.py:600
  62.5 3.4 %collective-permute-done.8.refs_1_.refs_5_ = bf16[256,512]{1,0:T(8,128)(2,1)S(1)} collective-permute-done((bf16[256,512]{1,0:T(8,128)(2,1)S(1)}, bf16[256,512]{1,0:T(8,128)(2,1)S(1)}, u32[]{:S(2)}, u32[]{:S(2)}) %collective-permute-start.8) | collective-permute-done | bytes 262176 | tf_op jit(solution)/shard_map/ppermute | solution.py:600
  66.0 5.8 %collective-permute-done.9.refs_2_.refs_6_ = bf16[256,512]{1,0:T(8,128)(2,1)S(1)} collective-permute-done((bf16[256,512]{1,0:T(8,128)(2,1)S(1)}, bf16[256,512]{1,0:T(8,128)(2,1)S(1)}, u32[]{:S(2)}, u32[]{:S(2)}) %collective-permute-start.9) | collective-permute-done | bytes 262176 | tf_op jit(solution)/shard_map/ppermute | solution.py:600
  73.8 6.3 %shard_map.200 = (bf16[512,1536]{1,0:T(8,128)(2,1)}, bf16[512,512]{1,0:T(8,128)(2,1)}, f32[512,512]{1,0:T(8,128)}, f32[512,128]{1,0:T(8,128)}, bf16[512,512]{1,0...) custom-call(s32[12]{0:T(128)S(1)} %concatenate.7.scal, ...), custom_call_target="tpu_custom_call" | custom-call | flops 1073741824 | bytes 10623024 | tf_op jit(solution)/shard_map/pallas_call | solution.py:459
  80.2 4.7 %all-to-all-start.1 = ((f32[8,128,512]{2,1,0:T(8,128)}), f32[8,128,512]{2,1,0:T(8,128)S(1)}, u32[]{:S(2)}, u32[]{:S(2)}) async-start(f32[8,128,512]{2,1,0:T(8,128)} %get-tuple-element.55), calls=%async_computation.1 | async-start | bytes 4194304 | tf_op jit(solution)/shard_map/all_to_all | solution.py:608
  90.8 2.8 %collective-permute-done.15.refs_1_ = bf16[192,512]{1,0:T(8,128)(2,1)S(1)} collective-permute-done((bf16[192,512]{1,0:T(8,128)(2,1)S(1)}, bf16[192,512]{1,0:T(8,128)(2,1)S(1)}, u32[]{:S(2)}, u32[]{:S(2)}) %collective-permute-start.15) | collective-permute-done | bytes 196640 | tf_op jit(solution)/shard_map/ppermute | solution.py:600
  93.6 4.0 %collective-permute-done.16.refs_2_ = bf16[192,512]{1,0:T(8,128)(2,1)S(1)} collective-permute-done((bf16[192,512]{1,0:T(8,128)(2,1)S(1)}, bf16[192,512]{1,0:T(8,128)(2,1)S(1)}, u32[]{:S(2)}, u32[]{:S(2)}) %collective-permute-start.16) | collective-permute-done | bytes 196640 | tf_op jit(solution)/shard_map/ppermute | solution.py:600
  99.4 12.3 %all-to-all-done.1.spread = f32[8,128,512]{2,1,0:T(8,128)S(1)} async-done(((f32[8,128,512]{2,1,0:T(8,128)}), f32[8,128,512]{2,1,0:T(8,128)S(1)}, u32[]{:S(2)}, u32[]{:S(2)}) %all-to-all-start.1) | async-done | bytes 2097184 | tf_op jit(solution)/shard_map/all_to_all | solution.py:608
  111.7 4.0 %shard_map.201 = (bf16[8,512,128]{2,1,0:T(8,128)(2,1)S(1)}, bf16[512,128]{1,0:T(8,128)(2,1)}, f32[512,128]{1,0:T(8,128)}, bf16[128,1024]{1,0:T(8,128)(2,1)}, bf1...) custom-call(s32[3]{0:T(128)S(1)} %pad_add_fusion.scal, ...), custom_call_target="tpu_custom_call" | custom-call | flops 402653184 | bytes 6031372 | tf_op jit(solution)/shard_map/pallas_call | solution.py:459
  115.6 22.0 %all_to_all.20.d_agg = bf16[8,512,128]{2,1,0:T(8,128)(2,1)S(1)} all-to-all(bf16[8,512,128]{2,1,0:T(8,128)(2,1)S(1)} %get-tuple-element.59), channel_id=1, replica_groups=mesh['y'=4,'xl'=2,'c'=2,'xh'=2,'z'=4] {'xh','z'}, dimensions={0} | all-to-all | bytes 2097152 | tf_op jit(solution)/shard_map/all_to_all | solution.py:608
  137.7 6.3 %shard_map.202 = (bf16[512,512]{1,0:T(8,128)(2,1)S(1)}, bf16[512,512]{1,0:T(8,128)(2,1)}, bf16[4,256,512]{2,1,0:T(8,128)(2,1)S(1)}, bf16[4,256,512]{2,1,0:T(8,128)(2,1)}) custom-call(s32[12]{0:T(128)S(1)} %concatenate.7.scal, bf16[8,512,128]{2,1,0:T(8,128)(2,1)S(1)} %all_to_all.20.d_agg, bf16[512,512]{1,0:T(8,128)(2,1)S(1)} %copy-done.6, ...), custom_call_target="tpu_custom_call" | custom-call | flops 1342177280 | bytes 10229808 | tf_op jit(solution)/shard_map/pallas_call | solution.py:459
  144.1 3.3 %shard_map.207 = (bf16[4,192,512]{2,1,0:T(8,128)(2,1)S(1)}, bf16[4,192,512]{2,1,0:T(8,128)(2,1)}) custom-call(s32[3]{0:T(128)S(1)} %pad_add_fusion.scal, bf16[128,1024]{1,0:T(8,128)(2,1)} %get-tuple-element.76.refs_0_, bf16[128,512]{1,0:T(8,128)(2,1)} %get-tuple-element.77.refs_1_, bf16[128,512]{1,0:T(8,128)(2,1)} %get-tuple-element.78.refs_2_, ...), custom_call_target="tpu_custom_call" | custom-call | flops 201326592 | bytes 2228236 | tf_op jit(solution)/shard_map/pallas_call | solution.py:459
  148.0 3.8 %shard_map.203 = (f32[8,512,128]{2,1,0:T(8,128)S(1)}, bf16[512,256]{1,0:T(8,128)(2,1)S(1)}, bf16[512,256]{1,0:T(8,128)(2,1)S(1)}) custom-call(s32[12]{0:T(128)S(1)} %concatenate.7.scal, bf16[512,512]{1,0:T(8,128)(2,1)S(1)} %get-tuple-element.64.d_first, s32[2,4,128]{2,1,0:T(4,128)S(1)} %reshape.65.offsets, f32[512,128]{1,0:T(8,128)} %get-tuple-element.65.direct_in, ...), custom_call_target="tpu_custom_call" | custom-call | flops 536870912 | bytes 5509168 | tf_op jit(solution)/shard_map/pallas_call | solution.py:459
  153.1 3.0 %collective-permute-start.23 = (bf16[512,256]{1,0:T(8,128)(2,1)S(1)}, bf16[512,256]{1,0:T(8,128)(2,1)S(1)}, u32[]{:S(2)}, u32[]{:S(2)}) collective-permute-start(bf16[512,256]{1,0:T(8,128)(2,1)S(1)} %get-tuple-element.68), channel_id=1, source_target_pairs={{0,8},{8,16},{16,24},{24,32},{32,40},{40,48},{48,56},{56,64},{64,7... | collective-permute-start | bytes 786440 | tf_op jit(solution)/shard_map/ppermute | solution.py:33
  159.3 3.6 %all-to-all-start.3 = ((bf16[8,64,1152]{2,1,0:T(8,128)(2,1)}), bf16[8,64,1152]{2,1,0:T(8,128)(2,1)S(1)}, u32[]{:S(2)}, u32[]{:S(2)}) async-start(bf16[8,64,1152]{2,1,0:T(8,128)(2,1)} %shard_map.204), calls=%async_computation.3 | async-start | bytes 2359296 | tf_op jit(solution)/shard_map/all_to_all | solution.py:608
  164.3 6.8 %collective-permute-start.29 = (bf16[192,512]{1,0:T(8,128)(2,1)S(1)}, bf16[192,512]{1,0:T(8,128)(2,1)S(1)}, u32[]{:S(2)}, u32[]{:S(2)}) collective-permute-start(bf16[192,512]{1,0:T(8,128)(2,1)S(1)} %get-tuple-element.100), channel_id=1, source_target_pairs={{0,32},{32,64},{64,96},{96,0},{1,33},{33,65},{65,97},{97,1},{2,34}... | collective-permute-start | bytes 589832 | tf_op jit(solution)/shard_map/ppermute | solution.py:600
  180.6 12.1 %collective-permute-done.30.n2 = bf16[192,512]{1,0:T(8,128)(2,1)S(1)} collective-permute-done((bf16[192,512]{1,0:T(8,128)(2,1)S(1)}, bf16[192,512]{1,0:T(8,128)(2,1)S(1)}, u32[]{:S(2)}, u32[]{:S(2)}) %collective-permute-start.30) | collective-permute-done | bytes 196640 | tf_op jit(solution)/shard_map/ppermute | solution.py:600
  205.6 3.1 %collective-permute-start.35 = (bf16[32,512]{1,0:T(8,128)(2,1)S(1)}, bf16[32,512]{1,0:T(8,128)(2,1)S(1)}, u32[]{:S(2)}, u32[]{:S(2)}) collective-permute-start(bf16[32,512]{1,0:T(8,128)(2,1)S(1)} %get-tuple-element.87), channel_id=1, source_target_pairs={{0,4},{4,16},{16,20},{20,0},{1,5},{5,17},{17,21},{21,1},{2,6},{6,1... | collective-permute-start | bytes 98312 | tf_op jit(solution)/shard_map/ppermute | solution.py:600
  210.2 3.8 %shard_map.206 = bf16[512,512]{1,0:T(8,128)(2,1)} custom-call(s32[12]{0:T(128)S(1)} %concatenate.7.scal, bf16[512,512]{1,0:T(8,128)(2,1)} %get-tuple-element.73.d_first_in, bf16[512,512]{1,0:T(8,128)(2,1)} %cot_in.1, bf16[256,512]{1,0:T(8,128)(2,1)} %copy-done, bf16[256,512]{1,0:T(8,128)(2,1)} %copy-done.1, bf16[256,512]{1,0:T(8,128)(2,1)} %copy-done.2, ...), custom_call_target="tpu_custom_call" | custom-call | flops 268435456 | bytes 3670064 | tf_op jit(solution)/shard_map/pallas_call | solution.py:459
  (116 shorter events, 63.2 us)
Async XLA Ops:
  11.4 62.4 %all-to-all-start = ((bf16[8,64,1664]{2,1,0:T(8,128)(2,1)}), bf16[8,64,1664]{2,1,0:T(8,128)(2,1)S(1)}, u32[]{:S(2)}, u32[]{:S(2)}) async-start(bf16[8,64,1664]{2,1,0:T(8,128)(2,1)} %shard_map.198), calls=%async_computation | async-start | bytes 3407872 | tf_op jit(solution)/shard_map/all_to_all | solution.py:608
  19.0 24.5 %collective-permute-start.2 = (bf16[32,512]{1,0:T(8,128)(2,1)S(1)}, bf16[32,512]{1,0:T(8,128)(2,1)S(1)}, u32[]{:S(2)}, u32[]{:S(2)}) collective-permute-start(bf16[32,512]{1,0:T(8,128)(2,1)S(1)} %get-tuple-element.53), channel_id=1, source_target_pairs={{0,4},{4,16},{16,20},{20,0},{1,5},{5,17},{17,21},{21,1},{2,6},{6,1... | collective-permute-start | bytes 98312 | tf_op jit(solution)/shard_map/ppermute | solution.py:600
  22.6 21.0 %collective-permute-start.3 = (bf16[32,512]{1,0:T(8,128)(2,1)S(1)}, bf16[32,512]{1,0:T(8,128)(2,1)S(1)}, u32[]{:S(2)}, u32[]{:S(2)}) collective-permute-start(bf16[32,512]{1,0:T(8,128)(2,1)S(1)} %get-tuple-element.53), channel_id=1, source_target_pairs={{0,16},{4,20},{16,0},{20,4},{1,17},{5,21},{17,1},{21,5},{2,18},{6,... | collective-permute-start | bytes 98312 | tf_op jit(solution)/shard_map/ppermute | solution.py:600
  24.5 19.1 %collective-permute-start.4 = (bf16[32,512]{1,0:T(8,128)(2,1)S(1)}, bf16[32,512]{1,0:T(8,128)(2,1)S(1)}, u32[]{:S(2)}, u32[]{:S(2)}) collective-permute-start(bf16[32,512]{1,0:T(8,128)(2,1)S(1)} %get-tuple-element.53), channel_id=1, source_target_pairs={{0,20},{4,0},{16,4},{20,16},{1,21},{5,1},{17,5},{21,17},{2,22},{6,... | collective-permute-start | bytes 98312 | tf_op jit(solution)/shard_map/ppermute | solution.py:600
  45.1 9.1 %collective-permute-start.6 = (bf16[128,512]{1,0:T(8,128)(2,1)S(1)}, bf16[128,512]{1,0:T(8,128)(2,1)S(1)}, u32[]{:S(2)}, u32[]{:S(2)}) collective-permute-start(bf16[128,512]{1,0:T(8,128)(2,1)S(1)} %constant_dynamic-update-slice_fusion.refs_0_), channel_id=1, source_target_pairs={{0,2},{1,3},{2,0},{3,1},{4,6},{5,7},{6,4},{7,5},{8,10},{9,11},{10,... | collective-permute-start | bytes 393224 | tf_op jit(solution)/shard_map/ppermute | solution.py:600
  55.5 10.4 %collective-permute-start.8 = (bf16[256,512]{1,0:T(8,128)(2,1)S(1)}, bf16[256,512]{1,0:T(8,128)(2,1)S(1)}, u32[]{:S(2)}, u32[]{:S(2)}) collective-permute-start(bf16[256,512]{1,0:T(8,128)(2,1)S(1)} %get-tuple-element.54.refs_0_.refs_4_), channel_id=1, source_target_pairs={{0,32},{32,64},{64,96},{96,0},{1,33},{33,65},{65,97},{97,1},{2,34}... | collective-permute-start | bytes 786440 | tf_op jit(solution)/shard_map/ppermute | solution.py:600
  58.3 13.5 %collective-permute-start.9 = (bf16[256,512]{1,0:T(8,128)(2,1)S(1)}, bf16[256,512]{1,0:T(8,128)(2,1)S(1)}, u32[]{:S(2)}, u32[]{:S(2)}) collective-permute-start(bf16[256,512]{1,0:T(8,128)(2,1)S(1)} %get-tuple-element.54.refs_0_.refs_4_), channel_id=1, source_target_pairs={{0,64},{32,96},{64,0},{96,32},{1,65},{33,97},{65,1},{97,33},{2,66}... | collective-permute-start | bytes 786440 | tf_op jit(solution)/shard_map/ppermute | solution.py:600
  61.2 10.6 %collective-permute-start.10 = (bf16[256,512]{1,0:T(8,128)(2,1)S(1)}, bf16[256,512]{1,0:T(8,128)(2,1)S(1)}, u32[]{:S(2)}, u32[]{:S(2)}) collective-permute-start(bf16[256,512]{1,0:T(8,128)(2,1)S(1)} %get-tuple-element.54.refs_0_.refs_4_), channel_id=1, source_target_pairs={{0,96},{32,0},{64,32},{96,64},{1,97},{33,1},{65,33},{97,65},{2,98}... | collective-permute-start | bytes 786440 | tf_op jit(solution)/shard_map/ppermute | solution.py:600
  62.5 10.6 %collective-permute-start.11 = (bf16[256,512]{1,0:T(8,128)(2,1)S(1)}, bf16[256,512]{1,0:T(8,128)(2,1)S(1)}, u32[]{:S(2)}, u32[]{:S(2)}) collective-permute-start(bf16[256,512]{1,0:T(8,128)(2,1)S(1)} %get-tuple-element.54.refs_0_.refs_4_), channel_id=1, source_target_pairs={{0,8},{8,0},{1,9},{9,1},{2,10},{10,2},{3,11},{11,3},{4,12},{12,4},... | collective-permute-start | bytes 786440 | tf_op jit(solution)/shard_map/ppermute | solution.py:595
  80.2 31.4 %all-to-all-start.1 = ((f32[8,128,512]{2,1,0:T(8,128)}), f32[8,128,512]{2,1,0:T(8,128)S(1)}, u32[]{:S(2)}, u32[]{:S(2)}) async-start(f32[8,128,512]{2,1,0:T(8,128)} %get-tuple-element.55), calls=%async_computation.1 | async-start | bytes 4194304 | tf_op jit(solution)/shard_map/all_to_all | solution.py:608
  84.9 8.6 %collective-permute-start.15 = (bf16[192,512]{1,0:T(8,128)(2,1)S(1)}, bf16[192,512]{1,0:T(8,128)(2,1)S(1)}, u32[]{:S(2)}, u32[]{:S(2)}) collective-permute-start(bf16[192,512]{1,0:T(8,128)(2,1)S(1)} %copy-done.8), channel_id=1, source_target_pairs={{0,32},{32,64},{64,96},{96,0},{1,33},{33,65},{65,97},{97,1},{2,34}... | collective-permute-start | bytes 589832 | tf_op jit(solution)/shard_map/ppermute | solution.py:600
  86.3 11.2 %collective-permute-start.16 = (bf16[192,512]{1,0:T(8,128)(2,1)S(1)}, bf16[192,512]{1,0:T(8,128)(2,1)S(1)}, u32[]{:S(2)}, u32[]{:S(2)}) collective-permute-start(bf16[192,512]{1,0:T(8,128)(2,1)S(1)} %copy-done.8), channel_id=1, source_target_pairs={{0,64},{32,96},{64,0},{96,32},{1,65},{33,97},{65,1},{97,33},{2,66}... | collective-permute-start | bytes 589832 | tf_op jit(solution)/shard_map/ppermute | solution.py:600
  88.7 9.0 %collective-permute-start.17 = (bf16[192,512]{1,0:T(8,128)(2,1)S(1)}, bf16[192,512]{1,0:T(8,128)(2,1)S(1)}, u32[]{:S(2)}, u32[]{:S(2)}) collective-permute-start(bf16[192,512]{1,0:T(8,128)(2,1)S(1)} %copy-done.8), channel_id=1, source_target_pairs={{0,96},{32,0},{64,32},{96,64},{1,97},{33,1},{65,33},{97,65},{2,98}... | collective-permute-start | bytes 589832 | tf_op jit(solution)/shard_map/ppermute | solution.py:600
  90.8 7.3 %collective-permute-start.18 = (bf16[192,512]{1,0:T(8,128)(2,1)S(1)}, bf16[192,512]{1,0:T(8,128)(2,1)S(1)}, u32[]{:S(2)}, u32[]{:S(2)}) collective-permute-start(bf16[192,512]{1,0:T(8,128)(2,1)S(1)} %copy-done.8), channel_id=1, source_target_pairs={{0,8},{8,0},{1,9},{9,1},{2,10},{10,2},{3,11},{11,3},{4,12},{12,4},... | collective-permute-start | bytes 589832 | tf_op jit(solution)/shard_map/ppermute | solution.py:595
  144.0 27.1 %collective-permute-start.24 = (bf16[4,256,512]{2,1,0:T(8,128)(2,1)}, bf16[4,256,512]{2,1,0:T(8,128)(2,1)}, u32[]{:S(2)}, u32[]{:S(2)}) collective-permute-start(bf16[4,256,512]{2,1,0:T(8,128)(2,1)} %get-tuple-element.75), channel_id=1, source_target_pairs={{0,8},{8,0},{1,9},{9,1},{2,10},{10,2},{3,11},{11,3},{4,12},{12,4},... | collective-permute-start | bytes 3145736 | tf_op jit(solution)/shard_map/ppermute | solution.py:595
  147.4 15.5 %collective-permute-start.28 = (bf16[4,192,512]{2,1,0:T(8,128)(2,1)}, bf16[4,192,512]{2,1,0:T(8,128)(2,1)}, u32[]{:S(2)}, u32[]{:S(2)}) collective-permute-start(bf16[4,192,512]{2,1,0:T(8,128)(2,1)} %get-tuple-element.81), channel_id=1, source_target_pairs={{0,8},{8,0},{1,9},{9,1},{2,10},{10,2},{3,11},{11,3},{4,12},{12,4},... | collective-permute-start | bytes 2359304 | tf_op jit(solution)/shard_map/ppermute | solution.py:595
  159.3 54.7 %all-to-all-start.3 = ((bf16[8,64,1152]{2,1,0:T(8,128)(2,1)}), bf16[8,64,1152]{2,1,0:T(8,128)(2,1)S(1)}, u32[]{:S(2)}, u32[]{:S(2)}) async-start(bf16[8,64,1152]{2,1,0:T(8,128)(2,1)} %shard_map.204), calls=%async_computation.3 | async-start | bytes 2359296 | tf_op jit(solution)/shard_map/all_to_all | solution.py:608
  164.3 14.5 %collective-permute-start.29 = (bf16[192,512]{1,0:T(8,128)(2,1)S(1)}, bf16[192,512]{1,0:T(8,128)(2,1)S(1)}, u32[]{:S(2)}, u32[]{:S(2)}) collective-permute-start(bf16[192,512]{1,0:T(8,128)(2,1)S(1)} %get-tuple-element.100), channel_id=1, source_target_pairs={{0,32},{32,64},{64,96},{96,0},{1,33},{33,65},{65,97},{97,1},{2,34}... | collective-permute-start | bytes 589832 | tf_op jit(solution)/shard_map/ppermute | solution.py:600
  172.6 22.0 %collective-permute-start.25 = (bf16[256,512]{1,0:T(8,128)(2,1)S(1)}, bf16[256,512]{1,0:T(8,128)(2,1)S(1)}, u32[]{:S(2)}, u32[]{:S(2)}) collective-permute-start(bf16[256,512]{1,0:T(8,128)(2,1)S(1)} %get-tuple-element.96), channel_id=1, source_target_pairs={{0,32},{32,64},{64,96},{96,0},{1,33},{33,65},{65,97},{97,1},{2,34}... | collective-permute-start | bytes 786440 | tf_op jit(solution)/shard_map/ppermute | solution.py:600
  174.1 20.5 %collective-permute-start.26 = (bf16[256,512]{1,0:T(8,128)(2,1)S(1)}, bf16[256,512]{1,0:T(8,128)(2,1)S(1)}, u32[]{:S(2)}, u32[]{:S(2)}) collective-permute-start(bf16[256,512]{1,0:T(8,128)(2,1)S(1)} %get-tuple-element.95), channel_id=1, source_target_pairs={{0,64},{32,96},{64,0},{96,32},{1,65},{33,97},{65,1},{97,33},{2,66}... | collective-permute-start | bytes 786440 | tf_op jit(solution)/shard_map/ppermute | solution.py:600
  175.9 18.7 %collective-permute-start.27 = (bf16[256,512]{1,0:T(8,128)(2,1)S(1)}, bf16[256,512]{1,0:T(8,128)(2,1)S(1)}, u32[]{:S(2)}, u32[]{:S(2)}) collective-permute-start(bf16[256,512]{1,0:T(8,128)(2,1)S(1)} %get-tuple-element.94), channel_id=1, source_target_pairs={{0,96},{32,0},{64,32},{96,64},{1,97},{33,1},{65,33},{97,65},{2,98}... | collective-permute-start | bytes 786440 | tf_op jit(solution)/shard_map/ppermute | solution.py:600
  178.4 14.2 %collective-permute-start.30 = (bf16[192,512]{1,0:T(8,128)(2,1)S(1)}, bf16[192,512]{1,0:T(8,128)(2,1)S(1)}, u32[]{:S(2)}, u32[]{:S(2)}) collective-permute-start(bf16[192,512]{1,0:T(8,128)(2,1)S(1)} %get-tuple-element.99), channel_id=1, source_target_pairs={{0,64},{32,96},{64,0},{96,32},{1,65},{33,97},{65,1},{97,33},{2,66}... | collective-permute-start | bytes 589832 | tf_op jit(solution)/shard_map/ppermute | solution.py:600
  178.8 15.8 %collective-permute-start.31 = (bf16[192,512]{1,0:T(8,128)(2,1)S(1)}, bf16[192,512]{1,0:T(8,128)(2,1)S(1)}, u32[]{:S(2)}, u32[]{:S(2)}) collective-permute-start(bf16[192,512]{1,0:T(8,128)(2,1)S(1)} %get-tuple-element.98), channel_id=1, source_target_pairs={{0,96},{32,0},{64,32},{96,64},{1,97},{33,1},{65,33},{97,65},{2,98}... | collective-permute-start | bytes 589832 | tf_op jit(solution)/shard_map/ppermute | solution.py:600
  205.6 9.2 %collective-permute-start.35 = (bf16[32,512]{1,0:T(8,128)(2,1)S(1)}, bf16[32,512]{1,0:T(8,128)(2,1)S(1)}, u32[]{:S(2)}, u32[]{:S(2)}) collective-permute-start(bf16[32,512]{1,0:T(8,128)(2,1)S(1)} %get-tuple-element.87), channel_id=1, source_target_pairs={{0,4},{4,16},{16,20},{20,0},{1,5},{5,17},{17,21},{21,1},{2,6},{6,1... | collective-permute-start | bytes 98312 | tf_op jit(solution)/shard_map/ppermute | solution.py:600
  (33 other events, 419.1 us)
